TPU v7x, 256 devices: a whole 4x4x8 slice. The times are simulated.
256 devices in a mesh: img: 16 (over z, core), txt: 16 (over x, y).
Axes of the slice: x: 4, y: 4, z: 8, core: 2. Of those that a mesh axis runs over, the one named last changes fastest.
Arguments:
- teacher_img: bfloat16 [16384, 1280], P('img'), may hold values from -40 to 40
- teacher_txt: bfloat16 [16384, 1280], P('txt'), may hold values from -40 to 40
- student_img: bfloat16 [16384, 512], P('img'), may hold values from -40 to 40
- student_txt: bfloat16 [16384, 512], P('txt'), may hold values from -40 to 40
Outputs:
- loss: float32 [], replicated
- grad_img: float32 [16384, 512], P(('img', 'txt'))
- grad_txt: float32 [16384, 512], P(('txt', 'img'))
All inputs are finite; a program needn't handle non-finite values.
Results may differ from a plain program's by a relative error of at most 0.0033.
Values sent between devices are 32-bit elements; how exact they have to be, the bound alone decides.
No kernel may reach another device: no remote copies, remote signals or barrier semaphores. Data moves between devices by JAX's collectives and lax.ppermute only.
A program may use at most 64 MiB of HBM per device.

v0:
```python
import math

import jax
import jax.numpy as jnp
from jax import lax
from jax.sharding import Mesh
from jax.sharding import PartitionSpec as P

IMG = ("img_0", "img_1")
TXT = ("txt_0", "txt_1")
IMG_TXT = ("img_0", "img_1", "txt_0", "txt_1")
TXT_IMG = ("txt_0", "txt_1", "img_0", "img_1")


def from_everyone(shard, axis):
    copies = jnp.broadcast_to(shard, (lax.axis_size(axis), *shard.shape))
    return lax.all_to_all(copies, axis, split_axis=0, concat_axis=0, tiled=True)


def collected_together(shard, axis):
    leaves = jax.tree.leaves(shard)
    order = sorted(range(len(leaves)), key=lambda k: -leaves[k].size)
    width = (1, *leaves[order[0]].shape)[-1]
    lines = [
        jnp.pad(leaves[k].reshape(-1), (0, -leaves[k].size % width)).reshape(-1, width)
        for k in order
    ]
    both, at, found = (from_everyone(jnp.concatenate(lines), axis), 0, {})
    for k, line in zip(order, lines):
        piece = both[:, at : at + len(line)].reshape(len(both), -1)
        found[k] = piece[:, : leaves[k].size].reshape(-1, *leaves[k].shape)
        at += len(line)
    numbers = iter(range(len(leaves)))
    return jax.tree.map(lambda _: found[next(numbers)], shard)


def combined_pairwise(pieces, combine):
    while len(jax.tree.leaves(pieces)[0]) > 1:
        pieces = jax.vmap(combine)(
            *(jax.tree.map(lambda part: part[side::2], pieces) for side in (0, 1))
        )
    return jax.tree.map(lambda part: part[0], pieces)


def joined_all(shard, axis, combine):
    pieces = collected_together(shard, axis)
    return combined_pairwise(pieces, combine)


def over_axes(shard, axes):
    for axis in axes:
        shard = lax.psum(shard, axis)
    return shard


def split_up(shard, dim, size):
    dims = shard.shape
    parts = shard.reshape(*dims[:dim], size, dims[dim] // size, *dims[dim + 1 :])
    return jnp.moveaxis(parts, dim, 0)


def sum_by_chip(shard, chips, core, dim):
    sizes = (lax.axis_size(chips), lax.axis_size(core))
    parts = split_up(shard, dim, sizes[0] * sizes[1])
    inside = parts.shape[1:]
    parts = parts.reshape(*sizes, *inside).swapaxes(0, 1).reshape(-1, *inside)
    parts = lax.psum_scatter(parts, core, scatter_dimension=0, tiled=True)
    return lax.psum_scatter(parts, chips, scatter_dimension=0, tiled=True)[0]


def summed_on_arrival(shard, axis, dim):
    size = lax.axis_size(axis)
    parts = lax.all_to_all(split_up(shard, dim, size), axis, 0, 0, tiled=True)
    return jnp.sum(parts, axis=0)


def join_pair(peak_one, mass_one, peak_two, mass_two):
    highest = jnp.maximum(peak_one, peak_two)
    return (
        highest,
        mass_one * jnp.exp(peak_one - highest) + mass_two * jnp.exp(peak_two - highest),
    )


def combine_masses(first, second):
    teach_peak, teach_mass = join_pair(first[0], first[1], second[0], second[1])
    learn_peak, learn_mass = join_pair(first[2], first[3], second[2], second[3])
    return (teach_peak, teach_mass, learn_peak, learn_mass)


def local_masses(teacher, student, along):
    teach_peak = jnp.max(teacher, axis=along)
    learn_peak = jnp.max(student, axis=along)
    teach_mass = jnp.sum(jnp.exp(teacher - jnp.expand_dims(teach_peak, along)), axis=along)
    learn_mass = jnp.sum(jnp.exp(student - jnp.expand_dims(learn_peak, along)), axis=along)
    return (teach_peak, teach_mass, learn_peak, learn_mass)


def body(teacher_img, teacher_txt, student_img, student_txt):
    scale_teach = 3.0 / math.sqrt(teacher_img.shape[1])
    scale_learn = 3.0 / math.sqrt(student_img.shape[1])
    rows = teacher_img.shape[0]
    cols = teacher_txt.shape[0]
    img_count = lax.axis_size(IMG)
    txt_count = lax.axis_size(TXT)
    teacher = scale_teach * jnp.einsum(
        "id,jd->ij", teacher_img, teacher_txt, preferred_element_type=jnp.float32
    )
    student = scale_learn * jnp.einsum(
        "id,jd->ij", student_img, student_txt, preferred_element_type=jnp.float32
    )
    row_tpeak, row_tmass, row_lpeak, row_lmass = joined_all(
        local_masses(teacher, student, 1), TXT, combine_masses
    )
    col_tpeak, col_tmass, col_lpeak, col_lmass = joined_all(
        local_masses(teacher, student, 0), IMG, combine_masses
    )
    row_teach = row_tpeak + jnp.log(row_tmass)
    row_learn = row_lpeak + jnp.log(row_lmass)
    col_teach = col_tpeak + jnp.log(col_tmass)
    col_learn = col_lpeak + jnp.log(col_lmass)
    p_row = jnp.exp(teacher - row_teach[:, None])
    q_row = jnp.exp(student - row_learn[:, None])
    p_col = jnp.exp(teacher - col_teach[None, :])
    q_col = jnp.exp(student - col_learn[None, :])
    gap = teacher - student
    row_part = (jnp.sum(p_row * gap) + jnp.sum(row_learn - row_teach) / txt_count) / (
        rows * img_count
    )
    col_part = (jnp.sum(p_col * gap) + jnp.sum(col_learn - col_teach) / img_count) / (
        cols * txt_count
    )
    delta = (8.0 * (q_row - p_row + q_col - p_col)).astype(jnp.bfloat16)
    loss = 0.5 * over_axes(row_part + col_part, IMG_TXT)
    picked = delta
    grad_txt = sum_by_chip(
        scale_learn
        * jnp.einsum("ij,id->jd", picked, student_img, preferred_element_type=jnp.float32),
        "img_0",
        "img_1",
        0,
    )
    picked = delta
    grad_img = summed_on_arrival(
        scale_learn * jnp.dot(picked, student_txt, preferred_element_type=jnp.float32), TXT, 0
    )
    return (loss, grad_img, grad_txt)


def solution(mesh):
    torus = Mesh(mesh.devices.reshape(8, 2, 4, 4), ("img_0", "img_1", "txt_0", "txt_1"))
    in_specs = (P(IMG, None), P(TXT, None), P(IMG, None), P(TXT, None))
    out_specs = (P(), P(IMG_TXT, None), P(TXT_IMG, None))
    return jax.shard_map(body, mesh=torus, in_specs=in_specs, out_specs=out_specs, check_vma=False)
```

profile of v0, /device:TPU:1, one launch (start us, length us, event | category | flops | bytes accessed | tf_op | source)
XLA Modules:
  0.0 145.4 jit_solution(15397041045933169511)
XLA Ops:
  7.2 0.0 copy-start
  7.2 1.7 %copy-done = bf16[1024,1280]{1,0:T(8,128)(2,1)S(1)} copy-done((bf16[1024,1280]{1,0:T(8,128)(2,1)S(1)}, bf16[1024,1280]{1,0:T(8,128)(2,1)}, u32[]{:S(2)}) %copy-start) | copy-done | bytes 2621464
  8.9 4.8 %multiply_reduce_fusion.4 = (f32[1024]{0:T(1024)S(1)}, f32[1024]{0:T(1024)S(1)}, f32[1024,1024]{1,0:T(8,128)S(1)}) fusion(bf16[1024,1280]{1,0:T(8,128)(2,1)S(1)} %copy-done, bf16[1024,1280]{1,0:T(8,128)(2,1)} %param.5), kind=kOutput, calls=%fused_computation.12 | convolution fusion | flops 2687498240 | bytes 9445376 | tf_op jit(solution)/shard_map/id,jd->ij/dot_general | solution.py:106
  13.7 1.4 multiply_reduce_fusion.2
  15.1 0.6 copy-done.1
  15.7 1.6 %exponential_reduce_fusion.1 = (f32[1024]{0:T(1024)S(1)}, f32[1024]{0:T(1024)S(1)}) fusion(f32[1024,1024]{1,0:T(8,128)S(1)} %get-tuple-element.50, f32[1024]{0:T(1024)S(1)} %get-tuple-element.7, f32[1024]{0:T(1024)S(1)} %get-tuple-element.8), kind=kLoop, calls=%fused_computation.4 | loop fusion | flops 5240832 | bytes 4210688 | tf_op jit(solution)/shard_map/reduce_sum | solution.py:94
  17.3 1.6 %exponential_reduce_fusion = (f32[1024]{0:T(1024)S(1)}, f32[1024]{0:T(1024)S(1)}) fusion(f32[1024,1024]{1,0:T(8,128)S(1)} %get-tuple-element.49, f32[1024]{0:T(1024)S(1)} %get-tuple-element.11, f32[1024]{0:T(1024)S(1)} %get-tuple-element.12), kind=kLoop, calls=%fused_computation.3 | loop fusion | flops 5240832 | bytes 4210688 | tf_op jit(solution)/shard_map/reduce_sum | solution.py:95
  18.9 0.8 broadcast_in_dim.4
  19.6 7.6 %all-to-all-start = ((f32[16,4,1024]{2,1,0:T(4,128)}), f32[16,4,1024]{2,1,0:T(4,128)S(1)}, u32[]{:S(2)}, u32[]{:S(2)}) async-start(f32[16,4,1024]{2,1,0:T(4,128)} %broadcast_in_dim.4), calls=%async_computation | async-start | bytes 524288 | tf_op jit(solution)/shard_map/all_to_all | solution.py:17
  27.2 7.4 %all-to-all-done = f32[16,4,1024]{2,1,0:T(4,128)S(1)} async-done(((f32[16,4,1024]{2,1,0:T(4,128)}), f32[16,4,1024]{2,1,0:T(4,128)S(1)}, u32[]{:S(2)}, u32[]{:S(2)}) %all-to-all-start) | async-done | bytes 262176 | tf_op jit(solution)/shard_map/all_to_all | solution.py:17
  34.7 0.8 broadcast_in_dim.5
  35.4 10.5 %all-to-all-start.1 = ((f32[16,4,1024]{2,1,0:T(4,128)}), f32[16,4,1024]{2,1,0:T(4,128)S(1)}, u32[]{:S(2)}, u32[]{:S(2)}) async-start(f32[16,4,1024]{2,1,0:T(4,128)} %broadcast_in_dim.5), calls=%async_computation.1 | async-start | bytes 524288 | tf_op jit(solution)/shard_map/all_to_all | solution.py:17
  45.9 0.2 reduce-scatter.3.cloned.1.call-start
  46.1 0.2 fusion.8
  47.2 10.4 %all-to-all-done.1 = f32[16,4,1024]{2,1,0:T(4,128)S(1)} async-done(((f32[16,4,1024]{2,1,0:T(4,128)}), f32[16,4,1024]{2,1,0:T(4,128)S(1)}, u32[]{:S(2)}, u32[]{:S(2)}) %all-to-all-start.1) | async-done | bytes 262176 | tf_op jit(solution)/shard_map/all_to_all | solution.py:17
  57.6 0.2 fusion.9
  58.6 0.7 subtract_reduce_fusion
  59.3 9.1 %multiply_reduce_fusion = (f32[]{:T(128)}, f32[]{:T(128)}, bf16[1024,1024]{1,0:T(8,128)(2,1)S(1)}) fusion(f32[1024,1024]{1,0:T(8,128)} %copy-done.2, f32[1024,1024]{1,0:T(8,128)} %copy-done.1, f32[1024]{0:T(1024)S(1)} %bitcast.50, f32[1024]{0:T(1024)S(1)} %bitcast.47, f32[1024]{0:T(1024)S(1)} %bitcast.49, f32[1024]{0:T(1024)S(1)} %bitcast.45), kind=kLoop, calls=%fused_computation.1 | loop fusion | flops 16777214 | bytes 10502152 | tf_op jit(solution)/shard_map/reduce_sum | solution.py:130
  68.4 1.3 convolution_multiply_fusion
  69.7 1.6 %copy.21 = f32[2,8,64,512]{3,2,1,0:T(8,128)} copy(f32[2,8,64,512]{3,2,0,1:T(8,128)S(1)} %bitcast.44) | data formatting | bytes 4194304 | tf_op jit(solution)/shard_map/transpose | solution.py:66
  71.3 0.0 reduce-scatter.3.cloned.1.call-update
  71.3 0.0 reduce-scatter.5.cloned.1.call-start
  71.3 8.9 %reduce-scatter.3.cloned.1.call-done = f32[8,64,512]{2,1,0:T(8,128)} async-done(((f32[16,64,512]{2,1,0:T(8,128)}), f32[8,64,512]{2,1,0:T(8,128)}) %reduce-scatter.3.cloned.1.call-update) | async-done | bytes 1048592 | tf_op jit(solution)/shard_map/reduce_scatter | solution.py:67
  80.3 0.0 reduce-scatter.5.cloned.1.call-update
  80.3 4.5 %convolution_multiply_fusion.1 = f32[1024,512]{1,0:T(8,128)} fusion(bf16[1024,1024]{1,0:T(8,128)(2,1)} %copy-done.3, bf16[1024,512]{1,0:T(8,128)(2,1)} %param.7), kind=kOutput, calls=%fused_computation.15 | convolution fusion | flops 1074266112 | bytes 5242880 | tf_op jit(solution)/shard_map/dot_general | solution.py:145
  84.8 6.5 %all-to-all-start.2 = ((f32[16,64,512]{2,1,0:T(8,128)}), f32[16,64,512]{2,1,0:T(8,128)}, u32[]{:S(2)}, u32[]{:S(2)}) async-start(f32[16,64,512]{2,1,0:T(8,128)} %bitcast.43), calls=%async_computation.2 | async-start | bytes 4194304 | tf_op jit(solution)/shard_map/all_to_all | solution.py:73
  91.2 0.6 subtract_reduce_fusion.1
  94.3 15.8 %psum.28 = f32[]{:T(128)} all-reduce(f32[]{:T(128)S(6)} %add.127), channel_id=1, replica_groups=mesh['img_0'=8,'img_1'=2,'txt_0'=4,'txt_1'=4] {'img_0'}, use_global_device_ids=true, to_apply=%region_12.13 | all-reduce | flops 1 | bytes 8 | tf_op jit(solution)/shard_map/psum | solution.py:52
  110.2 5.4 %psum.29 = f32[]{:T(128)} all-reduce(f32[]{:T(128)} %psum.28), channel_id=1, replica_groups=mesh['img_0'=8,'img_1'=2,'txt_0'=4,'txt_1'=4] {'img_1'}, use_global_device_ids=true, to_apply=%region_13.14 | all-reduce | flops 1 | bytes 8 | tf_op jit(solution)/shard_map/psum | solution.py:52
  115.6 9.9 %psum.30 = f32[]{:T(128)} all-reduce(f32[]{:T(128)} %psum.29), channel_id=1, replica_groups=mesh['img_0'=8,'img_1'=2,'txt_0'=4,'txt_1'=4] {'txt_0'}, use_global_device_ids=true, to_apply=%region_14.15 | all-reduce | flops 1 | bytes 8 | tf_op jit(solution)/shard_map/psum | solution.py:52
  125.4 8.9 %psum.31 = f32[]{:T(128)} all-reduce(f32[]{:T(128)} %psum.30), channel_id=1, replica_groups=mesh['img_0'=8,'img_1'=2,'txt_0'=4,'txt_1'=4] {'txt_1'}, use_global_device_ids=true, to_apply=%region_15.16 | all-reduce | flops 1 | bytes 8 | tf_op jit(solution)/shard_map/psum | solution.py:52
  135.0 2.4 %reduce_sum.89 = f32[64,512]{1,0:T(8,128)} reduce(f32[16,64,512]{2,1,0:T(8,128)} %all-to-all-done.2, f32[]{:T(128)} %constant.4.clone.1), dimensions={0}, to_apply=%region_16.17 | reduce | flops 491520 | bytes 2228228 | tf_op jit(solution)/shard_map/reduce_sum | solution.py:74
  (81 shorter events, 1.6 us)
Async XLA Ops:
  7.2 1.7 %copy-start = (bf16[1024,1280]{1,0:T(8,128)(2,1)S(1)}, bf16[1024,1280]{1,0:T(8,128)(2,1)}, u32[]{:S(2)}) copy-start(bf16[1024,1280]{1,0:T(8,128)(2,1)} %param.4) | copy-start | bytes 7864324
  7.2 6.5 %copy-start.4 = (bf16[1024,512]{1,0:T(8,128)(2,1)S(1)}, bf16[1024,512]{1,0:T(8,128)(2,1)}, u32[]{:S(2)}) copy-start(bf16[1024,512]{1,0:T(8,128)(2,1)} %param.6) | copy-start | bytes 3145732
  8.9 4.8 %copy-start.6 = (bf16[1024,512]{1,0:T(8,128)(2,1)S(1)}, bf16[1024,512]{1,0:T(8,128)(2,1)}, u32[]{:S(2)}) copy-start(bf16[1024,512]{1,0:T(8,128)(2,1)} %param.7) | copy-start | bytes 3145732
  13.7 2.0 %copy-start.1 = (f32[1024,1024]{1,0:T(8,128)}, f32[1024,1024]{1,0:T(8,128)S(1)}, u32[]{:S(2)}) copy-start(f32[1024,1024]{1,0:T(8,128)S(1)} %get-tuple-element.50) | copy-start | bytes 12582916
  15.1 3.7 %copy-start.2 = (f32[1024,1024]{1,0:T(8,128)}, f32[1024,1024]{1,0:T(8,128)S(1)}, u32[]{:S(2)}) copy-start(f32[1024,1024]{1,0:T(8,128)S(1)} %get-tuple-element.49) | copy-start | bytes 12582916
  19.6 15.0 %all-to-all-start = ((f32[16,4,1024]{2,1,0:T(4,128)}), f32[16,4,1024]{2,1,0:T(4,128)S(1)}, u32[]{:S(2)}, u32[]{:S(2)}) async-start(f32[16,4,1024]{2,1,0:T(4,128)} %broadcast_in_dim.4), calls=%async_computation | async-start | bytes 524288 | tf_op jit(solution)/shard_map/all_to_all | solution.py:17
  35.4 22.2 %all-to-all-start.1 = ((f32[16,4,1024]{2,1,0:T(4,128)}), f32[16,4,1024]{2,1,0:T(4,128)S(1)}, u32[]{:S(2)}, u32[]{:S(2)}) async-start(f32[16,4,1024]{2,1,0:T(4,128)} %broadcast_in_dim.5), calls=%async_computation.1 | async-start | bytes 524288 | tf_op jit(solution)/shard_map/all_to_all | solution.py:17
  45.9 34.3 %reduce-scatter.3.cloned.1.call-start = ((), (), s32[]{:S(2)}) async-start(), calls=%async_computation.5 | async-start | bytes 3145728 | tf_op jit(solution)/shard_map/reduce_scatter | solution.py:67
  59.3 9.1 %copy-start.5 = (bf16[1024,512]{1,0:T(8,128)(2,1)S(1)}, bf16[1024,512]{1,0:T(8,128)(2,1)}, u32[]{:S(2)}) copy-start(bf16[1024,512]{1,0:T(8,128)(2,1)} %param.6) | copy-start | bytes 3145732
  68.4 2.9 %copy-start.3 = (bf16[1024,1024]{1,0:T(8,128)(2,1)}, bf16[1024,1024]{1,0:T(8,128)(2,1)S(1)}, u32[]{:S(2)}) copy-start(bf16[1024,1024]{1,0:T(8,128)(2,1)S(1)} %get-tuple-element.40) | copy-start | bytes 6291460
  71.3 66.2 %reduce-scatter.5.cloned.1.call-start = ((), (), s32[]{:S(2)}) async-start(), calls=%async_computation.6 | async-start | bytes 1179648 | tf_op jit(solution)/shard_map/reduce_scatter | solution.py:68
  84.8 50.3 %all-to-all-start.2 = ((f32[16,64,512]{2,1,0:T(8,128)}), f32[16,64,512]{2,1,0:T(8,128)}, u32[]{:S(2)}, u32[]{:S(2)}) async-start(f32[16,64,512]{2,1,0:T(8,128)} %bitcast.43), calls=%async_computation.2 | async-start | bytes 4194304 | tf_op jit(solution)/shard_map/all_to_all | solution.py:73
Sparse Core Ops, SparseCore 0:
  71.4 8.8 reduce-scatter.2
  83.5 35.6 reduce-scatter.4
where the time goes:
time: 147 us; the launch traced here: 145 us
  blocking collectives  40 us (27%)
  waiting for transfers between devices  26.8 us (18%)
  starting transfers between devices  24.8 us (17%)
  between operations  18.6 us (13%)
  other arithmetic  16.3 us (11%)
  matrix products  11.9 us (8%)
  local copies, waits for them, and re-layouts  7.03 us (5%)
    psum x4, blocking collectives, over_axes(): shard = lax.psum(shard, axis)  40 us
    all_to_all x2, starting transfers between devices, from_everyone(): return lax.all_to_all(copies, axis, split_axis=0, concat_axis=0, tiled=True)  18.1 us
    all_to_all x2, waiting for transfers between devices, from_everyone(): return lax.all_to_all(copies, axis, split_axis=0, concat_axis=0, tiled=True)  17.8 us
    reduce_sum x1, other arithmetic, body(): jnp.sum(p_col * gap) + jnp.sum(col_learn - col_teach) / img_count  9.09 us
    reduce_scatter x1, waiting for transfers between devices, sum_by_chip(): parts = lax.psum_scatter(parts, core, scatter_dimension=0, tiled=True)  8.94 us
    all_to_all x1, starting transfers between devices, summed_on_arrival(): parts = lax.all_to_all(split_up(shard, dim, size), axis, 0, 0, tiled=True)  6.46 us
    dot_general x1, matrix products, body(): jnp.einsum('id,jd->ij', teacher_img, teacher_txt, preferred_element_type=...  4.8 us
    dot_general x1, matrix products, body(): jnp.dot(picked, student_txt, preferred_element_type=jnp.float32)  4.46 us
  transfers between devices with their start and end apart: 5, of which 3 were waited for; matrix products, arithmetic and copies ran while one was open for 6% of the time, Pallas kernels for 0%

commit v1 on v0

v1 whole, which is shorter than its diff:
```python
import math

import jax
import jax.numpy as jnp
from jax import lax
from jax.sharding import Mesh
from jax.sharding import PartitionSpec as P

IMG = ("img_0", "img_1")
TXT = ("txt_0", "txt_1")
IMG_TXT = ("img_0", "img_1", "txt_0", "txt_1")
TXT_IMG = ("txt_0", "txt_1", "img_0", "img_1")


def from_everyone(shard, axis):
    copies = jnp.broadcast_to(shard, (lax.axis_size(axis), *shard.shape))
    return lax.all_to_all(copies, axis, split_axis=0, concat_axis=0, tiled=True)


def local_stats(teacher, student, gap, along):
    teach_peak = jnp.max(teacher, axis=along, keepdims=True)
    learn_peak = jnp.max(student, axis=along, keepdims=True)
    weight = jnp.exp(teacher - teach_peak)
    teach_mass = jnp.sum(weight, axis=along)
    learn_mass = jnp.sum(jnp.exp(student - learn_peak), axis=along)
    gap_sum = jnp.sum(weight * gap, axis=along)
    return jnp.stack(
        [
            jnp.squeeze(teach_peak, along) + jnp.log(teach_mass),
            jnp.squeeze(learn_peak, along) + jnp.log(learn_mass),
            gap_sum / teach_mass,
        ]
    ).reshape(-1, 128)


def joined(parts):
    parts = parts.reshape(parts.shape[0], 3, -1)
    teach, learn, gap = parts[:, 0], parts[:, 1], parts[:, 2]
    teach_peak = jnp.max(teach, axis=0)
    learn_peak = jnp.max(learn, axis=0)
    weight = jnp.exp(teach - teach_peak)
    mass = jnp.sum(weight, axis=0)
    teach_norm = teach_peak + jnp.log(mass)
    learn_norm = learn_peak + jnp.log(jnp.sum(jnp.exp(learn - learn_peak), axis=0))
    gap_mean = jnp.sum(weight * gap, axis=0) / mass
    return teach_norm, learn_norm, jnp.sum(gap_mean + learn_norm - teach_norm)


def step_perm(size, shift):
    return [(k, (k + shift) % size) for k in range(size)]


def body(teacher_img, teacher_txt, student_img, student_txt):
    scale_teach = 3.0 / math.sqrt(teacher_img.shape[1])
    scale_learn = 3.0 / math.sqrt(student_img.shape[1])
    rows = teacher_img.shape[0]
    cols = teacher_txt.shape[0]
    img_count = lax.axis_size(IMG)
    txt_count = lax.axis_size(TXT)
    width = student_img.shape[1]
    teacher = scale_teach * jnp.einsum(
        "id,jd->ij", teacher_img, teacher_txt, preferred_element_type=jnp.float32
    )
    student = scale_learn * jnp.einsum(
        "id,jd->ij", student_img, student_txt, preferred_element_type=jnp.float32
    )
    gap = teacher - student
    row_teach, row_learn, row_loss = joined(
        from_everyone(local_stats(teacher, student, gap, 1), TXT)
    )
    col_teach, col_learn, col_loss = joined(
        from_everyone(local_stats(teacher, student, gap, 0), IMG)
    )
    q_row = jnp.exp(student - row_learn[:, None])
    p_row = jnp.exp(teacher - row_teach[:, None])
    q_col = jnp.exp(student - col_learn[None, :])
    p_col = jnp.exp(teacher - col_teach[None, :])
    delta = (8.0 * (q_row - p_row + q_col - p_col)).astype(jnp.bfloat16)

    def with_note(grad, pieces, note):
        grad = grad.reshape(pieces, -1, width)
        note = jnp.broadcast_to(note, (pieces, 8, width))
        return jnp.concatenate([grad, note], axis=1)

    to_txt = scale_learn * jnp.einsum(
        "ij,id->jd", delta, student_img, preferred_element_type=jnp.float32
    )
    to_txt = with_note(to_txt, img_count, row_loss)
    chips, cores = lax.axis_size("img_0"), lax.axis_size("img_1")
    to_txt = to_txt.reshape(chips, cores, -1, width)
    core = lax.axis_index("img_1")
    kept = lax.dynamic_index_in_dim(to_txt, core, 1, keepdims=False)
    sent = lax.dynamic_index_in_dim(to_txt, 1 - core, 1, keepdims=False)
    both = kept + lax.ppermute(sent, "img_1", step_perm(cores, 1))

    to_img = scale_learn * jnp.dot(delta, student_txt, preferred_element_type=jnp.float32)
    to_img = with_note(to_img, txt_count, col_loss)
    got_img = lax.all_to_all(to_img, TXT, 0, 0, tiled=True)

    place = lax.axis_index("img_0")

    def piece(shift):
        return lax.dynamic_index_in_dim(both, (place + shift) % chips, 0, keepdims=False)

    up, down = piece(chips // 2), piece(1 - chips // 2 + chips)
    for k in range(chips // 2 - 1, -1, -1):
        up = lax.ppermute(up, "img_0", step_perm(chips, 1))
        if k:
            up = up + piece(k)
    for k in range(chips // 2 - 2, -1, -1):
        down = lax.ppermute(down, "img_0", step_perm(chips, -1))
        if k:
            down = down + piece(chips - k)
    got_txt = up + down + piece(0)
    got_img = jnp.sum(got_img, axis=0)
    own = rows // txt_count
    loss = 0.5 * (got_txt[-1, 0] / (rows * img_count) + got_img[-1, 0] / (cols * txt_count))
    return (loss, got_img[:own], got_txt[: cols // img_count])


def solution(mesh):
    torus = Mesh(mesh.devices.reshape(8, 2, 4, 4), ("img_0", "img_1", "txt_0", "txt_1"))
    in_specs = (P(IMG, None), P(TXT, None), P(IMG, None), P(TXT, None))
    out_specs = (P(), P(IMG_TXT, None), P(TXT_IMG, None))
    return jax.shard_map(body, mesh=torus, in_specs=in_specs, out_specs=out_specs, check_vma=False)
```

time: 147 us -> 109 us (0.74)
  blocking collectives: 40 us -> 0 us
  between operations: 18.6 us -> 3.49 us
  starting transfers between devices: 24.8 us -> 31.1 us
  local copies, waits for them, and re-layouts: 7.03 us -> 12.1 us
  waiting for transfers between devices: 26.8 us -> 31.6 us
  other arithmetic: 16.3 us -> 20 us
  matrix products: 11.9 us -> 8.68 us
    psum x4 -> x0, blocking collectives: 40 us -> none  [over_axes(): shard = lax.psum(shard, axis)]
    ppermute x0 -> x8, waiting for transfers between devices: none -> 14.9 us  [the longest x4 14.9 us: body(): up = lax.ppermute(up, 'img_0', step_perm(chips, 1))]
    reduce_scatter x2 -> x0, waiting for transfers between devices: 8.94 us -> none  [the longest x1 8.94 us: sum_by_chip(): parts = lax.psum_scatter(parts, core, scatter_dimension=0, tiled=True)]
    ppermute x0 -> x8, starting transfers between devices: none -> 8.4 us  [the longest x3 8.06 us: body(): down = lax.ppermute(down, 'img_0', step_perm(chips, -1))]
    reduce_sum x6 -> x9, other arithmetic: 15.9 us -> 8.69 us  [the longest x1 4.72 us: local_stats(): gap_sum = jnp.sum(weight * gap, axis=along)]
    add x14 -> x7, other arithmetic: 0.34 us -> 5.81 us  [the longest x2 2.04 us: body(): down = down + piece(chips - k)]
    convert_element_type x0 -> x1, other arithmetic: none -> 5.05 us  [body(): delta = (8.0 * (q_row - p_row + q_col - p_col)).astype(jnp.bfloat16)]
    concatenate x0 -> x2, local copies, waits for them, and re-layouts: none -> 3.27 us  [with_note(): return jnp.concatenate([grad, note], axis=1)]
  transfers between devices with their start and end apart: 5 -> 11, of which waited for: 3 -> 7; matrix products, arithmetic and copies ran while one was open for 6% -> 11% of each run, Pallas kernels for 0% -> 0%
where the time goes in v1:
time: 109 us; the launch traced here: 107 us
  waiting for transfers between devices  31.6 us (29%)
  starting transfers between devices  31.1 us (29%)
  other arithmetic  20 us (18%)
  local copies, waits for them, and re-layouts  12.1 us (11%)
  matrix products  8.68 us (8%)
  between operations  3.49 us (3%)
    all_to_all x2, starting transfers between devices, from_everyone(): return lax.all_to_all(copies, axis, split_axis=0, concat_axis=0, tiled=True)  18 us
    all_to_all x2, waiting for transfers between devices, from_everyone(): return lax.all_to_all(copies, axis, split_axis=0, concat_axis=0, tiled=True)  16.4 us
    ppermute x4, waiting for transfers between devices, body(): up = lax.ppermute(up, 'img_0', step_perm(chips, 1))  14.9 us
    ppermute x3, starting transfers between devices, body(): down = lax.ppermute(down, 'img_0', step_perm(chips, -1))  8.06 us
    convert_element_type x1, other arithmetic, body(): delta = (8.0 * (q_row - p_row + q_col - p_col)).astype(jnp.bfloat16)  5.05 us
    dot_general x1, matrix products, body(): jnp.einsum('id,jd->ij', teacher_img, teacher_txt, preferred_element_type=...  4.8 us
    reduce_sum x1, other arithmetic, local_stats(): gap_sum = jnp.sum(weight * gap, axis=along)  4.72 us
    all_to_all x1, starting transfers between devices, body(): got_img = lax.all_to_all(to_img, TXT, 0, 0, tiled=True)  4.62 us
  transfers between devices with their start and end apart: 11, of which 7 were waited for; matrix products, arithmetic and copies ran while one was open for 11% of the time, Pallas kernels for 0%

profile of v1, /device:TPU:1, one launch (start us, length us, event | category | flops | bytes accessed | tf_op | source)
XLA Modules:
  0.0 106.9 jit_solution(1482588173171596455)
XLA Ops:
  0.7 1.7 %copy-done = bf16[1024,1280]{1,0:T(8,128)(2,1)S(1)} copy-done((bf16[1024,1280]{1,0:T(8,128)(2,1)S(1)}, bf16[1024,1280]{1,0:T(8,128)(2,1)}, u32[]{:S(2)}) %copy-start) | copy-done | bytes 2621464
  2.4 4.8 %multiply_reduce_fusion.5 = (f32[1024]{0:T(1024)S(1)}, f32[1024]{0:T(1024)S(1)}, f32[1024,1024]{1,0:T(8,128)S(1)}) fusion(bf16[1024,1280]{1,0:T(8,128)(2,1)S(1)} %copy-done, bf16[1024,1280]{1,0:T(8,128)(2,1)} %param.5), kind=kOutput, calls=%fused_computation.13 | convolution fusion | flops 2687498240 | bytes 9445376 | tf_op jit(solution)/shard_map/id,jd->ij/dot_general | solution.py:61
  7.2 1.4 %multiply_reduce_fusion.3 = (f32[1024]{0:T(1024)S(1)}, f32[1024,1024]{1,0:T(8,128)S(1)}) fusion(bf16[1024,512]{1,0:T(8,128)(2,1)S(1)} %copy-done.5, bf16[1024,512]{1,0:T(8,128)(2,1)S(1)} %copy-done.7), kind=kOutput, calls=%fused_computation.11 | convolution fusion | flops 1075837952 | bytes 6295552 | tf_op jit(solution)/shard_map/id,jd->ij/dot_general | solution.py:64
  9.2 4.7 %multiply_reduce_fusion.1 = (f32[1024]{0:T(1024)S(1)}, f32[1024]{0:T(1024)S(1)}, f32[1024]{0:T(1024)S(1)}, f32[1024]{0:T(1024)S(1)}, f32[1024]{0:T(1024)S(1)}, /*index=5*/f32[1024]{0:T(1024)S(1)}) fusion(f32[1024,1024]{1,0:T(8,128)S(1)} %get-tuple-element.43, f32[1024,1024]{1,0:T(8,128)S(1)} %get-tuple-element.41, f32[1024]{0:T(1024)S(1)} %get-tuple-element.9, ...), kind=kLoop, calls=%fused_computation.4 | loop fusion | flops 14673920 | bytes 8425472 | tf_op jit(solution)/shard_map/reduce_sum | solution.py:26
  13.9 0.7 exponential_reduce_fusion
  14.7 0.7 broadcast_in_dim.4
  15.4 7.6 %all-to-all-start = ((f32[16,24,128]{2,1,0:T(8,128)}), f32[16,24,128]{2,1,0:T(8,128)S(1)}, u32[]{:S(2)}, u32[]{:S(2)}) async-start(f32[16,24,128]{2,1,0:T(8,128)} %broadcast_in_dim.4), calls=%async_computation | async-start | bytes 393216 | tf_op jit(solution)/shard_map/all_to_all | solution.py:17
  23.1 7.1 %all-to-all-done = f32[16,24,128]{2,1,0:T(8,128)S(1)} async-done(((f32[16,24,128]{2,1,0:T(8,128)}), f32[16,24,128]{2,1,0:T(8,128)S(1)}, u32[]{:S(2)}, u32[]{:S(2)}) %all-to-all-start) | async-done | bytes 196640 | tf_op jit(solution)/shard_map/all_to_all | solution.py:17
  30.2 0.7 broadcast_in_dim.5
  30.9 10.5 %all-to-all-start.1 = ((f32[16,24,128]{2,1,0:T(8,128)}), f32[16,24,128]{2,1,0:T(8,128)S(1)}, u32[]{:S(2)}, u32[]{:S(2)}) async-start(f32[16,24,128]{2,1,0:T(8,128)} %broadcast_in_dim.5), calls=%async_computation.1 | async-start | bytes 393216 | tf_op jit(solution)/shard_map/all_to_all | solution.py:17
  42.3 9.3 %all-to-all-done.1 = f32[16,24,128]{2,1,0:T(8,128)S(1)} async-done(((f32[16,24,128]{2,1,0:T(8,128)}), f32[16,24,128]{2,1,0:T(8,128)S(1)}, u32[]{:S(2)}, u32[]{:S(2)}) %all-to-all-start.1) | async-done | bytes 196640 | tf_op jit(solution)/shard_map/all_to_all | solution.py:17
  52.6 5.0 %multiply_convert_fusion = bf16[1024,1024]{1,0:T(8,128)(2,1)S(1)} fusion(f32[1024,1024]{1,0:T(8,128)} %copy-done.1, f32[1024,1024]{1,0:T(8,128)} %copy-done.2, f32[1024]{0:T(1024)S(1)} %get-tuple-element.36, f32[1024]{0:T(1024)S(1)} %get-tuple-element.20, f32[1024]{0:T(1024)S(1)} %get-tuple-element.35, f32[1024]{0:T(1024)S(1)} %get-tuple-element.22), kind=kLoop, calls=%fused_computation | loop fusion | flops 11534336 | bytes 10502144 | tf_op jit(solution)/shard_map/convert_element_type | solution.py:78
  57.7 1.3 %convolution_multiply_fusion.1 = f32[1024,512]{1,0:T(8,128)S(1)} fusion(bf16[1024,1024]{1,0:T(8,128)(2,1)S(1)} %multiply_convert_fusion, bf16[1024,512]{1,0:T(8,128)(2,1)S(1)} %copy-done.6), kind=kOutput, calls=%fused_computation.15 | convolution fusion | flops 1074266112 | bytes 5242880 | tf_op jit(solution)/shard_map/ij,id->jd/dot_general | solution.py:85
  59.0 1.0 concatenate.6
  60.0 1.4 %dynamic-slice_bitcast_fusion = f32[8,72,512]{2,1,0:T(8,128)} fusion(f32[8,2,72,512]{3,2,1,0:T(8,128)S(1)} %bitcast.78, s32[]{:T(128)S(6)} %select_n.68), kind=kLoop, calls=%fused_computation.17 | loop fusion | bytes 2359300 | tf_op jit(solution)/shard_map/jit(dynamic_index_in_dim)/squeeze | solution.py:93
  61.4 1.2 %convolution_multiply_fusion = f32[1024,512]{1,0:T(8,128)S(1)} fusion(bf16[1024,1024]{1,0:T(8,128)(2,1)S(1)} %multiply_convert_fusion, bf16[1024,512]{1,0:T(8,128)(2,1)S(1)} %copy-done.8), kind=kOutput, calls=%fused_computation.14 | convolution fusion | flops 1074266112 | bytes 5242880 | tf_op jit(solution)/shard_map/dot_general | solution.py:96
  62.6 2.3 %concatenate.7 = f32[16,72,512]{2,1,0:T(8,128)} pad(f32[16,64,512]{2,1,0:T(8,128)S(1)} %bitcast.80, f32[]{:T(128)} %get-tuple-element.19), padding=0_0x0_8x0_0 | pad | bytes 4456452 | tf_op jit(solution)/shard_map/concatenate | solution.py:83
  64.9 4.6 %all-to-all-start.2 = ((f32[16,72,512]{2,1,0:T(8,128)}), f32[16,72,512]{2,1,0:T(8,128)}, u32[]{:S(2)}, u32[]{:S(2)}) async-start(f32[16,72,512]{2,1,0:T(8,128)} %concatenate.7), calls=%async_computation.2 | async-start | bytes 4718592 | tf_op jit(solution)/shard_map/all_to_all | solution.py:98
  69.6 1.9 %bitcast_add_fusion = f32[8,72,512]{2,1,0:T(8,128)S(1)} fusion(f32[8,72,512]{2,1,0:T(8,128)} %collective-permute-done, f32[8,2,72,512]{3,2,1,0:T(8,128)} %bitcast.79, s32[]{:T(128)S(6)} %select_n.67), kind=kLoop, calls=%fused_computation.16 | loop fusion | flops 294912 | bytes 3538948 | tf_op jit(solution)/shard_map/add | solution.py:94
  71.5 1.0 copy-done.4
  72.7 2.6 %collective-permute-start.5 = (f32[72,512]{1,0:T(8,128)S(1)}, f32[72,512]{1,0:T(8,128)S(1)}, u32[]{:S(2)}, u32[]{:S(2)}) collective-permute-start(f32[72,512]{1,0:T(8,128)S(1)} %get-tuple-element.27), channel_id=1, source_target_pairs={{0,224},{32,0},{64,32},{96,64},{128,96},{160,128},{192,160},{224,1... | collective-permute-start | bytes 442376 | tf_op jit(solution)/shard_map/ppermute | solution.py:111
  75.3 3.5 %collective-permute-done.1 = f32[72,512]{1,0:T(8,128)S(1)} collective-permute-done((f32[72,512]{1,0:T(8,128)S(1)}, f32[72,512]{1,0:T(8,128)S(1)}, u32[]{:S(2)}, u32[]{:S(2)}) %collective-permute-start.1) | collective-permute-done | bytes 147488 | tf_op jit(solution)/shard_map/ppermute | solution.py:107
  78.8 0.9 bitcast_add_fusion.6
  79.9 5.6 %collective-permute-done.2 = f32[72,512]{1,0:T(8,128)S(1)} collective-permute-done((f32[72,512]{1,0:T(8,128)S(1)}, f32[72,512]{1,0:T(8,128)S(1)}, u32[]{:S(2)}, u32[]{:S(2)}) %collective-permute-start.2) | collective-permute-done | bytes 147488 | tf_op jit(solution)/shard_map/ppermute | solution.py:107
  85.5 1.0 bitcast_add_fusion.3
  86.6 2.7 %collective-permute-start.6 = (f32[72,512]{1,0:T(8,128)S(1)}, f32[72,512]{1,0:T(8,128)S(1)}, u32[]{:S(2)}, u32[]{:S(2)}) collective-permute-start(f32[72,512]{1,0:T(8,128)S(1)} %get-tuple-element.25), channel_id=1, source_target_pairs={{0,224},{32,0},{64,32},{96,64},{128,96},{160,128},{192,160},{224,1... | collective-permute-start | bytes 442376 | tf_op jit(solution)/shard_map/ppermute | solution.py:111
  89.2 2.9 %collective-permute-done.3 = f32[72,512]{1,0:T(8,128)S(1)} collective-permute-done((f32[72,512]{1,0:T(8,128)S(1)}, f32[72,512]{1,0:T(8,128)S(1)}, u32[]{:S(2)}, u32[]{:S(2)}) %collective-permute-start.3) | collective-permute-done | bytes 147488 | tf_op jit(solution)/shard_map/ppermute | solution.py:107
  92.2 1.0 bitcast_add_fusion.2
  93.3 2.7 %collective-permute-start.7 = (f32[72,512]{1,0:T(8,128)S(1)}, f32[72,512]{1,0:T(8,128)S(1)}, u32[]{:S(2)}, u32[]{:S(2)}) collective-permute-start(f32[72,512]{1,0:T(8,128)S(1)} %get-tuple-element.23), channel_id=1, source_target_pairs={{0,224},{32,0},{64,32},{96,64},{128,96},{160,128},{192,160},{224,1... | collective-permute-start | bytes 442376 | tf_op jit(solution)/shard_map/ppermute | solution.py:111
  96.0 2.8 %collective-permute-done.4 = f32[72,512]{1,0:T(8,128)S(1)} collective-permute-done((f32[72,512]{1,0:T(8,128)S(1)}, f32[72,512]{1,0:T(8,128)S(1)}, u32[]{:S(2)}, u32[]{:S(2)}) %collective-permute-start.4) | collective-permute-done | bytes 147488 | tf_op jit(solution)/shard_map/ppermute | solution.py:107
  98.9 0.9 bitcast_add_fusion.1
  101.3 1.9 %reduce_sum.149 = f32[72,512]{1,0:T(8,128)S(1)} reduce(f32[16,72,512]{2,1,0:T(8,128)} %all-to-all-done.2, f32[]{:T(128)} %constant.93.clone.1), dimensions={0}, to_apply=%region_22.23 | reduce | flops 552960 | bytes 2506756 | tf_op jit(solution)/shard_map/reduce_sum | solution.py:115
  (47 shorter events, 5.7 us)
Async XLA Ops:
  0.6 1.7 %copy-start = (bf16[1024,1280]{1,0:T(8,128)(2,1)S(1)}, bf16[1024,1280]{1,0:T(8,128)(2,1)}, u32[]{:S(2)}) copy-start(bf16[1024,1280]{1,0:T(8,128)(2,1)} %param.4) | copy-start | bytes 7864324
  0.6 6.5 %copy-start.5 = (bf16[1024,512]{1,0:T(8,128)(2,1)S(1)}, bf16[1024,512]{1,0:T(8,128)(2,1)}, u32[]{:S(2)}) copy-start(bf16[1024,512]{1,0:T(8,128)(2,1)} %param.6) | copy-start | bytes 3145732
  2.4 4.8 %copy-start.7 = (bf16[1024,512]{1,0:T(8,128)(2,1)S(1)}, bf16[1024,512]{1,0:T(8,128)(2,1)}, u32[]{:S(2)}) copy-start(bf16[1024,512]{1,0:T(8,128)(2,1)} %param.7) | copy-start | bytes 3145732
  7.2 2.0 %copy-start.2 = (f32[1024,1024]{1,0:T(8,128)}, f32[1024,1024]{1,0:T(8,128)S(1)}, u32[]{:S(2)}) copy-start(f32[1024,1024]{1,0:T(8,128)S(1)} %get-tuple-element.41) | copy-start | bytes 12582916
  8.6 5.3 %copy-start.1 = (f32[1024,1024]{1,0:T(8,128)}, f32[1024,1024]{1,0:T(8,128)S(1)}, u32[]{:S(2)}) copy-start(f32[1024,1024]{1,0:T(8,128)S(1)} %get-tuple-element.43) | copy-start | bytes 12582916
  15.4 14.7 %all-to-all-start = ((f32[16,24,128]{2,1,0:T(8,128)}), f32[16,24,128]{2,1,0:T(8,128)S(1)}, u32[]{:S(2)}, u32[]{:S(2)}) async-start(f32[16,24,128]{2,1,0:T(8,128)} %broadcast_in_dim.4), calls=%async_computation | async-start | bytes 393216 | tf_op jit(solution)/shard_map/all_to_all | solution.py:17
  30.9 20.8 %all-to-all-start.1 = ((f32[16,24,128]{2,1,0:T(8,128)}), f32[16,24,128]{2,1,0:T(8,128)S(1)}, u32[]{:S(2)}, u32[]{:S(2)}) async-start(f32[16,24,128]{2,1,0:T(8,128)} %broadcast_in_dim.5), calls=%async_computation.1 | async-start | bytes 393216 | tf_op jit(solution)/shard_map/all_to_all | solution.py:17
  52.6 5.1 %copy-start.6 = (bf16[1024,512]{1,0:T(8,128)(2,1)S(1)}, bf16[1024,512]{1,0:T(8,128)(2,1)}, u32[]{:S(2)}) copy-start(bf16[1024,512]{1,0:T(8,128)(2,1)} %param.6) | copy-start | bytes 3145732
  59.0 2.4 %copy-start.8 = (bf16[1024,512]{1,0:T(8,128)(2,1)S(1)}, bf16[1024,512]{1,0:T(8,128)(2,1)}, u32[]{:S(2)}) copy-start(bf16[1024,512]{1,0:T(8,128)(2,1)} %param.7) | copy-start | bytes 3145732
  60.0 2.6 %copy-start.3 = (f32[16,72,512]{2,1,0:T(8,128)}, f32[16,72,512]{2,1,0:T(8,128)S(1)}, u32[]{:S(2)}) copy-start(f32[16,72,512]{2,1,0:T(8,128)S(1)} %concatenate.6) | copy-start | bytes 7077892
  61.4 8.2 %collective-permute-start = (f32[8,72,512]{2,1,0:T(8,128)}, f32[8,72,512]{2,1,0:T(8,128)}, u32[]{:S(2)}, u32[]{:S(2)}) collective-permute-start(f32[8,72,512]{2,1,0:T(8,128)} %dynamic-slice_bitcast_fusion), channel_id=1, source_target_pairs={{0,16},{16,0},{1,17},{17,1},{2,18},{18,2},{3,19},{19,3},{4,20},{20... | collective-permute-start | bytes 3538952 | tf_op jit(solution)/shard_map/ppermute | solution.py:94
  64.9 36.4 %all-to-all-start.2 = ((f32[16,72,512]{2,1,0:T(8,128)}), f32[16,72,512]{2,1,0:T(8,128)}, u32[]{:S(2)}, u32[]{:S(2)}) async-start(f32[16,72,512]{2,1,0:T(8,128)} %concatenate.7), calls=%async_computation.2 | async-start | bytes 4718592 | tf_op jit(solution)/shard_map/all_to_all | solution.py:98
  71.5 1.1 copy-start.4
  72.5 6.3 %collective-permute-start.1 = (f32[72,512]{1,0:T(8,128)S(1)}, f32[72,512]{1,0:T(8,128)S(1)}, u32[]{:S(2)}, u32[]{:S(2)}) collective-permute-start(f32[72,512]{1,0:T(8,128)S(1)} %get-tuple-element.28), channel_id=1, source_target_pairs={{0,32},{32,64},{64,96},{96,128},{128,160},{160,192},{192,224},{224... | collective-permute-start | bytes 442376 | tf_op jit(solution)/shard_map/ppermute | solution.py:107
  72.7 7.2 %collective-permute-start.5 = (f32[72,512]{1,0:T(8,128)S(1)}, f32[72,512]{1,0:T(8,128)S(1)}, u32[]{:S(2)}, u32[]{:S(2)}) collective-permute-start(f32[72,512]{1,0:T(8,128)S(1)} %get-tuple-element.27), channel_id=1, source_target_pairs={{0,224},{32,0},{64,32},{96,64},{128,96},{160,128},{192,160},{224,1... | collective-permute-start | bytes 442376 | tf_op jit(solution)/shard_map/ppermute | solution.py:111
  79.8 5.7 %collective-permute-start.2 = (f32[72,512]{1,0:T(8,128)S(1)}, f32[72,512]{1,0:T(8,128)S(1)}, u32[]{:S(2)}, u32[]{:S(2)}) collective-permute-start(f32[72,512]{1,0:T(8,128)S(1)} %bitcast_add_fusion.6), channel_id=1, source_target_pairs={{0,32},{32,64},{64,96},{96,128},{128,160},{160,192},{192,224},{224... | collective-permute-start | bytes 442376 | tf_op jit(solution)/shard_map/ppermute | solution.py:107
  86.5 5.7 %collective-permute-start.3 = (f32[72,512]{1,0:T(8,128)S(1)}, f32[72,512]{1,0:T(8,128)S(1)}, u32[]{:S(2)}, u32[]{:S(2)}) collective-permute-start(f32[72,512]{1,0:T(8,128)S(1)} %get-tuple-element.26), channel_id=1, source_target_pairs={{0,32},{32,64},{64,96},{96,128},{128,160},{160,192},{192,224},{224... | collective-permute-start | bytes 442376 | tf_op jit(solution)/shard_map/ppermute | solution.py:107
  86.6 5.6 %collective-permute-start.6 = (f32[72,512]{1,0:T(8,128)S(1)}, f32[72,512]{1,0:T(8,128)S(1)}, u32[]{:S(2)}, u32[]{:S(2)}) collective-permute-start(f32[72,512]{1,0:T(8,128)S(1)} %get-tuple-element.25), channel_id=1, source_target_pairs={{0,224},{32,0},{64,32},{96,64},{128,96},{160,128},{192,160},{224,1... | collective-permute-start | bytes 442376 | tf_op jit(solution)/shard_map/ppermute | solution.py:111
  93.2 5.7 %collective-permute-start.4 = (f32[72,512]{1,0:T(8,128)S(1)}, f32[72,512]{1,0:T(8,128)S(1)}, u32[]{:S(2)}, u32[]{:S(2)}) collective-permute-start(f32[72,512]{1,0:T(8,128)S(1)} %get-tuple-element.24), channel_id=1, source_target_pairs={{0,32},{32,64},{64,96},{96,128},{128,160},{160,192},{192,224},{224... | collective-permute-start | bytes 442376 | tf_op jit(solution)/shard_map/ppermute | solution.py:107
  93.3 5.6 %collective-permute-start.7 = (f32[72,512]{1,0:T(8,128)S(1)}, f32[72,512]{1,0:T(8,128)S(1)}, u32[]{:S(2)}, u32[]{:S(2)}) collective-permute-start(f32[72,512]{1,0:T(8,128)S(1)} %get-tuple-element.23), channel_id=1, source_target_pairs={{0,224},{32,0},{64,32},{96,64},{128,96},{160,128},{192,160},{224,1... | collective-permute-start | bytes 442376 | tf_op jit(solution)/shard_map/ppermute | solution.py:111

commit v2 on v1

v2 whole, which is shorter than its diff:
```python
import functools
import math

import jax
import jax.numpy as jnp
from jax import lax
from jax.experimental import pallas as pl
from jax.experimental.pallas import tpu as pltpu
from jax.sharding import Mesh
from jax.sharding import PartitionSpec as P

IMG = ("img_0", "img_1")
TXT = ("txt_0", "txt_1")
IMG_TXT = ("img_0", "img_1", "txt_0", "txt_1")
TXT_IMG = ("txt_0", "txt_1", "img_0", "img_1")
LANES = 128
NOTE = 8
VMEM_LIMIT = 48 * 1024 * 1024
LN2 = math.log(2.0)
F32 = jnp.float32
WHOLE = pl.BlockSpec(memory_space=pltpu.VMEM)
ANYWHERE = pl.BlockSpec(memory_space=pl.ANY)


def cost(flops, size, transcendentals=0):
    return pl.CostEstimate(flops=flops, bytes_accessed=size, transcendentals=transcendentals)


def stats_kernel(scale_teach, scale_learn, ti_hbm, tt_hbm, si_hbm, st_hbm, t_hbm, s_hbm,
                 row_out, col_out, ti, tt, si, st, t, s, peaks, sums, col_peaks, col_sums, sems):
    loads = [
        pltpu.make_async_copy(src, dst, sems.at[k])
        for k, (src, dst) in enumerate(((st_hbm, st), (si_hbm, si), (tt_hbm, tt), (ti_hbm, ti)))
    ]
    for load in loads:
        load.start()
    rows, cols = t.shape
    wide = 256

    def logits(left, right, out, scale, which):
        @pl.loop(0, cols // wide)
        def _(n):
            at = pl.multiple_of(n * wide, wide)
            block = scale * lax.dot_general(
                left[...], right[pl.ds(at, wide), :], (((1,), (1,)), ((), ())),
                preferred_element_type=F32,
            )
            out[:, pl.ds(at, wide)] = block
            col_peaks[which, :, pl.ds(at, wide)] = jnp.max(
                block.reshape(rows // 8, 8, wide), axis=0
            )
            top = jnp.maximum(block[:, :LANES], block[:, LANES:])

            @pl.when(n == 0)
            def _():
                peaks[which] = top

            @pl.when(n > 0)
            def _():
                peaks[which] = jnp.maximum(peaks[which], top)

        peaks[which] = jnp.broadcast_to(
            jnp.max(peaks[which], axis=1, keepdims=True), (rows, LANES)
        )
        col_peaks[which] = jnp.broadcast_to(
            jnp.max(col_peaks[which], axis=0, keepdims=True), (8, cols)
        )

    loads[0].wait()
    loads[1].wait()
    logits(si, st, s, scale_learn, 1)
    save_s = pltpu.make_async_copy(s, s_hbm, sems.at[4])
    save_s.start()
    loads[2].wait()
    loads[3].wait()
    logits(ti, tt, t, scale_teach, 0)
    save_t = pltpu.make_async_copy(t, t_hbm, sems.at[5])
    save_t.start()

    group = 4 * LANES
    for h in range(cols // group):
        def strip(r, carry):
            at = pl.multiple_of(r * 8, 8)
            down = pl.ds(at, 8)
            row_peak_t, row_peak_s = peaks[0, down, :], peaks[1, down, :]
            row_t = row_s = row_g = None
            new = []
            for k in range(group // LANES):
                across = slice(h * group + k * LANES, h * group + (k + 1) * LANES)
                tv, sv = t[down, across], s[down, across]
                gap = tv - sv
                wr = jnp.exp2(tv - row_peak_t)
                vr = jnp.exp2(sv - row_peak_s)
                wc = jnp.exp2(tv - col_peaks[0, :, across])
                vc = jnp.exp2(sv - col_peaks[1, :, across])
                row_t = wr if row_t is None else row_t + wr
                row_s = vr if row_s is None else row_s + vr
                row_g = wr * gap if row_g is None else row_g + wr * gap
                ct, cs, cg = carry[3 * k : 3 * k + 3]
                new += [ct + wc, cs + vc, cg + wc * gap]
            for q, value in enumerate((row_t, row_s, row_g)):
                if h:
                    value = value + sums[q, down, :]
                sums[q, down, :] = value
            return tuple(new)

        zeros = tuple(jnp.zeros((8, LANES), F32) for _ in range(3 * group // LANES))
        found = lax.fori_loop(0, rows // 8, strip, zeros, unroll=4)
        for k in range(group // LANES):
            across = slice(h * group + k * LANES, h * group + (k + 1) * LANES)
            for q in range(3):
                col_sums[q, :, across] = found[3 * k + q]

    def publish(out, peak_t, peak_s, mass_t, mass_s, gap):
        lse_t = peak_t + jnp.log2(mass_t)
        lse_s = peak_s + jnp.log2(mass_s)
        mean = gap / mass_t
        for q, value in enumerate((lse_t, lse_s, mean)):
            for b in range(value.shape[1] // LANES):
                line = value[:, b * LANES : (b + 1) * LANES]
                for k in range(out.shape[0]):
                    out[k, q * 8 + b : q * 8 + b + 1, :] = line

    publish(
        col_out, col_peaks[0, :1, :], col_peaks[1, :1, :],
        *(jnp.sum(col_sums[q], axis=0, keepdims=True) for q in range(3)),
    )

    def across_lanes(value, weight):
        found = lax.dot_general(
            jnp.full((8, LANES), weight, F32), value, (((1,), (1,)), ((), ())),
            preferred_element_type=F32, precision=lax.Precision.HIGHEST,
        )
        return found[:1]

    publish(
        row_out,
        across_lanes(peaks[0], 1.0 / LANES), across_lanes(peaks[1], 1.0 / LANES),
        *(across_lanes(sums[q], 1.0) for q in range(3)),
    )
    save_s.wait()
    save_t.wait()


def local_stats(teacher_img, teacher_txt, student_img, student_txt, copies):
    rows, deep = teacher_img.shape
    cols, thin = student_txt.shape
    logit = jax.ShapeDtypeStruct((rows, cols), F32)
    kernel = functools.partial(
        stats_kernel, 3.0 / math.sqrt(deep) / LN2, 3.0 / math.sqrt(thin) / LN2
    )
    return pl.pallas_call(
        kernel,
        name="logits_and_statistics",
        out_shape=(
            logit, logit,
            jax.ShapeDtypeStruct((copies[0], 3 * 8, LANES), F32),
            jax.ShapeDtypeStruct((copies[1], 3 * 8, LANES), F32),
        ),
        in_specs=[ANYWHERE] * 4,
        out_specs=(ANYWHERE, ANYWHERE, WHOLE, WHOLE),
        scratch_shapes=[
            pltpu.VMEM((rows, deep), jnp.bfloat16), pltpu.VMEM((cols, deep), jnp.bfloat16),
            pltpu.VMEM((rows, thin), jnp.bfloat16), pltpu.VMEM((cols, thin), jnp.bfloat16),
            pltpu.VMEM((rows, cols), F32), pltpu.VMEM((rows, cols), F32),
            pltpu.VMEM((2, rows, LANES), F32), pltpu.VMEM((3, rows, LANES), F32),
            pltpu.VMEM((2, 8, cols), F32), pltpu.VMEM((3, 8, cols), F32),
            pltpu.SemaphoreType.DMA((6,)),
        ],
        compiler_params=pltpu.CompilerParams(vmem_limit_bytes=VMEM_LIMIT),
        cost_estimate=cost(2 * rows * cols * (deep + thin), 8 * rows * cols, 4 * rows * cols),
    )(teacher_img, teacher_txt, student_img, student_txt)


def joined(stats):
    teach, learn, gap = (stats[:, 8 * q : 8 * q + 8, :] for q in range(3))
    teach_peak = jnp.max(teach, axis=0)
    learn_peak = jnp.max(learn, axis=0)
    weight = jnp.exp2(teach - teach_peak[None])
    mass = jnp.sum(weight, axis=0)
    teach_norm = teach_peak + jnp.log2(mass)
    learn_norm = learn_peak + jnp.log2(jnp.sum(jnp.exp2(learn - learn_peak[None]), axis=0))
    mean = jnp.sum(weight * gap, axis=0) / mass
    return teach_norm, learn_norm, jnp.sum(mean + learn_norm - teach_norm)


def delta_kernel(scale, row_stats, col_stats, t, s, st, delta_out, img_out, note_out,
                 row_norms, col_norms, col_note):
    step = pl.program_id(0)
    tall = t.shape[0]

    @pl.when(step == 0)
    def _():
        for stats, norms, by_row in ((row_stats, row_norms, True), (col_stats, col_norms, False)):
            teach, learn, total = joined(stats[...])
            if by_row:
                note_out[...] = jnp.full(note_out.shape, total, F32)
            else:
                col_note[...] = jnp.full(col_note.shape, total, F32)
            for which, value in enumerate((teach, learn)):
                value = value - 3.0
                if by_row:
                    turned = jnp.concatenate([value] * (LANES // 8), axis=0).T
                for b in range(8):
                    if by_row:
                        norms[which, b * LANES : (b + 1) * LANES, :] = jnp.broadcast_to(
                            turned[:, b : b + 1], (LANES, LANES)
                        )
                    else:
                        norms[which, :, b * LANES : (b + 1) * LANES] = jnp.broadcast_to(
                            value[b : b + 1, :], (16, LANES)
                        )

    base = step * tall

    @pl.loop(0, tall // 16)
    def _(r):
        at = pl.multiple_of(r * 16, 16)
        down = pl.ds(at, 16)
        there = pl.ds(pl.multiple_of(base + at, 16), 16)
        row_t, row_s = row_norms[0, there, :], row_norms[1, there, :]
        for k in range(t.shape[1] // LANES):
            across = slice(k * LANES, (k + 1) * LANES)
            tv, sv = t[down, across], s[down, across]
            value = (
                jnp.exp2(sv - row_s) - jnp.exp2(tv - row_t)
                + jnp.exp2(sv - col_norms[1, :, across]) - jnp.exp2(tv - col_norms[0, :, across])
            )
            delta_out[down, across] = value.astype(jnp.bfloat16)

    grad = scale * jnp.dot(delta_out[...], st[...], preferred_element_type=F32)
    own = (img_out.shape[1] - NOTE) * LANES // st.shape[1]
    for k in range(img_out.shape[0]):
        for b in range(st.shape[1] // LANES):
            img_out[k, b * own : (b + 1) * own, :] = grad[
                k * own : (k + 1) * own, b * LANES : (b + 1) * LANES
            ]
        img_out[k, img_out.shape[1] - NOTE :, :] = col_note[...]


def delta_and_img(row_stats, col_stats, t, s, student_txt):
    rows, cols = t.shape
    thin = student_txt.shape[1]
    pieces = row_stats.shape[0]
    steps = 4
    tall = rows // steps
    lines = rows // pieces * thin // LANES + NOTE
    fixed = lambda shape: pl.BlockSpec(shape, lambda i: (0,) * len(shape))
    return pl.pallas_call(
        functools.partial(delta_kernel, 3.0 / math.sqrt(thin)),
        name="delta_and_image_gradient",
        grid=(steps,),
        out_shape=(
            jax.ShapeDtypeStruct((rows, cols), jnp.bfloat16),
            jax.ShapeDtypeStruct((pieces, lines, LANES), F32),
            jax.ShapeDtypeStruct((NOTE, thin), F32),
        ),
        in_specs=[
            fixed(row_stats.shape), fixed(col_stats.shape),
            pl.BlockSpec((tall, cols), lambda i: (i, 0)),
            pl.BlockSpec((tall, cols), lambda i: (i, 0)),
            fixed(student_txt.shape),
        ],
        out_specs=(
            pl.BlockSpec((tall, cols), lambda i: (i, 0)),
            pl.BlockSpec((pieces // steps, lines, LANES), lambda i: (i, 0, 0)),
            fixed((NOTE, thin)),
        ),
        scratch_shapes=[
            pltpu.VMEM((2, rows, LANES), F32), pltpu.VMEM((2, 16, cols), F32),
            pltpu.VMEM((NOTE, LANES), F32),
        ],
        compiler_params=pltpu.CompilerParams(vmem_limit_bytes=VMEM_LIMIT),
        cost_estimate=cost(2 * rows * cols * thin, 10 * rows * cols, 4 * rows * cols),
    )(row_stats, col_stats, t, s, student_txt)


def txt_kernel(scale, place, delta, si, note, out):
    tall = delta.shape[1]
    out[0, :tall, :] = scale * lax.dot_general(
        delta[...], si[...], (((0,), (0,)), ((), ())), preferred_element_type=F32
    )
    out[0, tall:, :] = note[...]


def txt_gradient(delta, student_img, note, upward, chips):
    rows, cols = delta.shape
    thin = student_img.shape[1]
    tall = cols // chips
    slots = chips // 2

    def dest(g, where):
        flow = where[1]
        up = where[0] + slots - g
        down = where[0] + slots + 1 + g
        return (0, lax.rem(jnp.where(flow == 0, up, down) + chips, chips))

    return pl.pallas_call(
        functools.partial(txt_kernel, 3.0 / math.sqrt(thin)),
        name="text_gradient",
        out_shape=jax.ShapeDtypeStruct((slots, tall + NOTE, thin), F32),
        grid_spec=pltpu.PrefetchScalarGridSpec(
            num_scalar_prefetch=1,
            grid=(slots,),
            in_specs=[
                pl.BlockSpec((rows, tall), dest),
                pl.BlockSpec((rows, thin), lambda g, where: (0, 0)),
                pl.BlockSpec((NOTE, thin), lambda g, where: (0, 0)),
            ],
            out_specs=pl.BlockSpec((1, tall + NOTE, thin), lambda g, where: (g, 0, 0)),
        ),
        compiler_params=pltpu.CompilerParams(vmem_limit_bytes=VMEM_LIMIT),
        cost_estimate=cost(rows * cols * thin, rows * cols * 2 + cols * thin * 2),
    )(upward, delta, student_img, note)


def sum_kernel(parts, out, note):
    own = out.shape[0]
    for b in range(out.shape[1] // LANES):
        total = parts[0, b * own : (b + 1) * own, :]
        for k in range(1, parts.shape[0]):
            total = total + parts[k, b * own : (b + 1) * own, :]
        out[:, b * LANES : (b + 1) * LANES] = total
    last = slice(parts.shape[1] - NOTE, parts.shape[1])
    total = parts[0, last, :]
    for k in range(1, parts.shape[0]):
        total = total + parts[k, last, :]
    note[...] = total


def summed(parts, thin):
    own = (parts.shape[1] - NOTE) * LANES // thin
    return pl.pallas_call(
        sum_kernel,
        name="sum_of_image_parts",
        out_shape=(jax.ShapeDtypeStruct((own, thin), F32), jax.ShapeDtypeStruct((NOTE, LANES), F32)),
        in_specs=[WHOLE],
        out_specs=(WHOLE, WHOLE),
        cost_estimate=cost(parts.size, 4 * parts.size),
    )(parts)


def body(teacher_img, teacher_txt, student_img, student_txt):
    rows, thin = student_img.shape
    cols = student_txt.shape[0]
    chips, cores = lax.axis_size("img_0"), lax.axis_size("img_1")
    img_count, txt_count = chips * cores, lax.axis_size(TXT)
    place, core = lax.axis_index("img_0"), lax.axis_index("img_1")

    t, s, row_stats, col_stats = local_stats(
        teacher_img, teacher_txt, student_img, student_txt, (txt_count, img_count)
    )
    row_stats = lax.all_to_all(row_stats, TXT, 0, 0, tiled=True)
    col_stats = lax.all_to_all(col_stats, IMG, 0, 0, tiled=True)
    delta, to_img, row_note = delta_and_img(row_stats, col_stats, t, s, student_txt)
    got_img = lax.all_to_all(to_img, TXT, 0, 0, tiled=True)

    theirs = txt_gradient(delta, student_img, row_note, jnp.stack([place, 1 - core]), chips)
    mine = txt_gradient(delta, student_img, row_note, jnp.stack([place, core]), chips)
    swap = [(k, 1 - k) for k in range(cores)]
    theirs = lax.ppermute(theirs, "img_1", swap)
    around = [
        (cores * z + c, cores * ((z + 1 - 2 * c) % chips) + c)
        for z in range(chips) for c in range(cores)
    ]
    flow = mine[0] + theirs[0]
    for k in range(1, chips // 2):
        flow = lax.ppermute(flow, IMG, around) + mine[k] + theirs[k]
    last = lax.ppermute(flow, IMG, [pair for pair in around if pair[0] % cores == 0])
    flow = jnp.where(core == 0, last, flow)
    halves = flow[:-NOTE].reshape(cores, -1, thin)
    note = flow[-NOTE:]
    keep = lax.dynamic_index_in_dim(halves, core, 0, keepdims=False)
    give = lax.dynamic_index_in_dim(halves, 1 - core, 0, keepdims=False)
    got = lax.ppermute(jnp.concatenate([give, note], axis=0), "img_1", swap)
    grad_txt = keep + got[:-NOTE]
    row_loss = note[0, 0] + got[-1, 0]

    grad_img, col_note = summed(got_img, thin)
    loss = (0.5 * LN2) * (
        row_loss / (rows * img_count) + col_note[0, 0] / (cols * txt_count)
    )
    return (loss, grad_img, grad_txt)


def solution(mesh):
    torus = Mesh(mesh.devices.reshape(8, 2, 4, 4), ("img_0", "img_1", "txt_0", "txt_1"))
    in_specs = (P(IMG, None), P(TXT, None), P(IMG, None), P(TXT, None))
    out_specs = (P(), P(IMG_TXT, None), P(TXT_IMG, None))
    return jax.shard_map(body, mesh=torus, in_specs=in_specs, out_specs=out_specs, check_vma=False)
```

time: 109 us -> 113 us (1.037); the launches traced: 107 us -> 112 us
  Pallas kernels: 0 us -> 27.8 us
  other arithmetic: 20 us -> 2.78 us
  blocking collectives: 0 us -> 14.5 us
  waiting for transfers between devices: 31.6 us -> 21.1 us
  matrix products: 8.68 us -> 0 us
  local copies, waits for them, and re-layouts: 12.1 us -> 8.83 us
  starting transfers between devices: 31.1 us -> 33.5 us
    pallas_call x0 -> x5, Pallas kernels: none -> 27.8 us  [the longest x1 12.4 us: local_stats(): pl.pallas_call(kernel, name='logits_and_statistics', out_shape=(logit, lo...]
    all_to_all x0 -> x1, blocking collectives: none -> 14.5 us  [body(): row_stats = lax.all_to_all(row_stats, TXT, 0, 0, tiled=True)]
    ppermute x8 -> x6, starting transfers between devices: 8.4 us -> 19.3 us  [the longest x1 15.4 us: body(): got = lax.ppermute(jnp.concatenate([give, note], axis=0), 'img_1', swap)]
    reduce_sum x9 -> x0, other arithmetic: 8.69 us -> none  [the longest x1 4.72 us: local_stats(): gap_sum = jnp.sum(weight * gap, axis=along)]
    dot_general x4 -> x0, matrix products: 8.68 us -> none  [the longest x1 4.8 us: body(): jnp.einsum('id,jd->ij', teacher_img, teacher_txt, preferred_element_type=...]
    all_to_all x2 -> x1, starting transfers between devices: 18 us -> 10.5 us  [body(): col_stats = lax.all_to_all(col_stats, IMG, 0, 0, tiled=True)]
    all_to_all x2 -> x1, waiting for transfers between devices: 16.4 us -> 10.2 us  [body(): col_stats = lax.all_to_all(col_stats, IMG, 0, 0, tiled=True)]
    convert_element_type x1 -> x0, other arithmetic: 5.05 us -> none  [body(): delta = (8.0 * (q_row - p_row + q_col - p_col)).astype(jnp.bfloat16)]
  transfers between devices with their start and end apart: 11 -> 8, of which waited for: 7 -> 5; matrix products, arithmetic and copies ran while one was open for 11% -> 3% of each run, Pallas kernels for 0% -> 4%
where the time goes in v2:
time: 113 us; the launch traced here: 112 us
  starting transfers between devices  33.5 us (30%)
  Pallas kernels  27.8 us (25%)
  waiting for transfers between devices  21.1 us (19%)
  blocking collectives  14.5 us (13%)
  local copies, waits for them, and re-layouts  8.83 us (8%)
  between operations  3.76 us (3%)
  other arithmetic  2.78 us (2%)
    ppermute x1, starting transfers between devices, body(): got = lax.ppermute(jnp.concatenate([give, note], axis=0), 'img_1', swap)  15.4 us
    all_to_all x1, blocking collectives, body(): row_stats = lax.all_to_all(row_stats, TXT, 0, 0, tiled=True)  14.5 us
    pallas_call x1, Pallas kernels, local_stats(): pl.pallas_call(kernel, name='logits_and_statistics', out_shape=(logit, lo...  12.4 us
    ppermute x3, waiting for transfers between devices, body(): flow = lax.ppermute(flow, IMG, around) + mine[k] + theirs[k]  10.5 us
    all_to_all x1, starting transfers between devices, body(): col_stats = lax.all_to_all(col_stats, IMG, 0, 0, tiled=True)  10.5 us
    all_to_all x1, waiting for transfers between devices, body(): col_stats = lax.all_to_all(col_stats, IMG, 0, 0, tiled=True)  10.2 us
    pallas_call x1, Pallas kernels, delta_and_img(): pl.pallas_call(functools.partial(delta_kernel, 3.0 / math.sqrt(thin)), na...  8.5 us
    unnamed x16, local copies, waits for them, and re-layouts  6.56 us
  transfers between devices with their start and end apart: 8, of which 5 were waited for; matrix products, arithmetic and copies ran while one was open for 3% of the time, Pallas kernels for 4%

profile of v2, /device:TPU:1, one launch (start us, length us, event | category | flops | bytes accessed | tf_op | source)
XLA Modules:
  0.0 112.4 jit_solution(8387762262176791175)
XLA Ops:
  0.6 1.2 %copy-done = bf16[1024,512]{1,0:T(8,128)(2,1)S(1)} copy-done((bf16[1024,512]{1,0:T(8,128)(2,1)S(1)}, bf16[1024,512]{1,0:T(8,128)(2,1)}, u32[]{:S(2)}) %copy-start) | copy-done | bytes 1048600
  1.9 1.2 %copy-done.2 = bf16[1024,512]{1,0:T(8,128)(2,1)S(1)} copy-done((bf16[1024,512]{1,0:T(8,128)(2,1)S(1)}, bf16[1024,512]{1,0:T(8,128)(2,1)}, u32[]{:S(2)}) %copy-start.2) | copy-done | bytes 1048600
  3.1 1.7 %copy-done.4 = bf16[1024,1280]{1,0:T(8,128)(2,1)S(1)} copy-done((bf16[1024,1280]{1,0:T(8,128)(2,1)S(1)}, bf16[1024,1280]{1,0:T(8,128)(2,1)}, u32[]{:S(2)}) %copy-start.4) | copy-done | bytes 2621464
  4.8 12.4 %logits_and_statistics.1 = (f32[1024,1024]{1,0:T(8,128)}, f32[1024,1024]{1,0:T(8,128)}, f32[16,24,128]{2,1,0:T(8,128)S(1)}, f32[16,24,128]{2,1,0:T(8,128)}) custom-call(bf16[1024,1280]{1,0:T(8,128)(2,1)S(1)} %copy-done.4, bf16[1024,1280]{1,0:T(8,128)(2,1)} %tt_hbm.1, bf16[1024,512]{1,0:T(8,128)(2,1)S(1)} %copy-done, bf16[1024,512]{1,0:T(8,128)(2,1)S(1)} %copy-done.2), custom_call_target="tpu_custom_call" | custom-call | flops 3758096384 | bytes 8388608 | tf_op jit(solution)/shard_map/logits_and_statistics/pallas_call | solution.py:152
  17.2 14.5 %all_to_all.15.row_stats = f32[16,24,128]{2,1,0:T(8,128)S(1)} all-to-all(f32[16,24,128]{2,1,0:T(8,128)S(1)} %get-tuple-element.12), channel_id=1, replica_groups=mesh['img_0'=8,'img_1'=2,'txt_0'=4,'txt_1'=4] {'txt_0','txt_1'}, dimensions={0} | all-to-all | bytes 393216 | tf_op jit(solution)/shard_map/all_to_all | solution.py:353
  31.8 10.5 %all-to-all-start.1 = ((f32[16,24,128]{2,1,0:T(8,128)}), f32[16,24,128]{2,1,0:T(8,128)S(1)}, u32[]{:S(2)}, u32[]{:S(2)}) async-start(f32[16,24,128]{2,1,0:T(8,128)} %get-tuple-element.13), calls=%async_computation.1 | async-start | bytes 393216 | tf_op jit(solution)/shard_map/all_to_all | solution.py:354
  42.2 0.1 pad_add_fusion.1.place
  42.3 10.2 %all-to-all-done.1.col_stats = f32[16,24,128]{2,1,0:T(8,128)S(1)} async-done(((f32[16,24,128]{2,1,0:T(8,128)}), f32[16,24,128]{2,1,0:T(8,128)S(1)}, u32[]{:S(2)}, u32[]{:S(2)}) %all-to-all-start.1) | async-done | bytes 196640 | tf_op jit(solution)/shard_map/all_to_all | solution.py:354
  52.6 8.5 %delta_and_image_gradient.1 = (bf16[1024,1024]{1,0:T(8,128)(2,1)S(1)}, f32[16,264,128]{2,1,0:T(8,128)}, f32[8,512]{1,0:T(8,128)S(1)}) custom-call(f32[16,24,128]{2,1,0:T(8,128)S(1)} %all_to_all.15.row_stats, f32[16,24,128]{2,1,0:T(8,128)S(1)} %all-to-all-done.1.col_stats, f32[1024,1024]{1,0:T(8,128)} %get-tuple-element.14.t, ...), custom_call_target="tpu_custom_call" | custom-call | flops 1073741824 | bytes 10485760 | tf_op jit(solution)/shard_map/delta_and_image_gradient/pallas_call | solution.py:249
  61.1 2.3 %text_gradient.3 = f32[4,136,512]{2,1,0:T(8,128)S(1)} custom-call(s32[2]{0:T(128)S(1)} %pad_add_fusion.1.place, bf16[1024,1024]{1,0:T(8,128)(2,1)S(1)} %get-tuple-element.16.delta, bf16[1024,512]{1,0:T(8,128)(2,1)S(1)} %copy-done.1, f32[8,512]{1,0:T(8,128)S(1)} %get-tuple-element.17.note), custom_call_target="tpu_custom_call" | custom-call | flops 536870912 | bytes 3145728 | tf_op jit(solution)/shard_map/text_gradient/pallas_call | solution.py:298
  63.3 0.1 collective-permute-start
  63.5 0.1 pad_add_fusion.place
  63.5 2.3 %text_gradient.2 = f32[4,136,512]{2,1,0:T(8,128)S(1)} custom-call(s32[2]{0:T(128)S(1)} %pad_add_fusion.place, bf16[1024,1024]{1,0:T(8,128)(2,1)S(1)} %get-tuple-element.16.delta, bf16[1024,512]{1,0:T(8,128)(2,1)S(1)} %copy-done.1, f32[8,512]{1,0:T(8,128)S(1)} %get-tuple-element.17.note), custom_call_target="tpu_custom_call" | custom-call | flops 536870912 | bytes 3145728 | tf_op jit(solution)/shard_map/text_gradient/pallas_call | solution.py:298
  65.8 0.4 collective-permute-done
  66.2 1.0 copy-done.6
  67.2 0.7 fusion.6
  67.9 3.7 %all-to-all-start.2 = ((f32[16,264,128]{2,1,0:T(8,128)}), f32[16,264,128]{2,1,0:T(8,128)S(1)}, u32[]{:S(2)}, u32[]{:S(2)}) async-start(f32[16,264,128]{2,1,0:T(8,128)} %get-tuple-element.18), calls=%async_computation.2 | async-start | bytes 4325376 | tf_op jit(solution)/shard_map/all_to_all | solution.py:356
  71.7 2.2 %collective-permute-done.1 = f32[136,512]{1,0:T(8,128)S(1)} collective-permute-done((f32[136,512]{1,0:T(8,128)}, f32[136,512]{1,0:T(8,128)S(1)}, u32[]{:S(2)}, u32[]{:S(2)}) %collective-permute-start.1) | collective-permute-done | bytes 278560 | tf_op jit(solution)/shard_map/ppermute | solution.py:368
  73.8 1.0 fusion.4
  74.9 1.0 collective-permute-start.2
  75.9 4.8 %collective-permute-done.2 = f32[136,512]{1,0:T(8,128)S(1)} collective-permute-done((f32[136,512]{1,0:T(8,128)S(1)}, f32[136,512]{1,0:T(8,128)S(1)}, u32[]{:S(2)}, u32[]{:S(2)}) %collective-permute-start.2) | collective-permute-done | bytes 278560 | tf_op jit(solution)/shard_map/ppermute | solution.py:368
  80.6 0.1 fusion.2
  80.7 2.2 %collective-permute-start.3 = (f32[136,512]{1,0:T(8,128)S(1)}, f32[136,512]{1,0:T(8,128)S(1)}, u32[]{:S(2)}, u32[]{:S(2)}) collective-permute-start(f32[136,512]{1,0:T(8,128)S(1)} %fusion.2), channel_id=1, source_target_pairs={{0,32},{16,240},{32,64},{48,16},{64,96},{80,48},{96,128},{112,80},... | collective-permute-start | bytes 835592 | tf_op jit(solution)/shard_map/ppermute | solution.py:368
  82.9 3.6 %collective-permute-done.3 = f32[136,512]{1,0:T(8,128)S(1)} collective-permute-done((f32[136,512]{1,0:T(8,128)S(1)}, f32[136,512]{1,0:T(8,128)S(1)}, u32[]{:S(2)}, u32[]{:S(2)}) %collective-permute-start.3) | collective-permute-done | bytes 278560 | tf_op jit(solution)/shard_map/ppermute | solution.py:368
  86.6 0.7 collective-permute-start.4
  87.4 15.4 %collective-permute-start.5 = (f32[72,512]{1,0:T(8,128)S(1)}, f32[72,512]{1,0:T(8,128)S(1)}, u32[]{:S(2)}, u32[]{:S(2)}) collective-permute-start(f32[72,512]{1,0:T(8,128)S(1)} %pad_maximum_fusion), channel_id=1, source_target_pairs={{0,16},{16,0},{1,17},{17,1},{2,18},{18,2},{3,19},{19,3},{4,20},{20... | collective-permute-start | bytes 442376 | tf_op jit(solution)/shard_map/ppermute | solution.py:375
  102.8 1.4 %copy-done.5 = f32[16,264,128]{2,1,0:T(8,128)} copy-done((f32[16,264,128]{2,1,0:T(8,128)}, f32[16,264,128]{2,1,0:T(8,128)S(1)}, u32[]{:S(2)}) %copy-start.5) | copy-done | bytes 2162712
  104.1 2.4 %sum_of_image_parts.1 = (f32[64,512]{1,0:T(8,128)}, f32[8,128]{1,0:T(8,128)}) custom-call(f32[16,264,128]{2,1,0:T(8,128)} %copy-done.5), custom_call_target="tpu_custom_call" | custom-call | flops 540672 | bytes 2162688 | tf_op jit(solution)/shard_map/sum_of_image_parts/pallas_call | solution.py:333
  106.5 1.2 %slice.55 = f32[1,1]{1,0:T(1,128)} slice(f32[8,128]{1,0:T(8,128)} %get-tuple-element.19), slice={[0:1], [0:1]} | slice | bytes 8 | tf_op jit(solution)/shard_map/slice | solution.py:381
  107.7 0.5 slice.65
  108.2 0.5 slice.68
  110.6 0.7 slice_add_fusion.1
  (21 shorter events, 0.2 us)
Async XLA Ops:
  0.6 1.2 %copy-start = (bf16[1024,512]{1,0:T(8,128)(2,1)S(1)}, bf16[1024,512]{1,0:T(8,128)(2,1)}, u32[]{:S(2)}) copy-start(bf16[1024,512]{1,0:T(8,128)(2,1)} %si.3) | copy-start | bytes 3145732
  1.9 1.2 %copy-start.2 = (bf16[1024,512]{1,0:T(8,128)(2,1)S(1)}, bf16[1024,512]{1,0:T(8,128)(2,1)}, u32[]{:S(2)}) copy-start(bf16[1024,512]{1,0:T(8,128)(2,1)} %st.1) | copy-start | bytes 3145732
  3.1 1.7 %copy-start.4 = (bf16[1024,1280]{1,0:T(8,128)(2,1)S(1)}, bf16[1024,1280]{1,0:T(8,128)(2,1)}, u32[]{:S(2)}) copy-start(bf16[1024,1280]{1,0:T(8,128)(2,1)} %ti_hbm.1) | copy-start | bytes 7864324
  4.8 47.7 %copy-start.3 = (bf16[1024,512]{1,0:T(8,128)(2,1)S(1)}, bf16[1024,512]{1,0:T(8,128)(2,1)}, u32[]{:S(2)}) copy-start(bf16[1024,512]{1,0:T(8,128)(2,1)} %st.1) | copy-start | bytes 3145732
  31.8 20.8 %all-to-all-start.1 = ((f32[16,24,128]{2,1,0:T(8,128)}), f32[16,24,128]{2,1,0:T(8,128)S(1)}, u32[]{:S(2)}, u32[]{:S(2)}) async-start(f32[16,24,128]{2,1,0:T(8,128)} %get-tuple-element.13), calls=%async_computation.1 | async-start | bytes 393216 | tf_op jit(solution)/shard_map/all_to_all | solution.py:354
  52.6 8.5 %copy-start.1 = (bf16[1024,512]{1,0:T(8,128)(2,1)S(1)}, bf16[1024,512]{1,0:T(8,128)(2,1)}, u32[]{:S(2)}) copy-start(bf16[1024,512]{1,0:T(8,128)(2,1)} %si.3) | copy-start | bytes 3145732
  63.3 2.8 %collective-permute-start = (f32[4,136,512]{2,1,0:T(8,128)S(1)}, f32[4,136,512]{2,1,0:T(8,128)S(1)}, u32[]{:S(2)}, u32[]{:S(2)}) collective-permute-start(f32[4,136,512]{2,1,0:T(8,128)S(1)} %text_gradient.3), channel_id=1, source_target_pairs={{0,16},{16,0},{1,17},{17,1},{2,18},{18,2},{3,19},{19,3},{4,20},{20... | collective-permute-start | bytes 3342344 | tf_op jit(solution)/shard_map/ppermute | solution.py:361
  66.2 1.0 copy-start.6
  67.9 5.9 %collective-permute-start.1 = (f32[136,512]{1,0:T(8,128)}, f32[136,512]{1,0:T(8,128)S(1)}, u32[]{:S(2)}, u32[]{:S(2)}) collective-permute-start(f32[136,512]{1,0:T(8,128)} %fusion.6), channel_id=1, source_target_pairs={{0,32},{16,240},{32,64},{48,16},{64,96},{80,48},{96,128},{112,80},... | collective-permute-start | bytes 835592 | tf_op jit(solution)/shard_map/ppermute | solution.py:368
  67.9 34.8 %all-to-all-start.2 = ((f32[16,264,128]{2,1,0:T(8,128)}), f32[16,264,128]{2,1,0:T(8,128)S(1)}, u32[]{:S(2)}, u32[]{:S(2)}) async-start(f32[16,264,128]{2,1,0:T(8,128)} %get-tuple-element.18), calls=%async_computation.2 | async-start | bytes 4325376 | tf_op jit(solution)/shard_map/all_to_all | solution.py:356
  71.7 9.0 %copy-start.7 = (f32[4,136,512]{2,1,0:T(8,128)S(1)}, f32[4,136,512]{2,1,0:T(8,128)}, u32[]{:S(2)}) copy-start(f32[4,136,512]{2,1,0:T(8,128)} %copy-done.6) | copy-start | bytes 3342340
  74.9 5.8 %collective-permute-start.2 = (f32[136,512]{1,0:T(8,128)S(1)}, f32[136,512]{1,0:T(8,128)S(1)}, u32[]{:S(2)}, u32[]{:S(2)}) collective-permute-start(f32[136,512]{1,0:T(8,128)S(1)} %fusion.4), channel_id=1, source_target_pairs={{0,32},{16,240},{32,64},{48,16},{64,96},{80,48},{96,128},{112,80},... | collective-permute-start | bytes 835592 | tf_op jit(solution)/shard_map/ppermute | solution.py:368
  80.7 5.8 %collective-permute-start.3 = (f32[136,512]{1,0:T(8,128)S(1)}, f32[136,512]{1,0:T(8,128)S(1)}, u32[]{:S(2)}, u32[]{:S(2)}) collective-permute-start(f32[136,512]{1,0:T(8,128)S(1)} %fusion.2), channel_id=1, source_target_pairs={{0,32},{16,240},{32,64},{48,16},{64,96},{80,48},{96,128},{112,80},... | collective-permute-start | bytes 835592 | tf_op jit(solution)/shard_map/ppermute | solution.py:368
  86.6 0.7 collective-permute-start.4
  87.4 20.8 %collective-permute-start.5 = (f32[72,512]{1,0:T(8,128)S(1)}, f32[72,512]{1,0:T(8,128)S(1)}, u32[]{:S(2)}, u32[]{:S(2)}) collective-permute-start(f32[72,512]{1,0:T(8,128)S(1)} %pad_maximum_fusion), channel_id=1, source_target_pairs={{0,16},{16,0},{1,17},{17,1},{2,18},{18,2},{3,19},{19,3},{4,20},{20... | collective-permute-start | bytes 442376 | tf_op jit(solution)/shard_map/ppermute | solution.py:375
  102.8 1.4 %copy-start.5 = (f32[16,264,128]{2,1,0:T(8,128)}, f32[16,264,128]{2,1,0:T(8,128)S(1)}, u32[]{:S(2)}) copy-start(f32[16,264,128]{2,1,0:T(8,128)S(1)} %all-to-all-done.2.parts) | copy-start | bytes 6488068

commit v3 on v2

v3 whole, which is shorter than its diff:
```python
import functools
import math

import jax
import jax.numpy as jnp
from jax import lax
from jax.experimental import pallas as pl
from jax.experimental.pallas import tpu as pltpu
from jax.sharding import Mesh
from jax.sharding import PartitionSpec as P

IMG = ("img_0", "img_1")
TXT = ("txt_0", "txt_1")
IMG_TXT = ("img_0", "img_1", "txt_0", "txt_1")
TXT_IMG = ("txt_0", "txt_1", "img_0", "img_1")
LANES = 128
NOTE = 8
VMEM_LIMIT = 40 * 1024 * 1024
STATS_LIMIT = 54 * 1024 * 1024
LN2 = math.log(2.0)
F32 = jnp.float32
WHOLE = pl.BlockSpec(memory_space=pltpu.VMEM)
ANYWHERE = pl.BlockSpec(memory_space=pl.ANY)


def cost(flops, size, transcendentals=0):
    return pl.CostEstimate(flops=flops, bytes_accessed=size, transcendentals=transcendentals)


def stats_kernel(scale_teach, scale_learn, ti_hbm, tt_hbm, si_hbm, st_hbm, t, s, row_out, col_out,
                 ti, tt, si, st, peaks, sums, col_peaks, col_sums, sems):
    rows, cols = t.shape
    tall = 256
    chunks = rows // tall

    def load(src, dst, at, size, which):
        copy = pltpu.make_async_copy(
            src.at[pl.ds(at, size), :], dst.at[pl.ds(at, size), :], sems.at[which]
        )
        copy.start()
        return copy

    tt_load = load(tt_hbm, tt, 0, cols, 0)
    ti_loads = [load(ti_hbm, ti, n * tall, tall, 1 + n) for n in range(chunks)]
    st_load = load(st_hbm, st, 0, cols, 1 + chunks)
    si_load = load(si_hbm, si, 0, rows, 2 + chunks)

    def logits(left, right, out, scale, which, arrivals):
        for n in range(chunks):
            if arrivals:
                arrivals[n].wait()
            down = slice(n * tall, (n + 1) * tall)
            block = scale * lax.dot_general(
                left[down, :], right[...], (((1,), (1,)), ((), ())), preferred_element_type=F32
            )
            out[down, :] = block
            top = jnp.max(block.reshape(tall // 8, 8, cols), axis=0)
            col_peaks[which] = jnp.maximum(col_peaks[which], top) if n else top
            side = block[:, :LANES]
            for k in range(1, cols // LANES):
                side = jnp.maximum(side, block[:, k * LANES : (k + 1) * LANES])
            peaks[which, down, :] = jnp.broadcast_to(
                jnp.max(side, axis=1, keepdims=True), (tall, LANES)
            )
        col_peaks[which] = jnp.broadcast_to(
            jnp.max(col_peaks[which], axis=0, keepdims=True), (8, cols)
        )

    tt_load.wait()
    logits(ti, tt, t, scale_teach, 0, ti_loads)
    st_load.wait()
    si_load.wait()
    logits(si, st, s, scale_learn, 1, None)

    group = 4 * LANES
    for h in range(cols // group):
        def strip(r, carry):
            at = pl.multiple_of(r * 8, 8)
            down = pl.ds(at, 8)
            row_peak_t, row_peak_s = peaks[0, down, :], peaks[1, down, :]
            row_t = row_s = row_g = None
            new = []
            for k in range(group // LANES):
                across = slice(h * group + k * LANES, h * group + (k + 1) * LANES)
                tv, sv = t[down, across], s[down, across]
                gap = tv - sv
                wr = jnp.exp2(tv - row_peak_t)
                vr = jnp.exp2(sv - row_peak_s)
                wc = jnp.exp2(tv - col_peaks[0, :, across])
                vc = jnp.exp2(sv - col_peaks[1, :, across])
                row_t = wr if row_t is None else row_t + wr
                row_s = vr if row_s is None else row_s + vr
                row_g = wr * gap if row_g is None else row_g + wr * gap
                ct, cs, cg = carry[3 * k : 3 * k + 3]
                new += [ct + wc, cs + vc, cg + wc * gap]
            for q, value in enumerate((row_t, row_s, row_g)):
                if h:
                    value = value + sums[q, down, :]
                sums[q, down, :] = value
            return tuple(new)

        zeros = tuple(jnp.zeros((8, LANES), F32) for _ in range(3 * group // LANES))
        found = lax.fori_loop(0, rows // 8, strip, zeros, unroll=4)
        for k in range(group // LANES):
            across = slice(h * group + k * LANES, h * group + (k + 1) * LANES)
            for q in range(3):
                col_sums[q, :, across] = found[3 * k + q]

    def publish(out, peak_t, peak_s, mass_t, mass_s, gap):
        lse_t = peak_t + jnp.log2(mass_t)
        lse_s = peak_s + jnp.log2(mass_s)
        mean = gap / mass_t
        for q, value in enumerate((lse_t, lse_s, mean)):
            for b in range(value.shape[1] // LANES):
                line = value[:, b * LANES : (b + 1) * LANES]
                out[q * 8 + b : q * 8 + b + 1, :] = line

    publish(
        col_out, col_peaks[0, :1, :], col_peaks[1, :1, :],
        *(jnp.sum(col_sums[q], axis=0, keepdims=True) for q in range(3)),
    )

    def across_lanes(value, weight):
        found = lax.dot_general(
            jnp.full((8, LANES), weight, F32), value, (((1,), (1,)), ((), ())),
            preferred_element_type=F32, precision=lax.Precision.HIGHEST,
        )
        return found[:1]

    publish(
        row_out,
        across_lanes(peaks[0], 1.0 / LANES), across_lanes(peaks[1], 1.0 / LANES),
        *(across_lanes(sums[q], 1.0) for q in range(3)),
    )


def local_stats(teacher_img, teacher_txt, student_img, student_txt):
    rows, deep = teacher_img.shape
    cols, thin = student_txt.shape
    kernel = functools.partial(
        stats_kernel, 3.0 / math.sqrt(deep) / LN2, 3.0 / math.sqrt(thin) / LN2
    )
    return pl.pallas_call(
        kernel,
        name="logits_and_statistics",
        out_shape=(
            pltpu.VMEM((rows, cols), F32), pltpu.VMEM((rows, cols), F32),
            jax.ShapeDtypeStruct((3 * rows // LANES, LANES), F32),
            jax.ShapeDtypeStruct((3 * cols // LANES, LANES), F32),
        ),
        in_specs=[ANYWHERE] * 4,
        out_specs=(WHOLE,) * 4,
        scratch_shapes=[
            pltpu.VMEM((rows, deep), jnp.bfloat16), pltpu.VMEM((cols, deep), jnp.bfloat16),
            pltpu.VMEM((rows, thin), jnp.bfloat16), pltpu.VMEM((cols, thin), jnp.bfloat16),
            pltpu.VMEM((2, rows, LANES), F32), pltpu.VMEM((3, rows, LANES), F32),
            pltpu.VMEM((2, 8, cols), F32), pltpu.VMEM((3, 8, cols), F32),
            pltpu.SemaphoreType.DMA((8,)),
        ],
        compiler_params=pltpu.CompilerParams(vmem_limit_bytes=STATS_LIMIT),
        cost_estimate=cost(2 * rows * cols * (deep + thin), 8 * rows * cols, 4 * rows * cols),
    )(teacher_img, teacher_txt, student_img, student_txt)


def joined(parts):
    teach, learn, gap = ([part[8 * q : 8 * q + 8, :] for part in parts] for q in range(3))
    teach_peak = functools.reduce(jnp.maximum, teach)
    learn_peak = functools.reduce(jnp.maximum, learn)
    weights = [jnp.exp2(part - teach_peak) for part in teach]
    mass = sum(weights[1:], weights[0])
    shares = [jnp.exp2(part - learn_peak) for part in learn]
    gaps = [weight * part for weight, part in zip(weights, gap)]
    return (
        teach_peak + jnp.log2(mass),
        learn_peak + jnp.log2(sum(shares[1:], shares[0])),
        sum(gaps[1:], gaps[0]) / mass,
    )


def join_kernel(groups, *refs):
    sources, outs = refs[: len(refs) - len(groups)], refs[len(refs) - len(groups) :]
    for group, out in zip(groups, outs):
        for q, value in enumerate(joined([sources[k][...] for k in group])):
            out[8 * q : 8 * q + 8, :] = value


def join(groups, *parts):
    return pl.pallas_call(
        functools.partial(join_kernel, groups),
        name="joined_statistics",
        out_shape=[jax.ShapeDtypeStruct(parts[group[0]].shape, F32) for group in groups],
        in_specs=[WHOLE] * len(parts),
        out_specs=[WHOLE] * len(groups),
        cost_estimate=cost(parts[0].size * 20, parts[0].size * 4 * len(parts), parts[0].size * 4),
    )(*parts)


def gradient_kernel(scale, *refs):
    row_parts, col_parts = refs[:4], refs[4:6]
    t, s, st, si, img_out, theirs, mine, delta, row_norms, col_norms = refs[6:]
    rows, cols = t.shape
    thin = st.shape[1]
    row_teach, row_learn, row_mean = joined([part[...] for part in row_parts])
    col_teach, col_learn, col_mean = joined([part[...] for part in col_parts])
    row_total = jnp.sum(row_mean + row_learn - row_teach)
    col_total = jnp.sum(col_mean + col_learn - col_teach)
    for which, (down, across) in enumerate(((row_teach, col_teach), (row_learn, col_learn))):
        turned = jnp.concatenate([down - 3.0] * (LANES // 8), axis=0).T
        for b in range(8):
            row_norms[which, b * LANES : (b + 1) * LANES, :] = jnp.broadcast_to(
                turned[:, b : b + 1], (LANES, LANES)
            )
            col_norms[which, :, b * LANES : (b + 1) * LANES] = jnp.broadcast_to(
                across[b : b + 1, :] - 3.0, (16, LANES)
            )

    def strip(r, carry):
        down = pl.ds(pl.multiple_of(r * 16, 16), 16)
        row_t, row_s = row_norms[0, down, :], row_norms[1, down, :]
        for k in range(cols // LANES):
            across = slice(k * LANES, (k + 1) * LANES)
            tv, sv = t[down, across], s[down, across]
            value = (
                jnp.exp2(sv - row_s) - jnp.exp2(tv - row_t)
                + jnp.exp2(sv - col_norms[1, :, across]) - jnp.exp2(tv - col_norms[0, :, across])
            )
            delta[down, across] = value.astype(jnp.bfloat16)
        return carry

    lax.fori_loop(0, rows // 16, strip, 0, unroll=2)

    place, core = lax.axis_index("img_0"), lax.axis_index("img_1")
    chips = lax.axis_size("img_0")
    tall = cols // chips
    half = tall // 2
    full_note = jnp.full((NOTE, thin), row_total, F32)

    def text_block(out, top, far, part, note):
        size = tall if part is None else half
        at = lax.rem(place + far + chips, chips) * tall
        across = pl.ds(pl.multiple_of(at, tall), tall)
        grad = scale * lax.dot_general(
            delta[:, across], si[...], (((0,), (0,)), ((), ())), preferred_element_type=F32
        )
        if part is not None:
            grad = jnp.where(part == 0, grad[:half], grad[half:])
        out[top : top + size, :] = grad
        out[top + size : top + size + NOTE, :] = note

    for out, flow in ((theirs, 1 - core), (mine, core)):
        sign = 1 - 2 * flow
        top = 0
        for far, part, note in (
            (2 * sign, None, full_note), (3 * sign, None, full_note), (sign, None, full_note),
            (chips // 2, flow, 0.5 * full_note), (0, flow, full_note),
        ):
            text_block(out, top, far, part, note)
            top += (tall if part is None else half) + NOTE

    pieces, lines, _ = img_out.shape
    own = rows // pieces
    some = 4
    for n in range(pieces // some):
        grad = scale * jnp.dot(
            delta[n * some * own : (n + 1) * some * own, :], st[...], preferred_element_type=F32
        )
        for k in range(some):
            for b in range(thin // LANES):
                img_out[n * some + k, b * own : (b + 1) * own, :] = grad[
                    k * own : (k + 1) * own, b * LANES : (b + 1) * LANES
                ]
    for k in range(pieces):
        img_out[k, lines - NOTE :, :] = jnp.full((NOTE, LANES), col_total, F32)


def flow_rows(tall):
    full, part = tall + NOTE, tall // 2 + NOTE
    return (full, full, full, part, part)


def gradients(row_parts, col_parts, t, s, student_txt, student_img, pieces, chips):
    rows, cols = t.shape
    thin = student_txt.shape[1]
    lines = rows // pieces * thin // LANES + NOTE
    flow = jax.ShapeDtypeStruct((sum(flow_rows(cols // chips)), thin), F32)
    return pl.pallas_call(
        functools.partial(gradient_kernel, 3.0 / math.sqrt(thin)),
        name="delta_and_gradients",
        out_shape=(jax.ShapeDtypeStruct((pieces, lines, LANES), F32), flow, flow),
        in_specs=[WHOLE] * (len(row_parts) + len(col_parts) + 4),
        out_specs=(WHOLE,) * 3,
        scratch_shapes=[
            pltpu.VMEM((rows, cols), jnp.bfloat16),
            pltpu.VMEM((2, rows, LANES), F32), pltpu.VMEM((2, 16, cols), F32),
        ],
        compiler_params=pltpu.CompilerParams(vmem_limit_bytes=VMEM_LIMIT),
        cost_estimate=cost(4 * rows * cols * thin, 8 * rows * cols, 4 * rows * cols),
    )(*row_parts, *col_parts, t, s, student_txt, student_img)


def add_kernel(mine, theirs, *outs):
    top = 0
    for out in outs:
        down = slice(top, top + out.shape[0])
        out[...] = mine[down, :] + theirs[down, :]
        top += out.shape[0]


def added(mine, theirs, chips):
    thin = mine.shape[1]
    sizes = flow_rows(2 * (mine.shape[0] - 5 * NOTE) // chips)
    return pl.pallas_call(
        add_kernel,
        name="both_cores_text_terms",
        out_shape=[jax.ShapeDtypeStruct((size, thin), F32) for size in sizes],
        in_specs=[WHOLE] * 2,
        out_specs=[WHOLE] * len(sizes),
        cost_estimate=cost(mine.size, 12 * mine.size),
    )(mine, theirs)


def relay_kernel(near, next_one, far, farthest, out):
    core = lax.axis_index("img_1")
    full = out.shape[0]
    half = (full - NOTE) // 2
    out[...] = near[...] + next_one[...] + far[...]
    down = pl.ds(pl.multiple_of(core * half, half), half)
    out[down, :] = out[down, :] + farthest[:half, :]
    out[full - NOTE :, :] = out[full - NOTE :, :] + farthest[half:, :]


def relayed(*parts):
    return pl.pallas_call(
        relay_kernel,
        name="relayed_text_terms",
        out_shape=jax.ShapeDtypeStruct(parts[0].shape, F32),
        in_specs=[WHOLE] * 4,
        out_specs=WHOLE,
        cost_estimate=cost(parts[0].size * 3, 16 * parts[0].size),
    )(*parts)


def sum_kernel(parts, out, note):
    own = out.shape[0]
    for b in range(out.shape[1] // LANES):
        total = parts[0, b * own : (b + 1) * own, :]
        for k in range(1, parts.shape[0]):
            total = total + parts[k, b * own : (b + 1) * own, :]
        out[:, b * LANES : (b + 1) * LANES] = total
    last = slice(parts.shape[1] - NOTE, parts.shape[1])
    total = parts[0, last, :]
    for k in range(1, parts.shape[0]):
        total = total + parts[k, last, :]
    note[...] = total


def summed(parts, thin):
    own = (parts.shape[1] - NOTE) * LANES // thin
    return pl.pallas_call(
        sum_kernel,
        name="sum_of_image_parts",
        out_shape=(jax.ShapeDtypeStruct((own, thin), F32), jax.ShapeDtypeStruct((NOTE, LANES), F32)),
        in_specs=[WHOLE],
        out_specs=(WHOLE, WHOLE),
        cost_estimate=cost(parts.size, 4 * parts.size),
    )(parts)


def finish_kernel(row_share, col_share, flow, other, own, col_note, out, loss):
    half = out.shape[0]
    core = lax.axis_index("img_1")
    down = pl.ds(pl.multiple_of(core * half, half), half)
    out[...] = flow[down, :] + other[down, :] + own[:half, :]
    row_note = flow[2 * half :, :LANES] + other[2 * half :, :LANES] + own[half:, :LANES]
    loss[...] = (0.5 * LN2) * (row_note * row_share + col_note[...] * col_share)


def finished(row_share, col_share, flow, other, own, col_note):
    thin = flow.shape[1]
    return pl.pallas_call(
        functools.partial(finish_kernel, row_share, col_share),
        name="text_gradient_and_loss",
        out_shape=(
            jax.ShapeDtypeStruct((own.shape[0] - NOTE, thin), F32),
            jax.ShapeDtypeStruct((NOTE, LANES), F32),
        ),
        in_specs=[WHOLE] * 4,
        out_specs=(WHOLE, WHOLE),
        cost_estimate=cost(own.size * 3, 16 * own.size),
    )(flow, other, own, col_note)


def turn(size, step):
    return [(k, (k + step) % size) for k in range(size)]


def body(teacher_img, teacher_txt, student_img, student_txt):
    rows = student_img.shape[0]
    cols, thin = student_txt.shape
    chips, cores = lax.axis_size("img_0"), lax.axis_size("img_1")
    img_count, txt_count = chips * cores, lax.axis_size(TXT)
    side = lax.axis_size("txt_0")

    t, s, row, col = local_stats(teacher_img, teacher_txt, student_img, student_txt)
    xs = [lax.ppermute(row, "txt_0", turn(side, k)) for k in (1, 3, 2)]
    below = lax.ppermute(col, "img_0", turn(chips, 1))
    above = lax.ppermute(col, "img_0", turn(chips, -1))
    row, three, two = join(((0, 1, 2, 3), (4, 5, 6), (4, 5)), row, *xs, col, below, above)
    ys = [lax.ppermute(row, "txt_1", turn(side, k)) for k in (1, 3, 2)]
    below = lax.ppermute(three, "img_0", turn(chips, 3))
    above = lax.ppermute(two, "img_0", turn(chips, -3))
    (col,) = join(((0, 1, 2),), three, below, above)
    swap = turn(cores, 1)
    other = lax.ppermute(col, "img_1", swap)

    to_img, theirs, mine = gradients(
        (row, *ys), (col, other), t, s, student_txt, student_img, txt_count, chips
    )
    theirs = lax.ppermute(theirs, "img_1", swap)
    got_img = lax.all_to_all(to_img, TXT, 0, 0, tiled=True)
    one, two, near, three, own = added(mine, theirs, chips)

    def outward(value, step):
        pairs = [
            (cores * z + c, cores * ((z + step * (1 - 2 * c)) % chips) + c)
            for z in range(chips) for c in range(cores)
        ]
        return lax.ppermute(value, IMG, pairs)

    flow = relayed(near, outward(one, 1), outward(two, 2), outward(three, 3))
    flow = outward(flow, 1)
    across = lax.ppermute(flow, "img_1", swap)
    grad_img, col_note = summed(got_img, thin)
    grad_txt, loss = finished(
        1.0 / (rows * img_count), 1.0 / (cols * txt_count), flow, across, own, col_note
    )
    return (loss[0, 0], grad_img, grad_txt)


def solution(mesh):
    torus = Mesh(mesh.devices.reshape(8, 2, 4, 4), ("img_0", "img_1", "txt_0", "txt_1"))
    in_specs = (P(IMG, None), P(TXT, None), P(IMG, None), P(TXT, None))
    out_specs = (P(), P(IMG_TXT, None), P(TXT_IMG, None))
    return jax.shard_map(body, mesh=torus, in_specs=in_specs, out_specs=out_specs, check_vma=False)
```

time: 113 us -> 113 us (level)
  blocking collectives: 14.5 us -> 0 us
  Pallas kernels: 27.8 us -> 34 us
  local copies, waits for them, and re-layouts: 8.83 us -> 14.9 us
  waiting for transfers between devices: 21.1 us -> 25.5 us
  starting transfers between devices: 33.5 us -> 37.5 us
  between operations: 3.76 us -> 0.75 us
  other arithmetic: 2.78 us -> 0 us
    all_to_all x1 -> x0, blocking collectives: 14.5 us -> none  [body(): row_stats = lax.all_to_all(row_stats, TXT, 0, 0, tiled=True)]
    ppermute x5 -> x16, starting transfers between devices: 19.2 us -> 32.4 us  [the longest x4 6.94 us: outward(): return lax.ppermute(value, IMG, pairs)]
    ppermute x5 -> x16, waiting for transfers between devices: 10.5 us -> 23.1 us  [the longest x4 18.3 us: outward(): return lax.ppermute(value, IMG, pairs)]
    all_to_all x1 -> x0, starting transfers between devices: 10.5 us -> none  [body(): col_stats = lax.all_to_all(col_stats, IMG, 0, 0, tiled=True)]
    all_to_all x1 -> x0, waiting for transfers between devices: 10.2 us -> none  [body(): col_stats = lax.all_to_all(col_stats, IMG, 0, 0, tiled=True)]
    unnamed x16 -> x42, local copies, waits for them, and re-layouts: 6.56 us -> 13.7 us
    pallas_call x4 -> x7, Pallas kernels: 25.4 us -> 31.7 us  [the longest x1 12.9 us: local_stats(): pl.pallas_call(kernel, name='logits_and_statistics', out_shape=(pltpu.VME...]
    add x5 -> x0, other arithmetic: 2.58 us -> none  [the longest x3 1.16 us: body(): flow = lax.ppermute(flow, IMG, around) + mine[k] + theirs[k]]
  transfers between devices with their start and end apart: 8 -> 18, of which waited for: 5 -> 7; matrix products, arithmetic and copies ran while one was open for 3% -> 0% of each run, Pallas kernels for 4% -> 7%
where the time goes in v3:
time: 113 us
  starting transfers between devices  37.5 us (33%)
  Pallas kernels  34 us (30%)
  waiting for transfers between devices  25.5 us (23%)
  local copies, waits for them, and re-layouts  14.9 us (13%)
    ppermute x4, waiting for transfers between devices, outward(): return lax.ppermute(value, IMG, pairs)  18.3 us
    unnamed x42, local copies, waits for them, and re-layouts  13.7 us
    pallas_call x1, Pallas kernels, local_stats(): pl.pallas_call(kernel, name='logits_and_statistics', out_shape=(pltpu.VME...  12.9 us
    pallas_call x1, Pallas kernels, gradients(): pl.pallas_call(functools.partial(gradient_kernel, 3.0 / math.sqrt(thin)),...  9.65 us
    ppermute x4, starting transfers between devices, outward(): return lax.ppermute(value, IMG, pairs)  6.94 us
    ppermute x1, starting transfers between devices, body(): above = lax.ppermute(col, 'img_0', turn(chips, -1))  6.4 us
    all_to_all x1, starting transfers between devices, body(): got_img = lax.all_to_all(to_img, TXT, 0, 0, tiled=True)  4.44 us
    ppermute x3, starting transfers between devices, body(): ys = [lax.ppermute(row, 'txt_1', turn(side, k)) for k in (1, 3, 2)]  4.38 us
  transfers between devices with their start and end apart: 18, of which 7 were waited for; matrix products, arithmetic and copies ran while one was open for 0% of the time, Pallas kernels for 7%

profile of v3, /device:TPU:1, one launch (start us, length us, event | category | flops | bytes accessed | tf_op | source)
XLA Modules:
  0.0 112.7 jit_solution(7773493562955496449)
XLA Ops:
  0.6 12.9 %logits_and_statistics.1 = (f32[1024,1024]{1,0:T(8,128)S(1)}, f32[1024,1024]{1,0:T(8,128)S(1)}, f32[24,128]{1,0:T(8,128)}, f32[24,128]{1,0:T(8,128)}) custom-call(bf16[1024,1280]{1,0:T(8,128)(2,1)} %ti_hbm.1, bf16[1024,1280]{1,0:T(8,128)(2,1)} %tt_hbm.1, bf16[1024,512]{1,0:T(8,128)(2,1)} %refs_9_.1, bf16[1024,512]{1,0:T(8,128)(2,1)} %refs_8_.1), custom_call_target="tpu_custom_call" | custom-call | flops 3758096384 | bytes 8388608 | tf_op jit(solution)/shard_map/logits_and_statistics/pallas_call | solution.py:143
  13.5 2.0 %copy-done = f32[1024,1024]{1,0:T(8,128)} copy-done((f32[1024,1024]{1,0:T(8,128)}, f32[1024,1024]{1,0:T(8,128)S(1)}, u32[]{:S(2)}) %copy-start) | copy-done | bytes 4194328
  15.5 2.0 %copy-done.2 = f32[1024,1024]{1,0:T(8,128)} copy-done((f32[1024,1024]{1,0:T(8,128)}, f32[1024,1024]{1,0:T(8,128)S(1)}, u32[]{:S(2)}) %copy-start.2) | copy-done | bytes 4194328
  17.5 6.4 %collective-permute-start.4 = (f32[24,128]{1,0:T(8,128)}, f32[24,128]{1,0:T(8,128)S(1)}, u32[]{:S(2)}, u32[]{:S(2)}) collective-permute-start(f32[24,128]{1,0:T(8,128)} %get-tuple-element.23.refs_4_), channel_id=1, source_target_pairs={{0,224},{32,0},{64,32},{96,64},{128,96},{160,128},{192,160},{224,1... | collective-permute-start | bytes 36872 | tf_op jit(solution)/shard_map/ppermute | solution.py:407
  23.9 2.7 %collective-permute-start.2 = (f32[24,128]{1,0:T(8,128)}, f32[24,128]{1,0:T(8,128)S(1)}, u32[]{:S(2)}, u32[]{:S(2)}) collective-permute-start(f32[24,128]{1,0:T(8,128)} %get-tuple-element.22.refs_0_), channel_id=1, source_target_pairs={{0,8},{4,12},{8,0},{12,4},{1,9},{5,13},{9,1},{13,5},{2,10},{6,14},... | collective-permute-start | bytes 36872 | tf_op jit(solution)/shard_map/ppermute | solution.py:405
  28.2 1.5 %collective-permute-done.1.refs_2_ = f32[24,128]{1,0:T(8,128)S(1)} collective-permute-done((f32[24,128]{1,0:T(8,128)}, f32[24,128]{1,0:T(8,128)S(1)}, u32[]{:S(2)}, u32[]{:S(2)}) %collective-permute-start.1) | collective-permute-done | bytes 12320 | tf_op jit(solution)/shard_map/ppermute | solution.py:405
  29.7 1.8 %collective-permute-done.refs_1_ = f32[24,128]{1,0:T(8,128)S(1)} collective-permute-done((f32[24,128]{1,0:T(8,128)}, f32[24,128]{1,0:T(8,128)S(1)}, u32[]{:S(2)}, u32[]{:S(2)}) %collective-permute-start) | collective-permute-done | bytes 12320 | tf_op jit(solution)/shard_map/ppermute | solution.py:405
  32.1 1.5 %joined_statistics.2 = (f32[24,128]{1,0:T(8,128)}, f32[24,128]{1,0:T(8,128)}, f32[24,128]{1,0:T(8,128)}) custom-call(f32[24,128]{1,0:T(8,128)} %get-tuple-element.22.refs_0_, f32[24,128]{1,0:T(8,128)} %copy-done.20, f32[24,128]{1,0:T(8,128)} %copy-done.19, f32[24,128]{1,0:T(8,128)} %copy-done.18, f32[24,128]{1,0:T(8,128)} %get-tuple-element.23.refs_4_, ...), custom_call_target="tpu_custom_call" | custom-call | flops 61440 | bytes 86016 | tf_op jit(solution)/shard_map/joined_statistics/pallas_call | solution.py:188
  33.5 2.3 %collective-permute-start.9 = (f32[24,128]{1,0:T(8,128)}, f32[24,128]{1,0:T(8,128)S(1)}, u32[]{:S(2)}, u32[]{:S(2)}) collective-permute-start(f32[24,128]{1,0:T(8,128)} %get-tuple-element.26), channel_id=1, source_target_pairs={{0,160},{32,192},{64,224},{96,0},{128,32},{160,64},{192,96},{224,1... | collective-permute-start | bytes 36872 | tf_op jit(solution)/shard_map/ppermute | solution.py:411
  35.9 0.9 collective-permute-start.8
  36.8 2.9 %collective-permute-start.7 = (f32[24,128]{1,0:T(8,128)}, f32[24,128]{1,0:T(8,128)S(1)}, u32[]{:S(2)}, u32[]{:S(2)}) collective-permute-start(f32[24,128]{1,0:T(8,128)} %get-tuple-element.24.refs_0_), channel_id=1, source_target_pairs={{0,2},{1,3},{2,0},{3,1},{4,6},{5,7},{6,4},{7,5},{8,10},{9,11},{10,... | collective-permute-start | bytes 36872 | tf_op jit(solution)/shard_map/ppermute | solution.py:409
  42.4 1.4 %joined_statistics.3.refs_4_ = f32[24,128]{1,0:T(8,128)} custom-call(f32[24,128]{1,0:T(8,128)} %get-tuple-element.25.refs_0_, f32[24,128]{1,0:T(8,128)} %copy-done.15, f32[24,128]{1,0:T(8,128)} %copy-done.14), custom_call_target="tpu_custom_call" | custom-call | flops 61440 | bytes 36864 | tf_op jit(solution)/shard_map/joined_statistics/pallas_call | solution.py:188
  43.8 4.2 %collective-permute-start.10 = (f32[24,128]{1,0:T(8,128)}, f32[24,128]{1,0:T(8,128)S(1)}, u32[]{:S(2)}, u32[]{:S(2)}) collective-permute-start(f32[24,128]{1,0:T(8,128)} %joined_statistics.3.refs_4_), channel_id=1, source_target_pairs={{0,16},{16,0},{1,17},{17,1},{2,18},{18,2},{3,19},{19,3},{4,20},{20... | collective-permute-start | bytes 36872 | tf_op jit(solution)/shard_map/ppermute | solution.py:414
  48.0 1.0 collective-permute-done.10.refs_5_
  49.1 2.2 %copy-done.1 = f32[1024,1024]{1,0:T(8,128)S(1)} copy-done((f32[1024,1024]{1,0:T(8,128)S(1)}, f32[1024,1024]{1,0:T(8,128)}, u32[]{:S(2)}) %copy-start.1) | copy-done | bytes 4194328
  51.2 1.2 %copy-done.5 = bf16[1024,512]{1,0:T(8,128)(2,1)S(1)} copy-done((bf16[1024,512]{1,0:T(8,128)(2,1)S(1)}, bf16[1024,512]{1,0:T(8,128)(2,1)}, u32[]{:S(2)}) %copy-start.5) | copy-done | bytes 1048600
  53.9 9.7 %delta_and_gradients.1 = (f32[16,264,128]{2,1,0:T(8,128)}, f32[552,512]{1,0:T(8,128)S(1)}, f32[552,512]{1,0:T(8,128)S(1)}) custom-call(f32[24,128]{1,0:T(8,128)S(1)} %copy-done.7, f32[24,128]{1,0:T(8,128)S(1)} %collective-permute-done.5.refs_1_, f32[24,128]{1,0:T(8,128)S(1)} %collective-permute-done.6.refs_2_, f32[24,128]{1,0:T(8,128)S(1)} %collective-permute-done.7.refs_3_, ...), custom_call_target="tpu_custom_call" | custom-call | flops 2147483648 | bytes 8388608 | tf_op jit(solution)/shard_map/delta_and_gradients/pallas_call | solution.py:286
  63.5 1.0 copy-done.3
  64.5 4.4 %all-to-all-start = ((f32[16,264,128]{2,1,0:T(8,128)}), f32[16,264,128]{2,1,0:T(8,128)}, u32[]{:S(2)}, u32[]{:S(2)}) async-start(f32[16,264,128]{2,1,0:T(8,128)} %get-tuple-element.36), calls=%async_computation | async-start | bytes 4325376 | tf_op jit(solution)/shard_map/all_to_all | solution.py:420
  69.6 2.4 %collective-permute-done.11.theirs = f32[552,512]{1,0:T(8,128)S(1)} collective-permute-done((f32[552,512]{1,0:T(8,128)S(1)}, f32[552,512]{1,0:T(8,128)S(1)}, u32[]{:S(2)}, u32[]{:S(2)}) %collective-permute-start.11) | collective-permute-done | bytes 1130528 | tf_op jit(solution)/shard_map/ppermute | solution.py:419
  72.0 1.0 copy-done.8
  73.0 2.6 %both_cores_text_terms.1 = (f32[136,512]{1,0:T(8,128)}, f32[136,512]{1,0:T(8,128)}, f32[136,512]{1,0:T(8,128)}, f32[72,512]{1,0:T(8,128)}, f32[72,512]{1,0:T(8,128)}) custom-call(f32[552,512]{1,0:T(8,128)} %copy-done.3, f32[552,512]{1,0:T(8,128)} %copy-done.8), custom_call_target="tpu_custom_call" | custom-call | flops 282624 | bytes 3391488 | tf_op jit(solution)/shard_map/both_cores_text_terms/pallas_call | solution.py:312
  75.6 4.0 %collective-permute-start.12 = (f32[136,512]{1,0:T(8,128)}, f32[136,512]{1,0:T(8,128)S(1)}, u32[]{:S(2)}, u32[]{:S(2)}) collective-permute-start(f32[136,512]{1,0:T(8,128)} %get-tuple-element.32), channel_id=1, source_target_pairs={{0,32},{16,240},{32,64},{48,16},{64,96},{80,48},{96,128},{112,80},... | collective-permute-start | bytes 835592 | tf_op jit(solution)/shard_map/ppermute | solution.py:428
  79.6 2.0 %collective-permute-start.14 = (f32[72,512]{1,0:T(8,128)}, f32[72,512]{1,0:T(8,128)S(1)}, u32[]{:S(2)}, u32[]{:S(2)}) collective-permute-start(f32[72,512]{1,0:T(8,128)} %get-tuple-element.34), channel_id=1, source_target_pairs={{0,96},{16,176},{32,128},{48,208},{64,160},{80,240},{96,192},{112,... | collective-permute-start | bytes 442376 | tf_op jit(solution)/shard_map/ppermute | solution.py:428
  81.6 12.5 %collective-permute-done.14.farthest = f32[72,512]{1,0:T(8,128)S(1)} collective-permute-done((f32[72,512]{1,0:T(8,128)}, f32[72,512]{1,0:T(8,128)S(1)}, u32[]{:S(2)}, u32[]{:S(2)}) %collective-permute-start.14) | collective-permute-done | bytes 147488 | tf_op jit(solution)/shard_map/ppermute | solution.py:428
  95.0 1.9 %relayed_text_terms.1 = f32[136,512]{1,0:T(8,128)} custom-call(f32[136,512]{1,0:T(8,128)} %get-tuple-element.31.near, f32[136,512]{1,0:T(8,128)} %copy-done.9, f32[136,512]{1,0:T(8,128)} %copy-done.10, f32[72,512]{1,0:T(8,128)} %copy-done.13), custom_call_target="tpu_custom_call" | custom-call | flops 208896 | bytes 1114112 | tf_op jit(solution)/shard_map/relayed_text_terms/pallas_call | solution.py:333
  97.0 0.9 collective-permute-start.15
  97.9 5.7 %collective-permute-done.15.flow = f32[136,512]{1,0:T(8,128)S(1)} collective-permute-done((f32[136,512]{1,0:T(8,128)}, f32[136,512]{1,0:T(8,128)S(1)}, u32[]{:S(2)}, u32[]{:S(2)}) %collective-permute-start.15) | collective-permute-done | bytes 278560 | tf_op jit(solution)/shard_map/ppermute | solution.py:428
  103.7 3.0 %collective-permute-start.16 = (f32[136,512]{1,0:T(8,128)S(1)}, f32[136,512]{1,0:T(8,128)S(1)}, u32[]{:S(2)}, u32[]{:S(2)}) collective-permute-start(f32[136,512]{1,0:T(8,128)S(1)} %collective-permute-done.15.flow), channel_id=1, source_target_pairs={{0,16},{16,0},{1,17},{17,1},{2,18},{18,2},{3,19},{19,3},{4,20},{20... | collective-permute-start | bytes 835592 | tf_op jit(solution)/shard_map/ppermute | solution.py:432
  106.6 2.4 %sum_of_image_parts.1 = (f32[64,512]{1,0:T(8,128)}, f32[8,128]{1,0:T(8,128)}) custom-call(f32[16,264,128]{2,1,0:T(8,128)} %all-to-all-done.parts), custom_call_target="tpu_custom_call" | custom-call | flops 540672 | bytes 2162688 | tf_op jit(solution)/shard_map/sum_of_image_parts/pallas_call | solution.py:359
  109.7 1.8 %text_gradient_and_loss.1 = (f32[64,512]{1,0:T(8,128)}, f32[8,128]{1,0:T(8,128)}) custom-call(f32[136,512]{1,0:T(8,128)} %copy-done.11, f32[136,512]{1,0:T(8,128)} %copy-done.12, f32[72,512]{1,0:T(8,128)} %get-tuple-element.35.own, f32[8,128]{1,0:T(8,128)} %get-tuple-element.37.col_note), custom_call_target="tpu_custom_call" | custom-call | flops 110592 | bytes 589824 | tf_op jit(solution)/shard_map/text_gradient_and_loss/pallas_call | solution.py:380
  111.5 1.2 %slice.3 = f32[1,1]{1,0:T(1,128)} slice(f32[8,128]{1,0:T(8,128)} %get-tuple-element.38), slice={[0:1], [0:1]} | slice | bytes 8 | tf_op jit(solution)/shard_map/slice | solution.py:437
  (55 shorter events, 8.4 us)
Async XLA Ops:
  0.6 48.4 %copy-start.4 = (bf16[1024,512]{1,0:T(8,128)(2,1)S(1)}, bf16[1024,512]{1,0:T(8,128)(2,1)}, u32[]{:S(2)}) copy-start(bf16[1024,512]{1,0:T(8,128)(2,1)} %refs_9_.1) | copy-start | bytes 3145732
  13.5 2.0 %copy-start = (f32[1024,1024]{1,0:T(8,128)}, f32[1024,1024]{1,0:T(8,128)S(1)}, u32[]{:S(2)}) copy-start(f32[1024,1024]{1,0:T(8,128)S(1)} %get-tuple-element.27.refs_6_) | copy-start | bytes 12582916
  15.5 2.0 %copy-start.2 = (f32[1024,1024]{1,0:T(8,128)}, f32[1024,1024]{1,0:T(8,128)S(1)}, u32[]{:S(2)}) copy-start(f32[1024,1024]{1,0:T(8,128)S(1)} %get-tuple-element.28.refs_7_) | copy-start | bytes 12582916
  17.5 10.6 %collective-permute-start.4 = (f32[24,128]{1,0:T(8,128)}, f32[24,128]{1,0:T(8,128)S(1)}, u32[]{:S(2)}, u32[]{:S(2)}) collective-permute-start(f32[24,128]{1,0:T(8,128)} %get-tuple-element.23.refs_4_), channel_id=1, source_target_pairs={{0,224},{32,0},{64,32},{96,64},{128,96},{160,128},{192,160},{224,1... | collective-permute-start | bytes 36872 | tf_op jit(solution)/shard_map/ppermute | solution.py:407
  23.9 4.2 %collective-permute-start.3 = (f32[24,128]{1,0:T(8,128)}, f32[24,128]{1,0:T(8,128)S(1)}, u32[]{:S(2)}, u32[]{:S(2)}) collective-permute-start(f32[24,128]{1,0:T(8,128)} %get-tuple-element.23.refs_4_), channel_id=1, source_target_pairs={{0,32},{32,64},{64,96},{96,128},{128,160},{160,192},{192,224},{224... | collective-permute-start | bytes 36872 | tf_op jit(solution)/shard_map/ppermute | solution.py:406
  23.9 4.3 %collective-permute-start.2 = (f32[24,128]{1,0:T(8,128)}, f32[24,128]{1,0:T(8,128)S(1)}, u32[]{:S(2)}, u32[]{:S(2)}) collective-permute-start(f32[24,128]{1,0:T(8,128)} %get-tuple-element.22.refs_0_), channel_id=1, source_target_pairs={{0,8},{4,12},{8,0},{12,4},{1,9},{5,13},{9,1},{13,5},{2,10},{6,14},... | collective-permute-start | bytes 36872 | tf_op jit(solution)/shard_map/ppermute | solution.py:405
  26.7 3.1 %collective-permute-start.1 = (f32[24,128]{1,0:T(8,128)}, f32[24,128]{1,0:T(8,128)S(1)}, u32[]{:S(2)}, u32[]{:S(2)}) collective-permute-start(f32[24,128]{1,0:T(8,128)} %get-tuple-element.22.refs_0_), channel_id=1, source_target_pairs={{0,12},{4,0},{8,4},{12,8},{1,13},{5,1},{9,5},{13,9},{2,14},{6,2},{... | collective-permute-start | bytes 36872 | tf_op jit(solution)/shard_map/ppermute | solution.py:405
  27.5 4.0 %collective-permute-start = (f32[24,128]{1,0:T(8,128)}, f32[24,128]{1,0:T(8,128)S(1)}, u32[]{:S(2)}, u32[]{:S(2)}) collective-permute-start(f32[24,128]{1,0:T(8,128)} %get-tuple-element.22.refs_0_), channel_id=1, source_target_pairs={{0,4},{4,8},{8,12},{12,0},{1,5},{5,9},{9,13},{13,1},{2,6},{6,10},{... | collective-permute-start | bytes 36872 | tf_op jit(solution)/shard_map/ppermute | solution.py:405
  28.1 3.4 %copy-start.16 = (f32[24,128]{1,0:T(8,128)}, f32[24,128]{1,0:T(8,128)S(1)}, u32[]{:S(2)}) copy-start(f32[24,128]{1,0:T(8,128)S(1)} %collective-permute-done.4.refs_6_) | copy-start | bytes 36868
  28.1 3.4 %copy-start.17 = (f32[24,128]{1,0:T(8,128)}, f32[24,128]{1,0:T(8,128)S(1)}, u32[]{:S(2)}) copy-start(f32[24,128]{1,0:T(8,128)S(1)} %collective-permute-done.3.refs_5_) | copy-start | bytes 36868
  28.2 3.3 %copy-start.18 = (f32[24,128]{1,0:T(8,128)}, f32[24,128]{1,0:T(8,128)S(1)}, u32[]{:S(2)}) copy-start(f32[24,128]{1,0:T(8,128)S(1)} %collective-permute-done.2.refs_3_) | copy-start | bytes 36868
  29.7 1.8 %copy-start.19 = (f32[24,128]{1,0:T(8,128)}, f32[24,128]{1,0:T(8,128)S(1)}, u32[]{:S(2)}) copy-start(f32[24,128]{1,0:T(8,128)S(1)} %collective-permute-done.1.refs_2_) | copy-start | bytes 36868
  33.5 7.6 %collective-permute-start.9 = (f32[24,128]{1,0:T(8,128)}, f32[24,128]{1,0:T(8,128)S(1)}, u32[]{:S(2)}, u32[]{:S(2)}) collective-permute-start(f32[24,128]{1,0:T(8,128)} %get-tuple-element.26), channel_id=1, source_target_pairs={{0,160},{32,192},{64,224},{96,0},{128,32},{160,64},{192,96},{224,1... | collective-permute-start | bytes 36872 | tf_op jit(solution)/shard_map/ppermute | solution.py:411
  35.9 5.8 %collective-permute-start.8 = (f32[24,128]{1,0:T(8,128)}, f32[24,128]{1,0:T(8,128)S(1)}, u32[]{:S(2)}, u32[]{:S(2)}) collective-permute-start(f32[24,128]{1,0:T(8,128)} %get-tuple-element.25.refs_0_), channel_id=1, source_target_pairs={{0,96},{32,128},{64,160},{96,192},{128,224},{160,0},{192,32},{224,... | collective-permute-start | bytes 36872 | tf_op jit(solution)/shard_map/ppermute | solution.py:410
  36.8 11.2 %collective-permute-start.7 = (f32[24,128]{1,0:T(8,128)}, f32[24,128]{1,0:T(8,128)S(1)}, u32[]{:S(2)}, u32[]{:S(2)}) collective-permute-start(f32[24,128]{1,0:T(8,128)} %get-tuple-element.24.refs_0_), channel_id=1, source_target_pairs={{0,2},{1,3},{2,0},{3,1},{4,6},{5,7},{6,4},{7,5},{8,10},{9,11},{10,... | collective-permute-start | bytes 36872 | tf_op jit(solution)/shard_map/ppermute | solution.py:409
  39.7 8.3 %collective-permute-start.6 = (f32[24,128]{1,0:T(8,128)}, f32[24,128]{1,0:T(8,128)S(1)}, u32[]{:S(2)}, u32[]{:S(2)}) collective-permute-start(f32[24,128]{1,0:T(8,128)} %get-tuple-element.24.refs_0_), channel_id=1, source_target_pairs={{0,3},{1,0},{2,1},{3,2},{4,7},{5,4},{6,5},{7,6},{8,11},{9,8},{10,9... | collective-permute-start | bytes 36872 | tf_op jit(solution)/shard_map/ppermute | solution.py:409
  40.5 7.5 %collective-permute-start.5 = (f32[24,128]{1,0:T(8,128)}, f32[24,128]{1,0:T(8,128)S(1)}, u32[]{:S(2)}, u32[]{:S(2)}) collective-permute-start(f32[24,128]{1,0:T(8,128)} %get-tuple-element.24.refs_0_), channel_id=1, source_target_pairs={{0,1},{1,2},{2,3},{3,0},{4,5},{5,6},{6,7},{7,4},{8,9},{9,10},{10,1... | collective-permute-start | bytes 36872 | tf_op jit(solution)/shard_map/ppermute | solution.py:409
  43.8 5.3 %collective-permute-start.10 = (f32[24,128]{1,0:T(8,128)}, f32[24,128]{1,0:T(8,128)S(1)}, u32[]{:S(2)}, u32[]{:S(2)}) collective-permute-start(f32[24,128]{1,0:T(8,128)} %joined_statistics.3.refs_4_), channel_id=1, source_target_pairs={{0,16},{16,0},{1,17},{17,1},{2,18},{18,2},{3,19},{19,3},{4,20},{20... | collective-permute-start | bytes 36872 | tf_op jit(solution)/shard_map/ppermute | solution.py:414
  49.0 2.2 %copy-start.1 = (f32[1024,1024]{1,0:T(8,128)S(1)}, f32[1024,1024]{1,0:T(8,128)}, u32[]{:S(2)}) copy-start(f32[1024,1024]{1,0:T(8,128)} %copy-done) | copy-start | bytes 12582916
  51.2 1.2 %copy-start.5 = (bf16[1024,512]{1,0:T(8,128)(2,1)S(1)}, bf16[1024,512]{1,0:T(8,128)(2,1)}, u32[]{:S(2)}) copy-start(bf16[1024,512]{1,0:T(8,128)(2,1)} %refs_8_.1) | copy-start | bytes 3145732
  63.5 1.0 copy-start.3
  64.5 42.1 %all-to-all-start = ((f32[16,264,128]{2,1,0:T(8,128)}), f32[16,264,128]{2,1,0:T(8,128)}, u32[]{:S(2)}, u32[]{:S(2)}) async-start(f32[16,264,128]{2,1,0:T(8,128)} %get-tuple-element.36), calls=%async_computation | async-start | bytes 4325376 | tf_op jit(solution)/shard_map/all_to_all | solution.py:420
  69.0 3.0 %collective-permute-start.11 = (f32[552,512]{1,0:T(8,128)S(1)}, f32[552,512]{1,0:T(8,128)S(1)}, u32[]{:S(2)}, u32[]{:S(2)}) collective-permute-start(f32[552,512]{1,0:T(8,128)S(1)} %get-tuple-element.30), channel_id=1, source_target_pairs={{0,16},{16,0},{1,17},{17,1},{2,18},{18,2},{3,19},{19,3},{4,20},{20... | collective-permute-start | bytes 3391496 | tf_op jit(solution)/shard_map/ppermute | solution.py:419
  72.0 1.0 copy-start.8
  75.6 18.5 %collective-permute-start.12 = (f32[136,512]{1,0:T(8,128)}, f32[136,512]{1,0:T(8,128)S(1)}, u32[]{:S(2)}, u32[]{:S(2)}) collective-permute-start(f32[136,512]{1,0:T(8,128)} %get-tuple-element.32), channel_id=1, source_target_pairs={{0,32},{16,240},{32,64},{48,16},{64,96},{80,48},{96,128},{112,80},... | collective-permute-start | bytes 835592 | tf_op jit(solution)/shard_map/ppermute | solution.py:428
  79.6 14.5 %collective-permute-start.13 = (f32[136,512]{1,0:T(8,128)}, f32[136,512]{1,0:T(8,128)S(1)}, u32[]{:S(2)}, u32[]{:S(2)}) collective-permute-start(f32[136,512]{1,0:T(8,128)} %get-tuple-element.33), channel_id=1, source_target_pairs={{0,64},{16,208},{32,96},{48,240},{64,128},{80,16},{96,160},{112,48... | collective-permute-start | bytes 835592 | tf_op jit(solution)/shard_map/ppermute | solution.py:428
  79.6 14.5 %collective-permute-start.14 = (f32[72,512]{1,0:T(8,128)}, f32[72,512]{1,0:T(8,128)S(1)}, u32[]{:S(2)}, u32[]{:S(2)}) collective-permute-start(f32[72,512]{1,0:T(8,128)} %get-tuple-element.34), channel_id=1, source_target_pairs={{0,96},{16,176},{32,128},{48,208},{64,160},{80,240},{96,192},{112,... | collective-permute-start | bytes 442376 | tf_op jit(solution)/shard_map/ppermute | solution.py:428
  94.2 0.8 copy-start.9
  94.2 0.9 copy-start.10
  97.0 6.7 %collective-permute-start.15 = (f32[136,512]{1,0:T(8,128)}, f32[136,512]{1,0:T(8,128)S(1)}, u32[]{:S(2)}, u32[]{:S(2)}) collective-permute-start(f32[136,512]{1,0:T(8,128)} %relayed_text_terms.1), channel_id=1, source_target_pairs={{0,32},{16,240},{32,64},{48,16},{64,96},{80,48},{96,128},{112,80},... | collective-permute-start | bytes 835592 | tf_op jit(solution)/shard_map/ppermute | solution.py:428
  103.7 5.4 %copy-start.11 = (f32[136,512]{1,0:T(8,128)}, f32[136,512]{1,0:T(8,128)S(1)}, u32[]{:S(2)}) copy-start(f32[136,512]{1,0:T(8,128)S(1)} %collective-permute-done.15.flow) | copy-start | bytes 835588
  103.7 5.3 %collective-permute-start.16 = (f32[136,512]{1,0:T(8,128)S(1)}, f32[136,512]{1,0:T(8,128)S(1)}, u32[]{:S(2)}, u32[]{:S(2)}) collective-permute-start(f32[136,512]{1,0:T(8,128)S(1)} %collective-permute-done.15.flow), channel_id=1, source_target_pairs={{0,16},{16,0},{1,17},{17,1},{2,18},{18,2},{3,19},{19,3},{4,20},{20... | collective-permute-start | bytes 835592 | tf_op jit(solution)/shard_map/ppermute | solution.py:432
  (7 other events, 4.6 us)

commit v4 on v3

--- a/solution.py
+++ b/solution.py
@@ -15,12 +15,13 @@
 TXT_IMG = ("txt_0", "txt_1", "img_0", "img_1")
 LANES = 128
 NOTE = 8
-VMEM_LIMIT = 40 * 1024 * 1024
-STATS_LIMIT = 54 * 1024 * 1024
+VMEM_LIMIT = 20 * 1024 * 1024
+STATS_LIMIT = 24 * 1024 * 1024
 LN2 = math.log(2.0)
 F32 = jnp.float32
+MIB = 1024 * 1024
 WHOLE = pl.BlockSpec(memory_space=pltpu.VMEM)
-ANYWHERE = pl.BlockSpec(memory_space=pl.ANY)
+FAR = pl.BlockSpec(memory_space=pltpu.HBM)
 
 
 def cost(flops, size, transcendentals=0):
@@ -41,9 +42,7 @@
         return copy
 
     tt_load = load(tt_hbm, tt, 0, cols, 0)
-    ti_loads = [load(ti_hbm, ti, n * tall, tall, 1 + n) for n in range(chunks)]
-    st_load = load(st_hbm, st, 0, cols, 1 + chunks)
-    si_load = load(si_hbm, si, 0, rows, 2 + chunks)
+    ti_loads = [load(ti_hbm, ti, n * tall, tall, 1 + n) for n in range(2)]
 
     def logits(left, right, out, scale, which, arrivals):
         for n in range(chunks):
@@ -67,10 +66,14 @@
         )
 
     tt_load.wait()
+    ti_loads += [load(ti_hbm, ti, n * tall, tall, 1 + n) for n in range(2, chunks)]
+    st_load = load(st_hbm, st, 0, cols, 1 + chunks)
+    si_load = load(si_hbm, si, 0, rows, 2 + chunks)
     logits(ti, tt, t, scale_teach, 0, ti_loads)
     st_load.wait()
     si_load.wait()
     logits(si, st, s, scale_learn, 1, None)
+    lane = lax.broadcasted_iota(jnp.int32, (8, LANES), 1)
 
     group = 4 * LANES
     for h in range(cols // group):
@@ -93,10 +96,16 @@
                 row_g = wr * gap if row_g is None else row_g + wr * gap
                 ct, cs, cg = carry[3 * k : 3 * k + 3]
                 new += [ct + wc, cs + vc, cg + wc * gap]
-            for q, value in enumerate((row_t, row_s, row_g)):
-                if h:
-                    value = value + sums[q, down, :]
-                sums[q, down, :] = value
+            if h < cols // group - 1:
+                for q, value in enumerate((row_t, row_s, row_g)):
+                    sums[q, down, :] = value + sums[q, down, :] if h else value
+            else:
+                packed = jnp.where(lane == 0, row_peak_t, row_peak_s)
+                for q, value in enumerate((row_t, row_s, row_g)):
+                    total = value + sums[q, down, :] if h else value
+                    total = jnp.sum(total, axis=1, keepdims=True)
+                    packed = jnp.where(lane == 2 + q, total, packed)
+                sums[0, down, :] = packed
             return tuple(new)
 
         zeros = tuple(jnp.zeros((8, LANES), F32) for _ in range(3 * group // LANES))
@@ -107,31 +116,22 @@
                 col_sums[q, :, across] = found[3 * k + q]
 
     def publish(out, peak_t, peak_s, mass_t, mass_s, gap):
-        lse_t = peak_t + jnp.log2(mass_t)
-        lse_s = peak_s + jnp.log2(mass_s)
-        mean = gap / mass_t
-        for q, value in enumerate((lse_t, lse_s, mean)):
-            for b in range(value.shape[1] // LANES):
-                line = value[:, b * LANES : (b + 1) * LANES]
-                out[q * 8 + b : q * 8 + b + 1, :] = line
+        found = (peak_t + jnp.log2(mass_t), peak_s + jnp.log2(mass_s), gap / mass_t)
+        for q, value in enumerate(found):
+            out[8 * q : 8 * q + 8, :] = value
+
+    def stacked(lines):
+        return jnp.concatenate(lines, axis=0)
+
+    def by_column(value):
+        return stacked([value[:, b * LANES : (b + 1) * LANES] for b in range(cols // LANES)])
 
     publish(
-        col_out, col_peaks[0, :1, :], col_peaks[1, :1, :],
-        *(jnp.sum(col_sums[q], axis=0, keepdims=True) for q in range(3)),
-    )
-
-    def across_lanes(value, weight):
-        found = lax.dot_general(
-            jnp.full((8, LANES), weight, F32), value, (((1,), (1,)), ((), ())),
-            preferred_element_type=F32, precision=lax.Precision.HIGHEST,
-        )
-        return found[:1]
-
-    publish(
-        row_out,
-        across_lanes(peaks[0], 1.0 / LANES), across_lanes(peaks[1], 1.0 / LANES),
-        *(across_lanes(sums[q], 1.0) for q in range(3)),
-    )
+        col_out, by_column(col_peaks[0, :1, :]), by_column(col_peaks[1, :1, :]),
+        *(by_column(jnp.sum(col_sums[q], axis=0, keepdims=True)) for q in range(3)),
+    )
+    turned = [sums[0, b * LANES : (b + 1) * LANES, :].T for b in range(rows // LANES)]
+    publish(row_out, *(stacked([block[q : q + 1, :] for block in turned]) for q in range(5)))
 
 
 def local_stats(teacher_img, teacher_txt, student_img, student_txt):
@@ -148,7 +148,7 @@
             jax.ShapeDtypeStruct((3 * rows // LANES, LANES), F32),
             jax.ShapeDtypeStruct((3 * cols // LANES, LANES), F32),
         ),
-        in_specs=[ANYWHERE] * 4,
+        in_specs=[FAR] * 4,
         out_specs=(WHOLE,) * 4,
         scratch_shapes=[
             pltpu.VMEM((rows, deep), jnp.bfloat16), pltpu.VMEM((cols, deep), jnp.bfloat16),
@@ -159,7 +159,10 @@
         ],
         compiler_params=pltpu.CompilerParams(vmem_limit_bytes=STATS_LIMIT),
         cost_estimate=cost(2 * rows * cols * (deep + thin), 8 * rows * cols, 4 * rows * cols),
-    )(teacher_img, teacher_txt, student_img, student_txt)
+    )(*(
+        pltpu.with_memory_space_constraint(x, pltpu.HBM)
+        for x in (teacher_img, teacher_txt, student_img, student_txt)
+    ))
 
 
 def joined(parts):
@@ -191,13 +194,21 @@
         out_shape=[jax.ShapeDtypeStruct(parts[group[0]].shape, F32) for group in groups],
         in_specs=[WHOLE] * len(parts),
         out_specs=[WHOLE] * len(groups),
+        compiler_params=pltpu.CompilerParams(vmem_limit_bytes=1 * MIB),
         cost_estimate=cost(parts[0].size * 20, parts[0].size * 4 * len(parts), parts[0].size * 4),
     )(*parts)
 
 
 def gradient_kernel(scale, *refs):
     row_parts, col_parts = refs[:4], refs[4:6]
-    t, s, st, si, img_out, theirs, mine, delta, row_norms, col_norms = refs[6:]
+    t, s, st_far, si_far, img_out, theirs_out, mine = refs[6:13]
+    delta, row_norms, col_norms, img_block, theirs, st, si, sems = refs[13:]
+    loads = [
+        pltpu.make_async_copy(src, dst, sems.at[sems.shape[0] - 1 - k])
+        for k, (src, dst) in enumerate(((st_far, st), (si_far, si)))
+    ]
+    for load in loads:
+        load.start()
     rows, cols = t.shape
     thin = st.shape[1]
     row_teach, row_learn, row_mean = joined([part[...] for part in row_parts])
@@ -228,6 +239,29 @@
         return carry
 
     lax.fori_loop(0, rows // 16, strip, 0, unroll=2)
+    for load in loads:
+        load.wait()
+
+    pieces, lines, _ = img_block.shape
+    own = rows // pieces
+    some = 4
+    for k in range(pieces):
+        img_block[k, lines - NOTE :, :] = jnp.full((NOTE, LANES), col_total, F32)
+    saves = []
+    for n in range(pieces // some):
+        grad = scale * jnp.dot(
+            delta[n * some * own : (n + 1) * some * own, :], st[...], preferred_element_type=F32
+        )
+        for k in range(some):
+            for b in range(thin // LANES):
+                img_block[n * some + k, b * own : (b + 1) * own, :] = grad[
+                    k * own : (k + 1) * own, b * LANES : (b + 1) * LANES
+                ]
+        save = pltpu.make_async_copy(
+            img_block.at[pl.ds(n * some, some)], img_out.at[pl.ds(n * some, some)], sems.at[n]
+        )
+        save.start()
+        saves.append(save)
 
     place, core = lax.axis_index("img_0"), lax.axis_index("img_1")
     chips = lax.axis_size("img_0")
@@ -256,21 +290,13 @@
         ):
             text_block(out, top, far, part, note)
             top += (tall if part is None else half) + NOTE
-
-    pieces, lines, _ = img_out.shape
-    own = rows // pieces
-    some = 4
-    for n in range(pieces // some):
-        grad = scale * jnp.dot(
-            delta[n * some * own : (n + 1) * some * own, :], st[...], preferred_element_type=F32
-        )
-        for k in range(some):
-            for b in range(thin // LANES):
-                img_out[n * some + k, b * own : (b + 1) * own, :] = grad[
-                    k * own : (k + 1) * own, b * LANES : (b + 1) * LANES
-                ]
-    for k in range(pieces):
-        img_out[k, lines - NOTE :, :] = jnp.full((NOTE, LANES), col_total, F32)
+        if out is theirs:
+            save = pltpu.make_async_copy(theirs, theirs_out, sems.at[len(saves)])
+            save.start()
+            saves.append(save)
+
+    for save in saves:
+        save.wait()
 
 
 def flow_rows(tall):
@@ -286,16 +312,24 @@
     return pl.pallas_call(
         functools.partial(gradient_kernel, 3.0 / math.sqrt(thin)),
         name="delta_and_gradients",
-        out_shape=(jax.ShapeDtypeStruct((pieces, lines, LANES), F32), flow, flow),
-        in_specs=[WHOLE] * (len(row_parts) + len(col_parts) + 4),
-        out_specs=(WHOLE,) * 3,
+        out_shape=(
+            pltpu.HBM((pieces, lines, LANES), F32), pltpu.HBM(flow.shape, F32), flow,
+        ),
+        in_specs=[WHOLE] * (len(row_parts) + len(col_parts) + 2) + [FAR] * 2,
+        out_specs=(FAR, FAR, WHOLE),
         scratch_shapes=[
             pltpu.VMEM((rows, cols), jnp.bfloat16),
             pltpu.VMEM((2, rows, LANES), F32), pltpu.VMEM((2, 16, cols), F32),
+            pltpu.VMEM((pieces, lines, LANES), F32), pltpu.VMEM(flow.shape, F32),
+            pltpu.VMEM(student_txt.shape, jnp.bfloat16), pltpu.VMEM(student_img.shape, jnp.bfloat16),
+            pltpu.SemaphoreType.DMA((pieces // 4 + 3,)),
         ],
         compiler_params=pltpu.CompilerParams(vmem_limit_bytes=VMEM_LIMIT),
         cost_estimate=cost(4 * rows * cols * thin, 8 * rows * cols, 4 * rows * cols),
-    )(*row_parts, *col_parts, t, s, student_txt, student_img)
+    )(
+        *row_parts, *col_parts, t, s,
+        *(pltpu.with_memory_space_constraint(x, pltpu.HBM) for x in (student_txt, student_img)),
+    )
 
 
 def add_kernel(mine, theirs, *outs):
@@ -315,6 +349,7 @@
         out_shape=[jax.ShapeDtypeStruct((size, thin), F32) for size in sizes],
         in_specs=[WHOLE] * 2,
         out_specs=[WHOLE] * len(sizes),
+        compiler_params=pltpu.CompilerParams(vmem_limit_bytes=8 * MIB),
         cost_estimate=cost(mine.size, 12 * mine.size),
     )(mine, theirs)
 
@@ -336,6 +371,7 @@
         out_shape=jax.ShapeDtypeStruct(parts[0].shape, F32),
         in_specs=[WHOLE] * 4,
         out_specs=WHOLE,
+        compiler_params=pltpu.CompilerParams(vmem_limit_bytes=4 * MIB),
         cost_estimate=cost(parts[0].size * 3, 16 * parts[0].size),
     )(*parts)
 
@@ -362,6 +398,7 @@
         out_shape=(jax.ShapeDtypeStruct((own, thin), F32), jax.ShapeDtypeStruct((NOTE, LANES), F32)),
         in_specs=[WHOLE],
         out_specs=(WHOLE, WHOLE),
+        compiler_params=pltpu.CompilerParams(vmem_limit_bytes=4 * MIB),
         cost_estimate=cost(parts.size, 4 * parts.size),
     )(parts)
 
@@ -372,7 +409,8 @@
     down = pl.ds(pl.multiple_of(core * half, half), half)
     out[...] = flow[down, :] + other[down, :] + own[:half, :]
     row_note = flow[2 * half :, :LANES] + other[2 * half :, :LANES] + own[half:, :LANES]
-    loss[...] = (0.5 * LN2) * (row_note * row_share + col_note[...] * col_share)
+    total = (0.5 * LN2) * (row_note * row_share + col_note[...] * col_share)
+    loss[0, 0] = total[0, 0]
 
 
 def finished(row_share, col_share, flow, other, own, col_note):
@@ -382,10 +420,11 @@
         name="text_gradient_and_loss",
         out_shape=(
             jax.ShapeDtypeStruct((own.shape[0] - NOTE, thin), F32),
-            jax.ShapeDtypeStruct((NOTE, LANES), F32),
+            jax.ShapeDtypeStruct((1, 1), F32),
         ),
         in_specs=[WHOLE] * 4,
-        out_specs=(WHOLE, WHOLE),
+        out_specs=(WHOLE, pl.BlockSpec(memory_space=pltpu.SMEM)),
+        compiler_params=pltpu.CompilerParams(vmem_limit_bytes=4 * MIB),
         cost_estimate=cost(own.size * 3, 16 * own.size),
     )(flow, other, own, col_note)
 
@@ -434,7 +473,7 @@
     grad_txt, loss = finished(
         1.0 / (rows * img_count), 1.0 / (cols * txt_count), flow, across, own, col_note
     )
-    return (loss[0, 0], grad_img, grad_txt)
+    return (loss.reshape(()), grad_img, grad_txt)
 
 
 def solution(mesh):

time: 113 us -> 87.7 us (0.78)
  local copies, waits for them, and re-layouts: 14.9 us -> 0 us
  Pallas kernels: 34 us -> 21.4 us
  starting transfers between devices: 37.5 us -> 39 us
    unnamed x42 -> x0, local copies, waits for them, and re-layouts: 13.7 us -> none
    pallas_call x2, Pallas kernels: 2.81 us -> 0.05 us  [join(): pl.pallas_call(functools.partial(join_kernel, groups), name='joined_stati...]
    pallas_call x1, Pallas kernels: 9.65 us -> 6.9 us  [gradients(): pl.pallas_call(functools.partial(gradient_kernel, 3.0 / math.sqrt(thin)),...]
    pallas_call x1, Pallas kernels: 2.64 us -> 0.12 us  [added(): pl.pallas_call(add_kernel, name='both_cores_text_terms', out_shape=[jax.S...]
    pallas_call x1, Pallas kernels: 1.95 us -> 0.06 us  [relayed(): pl.pallas_call(relay_kernel, name='relayed_text_terms', out_shape=jax.Sha...]
    pallas_call x1, Pallas kernels: 2.37 us -> 0.75 us  [summed(): pl.pallas_call(sum_kernel, name='sum_of_image_parts', out_shape=(jax.Shap...]
    slice x1 -> x0, local copies, waits for them, and re-layouts: 1.18 us -> none  [body(): return (loss[0, 0], grad_img, grad_txt)]
    ppermute x1, starting transfers between devices: 0.63 us -> 1.78 us  [body(): theirs = lax.ppermute(theirs, 'img_1', swap)]
  transfers between devices with their start and end apart: 18 -> 18, of which waited for: 7 -> 8; matrix products, arithmetic and copies ran while one was open for 0% -> 0% of each run, Pallas kernels for 7% -> 1%
where the time goes in v4:
time: 87.7 us; the launch traced here: 87.5 us
  starting transfers between devices  39 us (44%)
  waiting for transfers between devices  26.3 us (30%)
  Pallas kernels  21.4 us (24%)
    ppermute x4, waiting for transfers between devices, outward(): return lax.ppermute(value, IMG, pairs)  19 us
    pallas_call x1, Pallas kernels, local_stats(): pl.pallas_call(kernel, name='logits_and_statistics', out_shape=(pltpu.VME...  12.9 us
    pallas_call x1, Pallas kernels, gradients(): pl.pallas_call(functools.partial(gradient_kernel, 3.0 / math.sqrt(thin)),...  6.9 us
    ppermute x1, starting transfers between devices, body(): above = lax.ppermute(col, 'img_0', turn(chips, -1))  6.48 us
    ppermute x4, starting transfers between devices, outward(): return lax.ppermute(value, IMG, pairs)  5.96 us
    ppermute x1, starting transfers between devices, body(): other = lax.ppermute(col, 'img_1', swap)  4.64 us
    ppermute x3, starting transfers between devices, body(): ys = [lax.ppermute(row, 'txt_1', turn(side, k)) for k in (1, 3, 2)]  4.38 us
    all_to_all x1, starting transfers between devices, body(): got_img = lax.all_to_all(to_img, TXT, 0, 0, tiled=True)  4.3 us
  transfers between devices with their start and end apart: 18, of which 8 were waited for; matrix products, arithmetic and copies ran while one was open for 0% of the time, Pallas kernels for 1%

profile of v4, /device:TPU:1, one launch (start us, length us, event | category | flops | bytes accessed | tf_op | source)
XLA Modules:
  0.0 87.5 jit_solution(12260092062675179696)
XLA Ops:
  0.6 12.9 %logits_and_statistics.1 = (f32[1024,1024]{1,0:T(8,128)S(1)}, f32[1024,1024]{1,0:T(8,128)S(1)}, f32[24,128]{1,0:T(8,128)S(1)}, f32[24,128]{1,0:T(8,128)S(1)}) custom-call(bf16[1024,1280]{1,0:T(8,128)(2,1)} %ti_hbm.1, bf16[1024,1280]{1,0:T(8,128)(2,1)} %tt_hbm.1, bf16[1024,512]{1,0:T(8,128)(2,1)} %refs_9_.1, bf16[1024,512]{1,0:T(8,128)(2,1)} %refs_8_.1), custom_call_target="tpu_custom_call" | custom-call | flops 3758096384 | bytes 8388608 | tf_op jit(solution)/shard_map/logits_and_statistics/pallas_call | solution.py:143
  13.5 6.5 %collective-permute-start.4 = (f32[24,128]{1,0:T(8,128)S(1)}, f32[24,128]{1,0:T(8,128)S(1)}, u32[]{:S(2)}, u32[]{:S(2)}) collective-permute-start(f32[24,128]{1,0:T(8,128)S(1)} %get-tuple-element.23.refs_4_), channel_id=1, source_target_pairs={{0,224},{32,0},{64,32},{96,64},{128,96},{160,128},{192,160},{224,1... | collective-permute-start | bytes 36872 | tf_op jit(solution)/shard_map/ppermute | solution.py:446
  20.0 0.0 collective-permute-start.3
  20.0 2.7 %collective-permute-start.2 = (f32[24,128]{1,0:T(8,128)S(1)}, f32[24,128]{1,0:T(8,128)S(1)}, u32[]{:S(2)}, u32[]{:S(2)}) collective-permute-start(f32[24,128]{1,0:T(8,128)S(1)} %get-tuple-element.22.refs_0_), channel_id=1, source_target_pairs={{0,8},{4,12},{8,0},{12,4},{1,9},{5,13},{9,1},{13,5},{2,10},{6,14},... | collective-permute-start | bytes 36872 | tf_op jit(solution)/shard_map/ppermute | solution.py:444
  22.7 0.9 collective-permute-start.1
  23.6 0.6 collective-permute-start
  24.2 0.0 collective-permute-done.4.refs_6_
  24.2 1.4 %collective-permute-done.1.refs_2_ = f32[24,128]{1,0:T(8,128)S(1)} collective-permute-done((f32[24,128]{1,0:T(8,128)S(1)}, f32[24,128]{1,0:T(8,128)S(1)}, u32[]{:S(2)}, u32[]{:S(2)}) %collective-permute-start.1) | collective-permute-done | bytes 12320 | tf_op jit(solution)/shard_map/ppermute | solution.py:444
  25.6 1.8 %collective-permute-done.refs_1_ = f32[24,128]{1,0:T(8,128)S(1)} collective-permute-done((f32[24,128]{1,0:T(8,128)S(1)}, f32[24,128]{1,0:T(8,128)S(1)}, u32[]{:S(2)}, u32[]{:S(2)}) %collective-permute-start) | collective-permute-done | bytes 12320 | tf_op jit(solution)/shard_map/ppermute | solution.py:444
  27.4 2.4 %collective-permute-start.9 = (f32[24,128]{1,0:T(8,128)S(1)}, f32[24,128]{1,0:T(8,128)S(1)}, u32[]{:S(2)}, u32[]{:S(2)}) collective-permute-start(f32[24,128]{1,0:T(8,128)S(1)} %get-tuple-element.26), channel_id=1, source_target_pairs={{0,160},{32,192},{64,224},{96,0},{128,32},{160,64},{192,96},{224,1... | collective-permute-start | bytes 36872 | tf_op jit(solution)/shard_map/ppermute | solution.py:450
  29.8 0.9 %collective-permute-start.8 = (f32[24,128]{1,0:T(8,128)S(1)}, f32[24,128]{1,0:T(8,128)S(1)}, u32[]{:S(2)}, u32[]{:S(2)}) collective-permute-start(f32[24,128]{1,0:T(8,128)S(1)} %get-tuple-element.25.refs_0_), channel_id=1, source_target_pairs={{0,96},{32,128},{64,160},{96,192},{128,224},{160,0},{192,32},{224,... | collective-permute-start | bytes 36872 | tf_op jit(solution)/shard_map/ppermute | solution.py:449
  30.7 2.9 %collective-permute-start.7 = (f32[24,128]{1,0:T(8,128)S(1)}, f32[24,128]{1,0:T(8,128)S(1)}, u32[]{:S(2)}, u32[]{:S(2)}) collective-permute-start(f32[24,128]{1,0:T(8,128)S(1)} %get-tuple-element.24.refs_0_), channel_id=1, source_target_pairs={{0,2},{1,3},{2,0},{3,1},{4,6},{5,7},{6,4},{7,5},{8,10},{9,11},{10,... | collective-permute-start | bytes 36872 | tf_op jit(solution)/shard_map/ppermute | solution.py:448
  33.6 0.8 collective-permute-start.6
  34.4 0.7 collective-permute-start.5
  35.1 0.3 collective-permute-done.8.refs_1_
  35.4 4.6 %collective-permute-start.10 = (f32[24,128]{1,0:T(8,128)S(1)}, f32[24,128]{1,0:T(8,128)S(1)}, u32[]{:S(2)}, u32[]{:S(2)}) collective-permute-start(f32[24,128]{1,0:T(8,128)S(1)} %joined_statistics.3.refs_4_), channel_id=1, source_target_pairs={{0,16},{16,0},{1,17},{17,1},{2,18},{18,2},{3,19},{19,3},{4,20},{20... | collective-permute-start | bytes 36872 | tf_op jit(solution)/shard_map/ppermute | solution.py:453
  40.0 0.8 collective-permute-done.10.refs_5_
  40.9 6.9 %delta_and_gradients.1 = (f32[16,264,128]{2,1,0:T(8,128)}, f32[552,512]{1,0:T(8,128)}, f32[552,512]{1,0:T(8,128)S(1)}) custom-call(f32[24,128]{1,0:T(8,128)S(1)} %get-tuple-element.24.refs_0_, f32[24,128]{1,0:T(8,128)S(1)} %collective-permute-done.5.refs_1_, f32[24,128]{1,0:T(8,128)S(1)} %collective-permute-done.6.refs_2_, ...), custom_call_target="tpu_custom_call" | custom-call | flops 2147483648 | bytes 8388608 | tf_op jit(solution)/shard_map/delta_and_gradients/pallas_call | solution.py:312
  47.8 4.3 %all-to-all-start = ((f32[16,264,128]{2,1,0:T(8,128)}), f32[16,264,128]{2,1,0:T(8,128)S(1)}, u32[]{:S(2)}, u32[]{:S(2)}) async-start(f32[16,264,128]{2,1,0:T(8,128)} %get-tuple-element.36), calls=%async_computation | async-start | bytes 4325376 | tf_op jit(solution)/shard_map/all_to_all | solution.py:459
  52.1 1.8 %collective-permute-start.11 = (f32[552,512]{1,0:T(8,128)}, f32[552,512]{1,0:T(8,128)S(1)}, u32[]{:S(2)}, u32[]{:S(2)}) collective-permute-start(f32[552,512]{1,0:T(8,128)} %get-tuple-element.30), channel_id=1, source_target_pairs={{0,16},{16,0},{1,17},{17,1},{2,18},{18,2},{3,19},{19,3},{4,20},{20... | collective-permute-start | bytes 3391496 | tf_op jit(solution)/shard_map/ppermute | solution.py:458
  53.8 2.6 %collective-permute-done.11.theirs = f32[552,512]{1,0:T(8,128)S(1)} collective-permute-done((f32[552,512]{1,0:T(8,128)}, f32[552,512]{1,0:T(8,128)S(1)}, u32[]{:S(2)}, u32[]{:S(2)}) %collective-permute-start.11) | collective-permute-done | bytes 1130528 | tf_op jit(solution)/shard_map/ppermute | solution.py:458
  56.5 0.1 both_cores_text_terms.1
  56.6 4.3 %collective-permute-start.12 = (f32[136,512]{1,0:T(8,128)S(1)}, f32[136,512]{1,0:T(8,128)S(1)}, u32[]{:S(2)}, u32[]{:S(2)}) collective-permute-start(f32[136,512]{1,0:T(8,128)S(1)} %get-tuple-element.32), channel_id=1, source_target_pairs={{0,32},{16,240},{32,64},{48,16},{64,96},{80,48},{96,128},{112,80},... | collective-permute-start | bytes 835592 | tf_op jit(solution)/shard_map/ppermute | solution.py:467
  60.9 1.2 %collective-permute-start.14 = (f32[72,512]{1,0:T(8,128)S(1)}, f32[72,512]{1,0:T(8,128)S(1)}, u32[]{:S(2)}, u32[]{:S(2)}) collective-permute-start(f32[72,512]{1,0:T(8,128)S(1)} %get-tuple-element.34), channel_id=1, source_target_pairs={{0,96},{16,176},{32,128},{48,208},{64,160},{80,240},{96,192},{112,... | collective-permute-start | bytes 442376 | tf_op jit(solution)/shard_map/ppermute | solution.py:467
  62.1 13.0 %collective-permute-done.14.farthest = f32[72,512]{1,0:T(8,128)S(1)} collective-permute-done((f32[72,512]{1,0:T(8,128)S(1)}, f32[72,512]{1,0:T(8,128)S(1)}, u32[]{:S(2)}, u32[]{:S(2)}) %collective-permute-start.14) | collective-permute-done | bytes 147488 | tf_op jit(solution)/shard_map/ppermute | solution.py:467
  75.1 0.1 relayed_text_terms.1
  75.1 0.4 collective-permute-start.15
  75.6 6.0 %collective-permute-done.15.flow = f32[136,512]{1,0:T(8,128)S(1)} collective-permute-done((f32[136,512]{1,0:T(8,128)S(1)}, f32[136,512]{1,0:T(8,128)S(1)}, u32[]{:S(2)}, u32[]{:S(2)}) %collective-permute-start.15) | collective-permute-done | bytes 278560 | tf_op jit(solution)/shard_map/ppermute | solution.py:467
  81.6 3.9 %collective-permute-start.16 = (f32[136,512]{1,0:T(8,128)S(1)}, f32[136,512]{1,0:T(8,128)S(1)}, u32[]{:S(2)}, u32[]{:S(2)}) collective-permute-start(f32[136,512]{1,0:T(8,128)S(1)} %collective-permute-done.15.flow), channel_id=1, source_target_pairs={{0,16},{16,0},{1,17},{17,1},{2,18},{18,2},{3,19},{19,3},{4,20},{20... | collective-permute-start | bytes 835592 | tf_op jit(solution)/shard_map/ppermute | solution.py:471
  85.5 0.8 sum_of_image_parts.1
  86.3 0.4 collective-permute-done.16.other
  86.7 0.7 text_gradient_and_loss.1
  (12 shorter events, 0.1 us)
Async XLA Ops:
  13.5 10.7 %collective-permute-start.4 = (f32[24,128]{1,0:T(8,128)S(1)}, f32[24,128]{1,0:T(8,128)S(1)}, u32[]{:S(2)}, u32[]{:S(2)}) collective-permute-start(f32[24,128]{1,0:T(8,128)S(1)} %get-tuple-element.23.refs_4_), channel_id=1, source_target_pairs={{0,224},{32,0},{64,32},{96,64},{128,96},{160,128},{192,160},{224,1... | collective-permute-start | bytes 36872 | tf_op jit(solution)/shard_map/ppermute | solution.py:446
  20.0 4.2 %collective-permute-start.3 = (f32[24,128]{1,0:T(8,128)S(1)}, f32[24,128]{1,0:T(8,128)S(1)}, u32[]{:S(2)}, u32[]{:S(2)}) collective-permute-start(f32[24,128]{1,0:T(8,128)S(1)} %get-tuple-element.23.refs_4_), channel_id=1, source_target_pairs={{0,32},{32,64},{64,96},{96,128},{128,160},{160,192},{192,224},{224... | collective-permute-start | bytes 36872 | tf_op jit(solution)/shard_map/ppermute | solution.py:445
  20.0 4.2 %collective-permute-start.2 = (f32[24,128]{1,0:T(8,128)S(1)}, f32[24,128]{1,0:T(8,128)S(1)}, u32[]{:S(2)}, u32[]{:S(2)}) collective-permute-start(f32[24,128]{1,0:T(8,128)S(1)} %get-tuple-element.22.refs_0_), channel_id=1, source_target_pairs={{0,8},{4,12},{8,0},{12,4},{1,9},{5,13},{9,1},{13,5},{2,10},{6,14},... | collective-permute-start | bytes 36872 | tf_op jit(solution)/shard_map/ppermute | solution.py:444
  22.7 2.8 %collective-permute-start.1 = (f32[24,128]{1,0:T(8,128)S(1)}, f32[24,128]{1,0:T(8,128)S(1)}, u32[]{:S(2)}, u32[]{:S(2)}) collective-permute-start(f32[24,128]{1,0:T(8,128)S(1)} %get-tuple-element.22.refs_0_), channel_id=1, source_target_pairs={{0,12},{4,0},{8,4},{12,8},{1,13},{5,1},{9,5},{13,9},{2,14},{6,2},{... | collective-permute-start | bytes 36872 | tf_op jit(solution)/shard_map/ppermute | solution.py:444
  23.6 3.8 %collective-permute-start = (f32[24,128]{1,0:T(8,128)S(1)}, f32[24,128]{1,0:T(8,128)S(1)}, u32[]{:S(2)}, u32[]{:S(2)}) collective-permute-start(f32[24,128]{1,0:T(8,128)S(1)} %get-tuple-element.22.refs_0_), channel_id=1, source_target_pairs={{0,4},{4,8},{8,12},{12,0},{1,5},{5,9},{9,13},{13,1},{2,6},{6,10},{... | collective-permute-start | bytes 36872 | tf_op jit(solution)/shard_map/ppermute | solution.py:444
  27.4 7.7 %collective-permute-start.9 = (f32[24,128]{1,0:T(8,128)S(1)}, f32[24,128]{1,0:T(8,128)S(1)}, u32[]{:S(2)}, u32[]{:S(2)}) collective-permute-start(f32[24,128]{1,0:T(8,128)S(1)} %get-tuple-element.26), channel_id=1, source_target_pairs={{0,160},{32,192},{64,224},{96,0},{128,32},{160,64},{192,96},{224,1... | collective-permute-start | bytes 36872 | tf_op jit(solution)/shard_map/ppermute | solution.py:450
  29.8 5.6 %collective-permute-start.8 = (f32[24,128]{1,0:T(8,128)S(1)}, f32[24,128]{1,0:T(8,128)S(1)}, u32[]{:S(2)}, u32[]{:S(2)}) collective-permute-start(f32[24,128]{1,0:T(8,128)S(1)} %get-tuple-element.25.refs_0_), channel_id=1, source_target_pairs={{0,96},{32,128},{64,160},{96,192},{128,224},{160,0},{192,32},{224,... | collective-permute-start | bytes 36872 | tf_op jit(solution)/shard_map/ppermute | solution.py:449
  30.7 9.3 %collective-permute-start.7 = (f32[24,128]{1,0:T(8,128)S(1)}, f32[24,128]{1,0:T(8,128)S(1)}, u32[]{:S(2)}, u32[]{:S(2)}) collective-permute-start(f32[24,128]{1,0:T(8,128)S(1)} %get-tuple-element.24.refs_0_), channel_id=1, source_target_pairs={{0,2},{1,3},{2,0},{3,1},{4,6},{5,7},{6,4},{7,5},{8,10},{9,11},{10,... | collective-permute-start | bytes 36872 | tf_op jit(solution)/shard_map/ppermute | solution.py:448
  33.6 6.4 %collective-permute-start.6 = (f32[24,128]{1,0:T(8,128)S(1)}, f32[24,128]{1,0:T(8,128)S(1)}, u32[]{:S(2)}, u32[]{:S(2)}) collective-permute-start(f32[24,128]{1,0:T(8,128)S(1)} %get-tuple-element.24.refs_0_), channel_id=1, source_target_pairs={{0,3},{1,0},{2,1},{3,2},{4,7},{5,4},{6,5},{7,6},{8,11},{9,8},{10,9... | collective-permute-start | bytes 36872 | tf_op jit(solution)/shard_map/ppermute | solution.py:448
  34.4 5.6 %collective-permute-start.5 = (f32[24,128]{1,0:T(8,128)S(1)}, f32[24,128]{1,0:T(8,128)S(1)}, u32[]{:S(2)}, u32[]{:S(2)}) collective-permute-start(f32[24,128]{1,0:T(8,128)S(1)} %get-tuple-element.24.refs_0_), channel_id=1, source_target_pairs={{0,1},{1,2},{2,3},{3,0},{4,5},{5,6},{6,7},{7,4},{8,9},{9,10},{10,1... | collective-permute-start | bytes 36872 | tf_op jit(solution)/shard_map/ppermute | solution.py:448
  35.4 5.5 %collective-permute-start.10 = (f32[24,128]{1,0:T(8,128)S(1)}, f32[24,128]{1,0:T(8,128)S(1)}, u32[]{:S(2)}, u32[]{:S(2)}) collective-permute-start(f32[24,128]{1,0:T(8,128)S(1)} %joined_statistics.3.refs_4_), channel_id=1, source_target_pairs={{0,16},{16,0},{1,17},{17,1},{2,18},{18,2},{3,19},{19,3},{4,20},{20... | collective-permute-start | bytes 36872 | tf_op jit(solution)/shard_map/ppermute | solution.py:453
  47.8 37.7 %all-to-all-start = ((f32[16,264,128]{2,1,0:T(8,128)}), f32[16,264,128]{2,1,0:T(8,128)S(1)}, u32[]{:S(2)}, u32[]{:S(2)}) async-start(f32[16,264,128]{2,1,0:T(8,128)} %get-tuple-element.36), calls=%async_computation | async-start | bytes 4325376 | tf_op jit(solution)/shard_map/all_to_all | solution.py:459
  52.1 4.4 %collective-permute-start.11 = (f32[552,512]{1,0:T(8,128)}, f32[552,512]{1,0:T(8,128)S(1)}, u32[]{:S(2)}, u32[]{:S(2)}) collective-permute-start(f32[552,512]{1,0:T(8,128)} %get-tuple-element.30), channel_id=1, source_target_pairs={{0,16},{16,0},{1,17},{17,1},{2,18},{18,2},{3,19},{19,3},{4,20},{20... | collective-permute-start | bytes 3391496 | tf_op jit(solution)/shard_map/ppermute | solution.py:458
  56.6 18.5 %collective-permute-start.12 = (f32[136,512]{1,0:T(8,128)S(1)}, f32[136,512]{1,0:T(8,128)S(1)}, u32[]{:S(2)}, u32[]{:S(2)}) collective-permute-start(f32[136,512]{1,0:T(8,128)S(1)} %get-tuple-element.32), channel_id=1, source_target_pairs={{0,32},{16,240},{32,64},{48,16},{64,96},{80,48},{96,128},{112,80},... | collective-permute-start | bytes 835592 | tf_op jit(solution)/shard_map/ppermute | solution.py:467
  60.9 14.2 %collective-permute-start.13 = (f32[136,512]{1,0:T(8,128)S(1)}, f32[136,512]{1,0:T(8,128)S(1)}, u32[]{:S(2)}, u32[]{:S(2)}) collective-permute-start(f32[136,512]{1,0:T(8,128)S(1)} %get-tuple-element.33), channel_id=1, source_target_pairs={{0,64},{16,208},{32,96},{48,240},{64,128},{80,16},{96,160},{112,48... | collective-permute-start | bytes 835592 | tf_op jit(solution)/shard_map/ppermute | solution.py:467
  60.9 14.2 %collective-permute-start.14 = (f32[72,512]{1,0:T(8,128)S(1)}, f32[72,512]{1,0:T(8,128)S(1)}, u32[]{:S(2)}, u32[]{:S(2)}) collective-permute-start(f32[72,512]{1,0:T(8,128)S(1)} %get-tuple-element.34), channel_id=1, source_target_pairs={{0,96},{16,176},{32,128},{48,208},{64,160},{80,240},{96,192},{112,... | collective-permute-start | bytes 442376 | tf_op jit(solution)/shard_map/ppermute | solution.py:467
  75.1 6.5 %collective-permute-start.15 = (f32[136,512]{1,0:T(8,128)S(1)}, f32[136,512]{1,0:T(8,128)S(1)}, u32[]{:S(2)}, u32[]{:S(2)}) collective-permute-start(f32[136,512]{1,0:T(8,128)S(1)} %relayed_text_terms.1), channel_id=1, source_target_pairs={{0,32},{16,240},{32,64},{48,16},{64,96},{80,48},{96,128},{112,80},... | collective-permute-start | bytes 835592 | tf_op jit(solution)/shard_map/ppermute | solution.py:467
  81.6 5.1 %collective-permute-start.16 = (f32[136,512]{1,0:T(8,128)S(1)}, f32[136,512]{1,0:T(8,128)S(1)}, u32[]{:S(2)}, u32[]{:S(2)}) collective-permute-start(f32[136,512]{1,0:T(8,128)S(1)} %collective-permute-done.15.flow), channel_id=1, source_target_pairs={{0,16},{16,0},{1,17},{17,1},{2,18},{18,2},{3,19},{19,3},{4,20},{20... | collective-permute-start | bytes 835592 | tf_op jit(solution)/shard_map/ppermute | solution.py:471

commit v5 on v4

--- a/solution.py
+++ b/solution.py
@@ -15,8 +15,8 @@
 TXT_IMG = ("txt_0", "txt_1", "img_0", "img_1")
 LANES = 128
 NOTE = 8
-VMEM_LIMIT = 20 * 1024 * 1024
-STATS_LIMIT = 24 * 1024 * 1024
+VMEM_LIMIT = 28 * 1024 * 1024
+STATS_LIMIT = 32 * 1024 * 1024
 LN2 = math.log(2.0)
 F32 = jnp.float32
 MIB = 1024 * 1024
@@ -28,8 +28,8 @@
     return pl.CostEstimate(flops=flops, bytes_accessed=size, transcendentals=transcendentals)
 
 
-def stats_kernel(scale_teach, scale_learn, ti_hbm, tt_hbm, si_hbm, st_hbm, t, s, row_out, col_out,
-                 ti, tt, si, st, peaks, sums, col_peaks, col_sums, sems):
+def stats_kernel(scale_teach, scale_learn, ti_hbm, tt_hbm, si_hbm, st_hbm, t_hbm, s_hbm,
+                 row_out, col_out, ti, tt, si, st, t, s, peaks, sums, col_peaks, col_sums, sems):
     rows, cols = t.shape
     tall = 256
     chunks = rows // tall
@@ -41,10 +41,13 @@
         copy.start()
         return copy
 
+    st_load = load(st_hbm, st, 0, cols, 1 + chunks)
+    si_load = load(si_hbm, si, 0, rows, 2 + chunks)
     tt_load = load(tt_hbm, tt, 0, cols, 0)
-    ti_loads = [load(ti_hbm, ti, n * tall, tall, 1 + n) for n in range(2)]
-
-    def logits(left, right, out, scale, which, arrivals):
+
+    saves = []
+
+    def logits(left, right, out, far, scale, which, arrivals):
         for n in range(chunks):
             if arrivals:
                 arrivals[n].wait()
@@ -53,6 +56,7 @@
                 left[down, :], right[...], (((1,), (1,)), ((), ())), preferred_element_type=F32
             )
             out[down, :] = block
+            saves.append(load(out, far, n * tall, tall, sems.shape[0] - 1 - len(saves)))
             top = jnp.max(block.reshape(tall // 8, 8, cols), axis=0)
             col_peaks[which] = jnp.maximum(col_peaks[which], top) if n else top
             side = block[:, :LANES]
@@ -65,15 +69,12 @@
             jnp.max(col_peaks[which], axis=0, keepdims=True), (8, cols)
         )
 
-    tt_load.wait()
-    ti_loads += [load(ti_hbm, ti, n * tall, tall, 1 + n) for n in range(2, chunks)]
-    st_load = load(st_hbm, st, 0, cols, 1 + chunks)
-    si_load = load(si_hbm, si, 0, rows, 2 + chunks)
-    logits(ti, tt, t, scale_teach, 0, ti_loads)
     st_load.wait()
     si_load.wait()
-    logits(si, st, s, scale_learn, 1, None)
-    lane = lax.broadcasted_iota(jnp.int32, (8, LANES), 1)
+    ti_loads = [load(ti_hbm, ti, n * tall, tall, 1 + n) for n in range(chunks)]
+    logits(si, st, s, s_hbm, scale_learn, 1, None)
+    tt_load.wait()
+    logits(ti, tt, t, t_hbm, scale_teach, 0, ti_loads)
 
     group = 4 * LANES
     for h in range(cols // group):
@@ -96,20 +97,12 @@
                 row_g = wr * gap if row_g is None else row_g + wr * gap
                 ct, cs, cg = carry[3 * k : 3 * k + 3]
                 new += [ct + wc, cs + vc, cg + wc * gap]
-            if h < cols // group - 1:
-                for q, value in enumerate((row_t, row_s, row_g)):
-                    sums[q, down, :] = value + sums[q, down, :] if h else value
-            else:
-                packed = jnp.where(lane == 0, row_peak_t, row_peak_s)
-                for q, value in enumerate((row_t, row_s, row_g)):
-                    total = value + sums[q, down, :] if h else value
-                    total = jnp.sum(total, axis=1, keepdims=True)
-                    packed = jnp.where(lane == 2 + q, total, packed)
-                sums[0, down, :] = packed
+            for q, value in enumerate((row_t, row_s, row_g)):
+                sums[q, down, :] = value + sums[q, down, :] if h else value
             return tuple(new)
 
         zeros = tuple(jnp.zeros((8, LANES), F32) for _ in range(3 * group // LANES))
-        found = lax.fori_loop(0, rows // 8, strip, zeros, unroll=4)
+        found = lax.fori_loop(0, rows // 8, strip, zeros, unroll=8)
         for k in range(group // LANES):
             across = slice(h * group + k * LANES, h * group + (k + 1) * LANES)
             for q in range(3):
@@ -118,7 +111,8 @@
     def publish(out, peak_t, peak_s, mass_t, mass_s, gap):
         found = (peak_t + jnp.log2(mass_t), peak_s + jnp.log2(mass_s), gap / mass_t)
         for q, value in enumerate(found):
-            out[8 * q : 8 * q + 8, :] = value
+            for k in range(out.shape[0]):
+                out[k, 8 * q : 8 * q + 8, :] = value
 
     def stacked(lines):
         return jnp.concatenate(lines, axis=0)
@@ -130,11 +124,17 @@
         col_out, by_column(col_peaks[0, :1, :]), by_column(col_peaks[1, :1, :]),
         *(by_column(jnp.sum(col_sums[q], axis=0, keepdims=True)) for q in range(3)),
     )
-    turned = [sums[0, b * LANES : (b + 1) * LANES, :].T for b in range(rows // LANES)]
+    lane = lax.broadcasted_iota(jnp.int32, (rows, LANES), 1)
+    packed = jnp.where(lane == 0, peaks[0], peaks[1])
+    for q in range(3):
+        packed = jnp.where(lane == 2 + q, jnp.sum(sums[q], axis=1, keepdims=True), packed)
+    turned = [packed[b * LANES : (b + 1) * LANES, :].T for b in range(rows // LANES)]
     publish(row_out, *(stacked([block[q : q + 1, :] for block in turned]) for q in range(5)))
-
-
-def local_stats(teacher_img, teacher_txt, student_img, student_txt):
+    for save in saves:
+        save.wait()
+
+
+def local_stats(teacher_img, teacher_txt, student_img, student_txt, copies):
     rows, deep = teacher_img.shape
     cols, thin = student_txt.shape
     kernel = functools.partial(
@@ -144,18 +144,19 @@
         kernel,
         name="logits_and_statistics",
         out_shape=(
-            pltpu.VMEM((rows, cols), F32), pltpu.VMEM((rows, cols), F32),
-            jax.ShapeDtypeStruct((3 * rows // LANES, LANES), F32),
-            jax.ShapeDtypeStruct((3 * cols // LANES, LANES), F32),
+            pltpu.HBM((rows, cols), F32), pltpu.HBM((rows, cols), F32),
+            jax.ShapeDtypeStruct((1, 3 * rows // LANES, LANES), F32),
+            jax.ShapeDtypeStruct((copies, 3 * cols // LANES, LANES), F32),
         ),
         in_specs=[FAR] * 4,
-        out_specs=(WHOLE,) * 4,
+        out_specs=(FAR, FAR, WHOLE, WHOLE),
         scratch_shapes=[
             pltpu.VMEM((rows, deep), jnp.bfloat16), pltpu.VMEM((cols, deep), jnp.bfloat16),
             pltpu.VMEM((rows, thin), jnp.bfloat16), pltpu.VMEM((cols, thin), jnp.bfloat16),
+            pltpu.VMEM((rows, cols), F32), pltpu.VMEM((rows, cols), F32),
             pltpu.VMEM((2, rows, LANES), F32), pltpu.VMEM((3, rows, LANES), F32),
             pltpu.VMEM((2, 8, cols), F32), pltpu.VMEM((3, 8, cols), F32),
-            pltpu.SemaphoreType.DMA((8,)),
+            pltpu.SemaphoreType.DMA((16,)),
         ],
         compiler_params=pltpu.CompilerParams(vmem_limit_bytes=STATS_LIMIT),
         cost_estimate=cost(2 * rows * cols * (deep + thin), 8 * rows * cols, 4 * rows * cols),
@@ -199,12 +200,22 @@
     )(*parts)
 
 
-def gradient_kernel(scale, *refs):
-    row_parts, col_parts = refs[:4], refs[4:6]
-    t, s, st_far, si_far, img_out, theirs_out, mine = refs[6:13]
-    delta, row_norms, col_norms, img_block, theirs, st, si, sems = refs[13:]
+def delta_kernel(scale, *refs):
+    row_parts = refs[:4]
+    col_stats, t_far, s_far, st_far, si_far, delta, theirs_out, mine, st, col_note = refs[4:14]
+    row_norms, col_norms, t, s, theirs, si, sems = refs[14:]
+    tall = 256
+    arrivals = []
+    for n in range(t.shape[0] // tall):
+        down = pl.ds(n * tall, tall)
+        arrivals.append([
+            pltpu.make_async_copy(far.at[down, :], near.at[down, :], sems.at[3 + 2 * n + k])
+            for k, (far, near) in enumerate(((t_far, t), (s_far, s)))
+        ])
+        for copy in arrivals[-1]:
+            copy.start()
     loads = [
-        pltpu.make_async_copy(src, dst, sems.at[sems.shape[0] - 1 - k])
+        pltpu.make_async_copy(src, dst, sems.at[1 + k])
         for k, (src, dst) in enumerate(((st_far, st), (si_far, si)))
     ]
     for load in loads:
@@ -212,9 +223,12 @@
     rows, cols = t.shape
     thin = st.shape[1]
     row_teach, row_learn, row_mean = joined([part[...] for part in row_parts])
-    col_teach, col_learn, col_mean = joined([part[...] for part in col_parts])
+    col_teach, col_learn, col_mean = joined(
+        [col_stats[k] for k in range(col_stats.shape[0])]
+    )
     row_total = jnp.sum(row_mean + row_learn - row_teach)
     col_total = jnp.sum(col_mean + col_learn - col_teach)
+    col_note[...] = jnp.full(col_note.shape, col_total, F32)
     for which, (down, across) in enumerate(((row_teach, col_teach), (row_learn, col_learn))):
         turned = jnp.concatenate([down - 3.0] * (LANES // 8), axis=0).T
         for b in range(8):
@@ -238,15 +252,55 @@
             delta[down, across] = value.astype(jnp.bfloat16)
         return carry
 
-    lax.fori_loop(0, rows // 16, strip, 0, unroll=2)
+    for n, copies in enumerate(arrivals):
+        for copy in copies:
+            copy.wait()
+        lax.fori_loop(n * tall // 16, (n + 1) * tall // 16, strip, 0, unroll=2)
     for load in loads:
         load.wait()
 
+    place, core = lax.axis_index("img_0"), lax.axis_index("img_1")
+    chips = lax.axis_size("img_0")
+    tall = cols // chips
+    half = tall // 2
+    full_note = jnp.full((NOTE, thin), row_total, F32)
+
+    def text_block(out, top, far, part, note):
+        size = tall if part is None else half
+        at = lax.rem(place + far + chips, chips) * tall
+        across = pl.ds(pl.multiple_of(at, tall), tall)
+        grad = scale * lax.dot_general(
+            delta[:, across], si[...], (((0,), (0,)), ((), ())), preferred_element_type=F32
+        )
+        if part is not None:
+            grad = jnp.where(part == 0, grad[:half], grad[half:])
+        out[top : top + size, :] = grad
+        out[top + size : top + size + NOTE, :] = note
+
+    for out, flow in ((theirs, 1 - core), (mine, core)):
+        sign = 1 - 2 * flow
+        top = 0
+        for far, part, note in (
+            (2 * sign, None, full_note), (3 * sign, None, full_note), (sign, None, full_note),
+            (chips // 2, flow, 0.5 * full_note), (0, flow, full_note),
+        ):
+            text_block(out, top, far, part, note)
+            top += (tall if part is None else half) + NOTE
+        if out is theirs:
+            save = pltpu.make_async_copy(theirs, theirs_out, sems.at[0])
+            save.start()
+
+    save.wait()
+
+
+def image_kernel(scale, delta, st, col_note, img_out, img_block, sems):
+    rows = delta.shape[0]
+    thin = st.shape[1]
     pieces, lines, _ = img_block.shape
     own = rows // pieces
     some = 4
     for k in range(pieces):
-        img_block[k, lines - NOTE :, :] = jnp.full((NOTE, LANES), col_total, F32)
+        img_block[k, lines - NOTE :, :] = col_note[...]
     saves = []
     for n in range(pieces // some):
         grad = scale * jnp.dot(
@@ -263,38 +317,6 @@
         save.start()
         saves.append(save)
 
-    place, core = lax.axis_index("img_0"), lax.axis_index("img_1")
-    chips = lax.axis_size("img_0")
-    tall = cols // chips
-    half = tall // 2
-    full_note = jnp.full((NOTE, thin), row_total, F32)
-
-    def text_block(out, top, far, part, note):
-        size = tall if part is None else half
-        at = lax.rem(place + far + chips, chips) * tall
-        across = pl.ds(pl.multiple_of(at, tall), tall)
-        grad = scale * lax.dot_general(
-            delta[:, across], si[...], (((0,), (0,)), ((), ())), preferred_element_type=F32
-        )
-        if part is not None:
-            grad = jnp.where(part == 0, grad[:half], grad[half:])
-        out[top : top + size, :] = grad
-        out[top + size : top + size + NOTE, :] = note
-
-    for out, flow in ((theirs, 1 - core), (mine, core)):
-        sign = 1 - 2 * flow
-        top = 0
-        for far, part, note in (
-            (2 * sign, None, full_note), (3 * sign, None, full_note), (sign, None, full_note),
-            (chips // 2, flow, 0.5 * full_note), (0, flow, full_note),
-        ):
-            text_block(out, top, far, part, note)
-            top += (tall if part is None else half) + NOTE
-        if out is theirs:
-            save = pltpu.make_async_copy(theirs, theirs_out, sems.at[len(saves)])
-            save.start()
-            saves.append(save)
-
     for save in saves:
         save.wait()
 
@@ -304,32 +326,51 @@
     return (full, full, full, part, part)
 
 
-def gradients(row_parts, col_parts, t, s, student_txt, student_img, pieces, chips):
+def delta_and_text(row_parts, col_stats, t, s, student_txt, student_img, chips):
     rows, cols = t.shape
     thin = student_txt.shape[1]
-    lines = rows // pieces * thin // LANES + NOTE
-    flow = jax.ShapeDtypeStruct((sum(flow_rows(cols // chips)), thin), F32)
-    return pl.pallas_call(
-        functools.partial(gradient_kernel, 3.0 / math.sqrt(thin)),
-        name="delta_and_gradients",
+    flow = (sum(flow_rows(cols // chips)), thin)
+    return pl.pallas_call(
+        functools.partial(delta_kernel, 3.0 / math.sqrt(thin)),
+        name="delta_and_text_gradient",
         out_shape=(
-            pltpu.HBM((pieces, lines, LANES), F32), pltpu.HBM(flow.shape, F32), flow,
+            pltpu.VMEM((rows, cols), jnp.bfloat16), pltpu.HBM(flow, F32),
+            jax.ShapeDtypeStruct(flow, F32), pltpu.VMEM(student_txt.shape, jnp.bfloat16),
+            jax.ShapeDtypeStruct((NOTE, LANES), F32),
         ),
-        in_specs=[WHOLE] * (len(row_parts) + len(col_parts) + 2) + [FAR] * 2,
-        out_specs=(FAR, FAR, WHOLE),
+        in_specs=[WHOLE] * (len(row_parts) + 1) + [FAR] * 4,
+        out_specs=(WHOLE, FAR, WHOLE, WHOLE, WHOLE),
         scratch_shapes=[
-            pltpu.VMEM((rows, cols), jnp.bfloat16),
             pltpu.VMEM((2, rows, LANES), F32), pltpu.VMEM((2, 16, cols), F32),
-            pltpu.VMEM((pieces, lines, LANES), F32), pltpu.VMEM(flow.shape, F32),
-            pltpu.VMEM(student_txt.shape, jnp.bfloat16), pltpu.VMEM(student_img.shape, jnp.bfloat16),
-            pltpu.SemaphoreType.DMA((pieces // 4 + 3,)),
+            pltpu.VMEM((rows, cols), F32), pltpu.VMEM((rows, cols), F32),
+            pltpu.VMEM(flow, F32), pltpu.VMEM(student_img.shape, jnp.bfloat16),
+            pltpu.SemaphoreType.DMA((11,)),
         ],
         compiler_params=pltpu.CompilerParams(vmem_limit_bytes=VMEM_LIMIT),
-        cost_estimate=cost(4 * rows * cols * thin, 8 * rows * cols, 4 * rows * cols),
+        cost_estimate=cost(2 * rows * cols * thin, 8 * rows * cols, 4 * rows * cols),
     )(
-        *row_parts, *col_parts, t, s,
-        *(pltpu.with_memory_space_constraint(x, pltpu.HBM) for x in (student_txt, student_img)),
-    )
+        *row_parts, col_stats,
+        *(
+            pltpu.with_memory_space_constraint(x, pltpu.HBM)
+            for x in (t, s, student_txt, student_img)
+        ),
+    )
+
+
+def image_gradient(delta, student_txt, col_note, pieces):
+    rows, cols = delta.shape
+    thin = student_txt.shape[1]
+    shape = (pieces, rows // pieces * thin // LANES + NOTE, LANES)
+    return pl.pallas_call(
+        functools.partial(image_kernel, 3.0 / math.sqrt(thin)),
+        name="image_gradient",
+        out_shape=pltpu.HBM(shape, F32),
+        in_specs=[WHOLE] * 3,
+        out_specs=FAR,
+        scratch_shapes=[pltpu.VMEM(shape, F32), pltpu.SemaphoreType.DMA((pieces // 4,))],
+        compiler_params=pltpu.CompilerParams(vmem_limit_bytes=16 * MIB),
+        cost_estimate=cost(2 * rows * cols * thin, 4 * rows * thin + 2 * rows * cols),
+    )(delta, student_txt, col_note)
 
 
 def add_kernel(mine, theirs, *outs):
@@ -354,14 +395,16 @@
     )(mine, theirs)
 
 
-def relay_kernel(near, next_one, far, farthest, out):
-    core = lax.axis_index("img_1")
-    full = out.shape[0]
-    half = (full - NOTE) // 2
-    out[...] = near[...] + next_one[...] + far[...]
-    down = pl.ds(pl.multiple_of(core * half, half), half)
-    out[down, :] = out[down, :] + farthest[:half, :]
-    out[full - NOTE :, :] = out[full - NOTE :, :] + farthest[half:, :]
+def relay_kernel(near, full, *refs):
+    out = refs[-1]
+    out[...] = near[...] + full[...]
+    if len(refs) > 1:
+        part = refs[0]
+        size = out.shape[0] - NOTE
+        half = size // 2
+        down = pl.ds(pl.multiple_of(lax.axis_index("img_1") * half, half), half)
+        out[down, :] = out[down, :] + part[:half, :]
+        out[size:, :] = out[size:, :] + part[half:, :]
 
 
 def relayed(*parts):
@@ -369,10 +412,10 @@
         relay_kernel,
         name="relayed_text_terms",
         out_shape=jax.ShapeDtypeStruct(parts[0].shape, F32),
-        in_specs=[WHOLE] * 4,
+        in_specs=[WHOLE] * len(parts),
         out_specs=WHOLE,
         compiler_params=pltpu.CompilerParams(vmem_limit_bytes=4 * MIB),
-        cost_estimate=cost(parts[0].size * 3, 16 * parts[0].size),
+        cost_estimate=cost(parts[0].size * 3, 12 * parts[0].size),
     )(*parts)
 
 
@@ -440,24 +483,24 @@
     img_count, txt_count = chips * cores, lax.axis_size(TXT)
     side = lax.axis_size("txt_0")
 
-    t, s, row, col = local_stats(teacher_img, teacher_txt, student_img, student_txt)
-    xs = [lax.ppermute(row, "txt_0", turn(side, k)) for k in (1, 3, 2)]
-    below = lax.ppermute(col, "img_0", turn(chips, 1))
-    above = lax.ppermute(col, "img_0", turn(chips, -1))
-    row, three, two = join(((0, 1, 2, 3), (4, 5, 6), (4, 5)), row, *xs, col, below, above)
-    ys = [lax.ppermute(row, "txt_1", turn(side, k)) for k in (1, 3, 2)]
-    below = lax.ppermute(three, "img_0", turn(chips, 3))
-    above = lax.ppermute(two, "img_0", turn(chips, -3))
-    (col,) = join(((0, 1, 2),), three, below, above)
+    t, s, row, col = local_stats(
+        teacher_img, teacher_txt, student_img, student_txt, img_count
+    )
+    col = lax.all_to_all(col, IMG, 0, 0, tiled=True)
+    row = row[0]
+    for axis in TXT:
+        others = [lax.ppermute(row, axis, turn(side, k)) for k in (1, 3, 2)]
+        if axis == TXT[0]:
+            (row,) = join(((0, 1, 2, 3),), row, *others)
     swap = turn(cores, 1)
-    other = lax.ppermute(col, "img_1", swap)
-
-    to_img, theirs, mine = gradients(
-        (row, *ys), (col, other), t, s, student_txt, student_img, txt_count, chips
+
+    delta, theirs, mine, near_txt, col_note = delta_and_text(
+        (row, *others), col, t, s, student_txt, student_img, chips
     )
     theirs = lax.ppermute(theirs, "img_1", swap)
+    to_img = image_gradient(delta, near_txt, col_note, txt_count)
     got_img = lax.all_to_all(to_img, TXT, 0, 0, tiled=True)
-    one, two, near, three, own = added(mine, theirs, chips)
+    two, three, one, four, own = added(mine, theirs, chips)
 
     def outward(value, step):
         pairs = [
@@ -466,7 +509,9 @@
         ]
         return lax.ppermute(value, IMG, pairs)
 
-    flow = relayed(near, outward(one, 1), outward(two, 2), outward(three, 3))
+    four = outward(four, 2)
+    flow = relayed(two, outward(three, 1), four)
+    flow = relayed(one, outward(flow, 1))
     flow = outward(flow, 1)
     across = lax.ppermute(flow, "img_1", swap)
     grad_img, col_note = summed(got_img, thin)

time: 87.7 us -> 85.3 us (0.973)
  waiting for transfers between devices: 26.3 us -> 21.4 us
  Pallas kernels: 21.4 us -> 23 us
    ppermute x11 -> x6, starting transfers between devices: 23.1 us -> 8.67 us  [body(): others = [lax.ppermute(row, axis, turn(side, k)) for k in (1, 3, 2)]]
    all_to_all x0 -> x1, starting transfers between devices: none -> 9.99 us  [body(): col = lax.all_to_all(col, IMG, 0, 0, tiled=True)]
    ppermute x4, waiting for transfers between devices: 19 us -> 13.6 us  [outward(): return lax.ppermute(value, IMG, pairs)]
    ppermute x4, starting transfers between devices: 5.96 us -> 8.8 us  [outward(): return lax.ppermute(value, IMG, pairs)]
    ppermute x1, waiting for transfers between devices: 2.61 us -> 0.01 us  [body(): theirs = lax.ppermute(theirs, 'img_1', swap)]
    ppermute x11 -> x6, waiting for transfers between devices: 4.23 us -> 6.51 us  [body(): others = [lax.ppermute(row, axis, turn(side, k)) for k in (1, 3, 2)]]
    ppermute x1, starting transfers between devices: 1.78 us -> 3.58 us  [body(): theirs = lax.ppermute(theirs, 'img_1', swap)]
    all_to_all x1, waiting for transfers between devices: 0.01 us -> 1.28 us  [body(): got_img = lax.all_to_all(to_img, TXT, 0, 0, tiled=True)]
  transfers between devices with their start and end apart: 18 -> 14, of which waited for: 8 -> 8; matrix products, arithmetic and copies ran while one was open for 0% -> 0% of each run, Pallas kernels for 1% -> 5%
where the time goes in v5:
time: 85.3 us; the launch traced here: 85.1 us
  starting transfers between devices  39.8 us (47%)
  Pallas kernels  23 us (27%)
  waiting for transfers between devices  21.4 us (25%)
  between operations  0.86 us (1%)
    ppermute x4, waiting for transfers between devices, outward(): return lax.ppermute(value, IMG, pairs)  13.6 us
    pallas_call x1, Pallas kernels, local_stats(): pl.pallas_call(kernel, name='logits_and_statistics', out_shape=(pltpu.HBM...  10.8 us
    all_to_all x1, starting transfers between devices, body(): col = lax.all_to_all(col, IMG, 0, 0, tiled=True)  9.99 us
    ppermute x4, starting transfers between devices, outward(): return lax.ppermute(value, IMG, pairs)  8.8 us
    ppermute x6, starting transfers between devices, body(): others = [lax.ppermute(row, axis, turn(side, k)) for k in (1, 3, 2)]  8.67 us
    pallas_call x1, Pallas kernels, delta_and_text(): pl.pallas_call(functools.partial(delta_kernel, 3.0 / math.sqrt(thin)), na...  7.23 us
    ppermute x6, waiting for transfers between devices, body(): others = [lax.ppermute(row, axis, turn(side, k)) for k in (1, 3, 2)]  6.51 us
    ppermute x1, starting transfers between devices, body(): across = lax.ppermute(flow, 'img_1', swap)  4.99 us
  transfers between devices with their start and end apart: 14, of which 8 were waited for; matrix products, arithmetic and copies ran while one was open for 0% of the time, Pallas kernels for 5%

profile of v5, /device:TPU:1, one launch (start us, length us, event | category | flops | bytes accessed | tf_op | source)
XLA Modules:
  0.0 85.1 jit_solution(4049951213422114154)
XLA Ops:
  0.6 10.8 %logits_and_statistics.1 = (f32[1024,1024]{1,0:T(8,128)}, f32[1024,1024]{1,0:T(8,128)}, f32[1,24,128]{2,1,0:T(8,128)S(1)}, f32[16,24,128]{2,1,0:T(8,128)}) custom-call(bf16[1024,1280]{1,0:T(8,128)(2,1)} %ti_hbm.1, bf16[1024,1280]{1,0:T(8,128)(2,1)} %tt_hbm.1, bf16[1024,512]{1,0:T(8,128)(2,1)} %refs_8_.1, bf16[1024,512]{1,0:T(8,128)(2,1)} %refs_7_.1), custom_call_target="tpu_custom_call" | custom-call | flops 3758096384 | bytes 8388608 | tf_op jit(solution)/shard_map/logits_and_statistics/pallas_call | solution.py:143
  11.4 10.0 %all-to-all-start = ((f32[16,24,128]{2,1,0:T(8,128)}), f32[16,24,128]{2,1,0:T(8,128)S(1)}, u32[]{:S(2)}, u32[]{:S(2)}) async-start(f32[16,24,128]{2,1,0:T(8,128)} %get-tuple-element.22), calls=%async_computation | async-start | bytes 393216 | tf_op jit(solution)/shard_map/all_to_all | solution.py:489
  21.4 2.7 %collective-permute-start.2 = (f32[24,128]{1,0:T(8,128)S(1)}, f32[24,128]{1,0:T(8,128)S(1)}, u32[]{:S(2)}, u32[]{:S(2)}) collective-permute-start(f32[24,128]{1,0:T(8,128)S(1)} %bitcast.2), channel_id=1, source_target_pairs={{0,8},{4,12},{8,0},{12,4},{1,9},{5,13},{9,1},{13,5},{2,10},{6,14},... | collective-permute-start | bytes 36872 | tf_op jit(solution)/shard_map/ppermute | solution.py:492
  24.1 0.9 %collective-permute-start.1 = (f32[24,128]{1,0:T(8,128)S(1)}, f32[24,128]{1,0:T(8,128)S(1)}, u32[]{:S(2)}, u32[]{:S(2)}) collective-permute-start(f32[24,128]{1,0:T(8,128)S(1)} %bitcast.3), channel_id=1, source_target_pairs={{0,12},{4,0},{8,4},{12,8},{1,13},{5,1},{9,5},{13,9},{2,14},{6,2},{... | collective-permute-start | bytes 36872 | tf_op jit(solution)/shard_map/ppermute | solution.py:492
  25.0 0.6 collective-permute-start
  25.6 0.0 collective-permute-done.2.refs_3_
  25.6 1.4 %collective-permute-done.1.refs_2_ = f32[24,128]{1,0:T(8,128)S(1)} collective-permute-done((f32[24,128]{1,0:T(8,128)S(1)}, f32[24,128]{1,0:T(8,128)S(1)}, u32[]{:S(2)}, u32[]{:S(2)}) %collective-permute-start.1) | collective-permute-done | bytes 12320 | tf_op jit(solution)/shard_map/ppermute | solution.py:492
  27.0 2.1 %collective-permute-done.refs_1_ = f32[24,128]{1,0:T(8,128)S(1)} collective-permute-done((f32[24,128]{1,0:T(8,128)S(1)}, f32[24,128]{1,0:T(8,128)S(1)}, u32[]{:S(2)}, u32[]{:S(2)}) %collective-permute-start) | collective-permute-done | bytes 12320 | tf_op jit(solution)/shard_map/ppermute | solution.py:492
  29.1 3.0 %collective-permute-start.5 = (f32[24,128]{1,0:T(8,128)S(1)}, f32[24,128]{1,0:T(8,128)S(1)}, u32[]{:S(2)}, u32[]{:S(2)}) collective-permute-start(f32[24,128]{1,0:T(8,128)S(1)} %joined_statistics.1.refs_0_), channel_id=1, source_target_pairs={{0,2},{1,3},{2,0},{3,1},{4,6},{5,7},{6,4},{7,5},{8,10},{9,11},{10,... | collective-permute-start | bytes 36872 | tf_op jit(solution)/shard_map/ppermute | solution.py:492
  32.1 0.8 collective-permute-start.4
  32.8 0.7 collective-permute-start.3
  33.5 0.0 collective-permute-done.5.refs_3_
  33.5 1.4 %collective-permute-done.4.refs_2_ = f32[24,128]{1,0:T(8,128)S(1)} collective-permute-done((f32[24,128]{1,0:T(8,128)S(1)}, f32[24,128]{1,0:T(8,128)S(1)}, u32[]{:S(2)}, u32[]{:S(2)}) %collective-permute-start.4) | collective-permute-done | bytes 12320 | tf_op jit(solution)/shard_map/ppermute | solution.py:492
  34.9 1.7 %collective-permute-done.3.refs_1_ = f32[24,128]{1,0:T(8,128)S(1)} collective-permute-done((f32[24,128]{1,0:T(8,128)S(1)}, f32[24,128]{1,0:T(8,128)S(1)}, u32[]{:S(2)}, u32[]{:S(2)}) %collective-permute-start.3) | collective-permute-done | bytes 12320 | tf_op jit(solution)/shard_map/ppermute | solution.py:492
  36.6 0.0 all-to-all-done.refs_4_
  36.6 7.2 %delta_and_text_gradient.1 = (bf16[1024,1024]{1,0:T(8,128)(2,1)S(1)}, f32[552,512]{1,0:T(8,128)}, f32[552,512]{1,0:T(8,128)S(1)}, bf16[1024,512]{1,0:T(8,128)(2,1)S(1)}, f32[8,128]{1,0:T(8,128)S(1)}) custom-call(f32[24,128]{1,0:T(8,128)S(1)} %joined_statistics.1.refs_0_, f32[24,128]{1,0:T(8,128)S(1)} %collective-permute-done.3.refs_1_, ...), custom_call_target="tpu_custom_call" | custom-call | flops 1073741824 | bytes 8388608 | tf_op jit(solution)/shard_map/delta_and_text_gradient/pallas_call | solution.py:333
  43.8 3.6 %collective-permute-start.6 = (f32[552,512]{1,0:T(8,128)}, f32[552,512]{1,0:T(8,128)}, u32[]{:S(2)}, u32[]{:S(2)}) collective-permute-start(f32[552,512]{1,0:T(8,128)} %get-tuple-element.26), channel_id=1, source_target_pairs={{0,16},{16,0},{1,17},{17,1},{2,18},{18,2},{3,19},{19,3},{4,20},{20... | collective-permute-start | bytes 3391496 | tf_op jit(solution)/shard_map/ppermute | solution.py:500
  47.4 2.1 %image_gradient.1 = f32[16,264,128]{2,1,0:T(8,128)} custom-call(bf16[1024,1024]{1,0:T(8,128)(2,1)S(1)} %get-tuple-element.32.delta, bf16[1024,512]{1,0:T(8,128)(2,1)S(1)} %get-tuple-element.33.st, f32[8,128]{1,0:T(8,128)S(1)} %get-tuple-element.34.col_note), custom_call_target="tpu_custom_call" | custom-call | flops 1073741824 | bytes 4194304 | tf_op jit(solution)/shard_map/image_gradient/pallas_call | solution.py:364
  49.5 3.7 %all-to-all-start.1 = ((f32[16,264,128]{2,1,0:T(8,128)}), f32[16,264,128]{2,1,0:T(8,128)S(1)}, u32[]{:S(2)}, u32[]{:S(2)}) async-start(f32[16,264,128]{2,1,0:T(8,128)} %image_gradient.1), calls=%async_computation.1 | async-start | bytes 4325376 | tf_op jit(solution)/shard_map/all_to_all | solution.py:502
  53.3 0.0 collective-permute-done.6.theirs
  53.3 1.4 %both_cores_text_terms.1 = (f32[136,512]{1,0:T(8,128)S(1)}, f32[136,512]{1,0:T(8,128)S(1)}, f32[136,512]{1,0:T(8,128)S(1)}, f32[72,512]{1,0:T(8,128)S(1)}, f32[72,512]{1,0:T(8,128)S(1)}) custom-call(f32[552,512]{1,0:T(8,128)S(1)} %get-tuple-element.25.mine, f32[552,512]{1,0:T(8,128)} %collective-permute-done.6.theirs), custom_call_target="tpu_custom_call" | custom-call | flops 282624 | bytes 3391488 | tf_op jit(solution)/shard_map/both_cores_text_terms/pallas_call | solution.py:387
  54.6 2.9 %collective-permute-start.7 = (f32[136,512]{1,0:T(8,128)S(1)}, f32[136,512]{1,0:T(8,128)S(1)}, u32[]{:S(2)}, u32[]{:S(2)}) collective-permute-start(f32[136,512]{1,0:T(8,128)S(1)} %get-tuple-element.29), channel_id=1, source_target_pairs={{0,32},{16,240},{32,64},{48,16},{64,96},{80,48},{96,128},{112,80},... | collective-permute-start | bytes 835592 | tf_op jit(solution)/shard_map/ppermute | solution.py:510
  57.6 2.1 %collective-permute-start.8 = (f32[72,512]{1,0:T(8,128)S(1)}, f32[72,512]{1,0:T(8,128)S(1)}, u32[]{:S(2)}, u32[]{:S(2)}) collective-permute-start(f32[72,512]{1,0:T(8,128)S(1)} %get-tuple-element.30), channel_id=1, source_target_pairs={{0,64},{16,208},{32,96},{48,240},{64,128},{80,16},{96,160},{112,48... | collective-permute-start | bytes 442376 | tf_op jit(solution)/shard_map/ppermute | solution.py:510
  59.6 5.3 %collective-permute-done.8.refs_0_ = f32[72,512]{1,0:T(8,128)S(1)} collective-permute-done((f32[72,512]{1,0:T(8,128)S(1)}, f32[72,512]{1,0:T(8,128)S(1)}, u32[]{:S(2)}, u32[]{:S(2)}) %collective-permute-start.8) | collective-permute-done | bytes 147488 | tf_op jit(solution)/shard_map/ppermute | solution.py:510
  64.9 1.3 %collective-permute-start.9 = (f32[136,512]{1,0:T(8,128)S(1)}, f32[136,512]{1,0:T(8,128)S(1)}, u32[]{:S(2)}, u32[]{:S(2)}) collective-permute-start(f32[136,512]{1,0:T(8,128)S(1)} %relayed_text_terms.2), channel_id=1, source_target_pairs={{0,32},{16,240},{32,64},{48,16},{64,96},{80,48},{96,128},{112,80},... | collective-permute-start | bytes 835592 | tf_op jit(solution)/shard_map/ppermute | solution.py:510
  66.3 4.5 %collective-permute-done.9.full = f32[136,512]{1,0:T(8,128)S(1)} collective-permute-done((f32[136,512]{1,0:T(8,128)S(1)}, f32[136,512]{1,0:T(8,128)S(1)}, u32[]{:S(2)}, u32[]{:S(2)}) %collective-permute-start.9) | collective-permute-done | bytes 278560 | tf_op jit(solution)/shard_map/ppermute | solution.py:510
  70.7 2.5 %collective-permute-start.10 = (f32[136,512]{1,0:T(8,128)S(1)}, f32[136,512]{1,0:T(8,128)S(1)}, u32[]{:S(2)}, u32[]{:S(2)}) collective-permute-start(f32[136,512]{1,0:T(8,128)S(1)} %relayed_text_terms.3), channel_id=1, source_target_pairs={{0,32},{16,240},{32,64},{48,16},{64,96},{80,48},{96,128},{112,80},... | collective-permute-start | bytes 835592 | tf_op jit(solution)/shard_map/ppermute | solution.py:510
  73.3 3.9 %collective-permute-done.10.flow = f32[136,512]{1,0:T(8,128)S(1)} collective-permute-done((f32[136,512]{1,0:T(8,128)S(1)}, f32[136,512]{1,0:T(8,128)S(1)}, u32[]{:S(2)}, u32[]{:S(2)}) %collective-permute-start.10) | collective-permute-done | bytes 278560 | tf_op jit(solution)/shard_map/ppermute | solution.py:510
  77.2 5.0 %collective-permute-start.11 = (f32[136,512]{1,0:T(8,128)S(1)}, f32[136,512]{1,0:T(8,128)S(1)}, u32[]{:S(2)}, u32[]{:S(2)}) collective-permute-start(f32[136,512]{1,0:T(8,128)S(1)} %collective-permute-done.10.flow), channel_id=1, source_target_pairs={{0,16},{16,0},{1,17},{17,1},{2,18},{18,2},{3,19},{19,3},{4,20},{20... | collective-permute-start | bytes 835592 | tf_op jit(solution)/shard_map/ppermute | solution.py:516
  82.2 1.3 %all-to-all-done.1.parts = f32[16,264,128]{2,1,0:T(8,128)S(1)} async-done(((f32[16,264,128]{2,1,0:T(8,128)}), f32[16,264,128]{2,1,0:T(8,128)S(1)}, u32[]{:S(2)}, u32[]{:S(2)}) %all-to-all-start.1) | async-done | bytes 2162720 | tf_op jit(solution)/shard_map/all_to_all | solution.py:502
  83.4 0.8 sum_of_image_parts.1
  84.2 0.7 text_gradient_and_loss.1
  (5 shorter events, 0.1 us)
Async XLA Ops:
  11.4 25.2 %all-to-all-start = ((f32[16,24,128]{2,1,0:T(8,128)}), f32[16,24,128]{2,1,0:T(8,128)S(1)}, u32[]{:S(2)}, u32[]{:S(2)}) async-start(f32[16,24,128]{2,1,0:T(8,128)} %get-tuple-element.22), calls=%async_computation | async-start | bytes 393216 | tf_op jit(solution)/shard_map/all_to_all | solution.py:489
  21.4 4.2 %collective-permute-start.2 = (f32[24,128]{1,0:T(8,128)S(1)}, f32[24,128]{1,0:T(8,128)S(1)}, u32[]{:S(2)}, u32[]{:S(2)}) collective-permute-start(f32[24,128]{1,0:T(8,128)S(1)} %bitcast.2), channel_id=1, source_target_pairs={{0,8},{4,12},{8,0},{12,4},{1,9},{5,13},{9,1},{13,5},{2,10},{6,14},... | collective-permute-start | bytes 36872 | tf_op jit(solution)/shard_map/ppermute | solution.py:492
  24.1 2.8 %collective-permute-start.1 = (f32[24,128]{1,0:T(8,128)S(1)}, f32[24,128]{1,0:T(8,128)S(1)}, u32[]{:S(2)}, u32[]{:S(2)}) collective-permute-start(f32[24,128]{1,0:T(8,128)S(1)} %bitcast.3), channel_id=1, source_target_pairs={{0,12},{4,0},{8,4},{12,8},{1,13},{5,1},{9,5},{13,9},{2,14},{6,2},{... | collective-permute-start | bytes 36872 | tf_op jit(solution)/shard_map/ppermute | solution.py:492
  25.0 4.1 %collective-permute-start = (f32[24,128]{1,0:T(8,128)S(1)}, f32[24,128]{1,0:T(8,128)S(1)}, u32[]{:S(2)}, u32[]{:S(2)}) collective-permute-start(f32[24,128]{1,0:T(8,128)S(1)} %bitcast.4), channel_id=1, source_target_pairs={{0,4},{4,8},{8,12},{12,0},{1,5},{5,9},{9,13},{13,1},{2,6},{6,10},{... | collective-permute-start | bytes 36872 | tf_op jit(solution)/shard_map/ppermute | solution.py:492
  29.1 4.5 %collective-permute-start.5 = (f32[24,128]{1,0:T(8,128)S(1)}, f32[24,128]{1,0:T(8,128)S(1)}, u32[]{:S(2)}, u32[]{:S(2)}) collective-permute-start(f32[24,128]{1,0:T(8,128)S(1)} %joined_statistics.1.refs_0_), channel_id=1, source_target_pairs={{0,2},{1,3},{2,0},{3,1},{4,6},{5,7},{6,4},{7,5},{8,10},{9,11},{10,... | collective-permute-start | bytes 36872 | tf_op jit(solution)/shard_map/ppermute | solution.py:492
  32.1 2.8 %collective-permute-start.4 = (f32[24,128]{1,0:T(8,128)S(1)}, f32[24,128]{1,0:T(8,128)S(1)}, u32[]{:S(2)}, u32[]{:S(2)}) collective-permute-start(f32[24,128]{1,0:T(8,128)S(1)} %joined_statistics.1.refs_0_), channel_id=1, source_target_pairs={{0,3},{1,0},{2,1},{3,2},{4,7},{5,4},{6,5},{7,6},{8,11},{9,8},{10,9... | collective-permute-start | bytes 36872 | tf_op jit(solution)/shard_map/ppermute | solution.py:492
  32.8 3.8 %collective-permute-start.3 = (f32[24,128]{1,0:T(8,128)S(1)}, f32[24,128]{1,0:T(8,128)S(1)}, u32[]{:S(2)}, u32[]{:S(2)}) collective-permute-start(f32[24,128]{1,0:T(8,128)S(1)} %joined_statistics.1.refs_0_), channel_id=1, source_target_pairs={{0,1},{1,2},{2,3},{3,0},{4,5},{5,6},{6,7},{7,4},{8,9},{9,10},{10,1... | collective-permute-start | bytes 36872 | tf_op jit(solution)/shard_map/ppermute | solution.py:492
  43.8 9.4 %collective-permute-start.6 = (f32[552,512]{1,0:T(8,128)}, f32[552,512]{1,0:T(8,128)}, u32[]{:S(2)}, u32[]{:S(2)}) collective-permute-start(f32[552,512]{1,0:T(8,128)} %get-tuple-element.26), channel_id=1, source_target_pairs={{0,16},{16,0},{1,17},{17,1},{2,18},{18,2},{3,19},{19,3},{4,20},{20... | collective-permute-start | bytes 3391496 | tf_op jit(solution)/shard_map/ppermute | solution.py:500
  49.5 33.9 %all-to-all-start.1 = ((f32[16,264,128]{2,1,0:T(8,128)}), f32[16,264,128]{2,1,0:T(8,128)S(1)}, u32[]{:S(2)}, u32[]{:S(2)}) async-start(f32[16,264,128]{2,1,0:T(8,128)} %image_gradient.1), calls=%async_computation.1 | async-start | bytes 4325376 | tf_op jit(solution)/shard_map/all_to_all | solution.py:502
  54.6 10.2 %collective-permute-start.7 = (f32[136,512]{1,0:T(8,128)S(1)}, f32[136,512]{1,0:T(8,128)S(1)}, u32[]{:S(2)}, u32[]{:S(2)}) collective-permute-start(f32[136,512]{1,0:T(8,128)S(1)} %get-tuple-element.29), channel_id=1, source_target_pairs={{0,32},{16,240},{32,64},{48,16},{64,96},{80,48},{96,128},{112,80},... | collective-permute-start | bytes 835592 | tf_op jit(solution)/shard_map/ppermute | solution.py:510
  57.6 7.3 %collective-permute-start.8 = (f32[72,512]{1,0:T(8,128)S(1)}, f32[72,512]{1,0:T(8,128)S(1)}, u32[]{:S(2)}, u32[]{:S(2)}) collective-permute-start(f32[72,512]{1,0:T(8,128)S(1)} %get-tuple-element.30), channel_id=1, source_target_pairs={{0,64},{16,208},{32,96},{48,240},{64,128},{80,16},{96,160},{112,48... | collective-permute-start | bytes 442376 | tf_op jit(solution)/shard_map/ppermute | solution.py:510
  64.9 5.8 %collective-permute-start.9 = (f32[136,512]{1,0:T(8,128)S(1)}, f32[136,512]{1,0:T(8,128)S(1)}, u32[]{:S(2)}, u32[]{:S(2)}) collective-permute-start(f32[136,512]{1,0:T(8,128)S(1)} %relayed_text_terms.2), channel_id=1, source_target_pairs={{0,32},{16,240},{32,64},{48,16},{64,96},{80,48},{96,128},{112,80},... | collective-permute-start | bytes 835592 | tf_op jit(solution)/shard_map/ppermute | solution.py:510
  70.7 6.4 %collective-permute-start.10 = (f32[136,512]{1,0:T(8,128)S(1)}, f32[136,512]{1,0:T(8,128)S(1)}, u32[]{:S(2)}, u32[]{:S(2)}) collective-permute-start(f32[136,512]{1,0:T(8,128)S(1)} %relayed_text_terms.3), channel_id=1, source_target_pairs={{0,32},{16,240},{32,64},{48,16},{64,96},{80,48},{96,128},{112,80},... | collective-permute-start | bytes 835592 | tf_op jit(solution)/shard_map/ppermute | solution.py:510
  77.2 7.0 %collective-permute-start.11 = (f32[136,512]{1,0:T(8,128)S(1)}, f32[136,512]{1,0:T(8,128)S(1)}, u32[]{:S(2)}, u32[]{:S(2)}) collective-permute-start(f32[136,512]{1,0:T(8,128)S(1)} %collective-permute-done.10.flow), channel_id=1, source_target_pairs={{0,16},{16,0},{1,17},{17,1},{2,18},{18,2},{3,19},{19,3},{4,20},{20... | collective-permute-start | bytes 835592 | tf_op jit(solution)/shard_map/ppermute | solution.py:516

commit v6 on v5

--- a/solution.py
+++ b/solution.py
@@ -201,21 +201,21 @@
 
 
 def delta_kernel(scale, *refs):
-    row_parts = refs[:4]
-    col_stats, t_far, s_far, st_far, si_far, delta, theirs_out, mine, st, col_note = refs[4:14]
-    row_norms, col_norms, t, s, theirs, si, sems = refs[14:]
+    row_parts = refs[:2]
+    col_stats, t_far, s_far, st_far, si_far, delta, img_out, si, row_note = refs[2:11]
+    row_norms, col_norms, t, s, st, img_block, sems = refs[11:]
     tall = 256
     arrivals = []
     for n in range(t.shape[0] // tall):
         down = pl.ds(n * tall, tall)
         arrivals.append([
-            pltpu.make_async_copy(far.at[down, :], near.at[down, :], sems.at[3 + 2 * n + k])
+            pltpu.make_async_copy(far.at[down, :], near.at[down, :], sems.at[2 + 2 * n + k])
             for k, (far, near) in enumerate(((t_far, t), (s_far, s)))
         ])
         for copy in arrivals[-1]:
             copy.start()
     loads = [
-        pltpu.make_async_copy(src, dst, sems.at[1 + k])
+        pltpu.make_async_copy(src, dst, sems.at[k])
         for k, (src, dst) in enumerate(((st_far, st), (si_far, si)))
     ]
     for load in loads:
@@ -228,7 +228,7 @@
     )
     row_total = jnp.sum(row_mean + row_learn - row_teach)
     col_total = jnp.sum(col_mean + col_learn - col_teach)
-    col_note[...] = jnp.full(col_note.shape, col_total, F32)
+    row_note[...] = jnp.full(row_note.shape, row_total, F32)
     for which, (down, across) in enumerate(((row_teach, col_teach), (row_learn, col_learn))):
         turned = jnp.concatenate([down - 3.0] * (LANES // 8), axis=0).T
         for b in range(8):
@@ -259,11 +259,39 @@
     for load in loads:
         load.wait()
 
+    pieces, lines, _ = img_block.shape
+    own = rows // pieces
+    some = 4
+    for k in range(pieces):
+        img_block[k, lines - NOTE :, :] = jnp.full((NOTE, LANES), col_total, F32)
+    saves = []
+    for n in range(pieces // some):
+        grad = scale * jnp.dot(
+            delta[n * some * own : (n + 1) * some * own, :], st[...], preferred_element_type=F32
+        )
+        for k in range(some):
+            for b in range(thin // LANES):
+                img_block[n * some + k, b * own : (b + 1) * own, :] = grad[
+                    k * own : (k + 1) * own, b * LANES : (b + 1) * LANES
+                ]
+        save = pltpu.make_async_copy(
+            img_block.at[pl.ds(n * some, some)], img_out.at[pl.ds(n * some, some)], sems.at[10 + n]
+        )
+        save.start()
+        saves.append(save)
+
+    for save in saves:
+        save.wait()
+
+
+def text_kernel(scale, delta, si, row_note, theirs_out, mine, theirs, sem):
+    cols = delta.shape[1]
+    thin = si.shape[1]
     place, core = lax.axis_index("img_0"), lax.axis_index("img_1")
     chips = lax.axis_size("img_0")
     tall = cols // chips
     half = tall // 2
-    full_note = jnp.full((NOTE, thin), row_total, F32)
+    full_note = row_note[...]
 
     def text_block(out, top, far, part, note):
         size = tall if part is None else half
@@ -287,38 +315,10 @@
             text_block(out, top, far, part, note)
             top += (tall if part is None else half) + NOTE
         if out is theirs:
-            save = pltpu.make_async_copy(theirs, theirs_out, sems.at[0])
+            save = pltpu.make_async_copy(theirs, theirs_out, sem)
             save.start()
 
     save.wait()
-
-
-def image_kernel(scale, delta, st, col_note, img_out, img_block, sems):
-    rows = delta.shape[0]
-    thin = st.shape[1]
-    pieces, lines, _ = img_block.shape
-    own = rows // pieces
-    some = 4
-    for k in range(pieces):
-        img_block[k, lines - NOTE :, :] = col_note[...]
-    saves = []
-    for n in range(pieces // some):
-        grad = scale * jnp.dot(
-            delta[n * some * own : (n + 1) * some * own, :], st[...], preferred_element_type=F32
-        )
-        for k in range(some):
-            for b in range(thin // LANES):
-                img_block[n * some + k, b * own : (b + 1) * own, :] = grad[
-                    k * own : (k + 1) * own, b * LANES : (b + 1) * LANES
-                ]
-        save = pltpu.make_async_copy(
-            img_block.at[pl.ds(n * some, some)], img_out.at[pl.ds(n * some, some)], sems.at[n]
-        )
-        save.start()
-        saves.append(save)
-
-    for save in saves:
-        save.wait()
 
 
 def flow_rows(tall):
@@ -326,25 +326,25 @@
     return (full, full, full, part, part)
 
 
-def delta_and_text(row_parts, col_stats, t, s, student_txt, student_img, chips):
+def delta_and_image(row_parts, col_stats, t, s, student_txt, student_img, pieces):
     rows, cols = t.shape
     thin = student_txt.shape[1]
-    flow = (sum(flow_rows(cols // chips)), thin)
+    shape = (pieces, rows // pieces * thin // LANES + NOTE, LANES)
     return pl.pallas_call(
         functools.partial(delta_kernel, 3.0 / math.sqrt(thin)),
-        name="delta_and_text_gradient",
+        name="delta_and_image_gradient",
         out_shape=(
-            pltpu.VMEM((rows, cols), jnp.bfloat16), pltpu.HBM(flow, F32),
-            jax.ShapeDtypeStruct(flow, F32), pltpu.VMEM(student_txt.shape, jnp.bfloat16),
-            jax.ShapeDtypeStruct((NOTE, LANES), F32),
+            pltpu.VMEM((rows, cols), jnp.bfloat16), pltpu.HBM(shape, F32),
+            pltpu.VMEM(student_img.shape, jnp.bfloat16),
+            jax.ShapeDtypeStruct((NOTE, thin), F32),
         ),
         in_specs=[WHOLE] * (len(row_parts) + 1) + [FAR] * 4,
-        out_specs=(WHOLE, FAR, WHOLE, WHOLE, WHOLE),
+        out_specs=(WHOLE, FAR, WHOLE, WHOLE),
         scratch_shapes=[
             pltpu.VMEM((2, rows, LANES), F32), pltpu.VMEM((2, 16, cols), F32),
             pltpu.VMEM((rows, cols), F32), pltpu.VMEM((rows, cols), F32),
-            pltpu.VMEM(flow, F32), pltpu.VMEM(student_img.shape, jnp.bfloat16),
-            pltpu.SemaphoreType.DMA((11,)),
+            pltpu.VMEM(student_txt.shape, jnp.bfloat16), pltpu.VMEM(shape, F32),
+            pltpu.SemaphoreType.DMA((10 + pieces // 4,)),
         ],
         compiler_params=pltpu.CompilerParams(vmem_limit_bytes=VMEM_LIMIT),
         cost_estimate=cost(2 * rows * cols * thin, 8 * rows * cols, 4 * rows * cols),
@@ -357,20 +357,20 @@
     )
 
 
-def image_gradient(delta, student_txt, col_note, pieces):
+def text_gradient(delta, student_img, row_note, chips):
     rows, cols = delta.shape
-    thin = student_txt.shape[1]
-    shape = (pieces, rows // pieces * thin // LANES + NOTE, LANES)
-    return pl.pallas_call(
-        functools.partial(image_kernel, 3.0 / math.sqrt(thin)),
-        name="image_gradient",
-        out_shape=pltpu.HBM(shape, F32),
+    thin = student_img.shape[1]
+    flow = (sum(flow_rows(cols // chips)), thin)
+    return pl.pallas_call(
+        functools.partial(text_kernel, 3.0 / math.sqrt(thin)),
+        name="text_gradient",
+        out_shape=(pltpu.HBM(flow, F32), jax.ShapeDtypeStruct(flow, F32)),
         in_specs=[WHOLE] * 3,
-        out_specs=FAR,
-        scratch_shapes=[pltpu.VMEM(shape, F32), pltpu.SemaphoreType.DMA((pieces // 4,))],
+        out_specs=(FAR, WHOLE),
+        scratch_shapes=[pltpu.VMEM(flow, F32), pltpu.SemaphoreType.DMA],
         compiler_params=pltpu.CompilerParams(vmem_limit_bytes=16 * MIB),
         cost_estimate=cost(2 * rows * cols * thin, 4 * rows * thin + 2 * rows * cols),
-    )(delta, student_txt, col_note)
+    )(delta, student_img, row_note)
 
 
 def add_kernel(mine, theirs, *outs):
@@ -419,57 +419,53 @@
     )(*parts)
 
 
-def sum_kernel(parts, out, note):
-    own = out.shape[0]
-    for b in range(out.shape[1] // LANES):
-        total = parts[0, b * own : (b + 1) * own, :]
-        for k in range(1, parts.shape[0]):
-            total = total + parts[k, b * own : (b + 1) * own, :]
-        out[:, b * LANES : (b + 1) * LANES] = total
-    last = slice(parts.shape[1] - NOTE, parts.shape[1])
-    total = parts[0, last, :]
-    for k in range(1, parts.shape[0]):
-        total = total + parts[k, last, :]
-    note[...] = total
-
-
-def summed(parts, thin):
-    own = (parts.shape[1] - NOTE) * LANES // thin
-    return pl.pallas_call(
-        sum_kernel,
-        name="sum_of_image_parts",
-        out_shape=(jax.ShapeDtypeStruct((own, thin), F32), jax.ShapeDtypeStruct((NOTE, LANES), F32)),
-        in_specs=[WHOLE],
+def finish_kernel(flow, other, own, out, note):
+    half = out.shape[0]
+    down = pl.ds(pl.multiple_of(lax.axis_index("img_1") * half, half), half)
+    out[...] = flow[down, :] + other[down, :] + own[:half, :]
+    note[...] = flow[2 * half :, :LANES] + other[2 * half :, :LANES] + own[half:, :LANES]
+
+
+def finished(flow, other, own):
+    thin = flow.shape[1]
+    return pl.pallas_call(
+        finish_kernel,
+        name="text_gradient_total",
+        out_shape=(
+            jax.ShapeDtypeStruct((own.shape[0] - NOTE, thin), F32),
+            jax.ShapeDtypeStruct((NOTE, LANES), F32),
+        ),
+        in_specs=[WHOLE] * 3,
         out_specs=(WHOLE, WHOLE),
         compiler_params=pltpu.CompilerParams(vmem_limit_bytes=4 * MIB),
-        cost_estimate=cost(parts.size, 4 * parts.size),
-    )(parts)
-
-
-def finish_kernel(row_share, col_share, flow, other, own, col_note, out, loss):
-    half = out.shape[0]
-    core = lax.axis_index("img_1")
-    down = pl.ds(pl.multiple_of(core * half, half), half)
-    out[...] = flow[down, :] + other[down, :] + own[:half, :]
-    row_note = flow[2 * half :, :LANES] + other[2 * half :, :LANES] + own[half:, :LANES]
-    total = (0.5 * LN2) * (row_note * row_share + col_note[...] * col_share)
-    loss[0, 0] = total[0, 0]
-
-
-def finished(row_share, col_share, flow, other, own, col_note):
-    thin = flow.shape[1]
-    return pl.pallas_call(
-        functools.partial(finish_kernel, row_share, col_share),
-        name="text_gradient_and_loss",
-        out_shape=(
-            jax.ShapeDtypeStruct((own.shape[0] - NOTE, thin), F32),
-            jax.ShapeDtypeStruct((1, 1), F32),
-        ),
-        in_specs=[WHOLE] * 4,
+        cost_estimate=cost(own.size * 3, 16 * own.size),
+    )(flow, other, own)
+
+
+def sum_kernel(row_share, col_share, parts, row_note, out, loss):
+    own = out.shape[0]
+
+    def total(down):
+        return functools.reduce(jnp.add, [parts[k, down, :] for k in range(parts.shape[0])])
+
+    for b in range(out.shape[1] // LANES):
+        out[:, b * LANES : (b + 1) * LANES] = total(slice(b * own, (b + 1) * own))
+    col_note = total(slice(parts.shape[1] - NOTE, parts.shape[1]))
+    both = (0.5 * LN2) * (row_note[...] * row_share + col_note * col_share)
+    loss[0, 0] = both[0, 0]
+
+
+def summed(row_share, col_share, parts, row_note, thin):
+    own = (parts.shape[1] - NOTE) * LANES // thin
+    return pl.pallas_call(
+        functools.partial(sum_kernel, row_share, col_share),
+        name="sum_of_image_parts_and_loss",
+        out_shape=(jax.ShapeDtypeStruct((own, thin), F32), jax.ShapeDtypeStruct((1, 1), F32)),
+        in_specs=[WHOLE] * 2,
         out_specs=(WHOLE, pl.BlockSpec(memory_space=pltpu.SMEM)),
         compiler_params=pltpu.CompilerParams(vmem_limit_bytes=4 * MIB),
-        cost_estimate=cost(own.size * 3, 16 * own.size),
-    )(flow, other, own, col_note)
+        cost_estimate=cost(parts.size, 4 * parts.size),
+    )(parts, row_note)
 
 
 def turn(size, step):
@@ -489,17 +485,19 @@
     col = lax.all_to_all(col, IMG, 0, 0, tiled=True)
     row = row[0]
     for axis in TXT:
-        others = [lax.ppermute(row, axis, turn(side, k)) for k in (1, 3, 2)]
-        if axis == TXT[0]:
-            (row,) = join(((0, 1, 2, 3),), row, *others)
+        for first in (0, 1):
+            pairs = [(k, (k + 1 - 2 * ((k + first) % 2)) % side) for k in range(side)]
+            other = lax.ppermute(row, axis, pairs)
+            if (axis, first) != (TXT[1], 1):
+                (row,) = join(((0, 1),), row, other)
     swap = turn(cores, 1)
 
-    delta, theirs, mine, near_txt, col_note = delta_and_text(
-        (row, *others), col, t, s, student_txt, student_img, chips
-    )
+    delta, to_img, near_img, row_note = delta_and_image(
+        (row, other), col, t, s, student_txt, student_img, txt_count
+    )
+    got_img = lax.all_to_all(to_img, TXT, 0, 0, tiled=True)
+    theirs, mine = text_gradient(delta, near_img, row_note, chips)
     theirs = lax.ppermute(theirs, "img_1", swap)
-    to_img = image_gradient(delta, near_txt, col_note, txt_count)
-    got_img = lax.all_to_all(to_img, TXT, 0, 0, tiled=True)
     two, three, one, four, own = added(mine, theirs, chips)
 
     def outward(value, step):
@@ -514,9 +512,9 @@
     flow = relayed(one, outward(flow, 1))
     flow = outward(flow, 1)
     across = lax.ppermute(flow, "img_1", swap)
-    grad_img, col_note = summed(got_img, thin)
-    grad_txt, loss = finished(
-        1.0 / (rows * img_count), 1.0 / (cols * txt_count), flow, across, own, col_note
+    grad_txt, row_total = finished(flow, across, own)
+    grad_img, loss = summed(
+        1.0 / (rows * img_count), 1.0 / (cols * txt_count), got_img, row_total, thin
     )
     return (loss.reshape(()), grad_img, grad_txt)
 

time: 85.3 us -> 86.6 us (1.015)
  starting transfers between devices: 39.8 us -> 42 us
    all_to_all x1, starting transfers between devices: 3.73 us -> 6.3 us  [body(): got_img = lax.all_to_all(to_img, TXT, 0, 0, tiled=True)]
    all_to_all x1, waiting for transfers between devices: 1.28 us -> 0.01 us  [body(): got_img = lax.all_to_all(to_img, TXT, 0, 0, tiled=True)]
    ppermute x1, waiting for transfers between devices: 0.01 us -> 1.19 us  [body(): across = lax.ppermute(flow, 'img_1', swap)]
    ppermute x6 -> x4, waiting for transfers between devices: 6.51 us -> 5.54 us  [body(): other = lax.ppermute(row, axis, pairs)]
    ppermute x6 -> x4, starting transfers between devices: 8.67 us -> 7.97 us  [body(): other = lax.ppermute(row, axis, pairs)]
  transfers between devices with their start and end apart: 14 -> 12, of which waited for: 8 -> 8; matrix products, arithmetic and copies ran while one was open for 0% -> 0% of each run, Pallas kernels for 5% -> 3%
where the time goes in v6:
time: 86.6 us; the launch traced here: 86.4 us
  starting transfers between devices  42 us (48%)
  Pallas kernels  22.7 us (26%)
  waiting for transfers between devices  21 us (24%)
    ppermute x4, waiting for transfers between devices, outward(): return lax.ppermute(value, IMG, pairs)  14.2 us
    pallas_call x1, Pallas kernels, local_stats(): pl.pallas_call(kernel, name='logits_and_statistics', out_shape=(pltpu.HBM...  10.7 us
    all_to_all x1, starting transfers between devices, body(): col = lax.all_to_all(col, IMG, 0, 0, tiled=True)  10 us
    ppermute x4, starting transfers between devices, outward(): return lax.ppermute(value, IMG, pairs)  8.22 us
    ppermute x4, starting transfers between devices, body(): other = lax.ppermute(row, axis, pairs)  7.97 us
    pallas_call x1, Pallas kernels, delta_and_image(): pl.pallas_call(functools.partial(delta_kernel, 3.0 / math.sqrt(thin)), na...  6.5 us
    all_to_all x1, starting transfers between devices, body(): got_img = lax.all_to_all(to_img, TXT, 0, 0, tiled=True)  6.3 us
    ppermute x4, waiting for transfers between devices, body(): other = lax.ppermute(row, axis, pairs)  5.54 us
  transfers between devices with their start and end apart: 12, of which 8 were waited for; matrix products, arithmetic and copies ran while one was open for 0% of the time, Pallas kernels for 3%

profile of v6, /device:TPU:1, one launch (start us, length us, event | category | flops | bytes accessed | tf_op | source)
XLA Modules:
  0.0 86.4 jit_solution(7507896036395796763)
XLA Ops:
  0.6 10.7 %logits_and_statistics.1 = (f32[1024,1024]{1,0:T(8,128)}, f32[1024,1024]{1,0:T(8,128)}, f32[1,24,128]{2,1,0:T(8,128)S(1)}, f32[16,24,128]{2,1,0:T(8,128)}) custom-call(bf16[1024,1280]{1,0:T(8,128)(2,1)} %ti_hbm.1, bf16[1024,1280]{1,0:T(8,128)(2,1)} %tt_hbm.1, bf16[1024,512]{1,0:T(8,128)(2,1)} %refs_6_.1, bf16[1024,512]{1,0:T(8,128)(2,1)} %refs_5_.1), custom_call_target="tpu_custom_call" | custom-call | flops 3758096384 | bytes 8388608 | tf_op jit(solution)/shard_map/logits_and_statistics/pallas_call | solution.py:143
  11.4 10.0 %all-to-all-start = ((f32[16,24,128]{2,1,0:T(8,128)}), f32[16,24,128]{2,1,0:T(8,128)S(1)}, u32[]{:S(2)}, u32[]{:S(2)}) async-start(f32[16,24,128]{2,1,0:T(8,128)} %get-tuple-element.23), calls=%async_computation | async-start | bytes 393216 | tf_op jit(solution)/shard_map/all_to_all | solution.py:485
  21.4 1.2 %collective-permute-start = (f32[24,128]{1,0:T(8,128)S(1)}, f32[24,128]{1,0:T(8,128)S(1)}, u32[]{:S(2)}, u32[]{:S(2)}) collective-permute-start(f32[24,128]{1,0:T(8,128)S(1)} %bitcast.2), channel_id=1, source_target_pairs={{0,4},{4,0},{8,12},{12,8},{1,5},{5,1},{9,13},{13,9},{2,6},{6,2},{1... | collective-permute-start | bytes 36872 | tf_op jit(solution)/shard_map/ppermute | solution.py:490
  22.6 1.3 %collective-permute-done.refs_1_ = f32[24,128]{1,0:T(8,128)S(1)} collective-permute-done((f32[24,128]{1,0:T(8,128)S(1)}, f32[24,128]{1,0:T(8,128)S(1)}, u32[]{:S(2)}, u32[]{:S(2)}) %collective-permute-start) | collective-permute-done | bytes 12320 | tf_op jit(solution)/shard_map/ppermute | solution.py:490
  23.9 2.6 %collective-permute-start.1 = (f32[24,128]{1,0:T(8,128)S(1)}, f32[24,128]{1,0:T(8,128)S(1)}, u32[]{:S(2)}, u32[]{:S(2)}) collective-permute-start(f32[24,128]{1,0:T(8,128)S(1)} %joined_statistics.3.refs_0_), channel_id=1, source_target_pairs={{0,12},{4,8},{8,4},{12,0},{1,13},{5,9},{9,5},{13,1},{2,14},{6,10},... | collective-permute-start | bytes 36872 | tf_op jit(solution)/shard_map/ppermute | solution.py:490
  26.5 1.6 %collective-permute-done.1.refs_1_ = f32[24,128]{1,0:T(8,128)S(1)} collective-permute-done((f32[24,128]{1,0:T(8,128)S(1)}, f32[24,128]{1,0:T(8,128)S(1)}, u32[]{:S(2)}, u32[]{:S(2)}) %collective-permute-start.1) | collective-permute-done | bytes 12320 | tf_op jit(solution)/shard_map/ppermute | solution.py:490
  28.1 1.4 %collective-permute-start.2 = (f32[24,128]{1,0:T(8,128)S(1)}, f32[24,128]{1,0:T(8,128)S(1)}, u32[]{:S(2)}, u32[]{:S(2)}) collective-permute-start(f32[24,128]{1,0:T(8,128)S(1)} %joined_statistics.4.refs_0_), channel_id=1, source_target_pairs={{0,1},{1,0},{2,3},{3,2},{4,5},{5,4},{6,7},{7,6},{8,9},{9,8},{10,11... | collective-permute-start | bytes 36872 | tf_op jit(solution)/shard_map/ppermute | solution.py:490
  29.5 1.5 %collective-permute-done.2.refs_1_ = f32[24,128]{1,0:T(8,128)S(1)} collective-permute-done((f32[24,128]{1,0:T(8,128)S(1)}, f32[24,128]{1,0:T(8,128)S(1)}, u32[]{:S(2)}, u32[]{:S(2)}) %collective-permute-start.2) | collective-permute-done | bytes 12320 | tf_op jit(solution)/shard_map/ppermute | solution.py:490
  31.0 2.8 %collective-permute-start.3 = (f32[24,128]{1,0:T(8,128)S(1)}, f32[24,128]{1,0:T(8,128)S(1)}, u32[]{:S(2)}, u32[]{:S(2)}) collective-permute-start(f32[24,128]{1,0:T(8,128)S(1)} %joined_statistics.5.refs_0_), channel_id=1, source_target_pairs={{0,3},{1,2},{2,1},{3,0},{4,7},{5,6},{6,5},{7,4},{8,11},{9,10},{10,... | collective-permute-start | bytes 36872 | tf_op jit(solution)/shard_map/ppermute | solution.py:490
  33.8 1.1 %collective-permute-done.3.refs_1_ = f32[24,128]{1,0:T(8,128)S(1)} collective-permute-done((f32[24,128]{1,0:T(8,128)S(1)}, f32[24,128]{1,0:T(8,128)S(1)}, u32[]{:S(2)}, u32[]{:S(2)}) %collective-permute-start.3) | collective-permute-done | bytes 12320 | tf_op jit(solution)/shard_map/ppermute | solution.py:490
  34.9 0.0 all-to-all-done.refs_2_
  34.9 6.5 %delta_and_image_gradient.1 = (bf16[1024,1024]{1,0:T(8,128)(2,1)S(1)}, f32[16,264,128]{2,1,0:T(8,128)}, bf16[1024,512]{1,0:T(8,128)(2,1)S(1)}, f32[8,512]{1,0:T(8,128)S(1)}) custom-call(f32[24,128]{1,0:T(8,128)S(1)} %joined_statistics.5.refs_0_, f32[24,128]{1,0:T(8,128)S(1)} %collective-permute-done.3.refs_1_, f32[16,24,128]{2,1,0:T(8,128)S(1)} %all-to-all-done.refs_2_, ...), custom_call_target="tpu_custom_call" | custom-call | flops 1073741824 | bytes 8388608 | tf_op jit(solution)/shard_map/delta_and_image_gradient/pallas_call | solution.py:333
  41.4 2.6 %text_gradient.1 = (f32[552,512]{1,0:T(8,128)}, f32[552,512]{1,0:T(8,128)S(1)}) custom-call(bf16[1024,1024]{1,0:T(8,128)(2,1)S(1)} %get-tuple-element.27.delta, bf16[1024,512]{1,0:T(8,128)(2,1)S(1)} %get-tuple-element.28.si, f32[8,512]{1,0:T(8,128)S(1)} %get-tuple-element.29.row_note), custom_call_target="tpu_custom_call" | custom-call | flops 1073741824 | bytes 4194304 | tf_op jit(solution)/shard_map/text_gradient/pallas_call | solution.py:364
  44.0 4.2 %collective-permute-start.4 = (f32[552,512]{1,0:T(8,128)}, f32[552,512]{1,0:T(8,128)}, u32[]{:S(2)}, u32[]{:S(2)}) collective-permute-start(f32[552,512]{1,0:T(8,128)} %get-tuple-element.31), channel_id=1, source_target_pairs={{0,16},{16,0},{1,17},{17,1},{2,18},{18,2},{3,19},{19,3},{4,20},{20... | collective-permute-start | bytes 3391496 | tf_op jit(solution)/shard_map/ppermute | solution.py:500
  48.2 6.3 %all-to-all-start.1 = ((f32[16,264,128]{2,1,0:T(8,128)}), f32[16,264,128]{2,1,0:T(8,128)S(1)}, u32[]{:S(2)}, u32[]{:S(2)}) async-start(f32[16,264,128]{2,1,0:T(8,128)} %get-tuple-element.26), calls=%async_computation.1 | async-start | bytes 4325376 | tf_op jit(solution)/shard_map/all_to_all | solution.py:498
  54.6 0.0 collective-permute-done.4.theirs
  54.6 1.4 %both_cores_text_terms.1 = (f32[136,512]{1,0:T(8,128)S(1)}, f32[136,512]{1,0:T(8,128)S(1)}, f32[136,512]{1,0:T(8,128)S(1)}, f32[72,512]{1,0:T(8,128)S(1)}, f32[72,512]{1,0:T(8,128)S(1)}) custom-call(f32[552,512]{1,0:T(8,128)S(1)} %get-tuple-element.30.mine, f32[552,512]{1,0:T(8,128)} %collective-permute-done.4.theirs), custom_call_target="tpu_custom_call" | custom-call | flops 282624 | bytes 3391488 | tf_op jit(solution)/shard_map/both_cores_text_terms/pallas_call | solution.py:387
  55.9 2.9 %collective-permute-start.5 = (f32[136,512]{1,0:T(8,128)S(1)}, f32[136,512]{1,0:T(8,128)S(1)}, u32[]{:S(2)}, u32[]{:S(2)}) collective-permute-start(f32[136,512]{1,0:T(8,128)S(1)} %get-tuple-element.34), channel_id=1, source_target_pairs={{0,32},{16,240},{32,64},{48,16},{64,96},{80,48},{96,128},{112,80},... | collective-permute-start | bytes 835592 | tf_op jit(solution)/shard_map/ppermute | solution.py:508
  58.8 2.1 %collective-permute-start.6 = (f32[72,512]{1,0:T(8,128)S(1)}, f32[72,512]{1,0:T(8,128)S(1)}, u32[]{:S(2)}, u32[]{:S(2)}) collective-permute-start(f32[72,512]{1,0:T(8,128)S(1)} %get-tuple-element.35), channel_id=1, source_target_pairs={{0,64},{16,208},{32,96},{48,240},{64,128},{80,16},{96,160},{112,48... | collective-permute-start | bytes 442376 | tf_op jit(solution)/shard_map/ppermute | solution.py:508
  60.9 5.3 %collective-permute-done.6.refs_0_ = f32[72,512]{1,0:T(8,128)S(1)} collective-permute-done((f32[72,512]{1,0:T(8,128)S(1)}, f32[72,512]{1,0:T(8,128)S(1)}, u32[]{:S(2)}, u32[]{:S(2)}) %collective-permute-start.6) | collective-permute-done | bytes 147488 | tf_op jit(solution)/shard_map/ppermute | solution.py:508
  66.2 0.0 collective-permute-done.5.full
  66.2 1.0 %collective-permute-start.7 = (f32[136,512]{1,0:T(8,128)S(1)}, f32[136,512]{1,0:T(8,128)S(1)}, u32[]{:S(2)}, u32[]{:S(2)}) collective-permute-start(f32[136,512]{1,0:T(8,128)S(1)} %relayed_text_terms.2), channel_id=1, source_target_pairs={{0,32},{16,240},{32,64},{48,16},{64,96},{80,48},{96,128},{112,80},... | collective-permute-start | bytes 835592 | tf_op jit(solution)/shard_map/ppermute | solution.py:508
  67.3 4.8 %collective-permute-done.7.full = f32[136,512]{1,0:T(8,128)S(1)} collective-permute-done((f32[136,512]{1,0:T(8,128)S(1)}, f32[136,512]{1,0:T(8,128)S(1)}, u32[]{:S(2)}, u32[]{:S(2)}) %collective-permute-start.7) | collective-permute-done | bytes 278560 | tf_op jit(solution)/shard_map/ppermute | solution.py:508
  72.0 2.2 %collective-permute-start.8 = (f32[136,512]{1,0:T(8,128)S(1)}, f32[136,512]{1,0:T(8,128)S(1)}, u32[]{:S(2)}, u32[]{:S(2)}) collective-permute-start(f32[136,512]{1,0:T(8,128)S(1)} %relayed_text_terms.3), channel_id=1, source_target_pairs={{0,32},{16,240},{32,64},{48,16},{64,96},{80,48},{96,128},{112,80},... | collective-permute-start | bytes 835592 | tf_op jit(solution)/shard_map/ppermute | solution.py:508
  74.3 4.2 %collective-permute-done.8.flow = f32[136,512]{1,0:T(8,128)S(1)} collective-permute-done((f32[136,512]{1,0:T(8,128)S(1)}, f32[136,512]{1,0:T(8,128)S(1)}, u32[]{:S(2)}, u32[]{:S(2)}) %collective-permute-start.8) | collective-permute-done | bytes 278560 | tf_op jit(solution)/shard_map/ppermute | solution.py:508
  78.5 5.3 %collective-permute-start.9 = (f32[136,512]{1,0:T(8,128)S(1)}, f32[136,512]{1,0:T(8,128)S(1)}, u32[]{:S(2)}, u32[]{:S(2)}) collective-permute-start(f32[136,512]{1,0:T(8,128)S(1)} %collective-permute-done.8.flow), channel_id=1, source_target_pairs={{0,16},{16,0},{1,17},{17,1},{2,18},{18,2},{3,19},{19,3},{4,20},{20... | collective-permute-start | bytes 835592 | tf_op jit(solution)/shard_map/ppermute | solution.py:514
  83.7 1.2 %collective-permute-done.9.other = f32[136,512]{1,0:T(8,128)S(1)} collective-permute-done((f32[136,512]{1,0:T(8,128)S(1)}, f32[136,512]{1,0:T(8,128)S(1)}, u32[]{:S(2)}, u32[]{:S(2)}) %collective-permute-start.9) | collective-permute-done | bytes 278560 | tf_op jit(solution)/shard_map/ppermute | solution.py:514
  84.9 0.7 text_gradient_total.1
  85.6 0.0 all-to-all-done.1.parts
  85.6 0.8 sum_of_image_parts_and_loss.1
  (5 shorter events, 0.1 us)
Async XLA Ops:
  11.4 23.6 %all-to-all-start = ((f32[16,24,128]{2,1,0:T(8,128)}), f32[16,24,128]{2,1,0:T(8,128)S(1)}, u32[]{:S(2)}, u32[]{:S(2)}) async-start(f32[16,24,128]{2,1,0:T(8,128)} %get-tuple-element.23), calls=%async_computation | async-start | bytes 393216 | tf_op jit(solution)/shard_map/all_to_all | solution.py:485
  21.4 2.5 %collective-permute-start = (f32[24,128]{1,0:T(8,128)S(1)}, f32[24,128]{1,0:T(8,128)S(1)}, u32[]{:S(2)}, u32[]{:S(2)}) collective-permute-start(f32[24,128]{1,0:T(8,128)S(1)} %bitcast.2), channel_id=1, source_target_pairs={{0,4},{4,0},{8,12},{12,8},{1,5},{5,1},{9,13},{13,9},{2,6},{6,2},{1... | collective-permute-start | bytes 36872 | tf_op jit(solution)/shard_map/ppermute | solution.py:490
  23.9 4.1 %collective-permute-start.1 = (f32[24,128]{1,0:T(8,128)S(1)}, f32[24,128]{1,0:T(8,128)S(1)}, u32[]{:S(2)}, u32[]{:S(2)}) collective-permute-start(f32[24,128]{1,0:T(8,128)S(1)} %joined_statistics.3.refs_0_), channel_id=1, source_target_pairs={{0,12},{4,8},{8,4},{12,0},{1,13},{5,9},{9,5},{13,1},{2,14},{6,10},... | collective-permute-start | bytes 36872 | tf_op jit(solution)/shard_map/ppermute | solution.py:490
  28.1 2.9 %collective-permute-start.2 = (f32[24,128]{1,0:T(8,128)S(1)}, f32[24,128]{1,0:T(8,128)S(1)}, u32[]{:S(2)}, u32[]{:S(2)}) collective-permute-start(f32[24,128]{1,0:T(8,128)S(1)} %joined_statistics.4.refs_0_), channel_id=1, source_target_pairs={{0,1},{1,0},{2,3},{3,2},{4,5},{5,4},{6,7},{7,6},{8,9},{9,8},{10,11... | collective-permute-start | bytes 36872 | tf_op jit(solution)/shard_map/ppermute | solution.py:490
  31.0 3.9 %collective-permute-start.3 = (f32[24,128]{1,0:T(8,128)S(1)}, f32[24,128]{1,0:T(8,128)S(1)}, u32[]{:S(2)}, u32[]{:S(2)}) collective-permute-start(f32[24,128]{1,0:T(8,128)S(1)} %joined_statistics.5.refs_0_), channel_id=1, source_target_pairs={{0,3},{1,2},{2,1},{3,0},{4,7},{5,6},{6,5},{7,4},{8,11},{9,10},{10,... | collective-permute-start | bytes 36872 | tf_op jit(solution)/shard_map/ppermute | solution.py:490
  44.0 10.5 %collective-permute-start.4 = (f32[552,512]{1,0:T(8,128)}, f32[552,512]{1,0:T(8,128)}, u32[]{:S(2)}, u32[]{:S(2)}) collective-permute-start(f32[552,512]{1,0:T(8,128)} %get-tuple-element.31), channel_id=1, source_target_pairs={{0,16},{16,0},{1,17},{17,1},{2,18},{18,2},{3,19},{19,3},{4,20},{20... | collective-permute-start | bytes 3391496 | tf_op jit(solution)/shard_map/ppermute | solution.py:500
  48.2 37.4 %all-to-all-start.1 = ((f32[16,264,128]{2,1,0:T(8,128)}), f32[16,264,128]{2,1,0:T(8,128)S(1)}, u32[]{:S(2)}, u32[]{:S(2)}) async-start(f32[16,264,128]{2,1,0:T(8,128)} %get-tuple-element.26), calls=%async_computation.1 | async-start | bytes 4325376 | tf_op jit(solution)/shard_map/all_to_all | solution.py:498
  55.9 10.2 %collective-permute-start.5 = (f32[136,512]{1,0:T(8,128)S(1)}, f32[136,512]{1,0:T(8,128)S(1)}, u32[]{:S(2)}, u32[]{:S(2)}) collective-permute-start(f32[136,512]{1,0:T(8,128)S(1)} %get-tuple-element.34), channel_id=1, source_target_pairs={{0,32},{16,240},{32,64},{48,16},{64,96},{80,48},{96,128},{112,80},... | collective-permute-start | bytes 835592 | tf_op jit(solution)/shard_map/ppermute | solution.py:508
  58.8 7.4 %collective-permute-start.6 = (f32[72,512]{1,0:T(8,128)S(1)}, f32[72,512]{1,0:T(8,128)S(1)}, u32[]{:S(2)}, u32[]{:S(2)}) collective-permute-start(f32[72,512]{1,0:T(8,128)S(1)} %get-tuple-element.35), channel_id=1, source_target_pairs={{0,64},{16,208},{32,96},{48,240},{64,128},{80,16},{96,160},{112,48... | collective-permute-start | bytes 442376 | tf_op jit(solution)/shard_map/ppermute | solution.py:508
  66.2 5.8 %collective-permute-start.7 = (f32[136,512]{1,0:T(8,128)S(1)}, f32[136,512]{1,0:T(8,128)S(1)}, u32[]{:S(2)}, u32[]{:S(2)}) collective-permute-start(f32[136,512]{1,0:T(8,128)S(1)} %relayed_text_terms.2), channel_id=1, source_target_pairs={{0,32},{16,240},{32,64},{48,16},{64,96},{80,48},{96,128},{112,80},... | collective-permute-start | bytes 835592 | tf_op jit(solution)/shard_map/ppermute | solution.py:508
  72.0 6.4 %collective-permute-start.8 = (f32[136,512]{1,0:T(8,128)S(1)}, f32[136,512]{1,0:T(8,128)S(1)}, u32[]{:S(2)}, u32[]{:S(2)}) collective-permute-start(f32[136,512]{1,0:T(8,128)S(1)} %relayed_text_terms.3), channel_id=1, source_target_pairs={{0,32},{16,240},{32,64},{48,16},{64,96},{80,48},{96,128},{112,80},... | collective-permute-start | bytes 835592 | tf_op jit(solution)/shard_map/ppermute | solution.py:508
  78.5 6.5 %collective-permute-start.9 = (f32[136,512]{1,0:T(8,128)S(1)}, f32[136,512]{1,0:T(8,128)S(1)}, u32[]{:S(2)}, u32[]{:S(2)}) collective-permute-start(f32[136,512]{1,0:T(8,128)S(1)} %collective-permute-done.8.flow), channel_id=1, source_target_pairs={{0,16},{16,0},{1,17},{17,1},{2,18},{18,2},{3,19},{19,3},{4,20},{20... | collective-permute-start | bytes 835592 | tf_op jit(solution)/shard_map/ppermute | solution.py:514

commit v7 on v5

--- a/solution.py
+++ b/solution.py
@@ -201,9 +201,9 @@
 
 
 def delta_kernel(scale, *refs):
-    row_parts = refs[:4]
-    col_stats, t_far, s_far, st_far, si_far, delta, theirs_out, mine, st, col_note = refs[4:14]
-    row_norms, col_norms, t, s, theirs, si, sems = refs[14:]
+    row_parts = refs[:2]
+    col_stats, t_far, s_far, st_far, si_far, delta, theirs_out, mine, st, col_note = refs[2:12]
+    row_norms, col_norms, t, s, theirs, si, grads, sems = refs[12:]
     tall = 256
     arrivals = []
     for n in range(t.shape[0] // tall):
@@ -265,16 +265,19 @@
     half = tall // 2
     full_note = jnp.full((NOTE, thin), row_total, F32)
 
+    wide = 256
+    for n in range(cols // wide):
+        grads[n * wide : (n + 1) * wide, :] = scale * lax.dot_general(
+            delta[:, n * wide : (n + 1) * wide], si[...], (((0,), (0,)), ((), ())),
+            preferred_element_type=F32,
+        )
+
     def text_block(out, top, far, part, note):
         size = tall if part is None else half
         at = lax.rem(place + far + chips, chips) * tall
-        across = pl.ds(pl.multiple_of(at, tall), tall)
-        grad = scale * lax.dot_general(
-            delta[:, across], si[...], (((0,), (0,)), ((), ())), preferred_element_type=F32
-        )
         if part is not None:
-            grad = jnp.where(part == 0, grad[:half], grad[half:])
-        out[top : top + size, :] = grad
+            at = at + part * half
+        out[top : top + size, :] = grads[pl.ds(pl.multiple_of(at, half), size), :]
         out[top + size : top + size + NOTE, :] = note
 
     for out, flow in ((theirs, 1 - core), (mine, core)):
@@ -344,7 +347,7 @@
             pltpu.VMEM((2, rows, LANES), F32), pltpu.VMEM((2, 16, cols), F32),
             pltpu.VMEM((rows, cols), F32), pltpu.VMEM((rows, cols), F32),
             pltpu.VMEM(flow, F32), pltpu.VMEM(student_img.shape, jnp.bfloat16),
-            pltpu.SemaphoreType.DMA((11,)),
+            pltpu.VMEM((cols, thin), F32), pltpu.SemaphoreType.DMA((11,)),
         ],
         compiler_params=pltpu.CompilerParams(vmem_limit_bytes=VMEM_LIMIT),
         cost_estimate=cost(2 * rows * cols * thin, 8 * rows * cols, 4 * rows * cols),
@@ -419,57 +422,53 @@
     )(*parts)
 
 
-def sum_kernel(parts, out, note):
-    own = out.shape[0]
-    for b in range(out.shape[1] // LANES):
-        total = parts[0, b * own : (b + 1) * own, :]
-        for k in range(1, parts.shape[0]):
-            total = total + parts[k, b * own : (b + 1) * own, :]
-        out[:, b * LANES : (b + 1) * LANES] = total
-    last = slice(parts.shape[1] - NOTE, parts.shape[1])
-    total = parts[0, last, :]
-    for k in range(1, parts.shape[0]):
-        total = total + parts[k, last, :]
-    note[...] = total
-
-
-def summed(parts, thin):
-    own = (parts.shape[1] - NOTE) * LANES // thin
-    return pl.pallas_call(
-        sum_kernel,
-        name="sum_of_image_parts",
-        out_shape=(jax.ShapeDtypeStruct((own, thin), F32), jax.ShapeDtypeStruct((NOTE, LANES), F32)),
-        in_specs=[WHOLE],
+def finish_kernel(flow, other, own, out, note):
+    half = out.shape[0]
+    down = pl.ds(pl.multiple_of(lax.axis_index("img_1") * half, half), half)
+    out[...] = flow[down, :] + other[down, :] + own[:half, :]
+    note[...] = flow[2 * half :, :LANES] + other[2 * half :, :LANES] + own[half:, :LANES]
+
+
+def finished(flow, other, own):
+    thin = flow.shape[1]
+    return pl.pallas_call(
+        finish_kernel,
+        name="text_gradient_total",
+        out_shape=(
+            jax.ShapeDtypeStruct((own.shape[0] - NOTE, thin), F32),
+            jax.ShapeDtypeStruct((NOTE, LANES), F32),
+        ),
+        in_specs=[WHOLE] * 3,
         out_specs=(WHOLE, WHOLE),
         compiler_params=pltpu.CompilerParams(vmem_limit_bytes=4 * MIB),
-        cost_estimate=cost(parts.size, 4 * parts.size),
-    )(parts)
-
-
-def finish_kernel(row_share, col_share, flow, other, own, col_note, out, loss):
-    half = out.shape[0]
-    core = lax.axis_index("img_1")
-    down = pl.ds(pl.multiple_of(core * half, half), half)
-    out[...] = flow[down, :] + other[down, :] + own[:half, :]
-    row_note = flow[2 * half :, :LANES] + other[2 * half :, :LANES] + own[half:, :LANES]
-    total = (0.5 * LN2) * (row_note * row_share + col_note[...] * col_share)
-    loss[0, 0] = total[0, 0]
-
-
-def finished(row_share, col_share, flow, other, own, col_note):
-    thin = flow.shape[1]
-    return pl.pallas_call(
-        functools.partial(finish_kernel, row_share, col_share),
-        name="text_gradient_and_loss",
-        out_shape=(
-            jax.ShapeDtypeStruct((own.shape[0] - NOTE, thin), F32),
-            jax.ShapeDtypeStruct((1, 1), F32),
-        ),
-        in_specs=[WHOLE] * 4,
+        cost_estimate=cost(own.size * 3, 16 * own.size),
+    )(flow, other, own)
+
+
+def sum_kernel(row_share, col_share, parts, row_note, out, loss):
+    own = out.shape[0]
+
+    def total(down):
+        return functools.reduce(jnp.add, [parts[k, down, :] for k in range(parts.shape[0])])
+
+    for b in range(out.shape[1] // LANES):
+        out[:, b * LANES : (b + 1) * LANES] = total(slice(b * own, (b + 1) * own))
+    col_note = total(slice(parts.shape[1] - NOTE, parts.shape[1]))
+    both = (0.5 * LN2) * (row_note[...] * row_share + col_note * col_share)
+    loss[0, 0] = both[0, 0]
+
+
+def summed(row_share, col_share, parts, row_note, thin):
+    own = (parts.shape[1] - NOTE) * LANES // thin
+    return pl.pallas_call(
+        functools.partial(sum_kernel, row_share, col_share),
+        name="sum_of_image_parts_and_loss",
+        out_shape=(jax.ShapeDtypeStruct((own, thin), F32), jax.ShapeDtypeStruct((1, 1), F32)),
+        in_specs=[WHOLE] * 2,
         out_specs=(WHOLE, pl.BlockSpec(memory_space=pltpu.SMEM)),
         compiler_params=pltpu.CompilerParams(vmem_limit_bytes=4 * MIB),
-        cost_estimate=cost(own.size * 3, 16 * own.size),
-    )(flow, other, own, col_note)
+        cost_estimate=cost(parts.size, 4 * parts.size),
+    )(parts, row_note)
 
 
 def turn(size, step):
@@ -489,13 +488,15 @@
     col = lax.all_to_all(col, IMG, 0, 0, tiled=True)
     row = row[0]
     for axis in TXT:
-        others = [lax.ppermute(row, axis, turn(side, k)) for k in (1, 3, 2)]
-        if axis == TXT[0]:
-            (row,) = join(((0, 1, 2, 3),), row, *others)
+        for first in (0, 1):
+            pairs = [(k, (k + 1 - 2 * ((k + first) % 2)) % side) for k in range(side)]
+            other = lax.ppermute(row, axis, pairs)
+            if (axis, first) != (TXT[1], 1):
+                (row,) = join(((0, 1),), row, other)
     swap = turn(cores, 1)
 
     delta, theirs, mine, near_txt, col_note = delta_and_text(
-        (row, *others), col, t, s, student_txt, student_img, chips
+        (row, other), col, t, s, student_txt, student_img, chips
     )
     theirs = lax.ppermute(theirs, "img_1", swap)
     to_img = image_gradient(delta, near_txt, col_note, txt_count)
@@ -514,9 +515,9 @@
     flow = relayed(one, outward(flow, 1))
     flow = outward(flow, 1)
     across = lax.ppermute(flow, "img_1", swap)
-    grad_img, col_note = summed(got_img, thin)
-    grad_txt, loss = finished(
-        1.0 / (rows * img_count), 1.0 / (cols * txt_count), flow, across, own, col_note
+    grad_txt, row_total = finished(flow, across, own)
+    grad_img, loss = summed(
+        1.0 / (rows * img_count), 1.0 / (cols * txt_count), got_img, row_total, thin
     )
     return (loss.reshape(()), grad_img, grad_txt)
 

time: 85.3 us -> 86.6 us (1.015)
  starting transfers between devices: 39.8 us -> 41.9 us
    all_to_all x1, starting transfers between devices: 3.73 us -> 6.32 us  [body(): got_img = lax.all_to_all(to_img, TXT, 0, 0, tiled=True)]
    all_to_all x1, waiting for transfers between devices: 1.28 us -> 0.01 us  [body(): got_img = lax.all_to_all(to_img, TXT, 0, 0, tiled=True)]
    ppermute x1, waiting for transfers between devices: 0.01 us -> 1.19 us  [body(): across = lax.ppermute(flow, 'img_1', swap)]
    ppermute x6 -> x4, waiting for transfers between devices: 6.51 us -> 5.54 us  [body(): other = lax.ppermute(row, axis, pairs)]
    ppermute x6 -> x4, starting transfers between devices: 8.67 us -> 7.97 us  [body(): other = lax.ppermute(row, axis, pairs)]
  transfers between devices with their start and end apart: 14 -> 12, of which waited for: 8 -> 8; matrix products, arithmetic and copies ran while one was open for 0% -> 0% of each run, Pallas kernels for 5% -> 5%
where the time goes in v7:
time: 86.6 us; the launch traced here: 86.4 us
  starting transfers between devices  41.9 us (48%)
  Pallas kernels  22.8 us (26%)
  waiting for transfers between devices  21 us (24%)
    ppermute x4, waiting for transfers between devices, outward(): return lax.ppermute(value, IMG, pairs)  14.2 us
    pallas_call x1, Pallas kernels, local_stats(): pl.pallas_call(kernel, name='logits_and_statistics', out_shape=(pltpu.HBM...  10.7 us
    all_to_all x1, starting transfers between devices, body(): col = lax.all_to_all(col, IMG, 0, 0, tiled=True)  10 us
    ppermute x4, starting transfers between devices, outward(): return lax.ppermute(value, IMG, pairs)  8.18 us
    ppermute x4, starting transfers between devices, body(): other = lax.ppermute(row, axis, pairs)  7.97 us
    pallas_call x1, Pallas kernels, delta_and_text(): pl.pallas_call(functools.partial(delta_kernel, 3.0 / math.sqrt(thin)), na...  7.01 us
    all_to_all x1, starting transfers between devices, body(): got_img = lax.all_to_all(to_img, TXT, 0, 0, tiled=True)  6.32 us
    ppermute x4, waiting for transfers between devices, body(): other = lax.ppermute(row, axis, pairs)  5.54 us
  transfers between devices with their start and end apart: 12, of which 8 were waited for; matrix products, arithmetic and copies ran while one was open for 0% of the time, Pallas kernels for 5%

profile of v7, /device:TPU:1, one launch (start us, length us, event | category | flops | bytes accessed | tf_op | source)
XLA Modules:
  0.0 86.4 jit_solution(10811662805859677043)
XLA Ops:
  0.6 10.7 %logits_and_statistics.1 = (f32[1024,1024]{1,0:T(8,128)}, f32[1024,1024]{1,0:T(8,128)}, f32[1,24,128]{2,1,0:T(8,128)S(1)}, f32[16,24,128]{2,1,0:T(8,128)}) custom-call(bf16[1024,1280]{1,0:T(8,128)(2,1)} %ti_hbm.1, bf16[1024,1280]{1,0:T(8,128)(2,1)} %tt_hbm.1, bf16[1024,512]{1,0:T(8,128)(2,1)} %refs_6_.1, bf16[1024,512]{1,0:T(8,128)(2,1)} %refs_5_.1), custom_call_target="tpu_custom_call" | custom-call | flops 3758096384 | bytes 8388608 | tf_op jit(solution)/shard_map/logits_and_statistics/pallas_call | solution.py:143
  11.4 10.0 %all-to-all-start = ((f32[16,24,128]{2,1,0:T(8,128)}), f32[16,24,128]{2,1,0:T(8,128)S(1)}, u32[]{:S(2)}, u32[]{:S(2)}) async-start(f32[16,24,128]{2,1,0:T(8,128)} %get-tuple-element.22), calls=%async_computation | async-start | bytes 393216 | tf_op jit(solution)/shard_map/all_to_all | solution.py:488
  21.4 1.2 %collective-permute-start = (f32[24,128]{1,0:T(8,128)S(1)}, f32[24,128]{1,0:T(8,128)S(1)}, u32[]{:S(2)}, u32[]{:S(2)}) collective-permute-start(f32[24,128]{1,0:T(8,128)S(1)} %bitcast.2), channel_id=1, source_target_pairs={{0,4},{4,0},{8,12},{12,8},{1,5},{5,1},{9,13},{13,9},{2,6},{6,2},{1... | collective-permute-start | bytes 36872 | tf_op jit(solution)/shard_map/ppermute | solution.py:493
  22.6 1.3 %collective-permute-done.refs_1_ = f32[24,128]{1,0:T(8,128)S(1)} collective-permute-done((f32[24,128]{1,0:T(8,128)S(1)}, f32[24,128]{1,0:T(8,128)S(1)}, u32[]{:S(2)}, u32[]{:S(2)}) %collective-permute-start) | collective-permute-done | bytes 12320 | tf_op jit(solution)/shard_map/ppermute | solution.py:493
  23.9 2.6 %collective-permute-start.1 = (f32[24,128]{1,0:T(8,128)S(1)}, f32[24,128]{1,0:T(8,128)S(1)}, u32[]{:S(2)}, u32[]{:S(2)}) collective-permute-start(f32[24,128]{1,0:T(8,128)S(1)} %joined_statistics.3.refs_0_), channel_id=1, source_target_pairs={{0,12},{4,8},{8,4},{12,0},{1,13},{5,9},{9,5},{13,1},{2,14},{6,10},... | collective-permute-start | bytes 36872 | tf_op jit(solution)/shard_map/ppermute | solution.py:493
  26.5 1.6 %collective-permute-done.1.refs_1_ = f32[24,128]{1,0:T(8,128)S(1)} collective-permute-done((f32[24,128]{1,0:T(8,128)S(1)}, f32[24,128]{1,0:T(8,128)S(1)}, u32[]{:S(2)}, u32[]{:S(2)}) %collective-permute-start.1) | collective-permute-done | bytes 12320 | tf_op jit(solution)/shard_map/ppermute | solution.py:493
  28.1 1.4 %collective-permute-start.2 = (f32[24,128]{1,0:T(8,128)S(1)}, f32[24,128]{1,0:T(8,128)S(1)}, u32[]{:S(2)}, u32[]{:S(2)}) collective-permute-start(f32[24,128]{1,0:T(8,128)S(1)} %joined_statistics.4.refs_0_), channel_id=1, source_target_pairs={{0,1},{1,0},{2,3},{3,2},{4,5},{5,4},{6,7},{7,6},{8,9},{9,8},{10,11... | collective-permute-start | bytes 36872 | tf_op jit(solution)/shard_map/ppermute | solution.py:493
  29.5 1.5 %collective-permute-done.2.refs_1_ = f32[24,128]{1,0:T(8,128)S(1)} collective-permute-done((f32[24,128]{1,0:T(8,128)S(1)}, f32[24,128]{1,0:T(8,128)S(1)}, u32[]{:S(2)}, u32[]{:S(2)}) %collective-permute-start.2) | collective-permute-done | bytes 12320 | tf_op jit(solution)/shard_map/ppermute | solution.py:493
  31.0 2.8 %collective-permute-start.3 = (f32[24,128]{1,0:T(8,128)S(1)}, f32[24,128]{1,0:T(8,128)S(1)}, u32[]{:S(2)}, u32[]{:S(2)}) collective-permute-start(f32[24,128]{1,0:T(8,128)S(1)} %joined_statistics.5.refs_0_), channel_id=1, source_target_pairs={{0,3},{1,2},{2,1},{3,0},{4,7},{5,6},{6,5},{7,4},{8,11},{9,10},{10,... | collective-permute-start | bytes 36872 | tf_op jit(solution)/shard_map/ppermute | solution.py:493
  33.9 1.1 %collective-permute-done.3.refs_1_ = f32[24,128]{1,0:T(8,128)S(1)} collective-permute-done((f32[24,128]{1,0:T(8,128)S(1)}, f32[24,128]{1,0:T(8,128)S(1)}, u32[]{:S(2)}, u32[]{:S(2)}) %collective-permute-start.3) | collective-permute-done | bytes 12320 | tf_op jit(solution)/shard_map/ppermute | solution.py:493
  34.9 0.0 all-to-all-done.refs_2_
  34.9 7.0 %delta_and_text_gradient.1 = (bf16[1024,1024]{1,0:T(8,128)(2,1)S(1)}, f32[552,512]{1,0:T(8,128)}, f32[552,512]{1,0:T(8,128)S(1)}, bf16[1024,512]{1,0:T(8,128)(2,1)S(1)}, f32[8,128]{1,0:T(8,128)S(1)}) custom-call(f32[24,128]{1,0:T(8,128)S(1)} %joined_statistics.5.refs_0_, f32[24,128]{1,0:T(8,128)S(1)} %collective-permute-done.3.refs_1_, ...), custom_call_target="tpu_custom_call" | custom-call | flops 1073741824 | bytes 8388608 | tf_op jit(solution)/shard_map/delta_and_text_gradient/pallas_call | solution.py:336
  42.0 4.2 %collective-permute-start.4 = (f32[552,512]{1,0:T(8,128)}, f32[552,512]{1,0:T(8,128)}, u32[]{:S(2)}, u32[]{:S(2)}) collective-permute-start(f32[552,512]{1,0:T(8,128)} %get-tuple-element.29), channel_id=1, source_target_pairs={{0,16},{16,0},{1,17},{17,1},{2,18},{18,2},{3,19},{19,3},{4,20},{20... | collective-permute-start | bytes 3391496 | tf_op jit(solution)/shard_map/ppermute | solution.py:501
  46.2 2.1 %image_gradient.1 = f32[16,264,128]{2,1,0:T(8,128)} custom-call(bf16[1024,1024]{1,0:T(8,128)(2,1)S(1)} %get-tuple-element.25.delta, bf16[1024,512]{1,0:T(8,128)(2,1)S(1)} %get-tuple-element.26.st, f32[8,128]{1,0:T(8,128)S(1)} %get-tuple-element.27.col_note), custom_call_target="tpu_custom_call" | custom-call | flops 1073741824 | bytes 4194304 | tf_op jit(solution)/shard_map/image_gradient/pallas_call | solution.py:367
  48.3 6.3 %all-to-all-start.1 = ((f32[16,264,128]{2,1,0:T(8,128)}), f32[16,264,128]{2,1,0:T(8,128)S(1)}, u32[]{:S(2)}, u32[]{:S(2)}) async-start(f32[16,264,128]{2,1,0:T(8,128)} %image_gradient.1), calls=%async_computation.1 | async-start | bytes 4325376 | tf_op jit(solution)/shard_map/all_to_all | solution.py:503
  54.6 0.0 collective-permute-done.4.theirs
  54.6 1.4 %both_cores_text_terms.1 = (f32[136,512]{1,0:T(8,128)S(1)}, f32[136,512]{1,0:T(8,128)S(1)}, f32[136,512]{1,0:T(8,128)S(1)}, f32[72,512]{1,0:T(8,128)S(1)}, f32[72,512]{1,0:T(8,128)S(1)}) custom-call(f32[552,512]{1,0:T(8,128)S(1)} %get-tuple-element.28.mine, f32[552,512]{1,0:T(8,128)} %collective-permute-done.4.theirs), custom_call_target="tpu_custom_call" | custom-call | flops 282624 | bytes 3391488 | tf_op jit(solution)/shard_map/both_cores_text_terms/pallas_call | solution.py:390
  56.0 2.8 %collective-permute-start.5 = (f32[136,512]{1,0:T(8,128)S(1)}, f32[136,512]{1,0:T(8,128)S(1)}, u32[]{:S(2)}, u32[]{:S(2)}) collective-permute-start(f32[136,512]{1,0:T(8,128)S(1)} %get-tuple-element.32), channel_id=1, source_target_pairs={{0,32},{16,240},{32,64},{48,16},{64,96},{80,48},{96,128},{112,80},... | collective-permute-start | bytes 835592 | tf_op jit(solution)/shard_map/ppermute | solution.py:511
  58.9 2.1 %collective-permute-start.6 = (f32[72,512]{1,0:T(8,128)S(1)}, f32[72,512]{1,0:T(8,128)S(1)}, u32[]{:S(2)}, u32[]{:S(2)}) collective-permute-start(f32[72,512]{1,0:T(8,128)S(1)} %get-tuple-element.33), channel_id=1, source_target_pairs={{0,64},{16,208},{32,96},{48,240},{64,128},{80,16},{96,160},{112,48... | collective-permute-start | bytes 442376 | tf_op jit(solution)/shard_map/ppermute | solution.py:511
  60.9 5.3 %collective-permute-done.6.refs_0_ = f32[72,512]{1,0:T(8,128)S(1)} collective-permute-done((f32[72,512]{1,0:T(8,128)S(1)}, f32[72,512]{1,0:T(8,128)S(1)}, u32[]{:S(2)}, u32[]{:S(2)}) %collective-permute-start.6) | collective-permute-done | bytes 147488 | tf_op jit(solution)/shard_map/ppermute | solution.py:511
  66.2 0.0 collective-permute-done.5.full
  66.3 1.0 %collective-permute-start.7 = (f32[136,512]{1,0:T(8,128)S(1)}, f32[136,512]{1,0:T(8,128)S(1)}, u32[]{:S(2)}, u32[]{:S(2)}) collective-permute-start(f32[136,512]{1,0:T(8,128)S(1)} %relayed_text_terms.2), channel_id=1, source_target_pairs={{0,32},{16,240},{32,64},{48,16},{64,96},{80,48},{96,128},{112,80},... | collective-permute-start | bytes 835592 | tf_op jit(solution)/shard_map/ppermute | solution.py:511
  67.3 4.8 %collective-permute-done.7.full = f32[136,512]{1,0:T(8,128)S(1)} collective-permute-done((f32[136,512]{1,0:T(8,128)S(1)}, f32[136,512]{1,0:T(8,128)S(1)}, u32[]{:S(2)}, u32[]{:S(2)}) %collective-permute-start.7) | collective-permute-done | bytes 278560 | tf_op jit(solution)/shard_map/ppermute | solution.py:511
  72.1 2.2 %collective-permute-start.8 = (f32[136,512]{1,0:T(8,128)S(1)}, f32[136,512]{1,0:T(8,128)S(1)}, u32[]{:S(2)}, u32[]{:S(2)}) collective-permute-start(f32[136,512]{1,0:T(8,128)S(1)} %relayed_text_terms.3), channel_id=1, source_target_pairs={{0,32},{16,240},{32,64},{48,16},{64,96},{80,48},{96,128},{112,80},... | collective-permute-start | bytes 835592 | tf_op jit(solution)/shard_map/ppermute | solution.py:511
  74.3 4.2 %collective-permute-done.8.flow = f32[136,512]{1,0:T(8,128)S(1)} collective-permute-done((f32[136,512]{1,0:T(8,128)S(1)}, f32[136,512]{1,0:T(8,128)S(1)}, u32[]{:S(2)}, u32[]{:S(2)}) %collective-permute-start.8) | collective-permute-done | bytes 278560 | tf_op jit(solution)/shard_map/ppermute | solution.py:511
  78.5 5.3 %collective-permute-start.9 = (f32[136,512]{1,0:T(8,128)S(1)}, f32[136,512]{1,0:T(8,128)S(1)}, u32[]{:S(2)}, u32[]{:S(2)}) collective-permute-start(f32[136,512]{1,0:T(8,128)S(1)} %collective-permute-done.8.flow), channel_id=1, source_target_pairs={{0,16},{16,0},{1,17},{17,1},{2,18},{18,2},{3,19},{19,3},{4,20},{20... | collective-permute-start | bytes 835592 | tf_op jit(solution)/shard_map/ppermute | solution.py:517
  83.8 1.2 %collective-permute-done.9.other = f32[136,512]{1,0:T(8,128)S(1)} collective-permute-done((f32[136,512]{1,0:T(8,128)S(1)}, f32[136,512]{1,0:T(8,128)S(1)}, u32[]{:S(2)}, u32[]{:S(2)}) %collective-permute-start.9) | collective-permute-done | bytes 278560 | tf_op jit(solution)/shard_map/ppermute | solution.py:517
  84.9 0.7 text_gradient_total.1
  85.6 0.0 all-to-all-done.1.parts
  85.6 0.8 sum_of_image_parts_and_loss.1
  (5 shorter events, 0.1 us)
Async XLA Ops:
  11.4 23.6 %all-to-all-start = ((f32[16,24,128]{2,1,0:T(8,128)}), f32[16,24,128]{2,1,0:T(8,128)S(1)}, u32[]{:S(2)}, u32[]{:S(2)}) async-start(f32[16,24,128]{2,1,0:T(8,128)} %get-tuple-element.22), calls=%async_computation | async-start | bytes 393216 | tf_op jit(solution)/shard_map/all_to_all | solution.py:488
  21.4 2.5 %collective-permute-start = (f32[24,128]{1,0:T(8,128)S(1)}, f32[24,128]{1,0:T(8,128)S(1)}, u32[]{:S(2)}, u32[]{:S(2)}) collective-permute-start(f32[24,128]{1,0:T(8,128)S(1)} %bitcast.2), channel_id=1, source_target_pairs={{0,4},{4,0},{8,12},{12,8},{1,5},{5,1},{9,13},{13,9},{2,6},{6,2},{1... | collective-permute-start | bytes 36872 | tf_op jit(solution)/shard_map/ppermute | solution.py:493
  23.9 4.1 %collective-permute-start.1 = (f32[24,128]{1,0:T(8,128)S(1)}, f32[24,128]{1,0:T(8,128)S(1)}, u32[]{:S(2)}, u32[]{:S(2)}) collective-permute-start(f32[24,128]{1,0:T(8,128)S(1)} %joined_statistics.3.refs_0_), channel_id=1, source_target_pairs={{0,12},{4,8},{8,4},{12,0},{1,13},{5,9},{9,5},{13,1},{2,14},{6,10},... | collective-permute-start | bytes 36872 | tf_op jit(solution)/shard_map/ppermute | solution.py:493
  28.1 2.9 %collective-permute-start.2 = (f32[24,128]{1,0:T(8,128)S(1)}, f32[24,128]{1,0:T(8,128)S(1)}, u32[]{:S(2)}, u32[]{:S(2)}) collective-permute-start(f32[24,128]{1,0:T(8,128)S(1)} %joined_statistics.4.refs_0_), channel_id=1, source_target_pairs={{0,1},{1,0},{2,3},{3,2},{4,5},{5,4},{6,7},{7,6},{8,9},{9,8},{10,11... | collective-permute-start | bytes 36872 | tf_op jit(solution)/shard_map/ppermute | solution.py:493
  31.0 3.9 %collective-permute-start.3 = (f32[24,128]{1,0:T(8,128)S(1)}, f32[24,128]{1,0:T(8,128)S(1)}, u32[]{:S(2)}, u32[]{:S(2)}) collective-permute-start(f32[24,128]{1,0:T(8,128)S(1)} %joined_statistics.5.refs_0_), channel_id=1, source_target_pairs={{0,3},{1,2},{2,1},{3,0},{4,7},{5,6},{6,5},{7,4},{8,11},{9,10},{10,... | collective-permute-start | bytes 36872 | tf_op jit(solution)/shard_map/ppermute | solution.py:493
  42.0 12.7 %collective-permute-start.4 = (f32[552,512]{1,0:T(8,128)}, f32[552,512]{1,0:T(8,128)}, u32[]{:S(2)}, u32[]{:S(2)}) collective-permute-start(f32[552,512]{1,0:T(8,128)} %get-tuple-element.29), channel_id=1, source_target_pairs={{0,16},{16,0},{1,17},{17,1},{2,18},{18,2},{3,19},{19,3},{4,20},{20... | collective-permute-start | bytes 3391496 | tf_op jit(solution)/shard_map/ppermute | solution.py:501
  48.3 37.3 %all-to-all-start.1 = ((f32[16,264,128]{2,1,0:T(8,128)}), f32[16,264,128]{2,1,0:T(8,128)S(1)}, u32[]{:S(2)}, u32[]{:S(2)}) async-start(f32[16,264,128]{2,1,0:T(8,128)} %image_gradient.1), calls=%async_computation.1 | async-start | bytes 4325376 | tf_op jit(solution)/shard_map/all_to_all | solution.py:503
  56.0 10.2 %collective-permute-start.5 = (f32[136,512]{1,0:T(8,128)S(1)}, f32[136,512]{1,0:T(8,128)S(1)}, u32[]{:S(2)}, u32[]{:S(2)}) collective-permute-start(f32[136,512]{1,0:T(8,128)S(1)} %get-tuple-element.32), channel_id=1, source_target_pairs={{0,32},{16,240},{32,64},{48,16},{64,96},{80,48},{96,128},{112,80},... | collective-permute-start | bytes 835592 | tf_op jit(solution)/shard_map/ppermute | solution.py:511
  58.9 7.4 %collective-permute-start.6 = (f32[72,512]{1,0:T(8,128)S(1)}, f32[72,512]{1,0:T(8,128)S(1)}, u32[]{:S(2)}, u32[]{:S(2)}) collective-permute-start(f32[72,512]{1,0:T(8,128)S(1)} %get-tuple-element.33), channel_id=1, source_target_pairs={{0,64},{16,208},{32,96},{48,240},{64,128},{80,16},{96,160},{112,48... | collective-permute-start | bytes 442376 | tf_op jit(solution)/shard_map/ppermute | solution.py:511
  66.3 5.8 %collective-permute-start.7 = (f32[136,512]{1,0:T(8,128)S(1)}, f32[136,512]{1,0:T(8,128)S(1)}, u32[]{:S(2)}, u32[]{:S(2)}) collective-permute-start(f32[136,512]{1,0:T(8,128)S(1)} %relayed_text_terms.2), channel_id=1, source_target_pairs={{0,32},{16,240},{32,64},{48,16},{64,96},{80,48},{96,128},{112,80},... | collective-permute-start | bytes 835592 | tf_op jit(solution)/shard_map/ppermute | solution.py:511
  72.1 6.4 %collective-permute-start.8 = (f32[136,512]{1,0:T(8,128)S(1)}, f32[136,512]{1,0:T(8,128)S(1)}, u32[]{:S(2)}, u32[]{:S(2)}) collective-permute-start(f32[136,512]{1,0:T(8,128)S(1)} %relayed_text_terms.3), channel_id=1, source_target_pairs={{0,32},{16,240},{32,64},{48,16},{64,96},{80,48},{96,128},{112,80},... | collective-permute-start | bytes 835592 | tf_op jit(solution)/shard_map/ppermute | solution.py:511
  78.5 6.4 %collective-permute-start.9 = (f32[136,512]{1,0:T(8,128)S(1)}, f32[136,512]{1,0:T(8,128)S(1)}, u32[]{:S(2)}, u32[]{:S(2)}) collective-permute-start(f32[136,512]{1,0:T(8,128)S(1)} %collective-permute-done.8.flow), channel_id=1, source_target_pairs={{0,16},{16,0},{1,17},{17,1},{2,18},{18,2},{3,19},{19,3},{4,20},{20... | collective-permute-start | bytes 835592 | tf_op jit(solution)/shard_map/ppermute | solution.py:517

commit v8 on v6

--- a/solution.py
+++ b/solution.py
@@ -15,7 +15,7 @@
 TXT_IMG = ("txt_0", "txt_1", "img_0", "img_1")
 LANES = 128
 NOTE = 8
-VMEM_LIMIT = 28 * 1024 * 1024
+VMEM_LIMIT = 32 * 1024 * 1024
 STATS_LIMIT = 32 * 1024 * 1024
 LN2 = math.log(2.0)
 F32 = jnp.float32
@@ -185,14 +185,18 @@
     sources, outs = refs[: len(refs) - len(groups)], refs[len(refs) - len(groups) :]
     for group, out in zip(groups, outs):
         for q, value in enumerate(joined([sources[k][...] for k in group])):
-            out[8 * q : 8 * q + 8, :] = value
-
-
-def join(groups, *parts):
+            for k in range(out.shape[0]):
+                out[k, 8 * q : 8 * q + 8, :] = value
+
+
+def join(groups, copies, *parts):
     return pl.pallas_call(
         functools.partial(join_kernel, groups),
         name="joined_statistics",
-        out_shape=[jax.ShapeDtypeStruct(parts[group[0]].shape, F32) for group in groups],
+        out_shape=[
+            jax.ShapeDtypeStruct((count, *parts[group[0]].shape), F32)
+            for group, count in zip(groups, copies)
+        ],
         in_specs=[WHOLE] * len(parts),
         out_specs=[WHOLE] * len(groups),
         compiler_params=pltpu.CompilerParams(vmem_limit_bytes=1 * MIB),
@@ -202,8 +206,8 @@
 
 def delta_kernel(scale, *refs):
     row_parts = refs[:2]
-    col_stats, t_far, s_far, st_far, si_far, delta, img_out, si, row_note = refs[2:11]
-    row_norms, col_norms, t, s, st, img_block, sems = refs[11:]
+    col_stats, t_far, s_far, st_far, si_far, img_out, theirs_out, mine = refs[2:10]
+    row_norms, col_norms, t, s, st, si, delta, img_block, theirs, grads, sems = refs[10:]
     tall = 256
     arrivals = []
     for n in range(t.shape[0] // tall):
@@ -228,7 +232,6 @@
     )
     row_total = jnp.sum(row_mean + row_learn - row_teach)
     col_total = jnp.sum(col_mean + col_learn - col_teach)
-    row_note[...] = jnp.full(row_note.shape, row_total, F32)
     for which, (down, across) in enumerate(((row_teach, col_teach), (row_learn, col_learn))):
         turned = jnp.concatenate([down - 3.0] * (LANES // 8), axis=0).T
         for b in range(8):
@@ -280,29 +283,25 @@
         save.start()
         saves.append(save)
 
-    for save in saves:
-        save.wait()
-
-
-def text_kernel(scale, delta, si, row_note, theirs_out, mine, theirs, sem):
-    cols = delta.shape[1]
-    thin = si.shape[1]
     place, core = lax.axis_index("img_0"), lax.axis_index("img_1")
     chips = lax.axis_size("img_0")
     tall = cols // chips
     half = tall // 2
-    full_note = row_note[...]
+    full_note = jnp.full((NOTE, thin), row_total, F32)
+
+    wide = 256
+    for n in range(cols // wide):
+        grads[n * wide : (n + 1) * wide, :] = scale * lax.dot_general(
+            delta[:, n * wide : (n + 1) * wide], si[...], (((0,), (0,)), ((), ())),
+            preferred_element_type=F32,
+        )
 
     def text_block(out, top, far, part, note):
         size = tall if part is None else half
         at = lax.rem(place + far + chips, chips) * tall
-        across = pl.ds(pl.multiple_of(at, tall), tall)
-        grad = scale * lax.dot_general(
-            delta[:, across], si[...], (((0,), (0,)), ((), ())), preferred_element_type=F32
-        )
         if part is not None:
-            grad = jnp.where(part == 0, grad[:half], grad[half:])
-        out[top : top + size, :] = grad
+            at = at + part * half
+        out[top : top + size, :] = grads[pl.ds(pl.multiple_of(at, half), size), :]
         out[top + size : top + size + NOTE, :] = note
 
     for out, flow in ((theirs, 1 - core), (mine, core)):
@@ -315,10 +314,12 @@
             text_block(out, top, far, part, note)
             top += (tall if part is None else half) + NOTE
         if out is theirs:
-            save = pltpu.make_async_copy(theirs, theirs_out, sem)
+            save = pltpu.make_async_copy(theirs, theirs_out, sems.at[10 + len(saves)])
             save.start()
-
-    save.wait()
+            saves.append(save)
+
+    for save in saves:
+        save.wait()
 
 
 def flow_rows(tall):
@@ -326,28 +327,28 @@
     return (full, full, full, part, part)
 
 
-def delta_and_image(row_parts, col_stats, t, s, student_txt, student_img, pieces):
+def gradients(row_parts, col_stats, t, s, student_txt, student_img, pieces, chips):
     rows, cols = t.shape
     thin = student_txt.shape[1]
     shape = (pieces, rows // pieces * thin // LANES + NOTE, LANES)
+    flow = (sum(flow_rows(cols // chips)), thin)
     return pl.pallas_call(
         functools.partial(delta_kernel, 3.0 / math.sqrt(thin)),
-        name="delta_and_image_gradient",
-        out_shape=(
-            pltpu.VMEM((rows, cols), jnp.bfloat16), pltpu.HBM(shape, F32),
-            pltpu.VMEM(student_img.shape, jnp.bfloat16),
-            jax.ShapeDtypeStruct((NOTE, thin), F32),
-        ),
+        name="delta_and_gradients",
+        out_shape=(pltpu.HBM(shape, F32), pltpu.HBM(flow, F32), jax.ShapeDtypeStruct(flow, F32)),
         in_specs=[WHOLE] * (len(row_parts) + 1) + [FAR] * 4,
-        out_specs=(WHOLE, FAR, WHOLE, WHOLE),
+        out_specs=(FAR, FAR, WHOLE),
         scratch_shapes=[
             pltpu.VMEM((2, rows, LANES), F32), pltpu.VMEM((2, 16, cols), F32),
             pltpu.VMEM((rows, cols), F32), pltpu.VMEM((rows, cols), F32),
-            pltpu.VMEM(student_txt.shape, jnp.bfloat16), pltpu.VMEM(shape, F32),
-            pltpu.SemaphoreType.DMA((10 + pieces // 4,)),
+            pltpu.VMEM(student_txt.shape, jnp.bfloat16),
+            pltpu.VMEM(student_img.shape, jnp.bfloat16),
+            pltpu.VMEM((rows, cols), jnp.bfloat16), pltpu.VMEM(shape, F32),
+            pltpu.VMEM(flow, F32), pltpu.VMEM((cols, thin), F32),
+            pltpu.SemaphoreType.DMA((11 + pieces // 4,)),
         ],
         compiler_params=pltpu.CompilerParams(vmem_limit_bytes=VMEM_LIMIT),
-        cost_estimate=cost(2 * rows * cols * thin, 8 * rows * cols, 4 * rows * cols),
+        cost_estimate=cost(4 * rows * cols * thin, 8 * rows * cols, 4 * rows * cols),
     )(
         *row_parts, col_stats,
         *(
@@ -355,22 +356,6 @@
             for x in (t, s, student_txt, student_img)
         ),
     )
-
-
-def text_gradient(delta, student_img, row_note, chips):
-    rows, cols = delta.shape
-    thin = student_img.shape[1]
-    flow = (sum(flow_rows(cols // chips)), thin)
-    return pl.pallas_call(
-        functools.partial(text_kernel, 3.0 / math.sqrt(thin)),
-        name="text_gradient",
-        out_shape=(pltpu.HBM(flow, F32), jax.ShapeDtypeStruct(flow, F32)),
-        in_specs=[WHOLE] * 3,
-        out_specs=(FAR, WHOLE),
-        scratch_shapes=[pltpu.VMEM(flow, F32), pltpu.SemaphoreType.DMA],
-        compiler_params=pltpu.CompilerParams(vmem_limit_bytes=16 * MIB),
-        cost_estimate=cost(2 * rows * cols * thin, 4 * rows * thin + 2 * rows * cols),
-    )(delta, student_img, row_note)
 
 
 def add_kernel(mine, theirs, *outs):
@@ -480,23 +465,30 @@
     side = lax.axis_size("txt_0")
 
     t, s, row, col = local_stats(
-        teacher_img, teacher_txt, student_img, student_txt, img_count
-    )
-    col = lax.all_to_all(col, IMG, 0, 0, tiled=True)
+        teacher_img, teacher_txt, student_img, student_txt, 1
+    )
+    swap = turn(cores, 1)
+
+    def neighbour(value, axis, first):
+        pairs = [(k, (k + 1 - 2 * ((k + first) % 2)) % side) for k in range(side)]
+        return lax.ppermute(value, axis, pairs)
+
+    row, col = row[0], col[0]
+    other = neighbour(row, TXT[0], 0)
+    row, col = join(
+        ((0, 1), (2, 3)), (1, chips), row, other, col, lax.ppermute(col, "img_1", swap)
+    )
+    col = lax.all_to_all(col, "img_0", 0, 0, tiled=True)
+    for axis, first in ((TXT[0], 1), (TXT[1], 0)):
+        row = row[0]
+        (row,) = join(((0, 1),), (1,), row, neighbour(row, axis, first))
     row = row[0]
-    for axis in TXT:
-        for first in (0, 1):
-            pairs = [(k, (k + 1 - 2 * ((k + first) % 2)) % side) for k in range(side)]
-            other = lax.ppermute(row, axis, pairs)
-            if (axis, first) != (TXT[1], 1):
-                (row,) = join(((0, 1),), row, other)
-    swap = turn(cores, 1)
-
-    delta, to_img, near_img, row_note = delta_and_image(
-        (row, other), col, t, s, student_txt, student_img, txt_count
+    other = neighbour(row, TXT[1], 1)
+
+    to_img, theirs, mine = gradients(
+        (row, other), col, t, s, student_txt, student_img, txt_count, chips
     )
     got_img = lax.all_to_all(to_img, TXT, 0, 0, tiled=True)
-    theirs, mine = text_gradient(delta, near_img, row_note, chips)
     theirs = lax.ppermute(theirs, "img_1", swap)
     two, three, one, four, own = added(mine, theirs, chips)
 

time: 86.6 us -> 85.4 us (0.986)
  Pallas kernels: 22.7 us -> 21.4 us
  starting transfers between devices: 42 us -> 41.1 us
  waiting for transfers between devices: 21 us -> 21.9 us
    all_to_all x1, starting transfers between devices: 10 us -> 6.46 us  [body(): col = lax.all_to_all(col, 'img_0', 0, 0, tiled=True)]
    ppermute x4 -> x5, starting transfers between devices: 7.97 us -> 10 us  [the longest x4 6.67 us: neighbour(): return lax.ppermute(value, axis, pairs)]
    pallas_call x2 -> x1, Pallas kernels: 9.07 us -> 7.79 us  [gradients(): pl.pallas_call(functools.partial(delta_kernel, 3.0 / math.sqrt(thin)), na...]
    ppermute x4 -> x5, waiting for transfers between devices: 5.54 us -> 6.48 us  [the longest x4 5.65 us: neighbour(): return lax.ppermute(value, axis, pairs)]
  transfers between devices with their start and end apart: 12 -> 13, of which waited for: 8 -> 9; matrix products, arithmetic and copies ran while one was open for 0% -> 0% of each run, Pallas kernels for 3% -> 3%
where the time goes in v8:
time: 85.4 us; the launch traced here: 85.1 us
  starting transfers between devices  41.1 us (48%)
  waiting for transfers between devices  21.9 us (26%)
  Pallas kernels  21.4 us (25%)
    ppermute x4, waiting for transfers between devices, outward(): return lax.ppermute(value, IMG, pairs)  14.3 us
    pallas_call x1, Pallas kernels, local_stats(): pl.pallas_call(kernel, name='logits_and_statistics', out_shape=(pltpu.HBM...  10.1 us
    ppermute x4, starting transfers between devices, outward(): return lax.ppermute(value, IMG, pairs)  8.33 us
    pallas_call x1, Pallas kernels, gradients(): pl.pallas_call(functools.partial(delta_kernel, 3.0 / math.sqrt(thin)), na...  7.79 us
    ppermute x4, starting transfers between devices, neighbour(): return lax.ppermute(value, axis, pairs)  6.67 us
    all_to_all x1, starting transfers between devices, body(): col = lax.all_to_all(col, 'img_0', 0, 0, tiled=True)  6.46 us
    all_to_all x1, starting transfers between devices, body(): got_img = lax.all_to_all(to_img, TXT, 0, 0, tiled=True)  6.31 us
    ppermute x4, waiting for transfers between devices, neighbour(): return lax.ppermute(value, axis, pairs)  5.65 us
  transfers between devices with their start and end apart: 13, of which 9 were waited for; matrix products, arithmetic and copies ran while one was open for 0% of the time, Pallas kernels for 3%

profile of v8, /device:TPU:1, one launch (start us, length us, event | category | flops | bytes accessed | tf_op | source)
XLA Modules:
  0.0 85.1 jit_solution(3665821197229582113)
XLA Ops:
  0.6 10.1 %logits_and_statistics.1 = (f32[1024,1024]{1,0:T(8,128)}, f32[1024,1024]{1,0:T(8,128)}, f32[1,24,128]{2,1,0:T(8,128)S(1)}, f32[1,24,128]{2,1,0:T(8,128)S(1)}) custom-call(bf16[1024,1280]{1,0:T(8,128)(2,1)} %ti_hbm.1, bf16[1024,1280]{1,0:T(8,128)(2,1)} %tt_hbm.1, bf16[1024,512]{1,0:T(8,128)(2,1)} %refs_6_.1, bf16[1024,512]{1,0:T(8,128)(2,1)} %refs_5_.1), custom_call_target="tpu_custom_call" | custom-call | flops 3758096384 | bytes 8388608 | tf_op jit(solution)/shard_map/logits_and_statistics/pallas_call | solution.py:143
  10.7 3.3 %collective-permute-start.1 = (f32[24,128]{1,0:T(8,128)S(1)}, f32[24,128]{1,0:T(8,128)S(1)}, u32[]{:S(2)}, u32[]{:S(2)}) collective-permute-start(f32[24,128]{1,0:T(8,128)S(1)} %bitcast.12), channel_id=1, source_target_pairs={{0,16},{16,0},{1,17},{17,1},{2,18},{18,2},{3,19},{19,3},{4,20},{20... | collective-permute-start | bytes 36872 | tf_op jit(solution)/shard_map/ppermute | solution.py:479
  14.0 0.0 collective-permute-start
  14.0 0.8 collective-permute-done.1.refs_3_
  14.9 1.7 %collective-permute-done.refs_1_ = f32[24,128]{1,0:T(8,128)S(1)} collective-permute-done((f32[24,128]{1,0:T(8,128)S(1)}, f32[24,128]{1,0:T(8,128)S(1)}, u32[]{:S(2)}, u32[]{:S(2)}) %collective-permute-start) | collective-permute-done | bytes 12320 | tf_op jit(solution)/shard_map/ppermute | solution.py:474
  16.6 0.7 joined_statistics.3
  17.3 6.5 %all-to-all-start = ((f32[8,24,128]{2,1,0:T(8,128)}), f32[8,24,128]{2,1,0:T(8,128)S(1)}, u32[]{:S(2)}, u32[]{:S(2)}) async-start(f32[8,24,128]{2,1,0:T(8,128)} %get-tuple-element.24), calls=%async_computation | async-start | bytes 196608 | tf_op jit(solution)/shard_map/all_to_all | solution.py:481
  23.7 2.5 %collective-permute-start.2 = (f32[24,128]{1,0:T(8,128)S(1)}, f32[24,128]{1,0:T(8,128)S(1)}, u32[]{:S(2)}, u32[]{:S(2)}) collective-permute-start(f32[24,128]{1,0:T(8,128)S(1)} %bitcast.14), channel_id=1, source_target_pairs={{0,12},{4,8},{8,4},{12,0},{1,13},{5,9},{9,5},{13,1},{2,14},{6,10},... | collective-permute-start | bytes 36872 | tf_op jit(solution)/shard_map/ppermute | solution.py:474
  26.2 1.3 %collective-permute-done.2.refs_1_ = f32[24,128]{1,0:T(8,128)S(1)} collective-permute-done((f32[24,128]{1,0:T(8,128)S(1)}, f32[24,128]{1,0:T(8,128)S(1)}, u32[]{:S(2)}, u32[]{:S(2)}) %collective-permute-start.2) | collective-permute-done | bytes 12320 | tf_op jit(solution)/shard_map/ppermute | solution.py:474
  27.5 1.4 %collective-permute-start.3 = (f32[24,128]{1,0:T(8,128)S(1)}, f32[24,128]{1,0:T(8,128)S(1)}, u32[]{:S(2)}, u32[]{:S(2)}) collective-permute-start(f32[24,128]{1,0:T(8,128)S(1)} %bitcast.8), channel_id=1, source_target_pairs={{0,1},{1,0},{2,3},{3,2},{4,5},{5,4},{6,7},{7,6},{8,9},{9,8},{10,11... | collective-permute-start | bytes 36872 | tf_op jit(solution)/shard_map/ppermute | solution.py:474
  28.9 1.5 %collective-permute-done.3.refs_1_ = f32[24,128]{1,0:T(8,128)S(1)} collective-permute-done((f32[24,128]{1,0:T(8,128)S(1)}, f32[24,128]{1,0:T(8,128)S(1)}, u32[]{:S(2)}, u32[]{:S(2)}) %collective-permute-start.3) | collective-permute-done | bytes 12320 | tf_op jit(solution)/shard_map/ppermute | solution.py:474
  30.4 2.8 %collective-permute-start.4 = (f32[24,128]{1,0:T(8,128)S(1)}, f32[24,128]{1,0:T(8,128)S(1)}, u32[]{:S(2)}, u32[]{:S(2)}) collective-permute-start(f32[24,128]{1,0:T(8,128)S(1)} %bitcast.6), channel_id=1, source_target_pairs={{0,3},{1,2},{2,1},{3,0},{4,7},{5,6},{6,5},{7,4},{8,11},{9,10},{10,... | collective-permute-start | bytes 36872 | tf_op jit(solution)/shard_map/ppermute | solution.py:474
  33.2 1.1 %collective-permute-done.4.refs_1_ = f32[24,128]{1,0:T(8,128)S(1)} collective-permute-done((f32[24,128]{1,0:T(8,128)S(1)}, f32[24,128]{1,0:T(8,128)S(1)}, u32[]{:S(2)}, u32[]{:S(2)}) %collective-permute-start.4) | collective-permute-done | bytes 12320 | tf_op jit(solution)/shard_map/ppermute | solution.py:474
  34.3 0.0 all-to-all-done.refs_2_
  34.3 7.8 %delta_and_gradients.1 = (f32[16,264,128]{2,1,0:T(8,128)}, f32[552,512]{1,0:T(8,128)}, f32[552,512]{1,0:T(8,128)S(1)}) custom-call(f32[24,128]{1,0:T(8,128)S(1)} %bitcast.7, f32[24,128]{1,0:T(8,128)S(1)} %collective-permute-done.4.refs_1_, f32[8,24,128]{2,1,0:T(8,128)S(1)} %all-to-all-done.refs_2_, f32[1024,1024]{1,0:T(8,128)} %get-tuple-element.25.refs_3_, ...), custom_call_target="tpu_custom_call" | custom-call | flops 2147483648 | bytes 8388608 | tf_op jit(solution)/shard_map/delta_and_gradients/pallas_call | solution.py:335
  42.1 4.7 %collective-permute-start.5 = (f32[552,512]{1,0:T(8,128)}, f32[552,512]{1,0:T(8,128)}, u32[]{:S(2)}, u32[]{:S(2)}) collective-permute-start(f32[552,512]{1,0:T(8,128)} %get-tuple-element.29), channel_id=1, source_target_pairs={{0,16},{16,0},{1,17},{17,1},{2,18},{18,2},{3,19},{19,3},{4,20},{20... | collective-permute-start | bytes 3391496 | tf_op jit(solution)/shard_map/ppermute | solution.py:492
  46.8 6.3 %all-to-all-start.1 = ((f32[16,264,128]{2,1,0:T(8,128)}), f32[16,264,128]{2,1,0:T(8,128)S(1)}, u32[]{:S(2)}, u32[]{:S(2)}) async-start(f32[16,264,128]{2,1,0:T(8,128)} %get-tuple-element.27), calls=%async_computation.1 | async-start | bytes 4325376 | tf_op jit(solution)/shard_map/all_to_all | solution.py:491
  53.1 0.0 collective-permute-done.5.theirs
  53.2 1.4 %both_cores_text_terms.1 = (f32[136,512]{1,0:T(8,128)S(1)}, f32[136,512]{1,0:T(8,128)S(1)}, f32[136,512]{1,0:T(8,128)S(1)}, f32[72,512]{1,0:T(8,128)S(1)}, f32[72,512]{1,0:T(8,128)S(1)}) custom-call(f32[552,512]{1,0:T(8,128)S(1)} %get-tuple-element.28.mine, f32[552,512]{1,0:T(8,128)} %collective-permute-done.5.theirs), custom_call_target="tpu_custom_call" | custom-call | flops 282624 | bytes 3391488 | tf_op jit(solution)/shard_map/both_cores_text_terms/pallas_call | solution.py:372
  54.5 3.0 %collective-permute-start.6 = (f32[136,512]{1,0:T(8,128)S(1)}, f32[136,512]{1,0:T(8,128)S(1)}, u32[]{:S(2)}, u32[]{:S(2)}) collective-permute-start(f32[136,512]{1,0:T(8,128)S(1)} %get-tuple-element.32), channel_id=1, source_target_pairs={{0,32},{16,240},{32,64},{48,16},{64,96},{80,48},{96,128},{112,80},... | collective-permute-start | bytes 835592 | tf_op jit(solution)/shard_map/ppermute | solution.py:500
  57.6 2.1 %collective-permute-start.7 = (f32[72,512]{1,0:T(8,128)S(1)}, f32[72,512]{1,0:T(8,128)S(1)}, u32[]{:S(2)}, u32[]{:S(2)}) collective-permute-start(f32[72,512]{1,0:T(8,128)S(1)} %get-tuple-element.33), channel_id=1, source_target_pairs={{0,64},{16,208},{32,96},{48,240},{64,128},{80,16},{96,160},{112,48... | collective-permute-start | bytes 442376 | tf_op jit(solution)/shard_map/ppermute | solution.py:500
  59.6 5.3 %collective-permute-done.7.refs_0_ = f32[72,512]{1,0:T(8,128)S(1)} collective-permute-done((f32[72,512]{1,0:T(8,128)S(1)}, f32[72,512]{1,0:T(8,128)S(1)}, u32[]{:S(2)}, u32[]{:S(2)}) %collective-permute-start.7) | collective-permute-done | bytes 147488 | tf_op jit(solution)/shard_map/ppermute | solution.py:500
  64.9 0.0 collective-permute-done.6.full
  65.0 1.0 %collective-permute-start.8 = (f32[136,512]{1,0:T(8,128)S(1)}, f32[136,512]{1,0:T(8,128)S(1)}, u32[]{:S(2)}, u32[]{:S(2)}) collective-permute-start(f32[136,512]{1,0:T(8,128)S(1)} %relayed_text_terms.2), channel_id=1, source_target_pairs={{0,32},{16,240},{32,64},{48,16},{64,96},{80,48},{96,128},{112,80},... | collective-permute-start | bytes 835592 | tf_op jit(solution)/shard_map/ppermute | solution.py:500
  66.0 4.8 %collective-permute-done.8.full = f32[136,512]{1,0:T(8,128)S(1)} collective-permute-done((f32[136,512]{1,0:T(8,128)S(1)}, f32[136,512]{1,0:T(8,128)S(1)}, u32[]{:S(2)}, u32[]{:S(2)}) %collective-permute-start.8) | collective-permute-done | bytes 278560 | tf_op jit(solution)/shard_map/ppermute | solution.py:500
  70.8 2.2 %collective-permute-start.9 = (f32[136,512]{1,0:T(8,128)S(1)}, f32[136,512]{1,0:T(8,128)S(1)}, u32[]{:S(2)}, u32[]{:S(2)}) collective-permute-start(f32[136,512]{1,0:T(8,128)S(1)} %relayed_text_terms.3), channel_id=1, source_target_pairs={{0,32},{16,240},{32,64},{48,16},{64,96},{80,48},{96,128},{112,80},... | collective-permute-start | bytes 835592 | tf_op jit(solution)/shard_map/ppermute | solution.py:500
  73.0 4.2 %collective-permute-done.9.flow = f32[136,512]{1,0:T(8,128)S(1)} collective-permute-done((f32[136,512]{1,0:T(8,128)S(1)}, f32[136,512]{1,0:T(8,128)S(1)}, u32[]{:S(2)}, u32[]{:S(2)}) %collective-permute-start.9) | collective-permute-done | bytes 278560 | tf_op jit(solution)/shard_map/ppermute | solution.py:500
  77.2 5.3 %collective-permute-start.10 = (f32[136,512]{1,0:T(8,128)S(1)}, f32[136,512]{1,0:T(8,128)S(1)}, u32[]{:S(2)}, u32[]{:S(2)}) collective-permute-start(f32[136,512]{1,0:T(8,128)S(1)} %collective-permute-done.9.flow), channel_id=1, source_target_pairs={{0,16},{16,0},{1,17},{17,1},{2,18},{18,2},{3,19},{19,3},{4,20},{20... | collective-permute-start | bytes 835592 | tf_op jit(solution)/shard_map/ppermute | solution.py:506
  82.5 1.2 %collective-permute-done.10.other = f32[136,512]{1,0:T(8,128)S(1)} collective-permute-done((f32[136,512]{1,0:T(8,128)S(1)}, f32[136,512]{1,0:T(8,128)S(1)}, u32[]{:S(2)}, u32[]{:S(2)}) %collective-permute-start.10) | collective-permute-done | bytes 278560 | tf_op jit(solution)/shard_map/ppermute | solution.py:506
  83.7 0.7 text_gradient_total.1
  84.3 0.0 all-to-all-done.1.parts
  84.3 0.8 sum_of_image_parts_and_loss.1
  (4 shorter events, 0.1 us)
Async XLA Ops:
  10.7 4.2 %collective-permute-start.1 = (f32[24,128]{1,0:T(8,128)S(1)}, f32[24,128]{1,0:T(8,128)S(1)}, u32[]{:S(2)}, u32[]{:S(2)}) collective-permute-start(f32[24,128]{1,0:T(8,128)S(1)} %bitcast.12), channel_id=1, source_target_pairs={{0,16},{16,0},{1,17},{17,1},{2,18},{18,2},{3,19},{19,3},{4,20},{20... | collective-permute-start | bytes 36872 | tf_op jit(solution)/shard_map/ppermute | solution.py:479
  14.0 2.6 %collective-permute-start = (f32[24,128]{1,0:T(8,128)S(1)}, f32[24,128]{1,0:T(8,128)S(1)}, u32[]{:S(2)}, u32[]{:S(2)}) collective-permute-start(f32[24,128]{1,0:T(8,128)S(1)} %bitcast.10), channel_id=1, source_target_pairs={{0,4},{4,0},{8,12},{12,8},{1,5},{5,1},{9,13},{13,9},{2,6},{6,2},{1... | collective-permute-start | bytes 36872 | tf_op jit(solution)/shard_map/ppermute | solution.py:474
  17.3 17.1 %all-to-all-start = ((f32[8,24,128]{2,1,0:T(8,128)}), f32[8,24,128]{2,1,0:T(8,128)S(1)}, u32[]{:S(2)}, u32[]{:S(2)}) async-start(f32[8,24,128]{2,1,0:T(8,128)} %get-tuple-element.24), calls=%async_computation | async-start | bytes 196608 | tf_op jit(solution)/shard_map/all_to_all | solution.py:481
  23.7 3.8 %collective-permute-start.2 = (f32[24,128]{1,0:T(8,128)S(1)}, f32[24,128]{1,0:T(8,128)S(1)}, u32[]{:S(2)}, u32[]{:S(2)}) collective-permute-start(f32[24,128]{1,0:T(8,128)S(1)} %bitcast.14), channel_id=1, source_target_pairs={{0,12},{4,8},{8,4},{12,0},{1,13},{5,9},{9,5},{13,1},{2,14},{6,10},... | collective-permute-start | bytes 36872 | tf_op jit(solution)/shard_map/ppermute | solution.py:474
  27.5 2.9 %collective-permute-start.3 = (f32[24,128]{1,0:T(8,128)S(1)}, f32[24,128]{1,0:T(8,128)S(1)}, u32[]{:S(2)}, u32[]{:S(2)}) collective-permute-start(f32[24,128]{1,0:T(8,128)S(1)} %bitcast.8), channel_id=1, source_target_pairs={{0,1},{1,0},{2,3},{3,2},{4,5},{5,4},{6,7},{7,6},{8,9},{9,8},{10,11... | collective-permute-start | bytes 36872 | tf_op jit(solution)/shard_map/ppermute | solution.py:474
  30.4 3.9 %collective-permute-start.4 = (f32[24,128]{1,0:T(8,128)S(1)}, f32[24,128]{1,0:T(8,128)S(1)}, u32[]{:S(2)}, u32[]{:S(2)}) collective-permute-start(f32[24,128]{1,0:T(8,128)S(1)} %bitcast.6), channel_id=1, source_target_pairs={{0,3},{1,2},{2,1},{3,0},{4,7},{5,6},{6,5},{7,4},{8,11},{9,10},{10,... | collective-permute-start | bytes 36872 | tf_op jit(solution)/shard_map/ppermute | solution.py:474
  42.1 11.0 %collective-permute-start.5 = (f32[552,512]{1,0:T(8,128)}, f32[552,512]{1,0:T(8,128)}, u32[]{:S(2)}, u32[]{:S(2)}) collective-permute-start(f32[552,512]{1,0:T(8,128)} %get-tuple-element.29), channel_id=1, source_target_pairs={{0,16},{16,0},{1,17},{17,1},{2,18},{18,2},{3,19},{19,3},{4,20},{20... | collective-permute-start | bytes 3391496 | tf_op jit(solution)/shard_map/ppermute | solution.py:492
  46.8 37.5 %all-to-all-start.1 = ((f32[16,264,128]{2,1,0:T(8,128)}), f32[16,264,128]{2,1,0:T(8,128)S(1)}, u32[]{:S(2)}, u32[]{:S(2)}) async-start(f32[16,264,128]{2,1,0:T(8,128)} %get-tuple-element.27), calls=%async_computation.1 | async-start | bytes 4325376 | tf_op jit(solution)/shard_map/all_to_all | solution.py:491
  54.5 10.4 %collective-permute-start.6 = (f32[136,512]{1,0:T(8,128)S(1)}, f32[136,512]{1,0:T(8,128)S(1)}, u32[]{:S(2)}, u32[]{:S(2)}) collective-permute-start(f32[136,512]{1,0:T(8,128)S(1)} %get-tuple-element.32), channel_id=1, source_target_pairs={{0,32},{16,240},{32,64},{48,16},{64,96},{80,48},{96,128},{112,80},... | collective-permute-start | bytes 835592 | tf_op jit(solution)/shard_map/ppermute | solution.py:500
  57.6 7.4 %collective-permute-start.7 = (f32[72,512]{1,0:T(8,128)S(1)}, f32[72,512]{1,0:T(8,128)S(1)}, u32[]{:S(2)}, u32[]{:S(2)}) collective-permute-start(f32[72,512]{1,0:T(8,128)S(1)} %get-tuple-element.33), channel_id=1, source_target_pairs={{0,64},{16,208},{32,96},{48,240},{64,128},{80,16},{96,160},{112,48... | collective-permute-start | bytes 442376 | tf_op jit(solution)/shard_map/ppermute | solution.py:500
  65.0 5.8 %collective-permute-start.8 = (f32[136,512]{1,0:T(8,128)S(1)}, f32[136,512]{1,0:T(8,128)S(1)}, u32[]{:S(2)}, u32[]{:S(2)}) collective-permute-start(f32[136,512]{1,0:T(8,128)S(1)} %relayed_text_terms.2), channel_id=1, source_target_pairs={{0,32},{16,240},{32,64},{48,16},{64,96},{80,48},{96,128},{112,80},... | collective-permute-start | bytes 835592 | tf_op jit(solution)/shard_map/ppermute | solution.py:500
  70.8 6.4 %collective-permute-start.9 = (f32[136,512]{1,0:T(8,128)S(1)}, f32[136,512]{1,0:T(8,128)S(1)}, u32[]{:S(2)}, u32[]{:S(2)}) collective-permute-start(f32[136,512]{1,0:T(8,128)S(1)} %relayed_text_terms.3), channel_id=1, source_target_pairs={{0,32},{16,240},{32,64},{48,16},{64,96},{80,48},{96,128},{112,80},... | collective-permute-start | bytes 835592 | tf_op jit(solution)/shard_map/ppermute | solution.py:500
  77.2 6.5 %collective-permute-start.10 = (f32[136,512]{1,0:T(8,128)S(1)}, f32[136,512]{1,0:T(8,128)S(1)}, u32[]{:S(2)}, u32[]{:S(2)}) collective-permute-start(f32[136,512]{1,0:T(8,128)S(1)} %collective-permute-done.9.flow), channel_id=1, source_target_pairs={{0,16},{16,0},{1,17},{17,1},{2,18},{18,2},{3,19},{19,3},{4,20},{20... | collective-permute-start | bytes 835592 | tf_op jit(solution)/shard_map/ppermute | solution.py:506

commit v9 on v8

--- a/solution.py
+++ b/solution.py
@@ -208,6 +208,10 @@
     row_parts = refs[:2]
     col_stats, t_far, s_far, st_far, si_far, img_out, theirs_out, mine = refs[2:10]
     row_norms, col_norms, t, s, st, si, delta, img_block, theirs, grads, sems = refs[10:]
+    loads = [
+        pltpu.make_async_copy(src, dst, sems.at[k])
+        for k, (src, dst) in enumerate(((st_far, st), (si_far, si)))
+    ]
     tall = 256
     arrivals = []
     for n in range(t.shape[0] // tall):
@@ -218,12 +222,9 @@
         ])
         for copy in arrivals[-1]:
             copy.start()
-    loads = [
-        pltpu.make_async_copy(src, dst, sems.at[k])
-        for k, (src, dst) in enumerate(((st_far, st), (si_far, si)))
-    ]
-    for load in loads:
-        load.start()
+        if n == 0:
+            loads[0].start()
+    loads[1].start()
     rows, cols = t.shape
     thin = st.shape[1]
     row_teach, row_learn, row_mean = joined([part[...] for part in row_parts])
@@ -255,22 +256,20 @@
             delta[down, across] = value.astype(jnp.bfloat16)
         return carry
 
+    pieces, lines, _ = img_block.shape
+    own = rows // pieces
+    some = tall // own
+    for k in range(pieces):
+        img_block[k, lines - NOTE :, :] = jnp.full((NOTE, LANES), col_total, F32)
+    saves = []
     for n, copies in enumerate(arrivals):
         for copy in copies:
             copy.wait()
         lax.fori_loop(n * tall // 16, (n + 1) * tall // 16, strip, 0, unroll=2)
-    for load in loads:
-        load.wait()
-
-    pieces, lines, _ = img_block.shape
-    own = rows // pieces
-    some = 4
-    for k in range(pieces):
-        img_block[k, lines - NOTE :, :] = jnp.full((NOTE, LANES), col_total, F32)
-    saves = []
-    for n in range(pieces // some):
+        if n == 0:
+            loads[0].wait()
         grad = scale * jnp.dot(
-            delta[n * some * own : (n + 1) * some * own, :], st[...], preferred_element_type=F32
+            delta[n * tall : (n + 1) * tall, :], st[...], preferred_element_type=F32
         )
         for k in range(some):
             for b in range(thin // LANES):
@@ -282,6 +281,7 @@
         )
         save.start()
         saves.append(save)
+    loads[1].wait()
 
     place, core = lax.axis_index("img_0"), lax.axis_index("img_1")
     chips = lax.axis_size("img_0")
@@ -358,26 +358,33 @@
     )
 
 
-def add_kernel(mine, theirs, *outs):
-    top = 0
-    for out in outs:
-        down = slice(top, top + out.shape[0])
-        out[...] = mine[down, :] + theirs[down, :]
-        top += out.shape[0]
-
-
-def added(mine, theirs, chips):
+def add_kernel(tops, mine, theirs, *refs):
+    outs, near, sems = refs[: len(tops)], refs[len(tops) : -1], refs[-1]
+    copies = []
+    for k, (top, out) in enumerate(zip(tops, outs)):
+        down = pl.ds(top, out.shape[0])
+        copies.append(pltpu.make_async_copy(theirs.at[down, :], near[k], sems.at[k]))
+        copies[-1].start()
+    for k, (top, out) in enumerate(zip(tops, outs)):
+        copies[k].wait()
+        out[...] = mine[top : top + out.shape[0], :] + near[k][...]
+
+
+def added(slots, mine, theirs, chips):
     thin = mine.shape[1]
     sizes = flow_rows(2 * (mine.shape[0] - 5 * NOTE) // chips)
-    return pl.pallas_call(
-        add_kernel,
+    tops = [sum(sizes[:k]) for k in slots]
+    return pl.pallas_call(
+        functools.partial(add_kernel, tops),
         name="both_cores_text_terms",
-        out_shape=[jax.ShapeDtypeStruct((size, thin), F32) for size in sizes],
-        in_specs=[WHOLE] * 2,
-        out_specs=[WHOLE] * len(sizes),
+        out_shape=[jax.ShapeDtypeStruct((sizes[k], thin), F32) for k in slots],
+        in_specs=[WHOLE, FAR],
+        out_specs=[WHOLE] * len(slots),
+        scratch_shapes=[pltpu.VMEM((sizes[k], thin), F32) for k in slots]
+        + [pltpu.SemaphoreType.DMA((len(slots),))],
         compiler_params=pltpu.CompilerParams(vmem_limit_bytes=8 * MIB),
-        cost_estimate=cost(mine.size, 12 * mine.size),
-    )(mine, theirs)
+        cost_estimate=cost(mine.size, 6 * mine.size),
+    )(mine, pltpu.with_memory_space_constraint(theirs, pltpu.HBM))
 
 
 def relay_kernel(near, full, *refs):
@@ -490,7 +497,8 @@
     )
     got_img = lax.all_to_all(to_img, TXT, 0, 0, tiled=True)
     theirs = lax.ppermute(theirs, "img_1", swap)
-    two, three, one, four, own = added(mine, theirs, chips)
+    three, four = added((1, 3), mine, theirs, chips)
+    two, one, own = added((0, 2, 4), mine, theirs, chips)
 
     def outward(value, step):
         pairs = [

time: 85.4 us -> 85.9 us (level)
  Pallas kernels: 21.4 us -> 22.9 us
  waiting for transfers between devices: 21.9 us -> 20.8 us
    ppermute x4, waiting for transfers between devices: 14.3 us -> 13.1 us  [outward(): return lax.ppermute(value, IMG, pairs)]
    pallas_call x1 -> x2, Pallas kernels: 1.37 us -> 2.15 us  [added(): pl.pallas_call(functools.partial(add_kernel, tops), name='both_cores_text...]
where the time goes in v9:
time: 85.9 us; the launch traced here: 85.6 us
  starting transfers between devices  41.1 us (48%)
  Pallas kernels  22.9 us (27%)
  waiting for transfers between devices  20.8 us (24%)
  between operations  0.86 us (1%)
    ppermute x4, waiting for transfers between devices, outward(): return lax.ppermute(value, IMG, pairs)  13.1 us
    pallas_call x1, Pallas kernels, local_stats(): pl.pallas_call(kernel, name='logits_and_statistics', out_shape=(pltpu.HBM...  10.1 us
    pallas_call x1, Pallas kernels, gradients(): pl.pallas_call(functools.partial(delta_kernel, 3.0 / math.sqrt(thin)), na...  8.47 us
    ppermute x4, starting transfers between devices, outward(): return lax.ppermute(value, IMG, pairs)  8.35 us
    ppermute x4, starting transfers between devices, neighbour(): return lax.ppermute(value, axis, pairs)  6.69 us
    all_to_all x1, starting transfers between devices, body(): col = lax.all_to_all(col, 'img_0', 0, 0, tiled=True)  6.45 us
    all_to_all x1, starting transfers between devices, body(): got_img = lax.all_to_all(to_img, TXT, 0, 0, tiled=True)  6.3 us
    ppermute x4, waiting for transfers between devices, neighbour(): return lax.ppermute(value, axis, pairs)  5.63 us
  transfers between devices with their start and end apart: 13, of which 9 were waited for; matrix products, arithmetic and copies ran while one was open for 0% of the time, Pallas kernels for 3%

profile of v9, /device:TPU:1, one launch (start us, length us, event | category | flops | bytes accessed | tf_op | source)
XLA Modules:
  0.0 85.6 jit_solution(12143281470904878044)
XLA Ops:
  0.6 10.1 %logits_and_statistics.1 = (f32[1024,1024]{1,0:T(8,128)}, f32[1024,1024]{1,0:T(8,128)}, f32[1,24,128]{2,1,0:T(8,128)S(1)}, f32[1,24,128]{2,1,0:T(8,128)S(1)}) custom-call(bf16[1024,1280]{1,0:T(8,128)(2,1)} %ti_hbm.1, bf16[1024,1280]{1,0:T(8,128)(2,1)} %tt_hbm.1, bf16[1024,512]{1,0:T(8,128)(2,1)} %refs_6_.1, bf16[1024,512]{1,0:T(8,128)(2,1)} %refs_5_.1), custom_call_target="tpu_custom_call" | custom-call | flops 3758096384 | bytes 8388608 | tf_op jit(solution)/shard_map/logits_and_statistics/pallas_call | solution.py:143
  10.7 3.3 %collective-permute-start.1 = (f32[24,128]{1,0:T(8,128)S(1)}, f32[24,128]{1,0:T(8,128)S(1)}, u32[]{:S(2)}, u32[]{:S(2)}) collective-permute-start(f32[24,128]{1,0:T(8,128)S(1)} %bitcast.12), channel_id=1, source_target_pairs={{0,16},{16,0},{1,17},{17,1},{2,18},{18,2},{3,19},{19,3},{4,20},{20... | collective-permute-start | bytes 36872 | tf_op jit(solution)/shard_map/ppermute | solution.py:486
  14.0 0.0 collective-permute-start
  14.0 0.8 collective-permute-done.1.refs_3_
  14.9 1.7 %collective-permute-done.refs_1_ = f32[24,128]{1,0:T(8,128)S(1)} collective-permute-done((f32[24,128]{1,0:T(8,128)S(1)}, f32[24,128]{1,0:T(8,128)S(1)}, u32[]{:S(2)}, u32[]{:S(2)}) %collective-permute-start) | collective-permute-done | bytes 12320 | tf_op jit(solution)/shard_map/ppermute | solution.py:481
  16.6 0.7 joined_statistics.3
  17.3 6.5 %all-to-all-start = ((f32[8,24,128]{2,1,0:T(8,128)}), f32[8,24,128]{2,1,0:T(8,128)S(1)}, u32[]{:S(2)}, u32[]{:S(2)}) async-start(f32[8,24,128]{2,1,0:T(8,128)} %get-tuple-element.24), calls=%async_computation | async-start | bytes 196608 | tf_op jit(solution)/shard_map/all_to_all | solution.py:488
  23.7 2.5 %collective-permute-start.2 = (f32[24,128]{1,0:T(8,128)S(1)}, f32[24,128]{1,0:T(8,128)S(1)}, u32[]{:S(2)}, u32[]{:S(2)}) collective-permute-start(f32[24,128]{1,0:T(8,128)S(1)} %bitcast.14), channel_id=1, source_target_pairs={{0,12},{4,8},{8,4},{12,0},{1,13},{5,9},{9,5},{13,1},{2,14},{6,10},... | collective-permute-start | bytes 36872 | tf_op jit(solution)/shard_map/ppermute | solution.py:481
  26.2 1.3 %collective-permute-done.2.refs_1_ = f32[24,128]{1,0:T(8,128)S(1)} collective-permute-done((f32[24,128]{1,0:T(8,128)S(1)}, f32[24,128]{1,0:T(8,128)S(1)}, u32[]{:S(2)}, u32[]{:S(2)}) %collective-permute-start.2) | collective-permute-done | bytes 12320 | tf_op jit(solution)/shard_map/ppermute | solution.py:481
  27.5 1.4 %collective-permute-start.3 = (f32[24,128]{1,0:T(8,128)S(1)}, f32[24,128]{1,0:T(8,128)S(1)}, u32[]{:S(2)}, u32[]{:S(2)}) collective-permute-start(f32[24,128]{1,0:T(8,128)S(1)} %bitcast.8), channel_id=1, source_target_pairs={{0,1},{1,0},{2,3},{3,2},{4,5},{5,4},{6,7},{7,6},{8,9},{9,8},{10,11... | collective-permute-start | bytes 36872 | tf_op jit(solution)/shard_map/ppermute | solution.py:481
  28.9 1.5 %collective-permute-done.3.refs_1_ = f32[24,128]{1,0:T(8,128)S(1)} collective-permute-done((f32[24,128]{1,0:T(8,128)S(1)}, f32[24,128]{1,0:T(8,128)S(1)}, u32[]{:S(2)}, u32[]{:S(2)}) %collective-permute-start.3) | collective-permute-done | bytes 12320 | tf_op jit(solution)/shard_map/ppermute | solution.py:481
  30.4 2.8 %collective-permute-start.4 = (f32[24,128]{1,0:T(8,128)S(1)}, f32[24,128]{1,0:T(8,128)S(1)}, u32[]{:S(2)}, u32[]{:S(2)}) collective-permute-start(f32[24,128]{1,0:T(8,128)S(1)} %bitcast.6), channel_id=1, source_target_pairs={{0,3},{1,2},{2,1},{3,0},{4,7},{5,6},{6,5},{7,4},{8,11},{9,10},{10,... | collective-permute-start | bytes 36872 | tf_op jit(solution)/shard_map/ppermute | solution.py:481
  33.3 1.1 %collective-permute-done.4.refs_1_ = f32[24,128]{1,0:T(8,128)S(1)} collective-permute-done((f32[24,128]{1,0:T(8,128)S(1)}, f32[24,128]{1,0:T(8,128)S(1)}, u32[]{:S(2)}, u32[]{:S(2)}) %collective-permute-start.4) | collective-permute-done | bytes 12320 | tf_op jit(solution)/shard_map/ppermute | solution.py:481
  34.3 0.0 all-to-all-done.refs_2_
  34.3 8.5 %delta_and_gradients.1 = (f32[16,264,128]{2,1,0:T(8,128)}, f32[552,512]{1,0:T(8,128)}, f32[552,512]{1,0:T(8,128)S(1)}) custom-call(f32[24,128]{1,0:T(8,128)S(1)} %bitcast.7, f32[24,128]{1,0:T(8,128)S(1)} %collective-permute-done.4.refs_1_, f32[8,24,128]{2,1,0:T(8,128)S(1)} %all-to-all-done.refs_2_, f32[1024,1024]{1,0:T(8,128)} %get-tuple-element.25.refs_3_, ...), custom_call_target="tpu_custom_call" | custom-call | flops 2147483648 | bytes 8388608 | tf_op jit(solution)/shard_map/delta_and_gradients/pallas_call | solution.py:335
  42.8 4.7 %collective-permute-start.5 = (f32[552,512]{1,0:T(8,128)}, f32[552,512]{1,0:T(8,128)}, u32[]{:S(2)}, u32[]{:S(2)}) collective-permute-start(f32[552,512]{1,0:T(8,128)} %get-tuple-element.29), channel_id=1, source_target_pairs={{0,16},{16,0},{1,17},{17,1},{2,18},{18,2},{3,19},{19,3},{4,20},{20... | collective-permute-start | bytes 3391496 | tf_op jit(solution)/shard_map/ppermute | solution.py:499
  47.5 6.3 %all-to-all-start.1 = ((f32[16,264,128]{2,1,0:T(8,128)}), f32[16,264,128]{2,1,0:T(8,128)S(1)}, u32[]{:S(2)}, u32[]{:S(2)}) async-start(f32[16,264,128]{2,1,0:T(8,128)} %get-tuple-element.27), calls=%async_computation.1 | async-start | bytes 4325376 | tf_op jit(solution)/shard_map/all_to_all | solution.py:498
  53.8 0.0 collective-permute-done.5.theirs
  53.8 1.0 %both_cores_text_terms.3 = (f32[136,512]{1,0:T(8,128)S(1)}, f32[72,512]{1,0:T(8,128)S(1)}) custom-call(f32[552,512]{1,0:T(8,128)S(1)} %get-tuple-element.28.mine, f32[552,512]{1,0:T(8,128)} %collective-permute-done.5.theirs), custom_call_target="tpu_custom_call" | custom-call | flops 282624 | bytes 1695744 | tf_op jit(solution)/shard_map/both_cores_text_terms/pallas_call | solution.py:377
  54.9 3.0 %collective-permute-start.6 = (f32[136,512]{1,0:T(8,128)S(1)}, f32[136,512]{1,0:T(8,128)S(1)}, u32[]{:S(2)}, u32[]{:S(2)}) collective-permute-start(f32[136,512]{1,0:T(8,128)S(1)} %get-tuple-element.32), channel_id=1, source_target_pairs={{0,32},{16,240},{32,64},{48,16},{64,96},{80,48},{96,128},{112,80},... | collective-permute-start | bytes 835592 | tf_op jit(solution)/shard_map/ppermute | solution.py:508
  57.9 2.1 %collective-permute-start.7 = (f32[72,512]{1,0:T(8,128)S(1)}, f32[72,512]{1,0:T(8,128)S(1)}, u32[]{:S(2)}, u32[]{:S(2)}) collective-permute-start(f32[72,512]{1,0:T(8,128)S(1)} %get-tuple-element.33), channel_id=1, source_target_pairs={{0,64},{16,208},{32,96},{48,240},{64,128},{80,16},{96,160},{112,48... | collective-permute-start | bytes 442376 | tf_op jit(solution)/shard_map/ppermute | solution.py:508
  60.0 1.1 %both_cores_text_terms.2 = (f32[136,512]{1,0:T(8,128)S(1)}, f32[136,512]{1,0:T(8,128)S(1)}, f32[72,512]{1,0:T(8,128)S(1)}) custom-call(f32[552,512]{1,0:T(8,128)S(1)} %get-tuple-element.28.mine, f32[552,512]{1,0:T(8,128)} %collective-permute-done.5.theirs), custom_call_target="tpu_custom_call" | custom-call | flops 282624 | bytes 1695744 | tf_op jit(solution)/shard_map/both_cores_text_terms/pallas_call | solution.py:377
  61.1 4.1 %collective-permute-done.7.refs_0_ = f32[72,512]{1,0:T(8,128)S(1)} collective-permute-done((f32[72,512]{1,0:T(8,128)S(1)}, f32[72,512]{1,0:T(8,128)S(1)}, u32[]{:S(2)}, u32[]{:S(2)}) %collective-permute-start.7) | collective-permute-done | bytes 147488 | tf_op jit(solution)/shard_map/ppermute | solution.py:508
  65.3 1.0 %collective-permute-start.8 = (f32[136,512]{1,0:T(8,128)S(1)}, f32[136,512]{1,0:T(8,128)S(1)}, u32[]{:S(2)}, u32[]{:S(2)}) collective-permute-start(f32[136,512]{1,0:T(8,128)S(1)} %relayed_text_terms.2), channel_id=1, source_target_pairs={{0,32},{16,240},{32,64},{48,16},{64,96},{80,48},{96,128},{112,80},... | collective-permute-start | bytes 835592 | tf_op jit(solution)/shard_map/ppermute | solution.py:508
  66.3 4.8 %collective-permute-done.8.full = f32[136,512]{1,0:T(8,128)S(1)} collective-permute-done((f32[136,512]{1,0:T(8,128)S(1)}, f32[136,512]{1,0:T(8,128)S(1)}, u32[]{:S(2)}, u32[]{:S(2)}) %collective-permute-start.8) | collective-permute-done | bytes 278560 | tf_op jit(solution)/shard_map/ppermute | solution.py:508
  71.1 2.2 %collective-permute-start.9 = (f32[136,512]{1,0:T(8,128)S(1)}, f32[136,512]{1,0:T(8,128)S(1)}, u32[]{:S(2)}, u32[]{:S(2)}) collective-permute-start(f32[136,512]{1,0:T(8,128)S(1)} %relayed_text_terms.3), channel_id=1, source_target_pairs={{0,32},{16,240},{32,64},{48,16},{64,96},{80,48},{96,128},{112,80},... | collective-permute-start | bytes 835592 | tf_op jit(solution)/shard_map/ppermute | solution.py:508
  73.3 4.2 %collective-permute-done.9.flow = f32[136,512]{1,0:T(8,128)S(1)} collective-permute-done((f32[136,512]{1,0:T(8,128)S(1)}, f32[136,512]{1,0:T(8,128)S(1)}, u32[]{:S(2)}, u32[]{:S(2)}) %collective-permute-start.9) | collective-permute-done | bytes 278560 | tf_op jit(solution)/shard_map/ppermute | solution.py:508
  77.5 5.3 %collective-permute-start.10 = (f32[136,512]{1,0:T(8,128)S(1)}, f32[136,512]{1,0:T(8,128)S(1)}, u32[]{:S(2)}, u32[]{:S(2)}) collective-permute-start(f32[136,512]{1,0:T(8,128)S(1)} %collective-permute-done.9.flow), channel_id=1, source_target_pairs={{0,16},{16,0},{1,17},{17,1},{2,18},{18,2},{3,19},{19,3},{4,20},{20... | collective-permute-start | bytes 835592 | tf_op jit(solution)/shard_map/ppermute | solution.py:514
  82.8 1.2 %collective-permute-done.10.other = f32[136,512]{1,0:T(8,128)S(1)} collective-permute-done((f32[136,512]{1,0:T(8,128)S(1)}, f32[136,512]{1,0:T(8,128)S(1)}, u32[]{:S(2)}, u32[]{:S(2)}) %collective-permute-start.10) | collective-permute-done | bytes 278560 | tf_op jit(solution)/shard_map/ppermute | solution.py:514
  84.0 0.7 text_gradient_total.1
  84.7 0.0 all-to-all-done.1.parts
  84.7 0.8 sum_of_image_parts_and_loss.1
  (5 shorter events, 0.1 us)
Async XLA Ops:
  10.7 4.2 %collective-permute-start.1 = (f32[24,128]{1,0:T(8,128)S(1)}, f32[24,128]{1,0:T(8,128)S(1)}, u32[]{:S(2)}, u32[]{:S(2)}) collective-permute-start(f32[24,128]{1,0:T(8,128)S(1)} %bitcast.12), channel_id=1, source_target_pairs={{0,16},{16,0},{1,17},{17,1},{2,18},{18,2},{3,19},{19,3},{4,20},{20... | collective-permute-start | bytes 36872 | tf_op jit(solution)/shard_map/ppermute | solution.py:486
  14.0 2.6 %collective-permute-start = (f32[24,128]{1,0:T(8,128)S(1)}, f32[24,128]{1,0:T(8,128)S(1)}, u32[]{:S(2)}, u32[]{:S(2)}) collective-permute-start(f32[24,128]{1,0:T(8,128)S(1)} %bitcast.10), channel_id=1, source_target_pairs={{0,4},{4,0},{8,12},{12,8},{1,5},{5,1},{9,13},{13,9},{2,6},{6,2},{1... | collective-permute-start | bytes 36872 | tf_op jit(solution)/shard_map/ppermute | solution.py:481
  17.3 17.1 %all-to-all-start = ((f32[8,24,128]{2,1,0:T(8,128)}), f32[8,24,128]{2,1,0:T(8,128)S(1)}, u32[]{:S(2)}, u32[]{:S(2)}) async-start(f32[8,24,128]{2,1,0:T(8,128)} %get-tuple-element.24), calls=%async_computation | async-start | bytes 196608 | tf_op jit(solution)/shard_map/all_to_all | solution.py:488
  23.7 3.8 %collective-permute-start.2 = (f32[24,128]{1,0:T(8,128)S(1)}, f32[24,128]{1,0:T(8,128)S(1)}, u32[]{:S(2)}, u32[]{:S(2)}) collective-permute-start(f32[24,128]{1,0:T(8,128)S(1)} %bitcast.14), channel_id=1, source_target_pairs={{0,12},{4,8},{8,4},{12,0},{1,13},{5,9},{9,5},{13,1},{2,14},{6,10},... | collective-permute-start | bytes 36872 | tf_op jit(solution)/shard_map/ppermute | solution.py:481
  27.5 2.9 %collective-permute-start.3 = (f32[24,128]{1,0:T(8,128)S(1)}, f32[24,128]{1,0:T(8,128)S(1)}, u32[]{:S(2)}, u32[]{:S(2)}) collective-permute-start(f32[24,128]{1,0:T(8,128)S(1)} %bitcast.8), channel_id=1, source_target_pairs={{0,1},{1,0},{2,3},{3,2},{4,5},{5,4},{6,7},{7,6},{8,9},{9,8},{10,11... | collective-permute-start | bytes 36872 | tf_op jit(solution)/shard_map/ppermute | solution.py:481
  30.4 3.9 %collective-permute-start.4 = (f32[24,128]{1,0:T(8,128)S(1)}, f32[24,128]{1,0:T(8,128)S(1)}, u32[]{:S(2)}, u32[]{:S(2)}) collective-permute-start(f32[24,128]{1,0:T(8,128)S(1)} %bitcast.6), channel_id=1, source_target_pairs={{0,3},{1,2},{2,1},{3,0},{4,7},{5,6},{6,5},{7,4},{8,11},{9,10},{10,... | collective-permute-start | bytes 36872 | tf_op jit(solution)/shard_map/ppermute | solution.py:481
  42.8 11.0 %collective-permute-start.5 = (f32[552,512]{1,0:T(8,128)}, f32[552,512]{1,0:T(8,128)}, u32[]{:S(2)}, u32[]{:S(2)}) collective-permute-start(f32[552,512]{1,0:T(8,128)} %get-tuple-element.29), channel_id=1, source_target_pairs={{0,16},{16,0},{1,17},{17,1},{2,18},{18,2},{3,19},{19,3},{4,20},{20... | collective-permute-start | bytes 3391496 | tf_op jit(solution)/shard_map/ppermute | solution.py:499
  47.5 37.2 %all-to-all-start.1 = ((f32[16,264,128]{2,1,0:T(8,128)}), f32[16,264,128]{2,1,0:T(8,128)S(1)}, u32[]{:S(2)}, u32[]{:S(2)}) async-start(f32[16,264,128]{2,1,0:T(8,128)} %get-tuple-element.27), calls=%async_computation.1 | async-start | bytes 4325376 | tf_op jit(solution)/shard_map/all_to_all | solution.py:498
  54.9 10.4 %collective-permute-start.6 = (f32[136,512]{1,0:T(8,128)S(1)}, f32[136,512]{1,0:T(8,128)S(1)}, u32[]{:S(2)}, u32[]{:S(2)}) collective-permute-start(f32[136,512]{1,0:T(8,128)S(1)} %get-tuple-element.32), channel_id=1, source_target_pairs={{0,32},{16,240},{32,64},{48,16},{64,96},{80,48},{96,128},{112,80},... | collective-permute-start | bytes 835592 | tf_op jit(solution)/shard_map/ppermute | solution.py:508
  57.9 7.4 %collective-permute-start.7 = (f32[72,512]{1,0:T(8,128)S(1)}, f32[72,512]{1,0:T(8,128)S(1)}, u32[]{:S(2)}, u32[]{:S(2)}) collective-permute-start(f32[72,512]{1,0:T(8,128)S(1)} %get-tuple-element.33), channel_id=1, source_target_pairs={{0,64},{16,208},{32,96},{48,240},{64,128},{80,16},{96,160},{112,48... | collective-permute-start | bytes 442376 | tf_op jit(solution)/shard_map/ppermute | solution.py:508
  65.3 5.8 %collective-permute-start.8 = (f32[136,512]{1,0:T(8,128)S(1)}, f32[136,512]{1,0:T(8,128)S(1)}, u32[]{:S(2)}, u32[]{:S(2)}) collective-permute-start(f32[136,512]{1,0:T(8,128)S(1)} %relayed_text_terms.2), channel_id=1, source_target_pairs={{0,32},{16,240},{32,64},{48,16},{64,96},{80,48},{96,128},{112,80},... | collective-permute-start | bytes 835592 | tf_op jit(solution)/shard_map/ppermute | solution.py:508
  71.1 6.4 %collective-permute-start.9 = (f32[136,512]{1,0:T(8,128)S(1)}, f32[136,512]{1,0:T(8,128)S(1)}, u32[]{:S(2)}, u32[]{:S(2)}) collective-permute-start(f32[136,512]{1,0:T(8,128)S(1)} %relayed_text_terms.3), channel_id=1, source_target_pairs={{0,32},{16,240},{32,64},{48,16},{64,96},{80,48},{96,128},{112,80},... | collective-permute-start | bytes 835592 | tf_op jit(solution)/shard_map/ppermute | solution.py:508
  77.5 6.5 %collective-permute-start.10 = (f32[136,512]{1,0:T(8,128)S(1)}, f32[136,512]{1,0:T(8,128)S(1)}, u32[]{:S(2)}, u32[]{:S(2)}) collective-permute-start(f32[136,512]{1,0:T(8,128)S(1)} %collective-permute-done.9.flow), channel_id=1, source_target_pairs={{0,16},{16,0},{1,17},{17,1},{2,18},{18,2},{3,19},{19,3},{4,20},{20... | collective-permute-start | bytes 835592 | tf_op jit(solution)/shard_map/ppermute | solution.py:514

commit v10 on v8

--- a/solution.py
+++ b/solution.py
@@ -404,15 +404,15 @@
     )(*parts)
 
 
-def finish_kernel(flow, other, own, out, note):
+def finish_kernel(one, two, own, out, note):
     half = out.shape[0]
-    down = pl.ds(pl.multiple_of(lax.axis_index("img_1") * half, half), half)
-    out[...] = flow[down, :] + other[down, :] + own[:half, :]
-    note[...] = flow[2 * half :, :LANES] + other[2 * half :, :LANES] + own[half:, :LANES]
-
-
-def finished(flow, other, own):
-    thin = flow.shape[1]
+    total = one[...] + two[...] + own[...]
+    out[...] = total[:half, :]
+    note[...] = total[half:, :LANES]
+
+
+def finished(one, two, own):
+    thin = own.shape[1]
     return pl.pallas_call(
         finish_kernel,
         name="text_gradient_total",
@@ -424,7 +424,30 @@
         out_specs=(WHOLE, WHOLE),
         compiler_params=pltpu.CompilerParams(vmem_limit_bytes=4 * MIB),
         cost_estimate=cost(own.size * 3, 16 * own.size),
-    )(flow, other, own)
+    )(one, two, own)
+
+
+def part_kernel(near, full, same, cross):
+    half = same.shape[0] - NOTE
+    core = lax.axis_index("img_1")
+    note = slice(2 * half, 2 * half + NOTE)
+    for out, which in ((same, core), (cross, 1 - core)):
+        down = pl.ds(pl.multiple_of(which * half, half), half)
+        out[:half, :] = near[down, :] + full[down, :]
+        out[half:, :] = near[note, :] + full[note, :]
+
+
+def parted(near, full):
+    part = jax.ShapeDtypeStruct(((near.shape[0] + NOTE) // 2, near.shape[1]), F32)
+    return pl.pallas_call(
+        part_kernel,
+        name="parted_text_terms",
+        out_shape=(part, part),
+        in_specs=[WHOLE] * 2,
+        out_specs=(WHOLE, WHOLE),
+        compiler_params=pltpu.CompilerParams(vmem_limit_bytes=4 * MIB),
+        cost_estimate=cost(near.size, 12 * near.size),
+    )(near, full)
 
 
 def sum_kernel(row_share, col_share, parts, row_note, out, loss):
@@ -492,19 +515,17 @@
     theirs = lax.ppermute(theirs, "img_1", swap)
     two, three, one, four, own = added(mine, theirs, chips)
 
-    def outward(value, step):
+    def outward(value, step, cross=0):
         pairs = [
-            (cores * z + c, cores * ((z + step * (1 - 2 * c)) % chips) + c)
+            (cores * z + c, cores * ((z + step * (1 - 2 * c)) % chips) + (c + cross) % cores)
             for z in range(chips) for c in range(cores)
         ]
         return lax.ppermute(value, IMG, pairs)
 
     four = outward(four, 2)
     flow = relayed(two, outward(three, 1), four)
-    flow = relayed(one, outward(flow, 1))
-    flow = outward(flow, 1)
-    across = lax.ppermute(flow, "img_1", swap)
-    grad_txt, row_total = finished(flow, across, own)
+    same, cross = parted(one, outward(flow, 1))
+    grad_txt, row_total = finished(outward(same, 1), outward(cross, 1, 1), own)
     grad_img, loss = summed(
         1.0 / (rows * img_count), 1.0 / (cols * txt_count), got_img, row_total, thin
     )

time: 85.4 us -> 85.3 us (level)
  Pallas kernels: 21.4 us -> 20.2 us
  waiting for transfers between devices: 21.9 us -> 23 us
    ppermute x1 -> x0, starting transfers between devices: 5.27 us -> none  [body(): across = lax.ppermute(flow, 'img_1', swap)]
    ppermute x4 -> x5, starting transfers between devices: 8.33 us -> 13.5 us  [outward(): return lax.ppermute(value, IMG, pairs)]
    ppermute x1, waiting for transfers between devices: 0.01 us -> 2.61 us  [body(): theirs = lax.ppermute(theirs, 'img_1', swap)]
    pallas_call x1, Pallas kernels: 1.37 us -> 0.12 us  [added(): pl.pallas_call(add_kernel, name='both_cores_text_terms', out_shape=[jax.S...]
    ppermute x1 -> x0, waiting for transfers between devices: 1.19 us -> none  [body(): across = lax.ppermute(flow, 'img_1', swap)]
    ppermute x4 -> x5, waiting for transfers between devices: 14.3 us -> 13.9 us  [outward(): return lax.ppermute(value, IMG, pairs)]
  transfers between devices with their start and end apart: 13 -> 13, of which waited for: 9 -> 9; matrix products, arithmetic and copies ran while one was open for 0% -> 0% of each run, Pallas kernels for 3% -> 1%
where the time goes in v10:
time: 85.3 us; the launch traced here: 85.1 us
  starting transfers between devices  41.2 us (48%)
  waiting for transfers between devices  23 us (27%)
  Pallas kernels  20.2 us (24%)
    ppermute x5, waiting for transfers between devices, outward(): return lax.ppermute(value, IMG, pairs)  13.9 us
    ppermute x5, starting transfers between devices, outward(): return lax.ppermute(value, IMG, pairs)  13.5 us
    pallas_call x1, Pallas kernels, local_stats(): pl.pallas_call(kernel, name='logits_and_statistics', out_shape=(pltpu.HBM...  10.1 us
    pallas_call x1, Pallas kernels, gradients(): pl.pallas_call(functools.partial(delta_kernel, 3.0 / math.sqrt(thin)), na...  7.8 us
    ppermute x4, starting transfers between devices, neighbour(): return lax.ppermute(value, axis, pairs)  6.67 us
    all_to_all x1, starting transfers between devices, body(): col = lax.all_to_all(col, 'img_0', 0, 0, tiled=True)  6.46 us
    all_to_all x1, starting transfers between devices, body(): got_img = lax.all_to_all(to_img, TXT, 0, 0, tiled=True)  6.26 us
    ppermute x4, waiting for transfers between devices, neighbour(): return lax.ppermute(value, axis, pairs)  5.65 us
  transfers between devices with their start and end apart: 13, of which 9 were waited for; matrix products, arithmetic and copies ran while one was open for 0% of the time, Pallas kernels for 1%

profile of v10, /device:TPU:1, one launch (start us, length us, event | category | flops | bytes accessed | tf_op | source)
XLA Modules:
  0.0 85.1 jit_solution(12298349613891714160)
XLA Ops:
  0.6 10.1 %logits_and_statistics.1 = (f32[1024,1024]{1,0:T(8,128)}, f32[1024,1024]{1,0:T(8,128)}, f32[1,24,128]{2,1,0:T(8,128)S(1)}, f32[1,24,128]{2,1,0:T(8,128)S(1)}) custom-call(bf16[1024,1280]{1,0:T(8,128)(2,1)} %ti_hbm.1, bf16[1024,1280]{1,0:T(8,128)(2,1)} %tt_hbm.1, bf16[1024,512]{1,0:T(8,128)(2,1)} %refs_6_.1, bf16[1024,512]{1,0:T(8,128)(2,1)} %refs_5_.1), custom_call_target="tpu_custom_call" | custom-call | flops 3758096384 | bytes 8388608 | tf_op jit(solution)/shard_map/logits_and_statistics/pallas_call | solution.py:143
  10.7 3.3 %collective-permute-start.1 = (f32[24,128]{1,0:T(8,128)S(1)}, f32[24,128]{1,0:T(8,128)S(1)}, u32[]{:S(2)}, u32[]{:S(2)}) collective-permute-start(f32[24,128]{1,0:T(8,128)S(1)} %bitcast.12), channel_id=1, source_target_pairs={{0,16},{16,0},{1,17},{17,1},{2,18},{18,2},{3,19},{19,3},{4,20},{20... | collective-permute-start | bytes 36872 | tf_op jit(solution)/shard_map/ppermute | solution.py:502
  14.0 0.0 collective-permute-start
  14.0 0.8 collective-permute-done.1.refs_3_
  14.9 1.7 %collective-permute-done.refs_1_ = f32[24,128]{1,0:T(8,128)S(1)} collective-permute-done((f32[24,128]{1,0:T(8,128)S(1)}, f32[24,128]{1,0:T(8,128)S(1)}, u32[]{:S(2)}, u32[]{:S(2)}) %collective-permute-start) | collective-permute-done | bytes 12320 | tf_op jit(solution)/shard_map/ppermute | solution.py:497
  16.6 0.7 joined_statistics.3
  17.3 6.5 %all-to-all-start = ((f32[8,24,128]{2,1,0:T(8,128)}), f32[8,24,128]{2,1,0:T(8,128)S(1)}, u32[]{:S(2)}, u32[]{:S(2)}) async-start(f32[8,24,128]{2,1,0:T(8,128)} %get-tuple-element.26), calls=%async_computation | async-start | bytes 196608 | tf_op jit(solution)/shard_map/all_to_all | solution.py:504
  23.7 2.5 %collective-permute-start.2 = (f32[24,128]{1,0:T(8,128)S(1)}, f32[24,128]{1,0:T(8,128)S(1)}, u32[]{:S(2)}, u32[]{:S(2)}) collective-permute-start(f32[24,128]{1,0:T(8,128)S(1)} %bitcast.14), channel_id=1, source_target_pairs={{0,12},{4,8},{8,4},{12,0},{1,13},{5,9},{9,5},{13,1},{2,14},{6,10},... | collective-permute-start | bytes 36872 | tf_op jit(solution)/shard_map/ppermute | solution.py:497
  26.2 1.3 %collective-permute-done.2.refs_1_ = f32[24,128]{1,0:T(8,128)S(1)} collective-permute-done((f32[24,128]{1,0:T(8,128)S(1)}, f32[24,128]{1,0:T(8,128)S(1)}, u32[]{:S(2)}, u32[]{:S(2)}) %collective-permute-start.2) | collective-permute-done | bytes 12320 | tf_op jit(solution)/shard_map/ppermute | solution.py:497
  27.5 1.4 %collective-permute-start.3 = (f32[24,128]{1,0:T(8,128)S(1)}, f32[24,128]{1,0:T(8,128)S(1)}, u32[]{:S(2)}, u32[]{:S(2)}) collective-permute-start(f32[24,128]{1,0:T(8,128)S(1)} %bitcast.8), channel_id=1, source_target_pairs={{0,1},{1,0},{2,3},{3,2},{4,5},{5,4},{6,7},{7,6},{8,9},{9,8},{10,11... | collective-permute-start | bytes 36872 | tf_op jit(solution)/shard_map/ppermute | solution.py:497
  28.9 1.5 %collective-permute-done.3.refs_1_ = f32[24,128]{1,0:T(8,128)S(1)} collective-permute-done((f32[24,128]{1,0:T(8,128)S(1)}, f32[24,128]{1,0:T(8,128)S(1)}, u32[]{:S(2)}, u32[]{:S(2)}) %collective-permute-start.3) | collective-permute-done | bytes 12320 | tf_op jit(solution)/shard_map/ppermute | solution.py:497
  30.4 2.8 %collective-permute-start.4 = (f32[24,128]{1,0:T(8,128)S(1)}, f32[24,128]{1,0:T(8,128)S(1)}, u32[]{:S(2)}, u32[]{:S(2)}) collective-permute-start(f32[24,128]{1,0:T(8,128)S(1)} %bitcast.6), channel_id=1, source_target_pairs={{0,3},{1,2},{2,1},{3,0},{4,7},{5,6},{6,5},{7,4},{8,11},{9,10},{10,... | collective-permute-start | bytes 36872 | tf_op jit(solution)/shard_map/ppermute | solution.py:497
  33.2 1.1 %collective-permute-done.4.refs_1_ = f32[24,128]{1,0:T(8,128)S(1)} collective-permute-done((f32[24,128]{1,0:T(8,128)S(1)}, f32[24,128]{1,0:T(8,128)S(1)}, u32[]{:S(2)}, u32[]{:S(2)}) %collective-permute-start.4) | collective-permute-done | bytes 12320 | tf_op jit(solution)/shard_map/ppermute | solution.py:497
  34.3 0.0 all-to-all-done.refs_2_
  34.3 7.8 %delta_and_gradients.1 = (f32[16,264,128]{2,1,0:T(8,128)}, f32[552,512]{1,0:T(8,128)}, f32[552,512]{1,0:T(8,128)S(1)}) custom-call(f32[24,128]{1,0:T(8,128)S(1)} %bitcast.7, f32[24,128]{1,0:T(8,128)S(1)} %collective-permute-done.4.refs_1_, f32[8,24,128]{2,1,0:T(8,128)S(1)} %all-to-all-done.refs_2_, f32[1024,1024]{1,0:T(8,128)} %get-tuple-element.27.refs_3_, ...), custom_call_target="tpu_custom_call" | custom-call | flops 2147483648 | bytes 8388608 | tf_op jit(solution)/shard_map/delta_and_gradients/pallas_call | solution.py:335
  42.1 6.3 %all-to-all-start.1 = ((f32[16,264,128]{2,1,0:T(8,128)}), f32[16,264,128]{2,1,0:T(8,128)S(1)}, u32[]{:S(2)}, u32[]{:S(2)}) async-start(f32[16,264,128]{2,1,0:T(8,128)} %get-tuple-element.29), calls=%async_computation.1 | async-start | bytes 4325376 | tf_op jit(solution)/shard_map/all_to_all | solution.py:514
  48.4 5.0 %collective-permute-start.5 = (f32[552,512]{1,0:T(8,128)}, f32[552,512]{1,0:T(8,128)S(1)}, u32[]{:S(2)}, u32[]{:S(2)}) collective-permute-start(f32[552,512]{1,0:T(8,128)} %get-tuple-element.31), channel_id=1, source_target_pairs={{0,16},{16,0},{1,17},{17,1},{2,18},{18,2},{3,19},{19,3},{4,20},{20... | collective-permute-start | bytes 3391496 | tf_op jit(solution)/shard_map/ppermute | solution.py:515
  53.4 2.6 %collective-permute-done.5.theirs = f32[552,512]{1,0:T(8,128)S(1)} collective-permute-done((f32[552,512]{1,0:T(8,128)}, f32[552,512]{1,0:T(8,128)S(1)}, u32[]{:S(2)}, u32[]{:S(2)}) %collective-permute-start.5) | collective-permute-done | bytes 1130528 | tf_op jit(solution)/shard_map/ppermute | solution.py:515
  56.1 0.1 both_cores_text_terms.1
  56.2 3.0 %collective-permute-start.6 = (f32[136,512]{1,0:T(8,128)S(1)}, f32[136,512]{1,0:T(8,128)S(1)}, u32[]{:S(2)}, u32[]{:S(2)}) collective-permute-start(f32[136,512]{1,0:T(8,128)S(1)} %get-tuple-element.34), channel_id=1, source_target_pairs={{0,32},{16,240},{32,64},{48,16},{64,96},{80,48},{96,128},{112,80},... | collective-permute-start | bytes 835592 | tf_op jit(solution)/shard_map/ppermute | solution.py:523
  59.2 2.1 %collective-permute-start.7 = (f32[72,512]{1,0:T(8,128)S(1)}, f32[72,512]{1,0:T(8,128)S(1)}, u32[]{:S(2)}, u32[]{:S(2)}) collective-permute-start(f32[72,512]{1,0:T(8,128)S(1)} %get-tuple-element.35), channel_id=1, source_target_pairs={{0,64},{16,208},{32,96},{48,240},{64,128},{80,16},{96,160},{112,48... | collective-permute-start | bytes 442376 | tf_op jit(solution)/shard_map/ppermute | solution.py:523
  61.3 5.3 %collective-permute-done.7.refs_0_ = f32[72,512]{1,0:T(8,128)S(1)} collective-permute-done((f32[72,512]{1,0:T(8,128)S(1)}, f32[72,512]{1,0:T(8,128)S(1)}, u32[]{:S(2)}, u32[]{:S(2)}) %collective-permute-start.7) | collective-permute-done | bytes 147488 | tf_op jit(solution)/shard_map/ppermute | solution.py:523
  66.6 0.0 collective-permute-done.6.full
  66.6 1.3 %collective-permute-start.8 = (f32[136,512]{1,0:T(8,128)S(1)}, f32[136,512]{1,0:T(8,128)S(1)}, u32[]{:S(2)}, u32[]{:S(2)}) collective-permute-start(f32[136,512]{1,0:T(8,128)S(1)} %relayed_text_terms.1), channel_id=1, source_target_pairs={{0,32},{16,240},{32,64},{48,16},{64,96},{80,48},{96,128},{112,80},... | collective-permute-start | bytes 835592 | tf_op jit(solution)/shard_map/ppermute | solution.py:523
  67.9 4.2 %collective-permute-done.8.full = f32[136,512]{1,0:T(8,128)S(1)} collective-permute-done((f32[136,512]{1,0:T(8,128)S(1)}, f32[136,512]{1,0:T(8,128)S(1)}, u32[]{:S(2)}, u32[]{:S(2)}) %collective-permute-start.8) | collective-permute-done | bytes 278560 | tf_op jit(solution)/shard_map/ppermute | solution.py:523
  72.2 2.7 %collective-permute-start.9 = (f32[72,512]{1,0:T(8,128)S(1)}, f32[72,512]{1,0:T(8,128)S(1)}, u32[]{:S(2)}, u32[]{:S(2)}) collective-permute-start(f32[72,512]{1,0:T(8,128)S(1)} %get-tuple-element.36), channel_id=1, source_target_pairs={{0,32},{16,240},{32,64},{48,16},{64,96},{80,48},{96,128},{112,80},... | collective-permute-start | bytes 442376 | tf_op jit(solution)/shard_map/ppermute | solution.py:523
  74.9 4.3 %collective-permute-start.10 = (f32[72,512]{1,0:T(8,128)S(1)}, f32[72,512]{1,0:T(8,128)S(1)}, u32[]{:S(2)}, u32[]{:S(2)}) collective-permute-start(f32[72,512]{1,0:T(8,128)S(1)} %get-tuple-element.37), channel_id=1, source_target_pairs={{0,48},{16,224},{32,80},{48,0},{64,112},{80,32},{96,144},{112,64},... | collective-permute-start | bytes 442376 | tf_op jit(solution)/shard_map/ppermute | solution.py:523
  79.3 0.0 collective-permute-done.9.one
  79.3 4.4 %collective-permute-done.10.two = f32[72,512]{1,0:T(8,128)S(1)} collective-permute-done((f32[72,512]{1,0:T(8,128)S(1)}, f32[72,512]{1,0:T(8,128)S(1)}, u32[]{:S(2)}, u32[]{:S(2)}) %collective-permute-start.10) | collective-permute-done | bytes 147488 | tf_op jit(solution)/shard_map/ppermute | solution.py:523
  83.7 0.7 text_gradient_total.1
  84.3 0.0 all-to-all-done.1.parts
  84.4 0.8 sum_of_image_parts_and_loss.1
  (4 shorter events, 0.1 us)
Async XLA Ops:
  10.7 4.2 %collective-permute-start.1 = (f32[24,128]{1,0:T(8,128)S(1)}, f32[24,128]{1,0:T(8,128)S(1)}, u32[]{:S(2)}, u32[]{:S(2)}) collective-permute-start(f32[24,128]{1,0:T(8,128)S(1)} %bitcast.12), channel_id=1, source_target_pairs={{0,16},{16,0},{1,17},{17,1},{2,18},{18,2},{3,19},{19,3},{4,20},{20... | collective-permute-start | bytes 36872 | tf_op jit(solution)/shard_map/ppermute | solution.py:502
  14.0 2.6 %collective-permute-start = (f32[24,128]{1,0:T(8,128)S(1)}, f32[24,128]{1,0:T(8,128)S(1)}, u32[]{:S(2)}, u32[]{:S(2)}) collective-permute-start(f32[24,128]{1,0:T(8,128)S(1)} %bitcast.10), channel_id=1, source_target_pairs={{0,4},{4,0},{8,12},{12,8},{1,5},{5,1},{9,13},{13,9},{2,6},{6,2},{1... | collective-permute-start | bytes 36872 | tf_op jit(solution)/shard_map/ppermute | solution.py:497
  17.3 17.1 %all-to-all-start = ((f32[8,24,128]{2,1,0:T(8,128)}), f32[8,24,128]{2,1,0:T(8,128)S(1)}, u32[]{:S(2)}, u32[]{:S(2)}) async-start(f32[8,24,128]{2,1,0:T(8,128)} %get-tuple-element.26), calls=%async_computation | async-start | bytes 196608 | tf_op jit(solution)/shard_map/all_to_all | solution.py:504
  23.7 3.8 %collective-permute-start.2 = (f32[24,128]{1,0:T(8,128)S(1)}, f32[24,128]{1,0:T(8,128)S(1)}, u32[]{:S(2)}, u32[]{:S(2)}) collective-permute-start(f32[24,128]{1,0:T(8,128)S(1)} %bitcast.14), channel_id=1, source_target_pairs={{0,12},{4,8},{8,4},{12,0},{1,13},{5,9},{9,5},{13,1},{2,14},{6,10},... | collective-permute-start | bytes 36872 | tf_op jit(solution)/shard_map/ppermute | solution.py:497
  27.5 2.9 %collective-permute-start.3 = (f32[24,128]{1,0:T(8,128)S(1)}, f32[24,128]{1,0:T(8,128)S(1)}, u32[]{:S(2)}, u32[]{:S(2)}) collective-permute-start(f32[24,128]{1,0:T(8,128)S(1)} %bitcast.8), channel_id=1, source_target_pairs={{0,1},{1,0},{2,3},{3,2},{4,5},{5,4},{6,7},{7,6},{8,9},{9,8},{10,11... | collective-permute-start | bytes 36872 | tf_op jit(solution)/shard_map/ppermute | solution.py:497
  30.4 3.9 %collective-permute-start.4 = (f32[24,128]{1,0:T(8,128)S(1)}, f32[24,128]{1,0:T(8,128)S(1)}, u32[]{:S(2)}, u32[]{:S(2)}) collective-permute-start(f32[24,128]{1,0:T(8,128)S(1)} %bitcast.6), channel_id=1, source_target_pairs={{0,3},{1,2},{2,1},{3,0},{4,7},{5,6},{6,5},{7,4},{8,11},{9,10},{10,... | collective-permute-start | bytes 36872 | tf_op jit(solution)/shard_map/ppermute | solution.py:497
  42.1 42.2 %all-to-all-start.1 = ((f32[16,264,128]{2,1,0:T(8,128)}), f32[16,264,128]{2,1,0:T(8,128)S(1)}, u32[]{:S(2)}, u32[]{:S(2)}) async-start(f32[16,264,128]{2,1,0:T(8,128)} %get-tuple-element.29), calls=%async_computation.1 | async-start | bytes 4325376 | tf_op jit(solution)/shard_map/all_to_all | solution.py:514
  48.4 7.6 %collective-permute-start.5 = (f32[552,512]{1,0:T(8,128)}, f32[552,512]{1,0:T(8,128)S(1)}, u32[]{:S(2)}, u32[]{:S(2)}) collective-permute-start(f32[552,512]{1,0:T(8,128)} %get-tuple-element.31), channel_id=1, source_target_pairs={{0,16},{16,0},{1,17},{17,1},{2,18},{18,2},{3,19},{19,3},{4,20},{20... | collective-permute-start | bytes 3391496 | tf_op jit(solution)/shard_map/ppermute | solution.py:515
  56.2 10.4 %collective-permute-start.6 = (f32[136,512]{1,0:T(8,128)S(1)}, f32[136,512]{1,0:T(8,128)S(1)}, u32[]{:S(2)}, u32[]{:S(2)}) collective-permute-start(f32[136,512]{1,0:T(8,128)S(1)} %get-tuple-element.34), channel_id=1, source_target_pairs={{0,32},{16,240},{32,64},{48,16},{64,96},{80,48},{96,128},{112,80},... | collective-permute-start | bytes 835592 | tf_op jit(solution)/shard_map/ppermute | solution.py:523
  59.2 7.4 %collective-permute-start.7 = (f32[72,512]{1,0:T(8,128)S(1)}, f32[72,512]{1,0:T(8,128)S(1)}, u32[]{:S(2)}, u32[]{:S(2)}) collective-permute-start(f32[72,512]{1,0:T(8,128)S(1)} %get-tuple-element.35), channel_id=1, source_target_pairs={{0,64},{16,208},{32,96},{48,240},{64,128},{80,16},{96,160},{112,48... | collective-permute-start | bytes 442376 | tf_op jit(solution)/shard_map/ppermute | solution.py:523
  66.6 5.5 %collective-permute-start.8 = (f32[136,512]{1,0:T(8,128)S(1)}, f32[136,512]{1,0:T(8,128)S(1)}, u32[]{:S(2)}, u32[]{:S(2)}) collective-permute-start(f32[136,512]{1,0:T(8,128)S(1)} %relayed_text_terms.1), channel_id=1, source_target_pairs={{0,32},{16,240},{32,64},{48,16},{64,96},{80,48},{96,128},{112,80},... | collective-permute-start | bytes 835592 | tf_op jit(solution)/shard_map/ppermute | solution.py:523
  72.2 7.1 %collective-permute-start.9 = (f32[72,512]{1,0:T(8,128)S(1)}, f32[72,512]{1,0:T(8,128)S(1)}, u32[]{:S(2)}, u32[]{:S(2)}) collective-permute-start(f32[72,512]{1,0:T(8,128)S(1)} %get-tuple-element.36), channel_id=1, source_target_pairs={{0,32},{16,240},{32,64},{48,16},{64,96},{80,48},{96,128},{112,80},... | collective-permute-start | bytes 442376 | tf_op jit(solution)/shard_map/ppermute | solution.py:523
  74.9 8.7 %collective-permute-start.10 = (f32[72,512]{1,0:T(8,128)S(1)}, f32[72,512]{1,0:T(8,128)S(1)}, u32[]{:S(2)}, u32[]{:S(2)}) collective-permute-start(f32[72,512]{1,0:T(8,128)S(1)} %get-tuple-element.37), channel_id=1, source_target_pairs={{0,48},{16,224},{32,80},{48,0},{64,112},{80,32},{96,144},{112,64},... | collective-permute-start | bytes 442376 | tf_op jit(solution)/shard_map/ppermute | solution.py:523

commit v11 on v10

--- a/solution.py
+++ b/solution.py
@@ -404,29 +404,6 @@
     )(*parts)
 
 
-def finish_kernel(one, two, own, out, note):
-    half = out.shape[0]
-    total = one[...] + two[...] + own[...]
-    out[...] = total[:half, :]
-    note[...] = total[half:, :LANES]
-
-
-def finished(one, two, own):
-    thin = own.shape[1]
-    return pl.pallas_call(
-        finish_kernel,
-        name="text_gradient_total",
-        out_shape=(
-            jax.ShapeDtypeStruct((own.shape[0] - NOTE, thin), F32),
-            jax.ShapeDtypeStruct((NOTE, LANES), F32),
-        ),
-        in_specs=[WHOLE] * 3,
-        out_specs=(WHOLE, WHOLE),
-        compiler_params=pltpu.CompilerParams(vmem_limit_bytes=4 * MIB),
-        cost_estimate=cost(own.size * 3, 16 * own.size),
-    )(one, two, own)
-
-
 def part_kernel(near, full, same, cross):
     half = same.shape[0] - NOTE
     core = lax.axis_index("img_1")
@@ -450,30 +427,38 @@
     )(near, full)
 
 
-def sum_kernel(row_share, col_share, parts, row_note, out, loss):
-    own = out.shape[0]
+def totals_kernel(row_share, col_share, one, two, own, parts, txt_out, img_out, loss):
+    half = txt_out.shape[0]
+    text = one[...] + two[...] + own[...]
+    txt_out[...] = text[:half, :]
+    size = img_out.shape[0]
 
     def total(down):
         return functools.reduce(jnp.add, [parts[k, down, :] for k in range(parts.shape[0])])
 
-    for b in range(out.shape[1] // LANES):
-        out[:, b * LANES : (b + 1) * LANES] = total(slice(b * own, (b + 1) * own))
+    for b in range(img_out.shape[1] // LANES):
+        img_out[:, b * LANES : (b + 1) * LANES] = total(slice(b * size, (b + 1) * size))
     col_note = total(slice(parts.shape[1] - NOTE, parts.shape[1]))
-    both = (0.5 * LN2) * (row_note[...] * row_share + col_note * col_share)
+    both = (0.5 * LN2) * (text[half:, :LANES] * row_share + col_note * col_share)
     loss[0, 0] = both[0, 0]
 
 
-def summed(row_share, col_share, parts, row_note, thin):
-    own = (parts.shape[1] - NOTE) * LANES // thin
-    return pl.pallas_call(
-        functools.partial(sum_kernel, row_share, col_share),
-        name="sum_of_image_parts_and_loss",
-        out_shape=(jax.ShapeDtypeStruct((own, thin), F32), jax.ShapeDtypeStruct((1, 1), F32)),
-        in_specs=[WHOLE] * 2,
-        out_specs=(WHOLE, pl.BlockSpec(memory_space=pltpu.SMEM)),
-        compiler_params=pltpu.CompilerParams(vmem_limit_bytes=4 * MIB),
-        cost_estimate=cost(parts.size, 4 * parts.size),
-    )(parts, row_note)
+def totals(row_share, col_share, one, two, own, parts):
+    thin = own.shape[1]
+    size = (parts.shape[1] - NOTE) * LANES // thin
+    return pl.pallas_call(
+        functools.partial(totals_kernel, row_share, col_share),
+        name="gradient_totals_and_loss",
+        out_shape=(
+            jax.ShapeDtypeStruct((own.shape[0] - NOTE, thin), F32),
+            jax.ShapeDtypeStruct((size, thin), F32),
+            jax.ShapeDtypeStruct((1, 1), F32),
+        ),
+        in_specs=[WHOLE] * 4,
+        out_specs=(WHOLE, WHOLE, pl.BlockSpec(memory_space=pltpu.SMEM)),
+        compiler_params=pltpu.CompilerParams(vmem_limit_bytes=5 * MIB),
+        cost_estimate=cost(parts.size + own.size * 3, 4 * parts.size + 16 * own.size),
+    )(one, two, own, parts)
 
 
 def turn(size, step):
@@ -525,9 +510,9 @@
     four = outward(four, 2)
     flow = relayed(two, outward(three, 1), four)
     same, cross = parted(one, outward(flow, 1))
-    grad_txt, row_total = finished(outward(same, 1), outward(cross, 1, 1), own)
-    grad_img, loss = summed(
-        1.0 / (rows * img_count), 1.0 / (cols * txt_count), got_img, row_total, thin
+    grad_txt, grad_img, loss = totals(
+        1.0 / (rows * img_count), 1.0 / (cols * txt_count),
+        outward(same, 1), outward(cross, 1, 1), own, got_img,
     )
     return (loss.reshape(()), grad_img, grad_txt)
 

time: 85.3 us -> 84.7 us (level)
  transfers between devices with their start and end apart: 13 -> 13, of which waited for: 9 -> 9; matrix products, arithmetic and copies ran while one was open for 0% -> 0% of each run, Pallas kernels for 1% -> 0%
where the time goes in v11:
time: 84.7 us; the launch traced here: 84.5 us
  starting transfers between devices  41.2 us (49%)
  waiting for transfers between devices  23 us (27%)
  Pallas kernels  19.6 us (23%)
    ppermute x5, waiting for transfers between devices, outward(): return lax.ppermute(value, IMG, pairs)  13.9 us
    ppermute x5, starting transfers between devices, outward(): return lax.ppermute(value, IMG, pairs)  13.5 us
    pallas_call x1, Pallas kernels, local_stats(): pl.pallas_call(kernel, name='logits_and_statistics', out_shape=(pltpu.HBM...  10.1 us
    pallas_call x1, Pallas kernels, gradients(): pl.pallas_call(functools.partial(delta_kernel, 3.0 / math.sqrt(thin)), na...  7.79 us
    ppermute x4, starting transfers between devices, neighbour(): return lax.ppermute(value, axis, pairs)  6.67 us
    all_to_all x1, starting transfers between devices, body(): col = lax.all_to_all(col, 'img_0', 0, 0, tiled=True)  6.46 us
    all_to_all x1, starting transfers between devices, body(): got_img = lax.all_to_all(to_img, TXT, 0, 0, tiled=True)  6.26 us
    ppermute x4, waiting for transfers between devices, neighbour(): return lax.ppermute(value, axis, pairs)  5.65 us
  transfers between devices with their start and end apart: 13, of which 9 were waited for; matrix products, arithmetic and copies ran while one was open for 0% of the time, Pallas kernels for 0%

profile of v11, /device:TPU:1, one launch (start us, length us, event | category | flops | bytes accessed | tf_op | source)
XLA Modules:
  0.0 84.5 jit_solution(3433379094555414372)
XLA Ops:
  0.6 10.1 %logits_and_statistics.1 = (f32[1024,1024]{1,0:T(8,128)}, f32[1024,1024]{1,0:T(8,128)}, f32[1,24,128]{2,1,0:T(8,128)S(1)}, f32[1,24,128]{2,1,0:T(8,128)S(1)}) custom-call(bf16[1024,1280]{1,0:T(8,128)(2,1)} %ti_hbm.1, bf16[1024,1280]{1,0:T(8,128)(2,1)} %tt_hbm.1, bf16[1024,512]{1,0:T(8,128)(2,1)} %refs_6_.1, bf16[1024,512]{1,0:T(8,128)(2,1)} %refs_5_.1), custom_call_target="tpu_custom_call" | custom-call | flops 3758096384 | bytes 8388608 | tf_op jit(solution)/shard_map/logits_and_statistics/pallas_call | solution.py:143
  10.7 3.3 %collective-permute-start.1 = (f32[24,128]{1,0:T(8,128)S(1)}, f32[24,128]{1,0:T(8,128)S(1)}, u32[]{:S(2)}, u32[]{:S(2)}) collective-permute-start(f32[24,128]{1,0:T(8,128)S(1)} %bitcast.12), channel_id=1, source_target_pairs={{0,16},{16,0},{1,17},{17,1},{2,18},{18,2},{3,19},{19,3},{4,20},{20... | collective-permute-start | bytes 36872 | tf_op jit(solution)/shard_map/ppermute | solution.py:487
  14.0 0.0 collective-permute-start
  14.0 0.8 collective-permute-done.1.refs_3_
  14.9 1.7 %collective-permute-done.refs_1_ = f32[24,128]{1,0:T(8,128)S(1)} collective-permute-done((f32[24,128]{1,0:T(8,128)S(1)}, f32[24,128]{1,0:T(8,128)S(1)}, u32[]{:S(2)}, u32[]{:S(2)}) %collective-permute-start) | collective-permute-done | bytes 12320 | tf_op jit(solution)/shard_map/ppermute | solution.py:482
  16.6 0.7 joined_statistics.3
  17.3 6.5 %all-to-all-start = ((f32[8,24,128]{2,1,0:T(8,128)}), f32[8,24,128]{2,1,0:T(8,128)S(1)}, u32[]{:S(2)}, u32[]{:S(2)}) async-start(f32[8,24,128]{2,1,0:T(8,128)} %get-tuple-element.25), calls=%async_computation | async-start | bytes 196608 | tf_op jit(solution)/shard_map/all_to_all | solution.py:489
  23.7 2.5 %collective-permute-start.2 = (f32[24,128]{1,0:T(8,128)S(1)}, f32[24,128]{1,0:T(8,128)S(1)}, u32[]{:S(2)}, u32[]{:S(2)}) collective-permute-start(f32[24,128]{1,0:T(8,128)S(1)} %bitcast.14), channel_id=1, source_target_pairs={{0,12},{4,8},{8,4},{12,0},{1,13},{5,9},{9,5},{13,1},{2,14},{6,10},... | collective-permute-start | bytes 36872 | tf_op jit(solution)/shard_map/ppermute | solution.py:482
  26.2 1.3 %collective-permute-done.2.refs_1_ = f32[24,128]{1,0:T(8,128)S(1)} collective-permute-done((f32[24,128]{1,0:T(8,128)S(1)}, f32[24,128]{1,0:T(8,128)S(1)}, u32[]{:S(2)}, u32[]{:S(2)}) %collective-permute-start.2) | collective-permute-done | bytes 12320 | tf_op jit(solution)/shard_map/ppermute | solution.py:482
  27.5 1.4 %collective-permute-start.3 = (f32[24,128]{1,0:T(8,128)S(1)}, f32[24,128]{1,0:T(8,128)S(1)}, u32[]{:S(2)}, u32[]{:S(2)}) collective-permute-start(f32[24,128]{1,0:T(8,128)S(1)} %bitcast.8), channel_id=1, source_target_pairs={{0,1},{1,0},{2,3},{3,2},{4,5},{5,4},{6,7},{7,6},{8,9},{9,8},{10,11... | collective-permute-start | bytes 36872 | tf_op jit(solution)/shard_map/ppermute | solution.py:482
  28.9 1.5 %collective-permute-done.3.refs_1_ = f32[24,128]{1,0:T(8,128)S(1)} collective-permute-done((f32[24,128]{1,0:T(8,128)S(1)}, f32[24,128]{1,0:T(8,128)S(1)}, u32[]{:S(2)}, u32[]{:S(2)}) %collective-permute-start.3) | collective-permute-done | bytes 12320 | tf_op jit(solution)/shard_map/ppermute | solution.py:482
  30.4 2.8 %collective-permute-start.4 = (f32[24,128]{1,0:T(8,128)S(1)}, f32[24,128]{1,0:T(8,128)S(1)}, u32[]{:S(2)}, u32[]{:S(2)}) collective-permute-start(f32[24,128]{1,0:T(8,128)S(1)} %bitcast.6), channel_id=1, source_target_pairs={{0,3},{1,2},{2,1},{3,0},{4,7},{5,6},{6,5},{7,4},{8,11},{9,10},{10,... | collective-permute-start | bytes 36872 | tf_op jit(solution)/shard_map/ppermute | solution.py:482
  33.2 1.1 %collective-permute-done.4.refs_1_ = f32[24,128]{1,0:T(8,128)S(1)} collective-permute-done((f32[24,128]{1,0:T(8,128)S(1)}, f32[24,128]{1,0:T(8,128)S(1)}, u32[]{:S(2)}, u32[]{:S(2)}) %collective-permute-start.4) | collective-permute-done | bytes 12320 | tf_op jit(solution)/shard_map/ppermute | solution.py:482
  34.3 0.0 all-to-all-done.refs_2_
  34.3 7.8 %delta_and_gradients.1 = (f32[16,264,128]{2,1,0:T(8,128)}, f32[552,512]{1,0:T(8,128)}, f32[552,512]{1,0:T(8,128)S(1)}) custom-call(f32[24,128]{1,0:T(8,128)S(1)} %bitcast.7, f32[24,128]{1,0:T(8,128)S(1)} %collective-permute-done.4.refs_1_, f32[8,24,128]{2,1,0:T(8,128)S(1)} %all-to-all-done.refs_2_, f32[1024,1024]{1,0:T(8,128)} %get-tuple-element.26.refs_3_, ...), custom_call_target="tpu_custom_call" | custom-call | flops 2147483648 | bytes 8388608 | tf_op jit(solution)/shard_map/delta_and_gradients/pallas_call | solution.py:335
  42.1 6.3 %all-to-all-start.1 = ((f32[16,264,128]{2,1,0:T(8,128)}), f32[16,264,128]{2,1,0:T(8,128)S(1)}, u32[]{:S(2)}, u32[]{:S(2)}) async-start(f32[16,264,128]{2,1,0:T(8,128)} %get-tuple-element.37), calls=%async_computation.1 | async-start | bytes 4325376 | tf_op jit(solution)/shard_map/all_to_all | solution.py:499
  48.4 5.0 %collective-permute-start.5 = (f32[552,512]{1,0:T(8,128)}, f32[552,512]{1,0:T(8,128)S(1)}, u32[]{:S(2)}, u32[]{:S(2)}) collective-permute-start(f32[552,512]{1,0:T(8,128)} %get-tuple-element.29), channel_id=1, source_target_pairs={{0,16},{16,0},{1,17},{17,1},{2,18},{18,2},{3,19},{19,3},{4,20},{20... | collective-permute-start | bytes 3391496 | tf_op jit(solution)/shard_map/ppermute | solution.py:500
  53.4 2.6 %collective-permute-done.5.theirs = f32[552,512]{1,0:T(8,128)S(1)} collective-permute-done((f32[552,512]{1,0:T(8,128)}, f32[552,512]{1,0:T(8,128)S(1)}, u32[]{:S(2)}, u32[]{:S(2)}) %collective-permute-start.5) | collective-permute-done | bytes 1130528 | tf_op jit(solution)/shard_map/ppermute | solution.py:500
  56.0 0.1 both_cores_text_terms.1
  56.2 3.0 %collective-permute-start.6 = (f32[136,512]{1,0:T(8,128)S(1)}, f32[136,512]{1,0:T(8,128)S(1)}, u32[]{:S(2)}, u32[]{:S(2)}) collective-permute-start(f32[136,512]{1,0:T(8,128)S(1)} %get-tuple-element.32), channel_id=1, source_target_pairs={{0,32},{16,240},{32,64},{48,16},{64,96},{80,48},{96,128},{112,80},... | collective-permute-start | bytes 835592 | tf_op jit(solution)/shard_map/ppermute | solution.py:508
  59.2 2.1 %collective-permute-start.7 = (f32[72,512]{1,0:T(8,128)S(1)}, f32[72,512]{1,0:T(8,128)S(1)}, u32[]{:S(2)}, u32[]{:S(2)}) collective-permute-start(f32[72,512]{1,0:T(8,128)S(1)} %get-tuple-element.33), channel_id=1, source_target_pairs={{0,64},{16,208},{32,96},{48,240},{64,128},{80,16},{96,160},{112,48... | collective-permute-start | bytes 442376 | tf_op jit(solution)/shard_map/ppermute | solution.py:508
  61.3 5.3 %collective-permute-done.7.refs_0_ = f32[72,512]{1,0:T(8,128)S(1)} collective-permute-done((f32[72,512]{1,0:T(8,128)S(1)}, f32[72,512]{1,0:T(8,128)S(1)}, u32[]{:S(2)}, u32[]{:S(2)}) %collective-permute-start.7) | collective-permute-done | bytes 147488 | tf_op jit(solution)/shard_map/ppermute | solution.py:508
  66.6 0.0 collective-permute-done.6.full
  66.6 1.3 %collective-permute-start.8 = (f32[136,512]{1,0:T(8,128)S(1)}, f32[136,512]{1,0:T(8,128)S(1)}, u32[]{:S(2)}, u32[]{:S(2)}) collective-permute-start(f32[136,512]{1,0:T(8,128)S(1)} %relayed_text_terms.1), channel_id=1, source_target_pairs={{0,32},{16,240},{32,64},{48,16},{64,96},{80,48},{96,128},{112,80},... | collective-permute-start | bytes 835592 | tf_op jit(solution)/shard_map/ppermute | solution.py:508
  67.9 4.2 %collective-permute-done.8.full = f32[136,512]{1,0:T(8,128)S(1)} collective-permute-done((f32[136,512]{1,0:T(8,128)S(1)}, f32[136,512]{1,0:T(8,128)S(1)}, u32[]{:S(2)}, u32[]{:S(2)}) %collective-permute-start.8) | collective-permute-done | bytes 278560 | tf_op jit(solution)/shard_map/ppermute | solution.py:508
  72.2 2.7 %collective-permute-start.9 = (f32[72,512]{1,0:T(8,128)S(1)}, f32[72,512]{1,0:T(8,128)S(1)}, u32[]{:S(2)}, u32[]{:S(2)}) collective-permute-start(f32[72,512]{1,0:T(8,128)S(1)} %get-tuple-element.34), channel_id=1, source_target_pairs={{0,32},{16,240},{32,64},{48,16},{64,96},{80,48},{96,128},{112,80},... | collective-permute-start | bytes 442376 | tf_op jit(solution)/shard_map/ppermute | solution.py:508
  74.9 4.3 %collective-permute-start.10 = (f32[72,512]{1,0:T(8,128)S(1)}, f32[72,512]{1,0:T(8,128)S(1)}, u32[]{:S(2)}, u32[]{:S(2)}) collective-permute-start(f32[72,512]{1,0:T(8,128)S(1)} %get-tuple-element.35), channel_id=1, source_target_pairs={{0,48},{16,224},{32,80},{48,0},{64,112},{80,32},{96,144},{112,64},... | collective-permute-start | bytes 442376 | tf_op jit(solution)/shard_map/ppermute | solution.py:508
  79.3 0.0 collective-permute-done.9.one
  79.3 4.4 %collective-permute-done.10.two = f32[72,512]{1,0:T(8,128)S(1)} collective-permute-done((f32[72,512]{1,0:T(8,128)S(1)}, f32[72,512]{1,0:T(8,128)S(1)}, u32[]{:S(2)}, u32[]{:S(2)}) %collective-permute-start.10) | collective-permute-done | bytes 147488 | tf_op jit(solution)/shard_map/ppermute | solution.py:508
  83.7 0.0 all-to-all-done.1.parts
  83.7 0.8 gradient_totals_and_loss.1
  (4 shorter events, 0.1 us)
Async XLA Ops:
  10.7 4.2 %collective-permute-start.1 = (f32[24,128]{1,0:T(8,128)S(1)}, f32[24,128]{1,0:T(8,128)S(1)}, u32[]{:S(2)}, u32[]{:S(2)}) collective-permute-start(f32[24,128]{1,0:T(8,128)S(1)} %bitcast.12), channel_id=1, source_target_pairs={{0,16},{16,0},{1,17},{17,1},{2,18},{18,2},{3,19},{19,3},{4,20},{20... | collective-permute-start | bytes 36872 | tf_op jit(solution)/shard_map/ppermute | solution.py:487
  14.0 2.6 %collective-permute-start = (f32[24,128]{1,0:T(8,128)S(1)}, f32[24,128]{1,0:T(8,128)S(1)}, u32[]{:S(2)}, u32[]{:S(2)}) collective-permute-start(f32[24,128]{1,0:T(8,128)S(1)} %bitcast.10), channel_id=1, source_target_pairs={{0,4},{4,0},{8,12},{12,8},{1,5},{5,1},{9,13},{13,9},{2,6},{6,2},{1... | collective-permute-start | bytes 36872 | tf_op jit(solution)/shard_map/ppermute | solution.py:482
  17.3 17.1 %all-to-all-start = ((f32[8,24,128]{2,1,0:T(8,128)}), f32[8,24,128]{2,1,0:T(8,128)S(1)}, u32[]{:S(2)}, u32[]{:S(2)}) async-start(f32[8,24,128]{2,1,0:T(8,128)} %get-tuple-element.25), calls=%async_computation | async-start | bytes 196608 | tf_op jit(solution)/shard_map/all_to_all | solution.py:489
  23.7 3.8 %collective-permute-start.2 = (f32[24,128]{1,0:T(8,128)S(1)}, f32[24,128]{1,0:T(8,128)S(1)}, u32[]{:S(2)}, u32[]{:S(2)}) collective-permute-start(f32[24,128]{1,0:T(8,128)S(1)} %bitcast.14), channel_id=1, source_target_pairs={{0,12},{4,8},{8,4},{12,0},{1,13},{5,9},{9,5},{13,1},{2,14},{6,10},... | collective-permute-start | bytes 36872 | tf_op jit(solution)/shard_map/ppermute | solution.py:482
  27.5 2.9 %collective-permute-start.3 = (f32[24,128]{1,0:T(8,128)S(1)}, f32[24,128]{1,0:T(8,128)S(1)}, u32[]{:S(2)}, u32[]{:S(2)}) collective-permute-start(f32[24,128]{1,0:T(8,128)S(1)} %bitcast.8), channel_id=1, source_target_pairs={{0,1},{1,0},{2,3},{3,2},{4,5},{5,4},{6,7},{7,6},{8,9},{9,8},{10,11... | collective-permute-start | bytes 36872 | tf_op jit(solution)/shard_map/ppermute | solution.py:482
  30.4 3.9 %collective-permute-start.4 = (f32[24,128]{1,0:T(8,128)S(1)}, f32[24,128]{1,0:T(8,128)S(1)}, u32[]{:S(2)}, u32[]{:S(2)}) collective-permute-start(f32[24,128]{1,0:T(8,128)S(1)} %bitcast.6), channel_id=1, source_target_pairs={{0,3},{1,2},{2,1},{3,0},{4,7},{5,6},{6,5},{7,4},{8,11},{9,10},{10,... | collective-permute-start | bytes 36872 | tf_op jit(solution)/shard_map/ppermute | solution.py:482
  42.1 41.5 %all-to-all-start.1 = ((f32[16,264,128]{2,1,0:T(8,128)}), f32[16,264,128]{2,1,0:T(8,128)S(1)}, u32[]{:S(2)}, u32[]{:S(2)}) async-start(f32[16,264,128]{2,1,0:T(8,128)} %get-tuple-element.37), calls=%async_computation.1 | async-start | bytes 4325376 | tf_op jit(solution)/shard_map/all_to_all | solution.py:499
  48.4 7.6 %collective-permute-start.5 = (f32[552,512]{1,0:T(8,128)}, f32[552,512]{1,0:T(8,128)S(1)}, u32[]{:S(2)}, u32[]{:S(2)}) collective-permute-start(f32[552,512]{1,0:T(8,128)} %get-tuple-element.29), channel_id=1, source_target_pairs={{0,16},{16,0},{1,17},{17,1},{2,18},{18,2},{3,19},{19,3},{4,20},{20... | collective-permute-start | bytes 3391496 | tf_op jit(solution)/shard_map/ppermute | solution.py:500
  56.2 10.4 %collective-permute-start.6 = (f32[136,512]{1,0:T(8,128)S(1)}, f32[136,512]{1,0:T(8,128)S(1)}, u32[]{:S(2)}, u32[]{:S(2)}) collective-permute-start(f32[136,512]{1,0:T(8,128)S(1)} %get-tuple-element.32), channel_id=1, source_target_pairs={{0,32},{16,240},{32,64},{48,16},{64,96},{80,48},{96,128},{112,80},... | collective-permute-start | bytes 835592 | tf_op jit(solution)/shard_map/ppermute | solution.py:508
  59.2 7.4 %collective-permute-start.7 = (f32[72,512]{1,0:T(8,128)S(1)}, f32[72,512]{1,0:T(8,128)S(1)}, u32[]{:S(2)}, u32[]{:S(2)}) collective-permute-start(f32[72,512]{1,0:T(8,128)S(1)} %get-tuple-element.33), channel_id=1, source_target_pairs={{0,64},{16,208},{32,96},{48,240},{64,128},{80,16},{96,160},{112,48... | collective-permute-start | bytes 442376 | tf_op jit(solution)/shard_map/ppermute | solution.py:508
  66.6 5.5 %collective-permute-start.8 = (f32[136,512]{1,0:T(8,128)S(1)}, f32[136,512]{1,0:T(8,128)S(1)}, u32[]{:S(2)}, u32[]{:S(2)}) collective-permute-start(f32[136,512]{1,0:T(8,128)S(1)} %relayed_text_terms.1), channel_id=1, source_target_pairs={{0,32},{16,240},{32,64},{48,16},{64,96},{80,48},{96,128},{112,80},... | collective-permute-start | bytes 835592 | tf_op jit(solution)/shard_map/ppermute | solution.py:508
  72.2 7.1 %collective-permute-start.9 = (f32[72,512]{1,0:T(8,128)S(1)}, f32[72,512]{1,0:T(8,128)S(1)}, u32[]{:S(2)}, u32[]{:S(2)}) collective-permute-start(f32[72,512]{1,0:T(8,128)S(1)} %get-tuple-element.34), channel_id=1, source_target_pairs={{0,32},{16,240},{32,64},{48,16},{64,96},{80,48},{96,128},{112,80},... | collective-permute-start | bytes 442376 | tf_op jit(solution)/shard_map/ppermute | solution.py:508
  74.9 8.7 %collective-permute-start.10 = (f32[72,512]{1,0:T(8,128)S(1)}, f32[72,512]{1,0:T(8,128)S(1)}, u32[]{:S(2)}, u32[]{:S(2)}) collective-permute-start(f32[72,512]{1,0:T(8,128)S(1)} %get-tuple-element.35), channel_id=1, source_target_pairs={{0,48},{16,224},{32,80},{48,0},{64,112},{80,32},{96,144},{112,64},... | collective-permute-start | bytes 442376 | tf_op jit(solution)/shard_map/ppermute | solution.py:508
